TPU v7x, 32 devices: a whole 2x2x4 slice. The times are simulated.
32 devices in a mesh: rep: 4 (over y, core), shard: 8 (over z, x).
Axes of the slice: x: 2, y: 2, z: 4, core: 2. Of those that a mesh axis runs over, the one named last changes fastest.
Arguments:
- inputs: bfloat16 [32, 1024, 768], P(('rep', 'shard')), may hold values from -6 to 6
- piece_starts: int32 [32, 2], P(('rep', 'shard')), may hold values from 0 to 768
- routes: int32 [32, 1024, 2], P(('rep', 'shard')), may hold values from 0 to 3, all different within a row; in each aligned block of 1024 rows (0 to 1023, 1024 to 2047, ..., all dimensions but the last counted through in order) at most 576 rows name the same one
- attn_gain: bfloat16 [768], P('shard'), may hold values from 0.099609375 to 1.8984375
- query_weight: bfloat16 [768, 768], P('shard'), may hold values from -0.21875 to 0.21875
- key_weight: bfloat16 [768, 768], P('shard'), may hold values from -0.21875 to 0.21875
- value_weight: bfloat16 [768, 768], P('shard'), may hold values from -0.21875 to 0.21875
- out_weight: bfloat16 [768, 768], P('shard'), may hold values from -1.75 to 1.75
- ffn_gain: bfloat16 [768], P('shard'), may hold values from 0.099609375 to 1.8984375
- router_weight: bfloat16 [768, 4], P('shard'), may hold values from -0.21875 to 0.21875
- expert_gate: bfloat16 [4, 768, 2048], P(None, None, 'shard'), may hold values from -0.21875 to 0.21875
- expert_up: bfloat16 [4, 768, 2048], P(None, None, 'shard'), may hold values from -0.21875 to 0.21875
- expert_down: bfloat16 [4, 2048, 768], P(None, 'shard'), may hold values from -0.375 to 0.375
- shared_gate: bfloat16 [768, 2048], P(None, 'shard'), may hold values from -0.21875 to 0.21875
- shared_up: bfloat16 [768, 2048], P(None, 'shard'), may hold values from -0.21875 to 0.21875
- shared_down: bfloat16 [2048, 768], P('shard'), may hold values from -0.25 to 0.25
- cotangent: bfloat16 [32, 1024, 768], P(('rep', 'shard')), may hold values from -6 to 6
Outputs:
- outputs: bfloat16 [32, 1024, 768], P(('rep', 'shard'))
- grad_inputs: float32 [32, 1024, 768], P(('rep', 'shard'))
- grad_attn_gain: float32 [768], P('shard')
- grad_query: float32 [768, 768], P('shard')
- grad_key: float32 [768, 768], P('shard')
- grad_value: float32 [768, 768], P('shard')
- grad_out: float32 [768, 768], P('shard')
- grad_ffn_gain: float32 [768], P('shard')
- grad_router: float32 [768, 4], P('shard')
- grad_expert_gate: float32 [4, 768, 2048], P(None, None, 'shard')
- grad_expert_up: float32 [4, 768, 2048], P(None, None, 'shard')
- grad_expert_down: float32 [4, 2048, 768], P(None, 'shard')
- grad_shared_gate: float32 [768, 2048], P(None, 'shard')
- grad_shared_up: float32 [768, 2048], P(None, 'shard')
- grad_shared_down: float32 [2048, 768], P('shard')
Inputs may be any that keep to these rules, and one draw needn't show every extreme that they name: `routes`: each token names 2 different experts. Among the 1024 tokens of one device (aligned blocks), every expert is named by at most 576 tokens, a bound that some block reaches.
All inputs are finite; a program needn't handle non-finite values.
Results may differ from a plain program's by a relative error of at most 0.019.
Values may be sent and summed in bfloat16 or wider, within the bound.
A program may use at most 384 MiB of HBM per device.

v0:
```python
import jax
import jax.numpy as jnp
from jax import lax
from jax.sharding import PartitionSpec as P

HEADS = 12
PIECE = 256
CAP = 576


epsilon = 1e-06
masked_score = -1e30


def rms_scale(tensor):
    return lax.rsqrt(jnp.mean(tensor * tensor, axis=-1, keepdims=True) + epsilon)


def norm_back(grad_normed, unit_rows, scale_rows, gain_row):
    grad_gain = jnp.sum(grad_normed * unit_rows, axis=0)
    scaled_grad = grad_normed * gain_row
    inner_mean = jnp.mean(scaled_grad * unit_rows, axis=-1, keepdims=True)
    return (grad_gain, scale_rows * (scaled_grad - unit_rows * inner_mean))


def rope_tables(length, head_dim):
    positions = jnp.arange(length, dtype=jnp.float32)
    inverse_freq = 10000.0 ** (-2.0 * jnp.arange(head_dim // 2, dtype=jnp.float32) / head_dim)
    angle_table = positions[:, None] * inverse_freq[None, :]
    return (jnp.cos(angle_table)[:, None, :], jnp.sin(angle_table)[:, None, :])


def rotate(tensor, cosine_table, sine_table):
    half_dim = tensor.shape[-1] // 2
    first_half = tensor[..., :half_dim]
    second_half = tensor[..., half_dim:]
    return jnp.concatenate(
        [
            first_half * cosine_table - second_half * sine_table,
            second_half * cosine_table + first_half * sine_table,
        ],
        axis=-1,
    )


def rotate_back(tensor, cosine_table, sine_table):
    half_dim = tensor.shape[-1] // 2
    first_half = tensor[..., :half_dim]
    second_half = tensor[..., half_dim:]
    return jnp.concatenate(
        [
            first_half * cosine_table + second_half * sine_table,
            second_half * cosine_table - first_half * sine_table,
        ],
        axis=-1,
    )


def allowed_mask(query_pos, key_pos, starts):
    causal = key_pos[None, :] <= query_pos[:, None]
    query_in = (query_pos[None, :] >= starts[:, None]) & (
        query_pos[None, :] < starts[:, None] + PIECE
    )
    key_in = (key_pos[None, :] >= starts[:, None]) & (key_pos[None, :] < starts[:, None] + PIECE)
    return causal | jnp.any(query_in[:, :, None] & key_in[:, None, :], axis=0)


def attend_forward(query_rot, key_rot, value_heads, starts, row_block):
    length, head_count, head_dim = query_rot.shape
    score_scale = head_dim ** (-0.5)
    key_pos = jnp.arange(length)

    def one_block(block_index):
        offset = block_index * row_block
        query_tile = lax.dynamic_slice_in_dim(query_rot, offset, row_block, 0)
        scores = (
            jnp.einsum("qhd,khd->hqk", query_tile, key_rot, preferred_element_type=jnp.float32)
            * score_scale
        )
        allowed = allowed_mask(offset + jnp.arange(row_block), key_pos, starts)
        scores = jnp.where(allowed[None], scores, masked_score)
        row_max = jnp.max(scores, axis=-1, keepdims=True)
        exp_scores = jnp.exp(scores - row_max)
        row_total = jnp.sum(exp_scores, axis=-1, keepdims=True)
        block_probs = (exp_scores / row_total).astype(jnp.bfloat16)
        mixed = jnp.einsum(
            "hqk,khd->qhd", block_probs, value_heads, preferred_element_type=jnp.float32
        )
        return (mixed, (row_max + jnp.log(row_total))[..., 0])

    mixed, log_totals = lax.map(one_block, jnp.arange(length // row_block))
    return (mixed.reshape(length, head_count, head_dim), log_totals)


def attend_backward(query_rot, key_rot, value_heads, starts, log_totals, grad_heads, row_block):
    length, head_count, head_dim = query_rot.shape
    score_scale = head_dim ** (-0.5)
    key_pos = jnp.arange(length)

    def one_block(running, block_index):
        grad_keys, grad_values = running
        offset = block_index * row_block
        query_tile = lax.dynamic_slice_in_dim(query_rot, offset, row_block, 0)
        grad_tile = lax.dynamic_slice_in_dim(grad_heads, offset, row_block, 0)
        scores = (
            jnp.einsum("qhd,khd->hqk", query_tile, key_rot, preferred_element_type=jnp.float32)
            * score_scale
        )
        allowed = allowed_mask(offset + jnp.arange(row_block), key_pos, starts)
        scores = jnp.where(allowed[None], scores, masked_score)
        block_probs = jnp.exp(scores - log_totals[block_index][..., None])
        grad_probs = jnp.einsum(
            "qhd,khd->hqk", grad_tile, value_heads, preferred_element_type=jnp.float32
        )
        row_inner = jnp.sum(grad_probs * block_probs, axis=-1, keepdims=True)
        grad_scores = (block_probs * (grad_probs - row_inner)).astype(jnp.bfloat16)
        grad_values = grad_values + jnp.einsum(
            "hqk,qhd->khd",
            block_probs.astype(jnp.bfloat16),
            grad_tile,
            preferred_element_type=jnp.float32,
        )
        grad_keys = grad_keys + jnp.einsum(
            "hqk,qhd->khd", grad_scores, query_tile, preferred_element_type=jnp.float32
        )
        grad_query = (
            jnp.einsum("hqk,khd->qhd", grad_scores, key_rot, preferred_element_type=jnp.float32)
            * score_scale
        )
        return ((grad_keys, grad_values), grad_query)

    empty = jnp.zeros((length, head_count, head_dim), jnp.float32)
    (grad_keys, grad_values), grad_query = lax.scan(
        one_block, (empty, empty), jnp.arange(length // row_block)
    )
    return (grad_query.reshape(length, head_count, head_dim), grad_keys * score_scale, grad_values)


def swiglu_back(grad_hidden, gate_h, up_h):
    sigmoid_gate = jax.nn.sigmoid(gate_h)
    grad_gate = (grad_hidden * up_h * sigmoid_gate * (1.0 + gate_h * (1.0 - sigmoid_gate))).astype(
        jnp.bfloat16
    )
    grad_up = (grad_hidden * gate_h * sigmoid_gate).astype(jnp.bfloat16)
    return (grad_gate, grad_up)


def body(
    inputs,
    piece_starts,
    routes,
    attn_gain,
    query_weight,
    key_weight,
    value_weight,
    out_weight,
    ffn_gain,
    router_weight,
    expert_gate,
    expert_up,
    expert_down,
    shared_gate,
    shared_up,
    shared_down,
    cotangent,
):
    seq_count, length, model_width = inputs.shape
    tokens = seq_count * length
    head_dim = model_width // HEADS
    row_block = min(512, length)
    capacity = CAP
    cosine_table, sine_table = rope_tables(length, head_dim)
    head_shape = (seq_count, length, HEADS, head_dim)
    gain_one, query_all, key_all, value_all, out_all, gain_two, router_all = (
        lax.all_gather(attn_gain, "shard", axis=0, tiled=True),
        lax.all_gather(query_weight, "shard", axis=0, tiled=True),
        lax.all_gather(key_weight, "shard", axis=0, tiled=True),
        lax.all_gather(value_weight, "shard", axis=0, tiled=True),
        lax.all_gather(out_weight, "shard", axis=0, tiled=True),
        lax.all_gather(ffn_gain, "shard", axis=0, tiled=True),
        lax.all_gather(router_weight, "shard", axis=0, tiled=True),
    )
    (
        expert_gates_all,
        expert_ups_all,
        expert_downs_all,
        shared_gate_all,
        shared_up_all,
        shared_down_all,
    ) = (
        lax.all_gather(expert_gate, "shard", axis=2, tiled=True),
        lax.all_gather(expert_up, "shard", axis=2, tiled=True),
        lax.all_gather(expert_down, "shard", axis=1, tiled=True),
        lax.all_gather(shared_gate, "shard", axis=1, tiled=True),
        lax.all_gather(shared_up, "shard", axis=1, tiled=True),
        lax.all_gather(shared_down, "shard", axis=0, tiled=True),
    )
    residual = inputs.reshape(tokens, model_width).astype(jnp.float32)
    scale_one = rms_scale(residual)
    unit_one = residual * scale_one
    normed_one = (unit_one * gain_one.astype(jnp.float32)).astype(jnp.bfloat16)
    query_rot = rotate(
        jnp.dot(normed_one, query_all, preferred_element_type=jnp.float32).reshape(head_shape),
        cosine_table,
        sine_table,
    ).astype(jnp.bfloat16)
    key_rot = rotate(
        jnp.dot(normed_one, key_all, preferred_element_type=jnp.float32).reshape(head_shape),
        cosine_table,
        sine_table,
    ).astype(jnp.bfloat16)
    value_heads = (
        jnp.dot(normed_one, value_all, preferred_element_type=jnp.float32)
        .astype(jnp.bfloat16)
        .reshape(head_shape)
    )
    attended, log_totals = lax.map(
        lambda entry: attend_forward(entry[0], entry[1], entry[2], entry[3], row_block),
        (query_rot, key_rot, value_heads, piece_starts),
    )
    attended = attended.reshape(tokens, model_width).astype(jnp.bfloat16)
    middle = residual + jnp.dot(attended, out_all, preferred_element_type=jnp.float32)
    scale_two = rms_scale(middle)
    unit_two = middle * scale_two
    normed_two = (unit_two * gain_two.astype(jnp.float32)).astype(jnp.bfloat16)
    logits = jnp.dot(normed_two, router_all, preferred_element_type=jnp.float32)
    router_probs = jax.nn.softmax(logits, axis=-1)
    expert_count = router_all.shape[1]
    expert_ids = jnp.arange(expert_count)
    flat_routes = routes.reshape(tokens, routes.shape[-1])
    chosen = jnp.sum(
        (flat_routes[:, :, None] == expert_ids[None, None, :]).astype(jnp.int32), axis=1
    )
    gate_probs = router_probs * chosen.astype(jnp.float32)
    slot_rank = jnp.cumsum(chosen, axis=0) - 1
    target = jnp.where(chosen > 0, slot_rank, capacity)
    slot_tokens = (
        jnp.zeros((expert_count, capacity), jnp.int32)
        .at[expert_ids[None, :], target]
        .set(jnp.arange(tokens, dtype=jnp.int32)[:, None], mode="drop")
    )
    slot_valid = (jnp.arange(capacity)[None, :] < jnp.sum(chosen, axis=0)[:, None]).astype(
        jnp.float32
    )
    slot_gates = gate_probs[slot_tokens, expert_ids[:, None]] * slot_valid
    expert_rows = normed_two[slot_tokens]
    gate_hidden = jnp.einsum(
        "ecd,edf->ecf", expert_rows, expert_gates_all, preferred_element_type=jnp.float32
    )
    up_hidden = jnp.einsum(
        "ecd,edf->ecf", expert_rows, expert_ups_all, preferred_element_type=jnp.float32
    )
    hidden = (jax.nn.silu(gate_hidden) * up_hidden).astype(jnp.bfloat16)
    expert_out = jnp.einsum(
        "ecf,efd->ecd", hidden, expert_downs_all, preferred_element_type=jnp.float32
    )
    mixture = (
        jnp.zeros((tokens, model_width), jnp.float32)
        .at[slot_tokens]
        .add(expert_out * slot_gates[..., None])
    )
    shared_gate_h = jnp.dot(normed_two, shared_gate_all, preferred_element_type=jnp.float32)
    shared_up_h = jnp.dot(normed_two, shared_up_all, preferred_element_type=jnp.float32)
    shared_hidden = (jax.nn.silu(shared_gate_h) * shared_up_h).astype(jnp.bfloat16)
    mixture = mixture + jnp.dot(shared_hidden, shared_down_all, preferred_element_type=jnp.float32)
    outputs = (middle + mixture).reshape(seq_count, length, model_width).astype(jnp.bfloat16)
    gain_one, query_all, key_all, value_all, out_all, gain_two, router_all = (
        lax.all_gather(attn_gain, "shard", axis=0, tiled=True),
        lax.all_gather(query_weight, "shard", axis=0, tiled=True),
        lax.all_gather(key_weight, "shard", axis=0, tiled=True),
        lax.all_gather(value_weight, "shard", axis=0, tiled=True),
        lax.all_gather(out_weight, "shard", axis=0, tiled=True),
        lax.all_gather(ffn_gain, "shard", axis=0, tiled=True),
        lax.all_gather(router_weight, "shard", axis=0, tiled=True),
    )
    (
        expert_gates_all,
        expert_ups_all,
        expert_downs_all,
        shared_gate_all,
        shared_up_all,
        shared_down_all,
    ) = (
        lax.all_gather(expert_gate, "shard", axis=2, tiled=True),
        lax.all_gather(expert_up, "shard", axis=2, tiled=True),
        lax.all_gather(expert_down, "shard", axis=1, tiled=True),
        lax.all_gather(shared_gate, "shard", axis=1, tiled=True),
        lax.all_gather(shared_up, "shard", axis=1, tiled=True),
        lax.all_gather(shared_down, "shard", axis=0, tiled=True),
    )
    grad_branch_out = cotangent.reshape(tokens, model_width)
    grad_output = grad_branch_out.astype(jnp.float32)
    grad_sdown = jnp.einsum(
        "tf,td->fd", shared_hidden, grad_branch_out, preferred_element_type=jnp.float32
    )
    grad_shidden = jnp.einsum(
        "td,fd->tf", grad_branch_out, shared_down_all, preferred_element_type=jnp.float32
    )
    grad_sgate_h, grad_sup_h = swiglu_back(grad_shidden, shared_gate_h, shared_up_h)
    grad_sgate = jnp.einsum(
        "td,tf->df", normed_two, grad_sgate_h, preferred_element_type=jnp.float32
    )
    grad_sup = jnp.einsum("td,tf->df", normed_two, grad_sup_h, preferred_element_type=jnp.float32)
    grad_normed_two = jnp.einsum(
        "tf,df->td", grad_sgate_h, shared_gate_all, preferred_element_type=jnp.float32
    )
    grad_normed_two = grad_normed_two + jnp.einsum(
        "tf,df->td", grad_sup_h, shared_up_all, preferred_element_type=jnp.float32
    )
    grad_rows = grad_output[slot_tokens]
    grad_expert_out = (grad_rows * slot_gates[..., None]).astype(jnp.bfloat16)
    grad_slot_gates = jnp.sum(grad_rows * expert_out, axis=-1) * slot_valid
    grad_edown = jnp.einsum(
        "ecf,ecd->efd", hidden, grad_expert_out, preferred_element_type=jnp.float32
    )
    grad_hidden = jnp.einsum(
        "ecd,efd->ecf", grad_expert_out, expert_downs_all, preferred_element_type=jnp.float32
    )
    grad_gate_h, grad_up_h = swiglu_back(grad_hidden, gate_hidden, up_hidden)
    grad_egate = jnp.einsum(
        "ecd,ecf->edf", expert_rows, grad_gate_h, preferred_element_type=jnp.float32
    )
    expert_up_gradient = jnp.einsum(
        "ecd,ecf->edf", expert_rows, grad_up_h, preferred_element_type=jnp.float32
    )
    grad_rows_in = jnp.einsum(
        "ecf,edf->ecd", grad_gate_h, expert_gates_all, preferred_element_type=jnp.float32
    )
    grad_rows_in = grad_rows_in + jnp.einsum(
        "ecf,edf->ecd", grad_up_h, expert_ups_all, preferred_element_type=jnp.float32
    )
    grad_normed_two = grad_normed_two.at[slot_tokens].add(grad_rows_in)
    grad_gates = (
        jnp.zeros((tokens, expert_count), jnp.float32)
        .at[slot_tokens, expert_ids[:, None]]
        .add(grad_slot_gates)
    )
    grad_logits = (
        router_probs * (grad_gates - jnp.sum(grad_gates * router_probs, axis=-1, keepdims=True))
    ).astype(jnp.bfloat16)
    grad_rout = jnp.einsum("td,te->de", normed_two, grad_logits, preferred_element_type=jnp.float32)
    grad_normed_two = grad_normed_two + jnp.einsum(
        "te,de->td", grad_logits, router_all, preferred_element_type=jnp.float32
    )
    grad_gain_two, grad_middle_norm = norm_back(
        grad_normed_two, unit_two, scale_two, gain_two.astype(jnp.float32)
    )
    grad_middle = grad_output + grad_middle_norm
    (
        expert_gate_shard,
        expert_up_shard,
        expert_down_shard,
        shared_gate_shard,
        shared_up_shard,
        shared_down_shard,
    ) = (
        lax.psum_scatter(grad_egate, "shard", scatter_dimension=2, tiled=True),
        lax.psum_scatter(expert_up_gradient, "shard", scatter_dimension=2, tiled=True),
        lax.psum_scatter(grad_edown, "shard", scatter_dimension=1, tiled=True),
        lax.psum_scatter(grad_sgate, "shard", scatter_dimension=1, tiled=True),
        lax.psum_scatter(grad_sup, "shard", scatter_dimension=1, tiled=True),
        lax.psum_scatter(grad_sdown, "shard", scatter_dimension=0, tiled=True),
    )
    (
        expert_gate_shard,
        expert_up_shard,
        expert_down_shard,
        shared_gate_shard,
        shared_up_shard,
        shared_down_shard,
    ) = (
        lax.psum(expert_gate_shard.astype(jnp.bfloat16), "rep").astype(jnp.float32),
        lax.psum(expert_up_shard.astype(jnp.bfloat16), "rep").astype(jnp.float32),
        lax.psum(expert_down_shard.astype(jnp.bfloat16), "rep").astype(jnp.float32),
        lax.psum(shared_gate_shard.astype(jnp.bfloat16), "rep").astype(jnp.float32),
        lax.psum(shared_up_shard.astype(jnp.bfloat16), "rep").astype(jnp.float32),
        lax.psum(shared_down_shard.astype(jnp.bfloat16), "rep").astype(jnp.float32),
    )
    grad_branch = grad_middle.astype(jnp.bfloat16)
    grad_wout = jnp.einsum("td,te->de", attended, grad_branch, preferred_element_type=jnp.float32)
    grad_attended = jnp.einsum(
        "te,de->td", grad_branch, out_all, preferred_element_type=jnp.float32
    ).astype(jnp.bfloat16)
    grad_qrot, grad_krot, grad_vheads = lax.map(
        lambda entry: attend_backward(
            entry[0], entry[1], entry[2], entry[3], entry[4], entry[5], row_block
        ),
        (
            query_rot,
            key_rot,
            value_heads,
            piece_starts,
            log_totals,
            grad_attended.reshape(head_shape),
        ),
    )
    grad_query_rows = (
        rotate_back(grad_qrot, cosine_table, sine_table)
        .reshape(tokens, model_width)
        .astype(jnp.bfloat16)
    )
    grad_key_rows = (
        rotate_back(grad_krot, cosine_table, sine_table)
        .reshape(tokens, model_width)
        .astype(jnp.bfloat16)
    )
    grad_value_rows = grad_vheads.reshape(tokens, model_width).astype(jnp.bfloat16)
    grad_wq = jnp.einsum(
        "td,te->de", normed_one, grad_query_rows, preferred_element_type=jnp.float32
    )
    grad_wk = jnp.einsum("td,te->de", normed_one, grad_key_rows, preferred_element_type=jnp.float32)
    grad_wv = jnp.einsum(
        "td,te->de", normed_one, grad_value_rows, preferred_element_type=jnp.float32
    )
    grad_normed_one = jnp.einsum(
        "te,de->td", grad_query_rows, query_all, preferred_element_type=jnp.float32
    )
    grad_normed_one = grad_normed_one + jnp.einsum(
        "te,de->td", grad_key_rows, key_all, preferred_element_type=jnp.float32
    )
    grad_normed_one = grad_normed_one + jnp.einsum(
        "te,de->td", grad_value_rows, value_all, preferred_element_type=jnp.float32
    )
    grad_gain_one, grad_in_norm = norm_back(
        grad_normed_one, unit_one, scale_one, gain_one.astype(jnp.float32)
    )
    grad_inputs = (grad_middle + grad_in_norm).reshape(seq_count, length, model_width)
    shard_gone, shard_wq, shard_wk, shard_wv, shard_wout, shard_gtwo, shard_rout = (
        lax.psum_scatter(grad_gain_one, "shard", scatter_dimension=0, tiled=True),
        lax.psum_scatter(grad_wq, "shard", scatter_dimension=0, tiled=True),
        lax.psum_scatter(grad_wk, "shard", scatter_dimension=0, tiled=True),
        lax.psum_scatter(grad_wv, "shard", scatter_dimension=0, tiled=True),
        lax.psum_scatter(grad_wout, "shard", scatter_dimension=0, tiled=True),
        lax.psum_scatter(grad_gain_two, "shard", scatter_dimension=0, tiled=True),
        lax.psum_scatter(grad_rout, "shard", scatter_dimension=0, tiled=True),
    )
    shard_gone, shard_wq, shard_wk, shard_wv, shard_wout, shard_gtwo, shard_rout = (
        lax.psum(shard_gone.astype(jnp.bfloat16), "rep").astype(jnp.float32),
        lax.psum(shard_wq.astype(jnp.bfloat16), "rep").astype(jnp.float32),
        lax.psum(shard_wk.astype(jnp.bfloat16), "rep").astype(jnp.float32),
        lax.psum(shard_wv.astype(jnp.bfloat16), "rep").astype(jnp.float32),
        lax.psum(shard_wout.astype(jnp.bfloat16), "rep").astype(jnp.float32),
        lax.psum(shard_gtwo.astype(jnp.bfloat16), "rep").astype(jnp.float32),
        lax.psum(shard_rout.astype(jnp.bfloat16), "rep").astype(jnp.float32),
    )
    return (
        outputs,
        grad_inputs,
        shard_gone,
        shard_wq,
        shard_wk,
        shard_wv,
        shard_wout,
        shard_gtwo,
        shard_rout,
        expert_gate_shard,
        expert_up_shard,
        expert_down_shard,
        shared_gate_shard,
        shared_up_shard,
        shared_down_shard,
    )


def solution(mesh):
    in_specs = (
        P(("rep", "shard"), None, None),
        P(("rep", "shard"), None),
        P(("rep", "shard"), None, None),
        P("shard"),
        P("shard", None),
        P("shard", None),
        P("shard", None),
        P("shard", None),
        P("shard"),
        P("shard", None),
        P(None, None, "shard"),
        P(None, None, "shard"),
        P(None, "shard", None),
        P(None, "shard"),
        P(None, "shard"),
        P("shard", None),
        P(("rep", "shard"), None, None),
    )
    out_specs = (
        P(("rep", "shard"), None, None),
        P(("rep", "shard"), None, None),
        P("shard"),
        P("shard", None),
        P("shard", None),
        P("shard", None),
        P("shard", None),
        P("shard"),
        P("shard", None),
        P(None, None, "shard"),
        P(None, None, "shard"),
        P(None, "shard", None),
        P(None, "shard"),
        P(None, "shard"),
        P("shard", None),
    )
    return jax.shard_map(body, mesh=mesh, in_specs=in_specs, out_specs=out_specs, check_vma=False)
```

profile of v0, /device:TPU:0, one launch (start us, length us, event | category | flops | bytes accessed | tf_op | source)
XLA Modules:
  0.0 3003.3 jit_solution(14191626839201032503)
XLA Ops:
  17.1 23.1 all-reduce.5
  41.4 12.6 all-gather.14.cloned.1.call-done
  55.6 40.5 %all-gather.12.cloned.1.call-done = bf16[768,768]{1,0:T(8,128)(2,1)} async-done(((bf16[96,768]{1,0:T(8,128)(2,1)}), bf16[768,768]{1,0:T(8,128)(2,1)}) %all-gather.12.cloned.1.call-update) | async-done | bytes 1179664 | tf_op jit(solution)/shard_map/all_gather | solution.py:176
  104.2 34.0 %all-gather.16.cloned.1.call-done = bf16[768,768]{1,0:T(8,128)(2,1)} async-done(((bf16[96,768]{1,0:T(8,128)(2,1)}), bf16[768,768]{1,0:T(8,128)(2,1)}) %all-gather.16.cloned.1.call-update) | async-done | bytes 1179664 | tf_op jit(solution)/shard_map/all_gather | solution.py:178
  142.1 77.3 %while.50 = (s32[]{:T(128)}, bf16[2,512,12,64]{1,3,2,0:T(8,128)(2,1)}, f32[2,12,512]{2,1,0:T(8,128)S(1)}, s32[2]{0:T(128)S(1)}, s32[2]{0:T(128)S(1)}, /*index=5*...) while((s32[]{:T(128)}, ...), condition=%wide.region_5.6_spmd.clone.clone, body=%wide.region_1.5_spmd.clone.clone.sunk | while | flops 1688735232 | bytes 191337248 | solution.py:91
  144.7 12.2 fusion.190
  156.8 12.4 fusion.191
  172.4 8.5 bitcast_dynamic-update-slice_fusion.4
  183.3 12.1 fusion.190
  195.4 12.4 fusion.191
  210.9 8.5 bitcast_dynamic-update-slice_fusion.4
  230.1 13.7 all-gather.20.cloned.1.call-done
  243.8 8.0 fusion.96
  251.8 55.2 %all-gather.22.cloned.1.call-done = bf16[768,2048]{1,0:T(8,128)(2,1)} async-done(((bf16[768,256]{1,0:T(8,128)(2,1)}), bf16[768,2048]{1,0:T(8,128)(2,1)}) %all-gather.22.cloned.1.call-update) | async-done | bytes 3145744 | tf_op jit(solution)/shard_map/all_gather | solution.py:195
  307.0 7.5 fusion.97
  314.5 53.4 %all-gather.24.cloned.1.call-done = bf16[2048,768]{1,0:T(8,128)(2,1)} async-done(((bf16[256,768]{1,0:T(8,128)(2,1)}), bf16[2048,768]{1,0:T(8,128)(2,1)}) %all-gather.24.cloned.1.call-update) | async-done | bytes 3145744 | tf_op jit(solution)/shard_map/all_gather | solution.py:196
  367.8 14.6 multiply_convert_fusion.4
  389.7 7.5 fusion.107
  398.2 17.9 all-gather
  419.0 15.5 scatter_custom_fusion.2
  440.5 7.9 gather_fusion.2
  452.0 18.8 gather_fusion.1
  470.9 7.9 gather_fusion
  479.5 8.3 fusion.50
  489.7 7.4 fusion.100
  502.2 42.9 %all-gather.26.cloned.1.call-done = bf16[4,768,2048]{2,1,0:T(8,128)(2,1)} async-done(((bf16[4,768,256]{2,1,0:T(8,128)(2,1)}), bf16[4,768,2048]{2,1,0:T(8,128)(2,1)}) %all-gather.26.cloned.1.call-update) | async-done | bytes 12582928 | tf_op jit(solution)/shard_map/all_gather | solution.py:191
  545.2 15.7 fusion.98
  560.9 161.1 %all-gather.28.cloned.1.call-done = bf16[4,768,2048]{2,1,0:T(8,128)(2,1)} async-done(((bf16[4,768,256]{2,1,0:T(8,128)(2,1)}), bf16[4,768,2048]{2,1,0:T(8,128)(2,1)}) %all-gather.28.cloned.1.call-update) | async-done | bytes 12582928 | tf_op jit(solution)/shard_map/all_gather | solution.py:192
  722.0 15.4 fusion.99
  737.5 161.3 %all-gather.30.cloned.1.call-done = bf16[4,2048,768]{2,1,0:T(8,128)(2,1)} async-done(((bf16[4,256,768]{2,1,0:T(8,128)(2,1)}), bf16[4,2048,768]{2,1,0:T(8,128)(2,1)}) %all-gather.30.cloned.1.call-update) | async-done | bytes 12582928 | tf_op jit(solution)/shard_map/all_gather | solution.py:193
  898.7 30.5 %multiply_convert_fusion.1 = (bf16[4,576,2048]{2,1,0:T(8,128)(2,1)}, bf16[4,576,2048]{2,1,0:T(8,128)(2,1)}, bf16[4,576,2048]{2,1,0:T(8,128)(2,1)}) fusion(f32[4,576,2048]{2,1,0:T(8,128)} %fusion.98, f32[4,576,2048]{2,1,0:T(8,128)} %fusion.99, bf16[4,2048,768]{2,1,0:T(8,128)(2,1)} %all-gather.30.cloned.1.call-done, f32[4,576,768]{2,1,0:T(8,128)} %bitcast.252, ...), kind=kOutput, calls=%fused_computation.58 | convolution fusion | flops 7326793728 | bytes 85730304 | tf_op jit(solution)/shard_map/ecd,efd->ecf/dot_general | solution.py:316
  929.3 16.9 multiply_reduce_fusion.1
  946.3 16.8 scatter_custom_fusion.3
  966.7 15.9 fusion.102
  982.6 16.5 convolution_add_fusion
  999.2 19.1 scatter_fusion.1
  1030.4 242.9 %while.51 = (s32[]{:T(128)}, f32[1024,12,64]{0,2,1:T(8,128)}, f32[1024,12,64]{0,2,1:T(8,128)}, f32[2,512,12,64]{1,0,3,2:T(2,128)}, s32[2]{0:T(128)S(1)}, /*index...) while((s32[]{:T(128)}, f32[1024,12,64]{0,2,1:T(8,128)}, ...), condition=%wide.region_23.24_spmd.clone.clone, body=%wide.region_20.23_spmd.clone.clone.sunk | while | flops 4127067648 | bytes 230879632 | solution.py:133
  1032.0 11.5 fusion.201
  1046.6 18.2 multiply_reduce_fusion.8
  1064.8 22.2 multiply_convert_fusion.12
  1087.0 9.9 multiply_bitcast_fusion.3
  1099.9 28.7 dynamic_update_slice.36
  1128.7 9.0 bitcast_add_fusion.4
  1137.7 13.3 bitcast_add_fusion.5
  1152.3 11.5 fusion.201
  1166.8 18.2 multiply_reduce_fusion.8
  1185.1 22.3 multiply_convert_fusion.12
  1207.4 9.8 multiply_bitcast_fusion.3
  1220.2 28.7 dynamic_update_slice.36
  1248.9 9.9 bitcast_add_fusion.4
  1258.9 14.2 bitcast_add_fusion.5
  1302.4 20.0 fusion.64
  1324.4 17.5 fusion.104
  1342.0 17.5 fusion.105
  1370.6 55.9 %reduce-scatter.14.cloned.1.call-done = f32[96,768]{1,0:T(8,128)} async-done(((f32[768,768]{1,0:T(8,128)}), f32[96,768]{1,0:T(8,128)}) %reduce-scatter.14.cloned.1.call-update) | async-done | bytes 294928 | tf_op jit(solution)/shard_map/reduce_scatter | solution.py:430
  1428.2 70.0 %reduce-scatter.18.cloned.1.call-done = f32[96,768]{1,0:T(8,128)} async-done(((f32[768,768]{1,0:T(8,128)}), f32[96,768]{1,0:T(8,128)}) %reduce-scatter.18.cloned.1.call-update) | async-done | bytes 294928 | tf_op jit(solution)/shard_map/reduce_scatter | solution.py:432
  1499.7 69.8 %reduce-scatter.20.cloned.1.call-done = f32[96,768]{1,0:T(8,128)} async-done(((f32[768,768]{1,0:T(8,128)}), f32[96,768]{1,0:T(8,128)}) %reduce-scatter.20.cloned.1.call-update) | async-done | bytes 294928 | tf_op jit(solution)/shard_map/reduce_scatter | solution.py:433
  1571.1 404.8 %reduce-scatter.26.cloned.1.call-done = f32[4,256,768]{2,1,0:T(8,128)} async-done(((f32[4,2048,768]{2,1,0:T(8,128)}), f32[4,256,768]{2,1,0:T(8,128)}) %reduce-scatter.26.cloned.1.call-update) | async-done | bytes 3145744 | tf_op jit(solution)/shard_map/reduce_scatter | solution.py:359
  1979.2 404.0 %reduce-scatter.22.cloned.1.call-done = f32[4,768,256]{2,1,0:T(8,128)} async-done(((f32[4,768,2048]{2,1,0:T(8,128)}), f32[4,768,256]{2,1,0:T(8,128)}) %reduce-scatter.22.cloned.1.call-update) | async-done | bytes 3145744 | tf_op jit(solution)/shard_map/reduce_scatter | solution.py:357
  2386.5 404.2 %reduce-scatter.24.cloned.1.call-done = f32[4,768,256]{2,1,0:T(8,128)} async-done(((f32[4,768,2048]{2,1,0:T(8,128)}), f32[4,768,256]{2,1,0:T(8,128)}) %reduce-scatter.24.cloned.1.call-update) | async-done | bytes 3145744 | tf_op jit(solution)/shard_map/reduce_scatter | solution.py:358
  2795.7 8.3 convolution_add_fusion.1
  2815.5 19.7 all-reduce.4
  2844.6 19.3 scatter_fusion
  2873.9 108.9 %all-reduce.10.cloned.1.call-done = (bf16[96,768]{1,0:T(8,128)(2,1)}, bf16[96,768]{1,0:T(8,128)(2,1)}, bf16[96,768]{1,0:T(8,128)(2,1)}, bf16[96,768]{1,0:T(8,128...) async-done(((bf16[96,768]{1,0:T(8,128)(2,1)}, ...) | async-done | bytes 6488080 | tf_op jit(solution)/shard_map/psum | solution.py:439
  (401 shorter events, 199.0 us)
Async XLA Ops:
  7.2 46.9 %all-gather.14.cloned.1.call-start = ((), (), s32[]{:S(2)}) async-start(), calls=%async_computation.12 | async-start | bytes 1327104 | tf_op jit(solution)/shard_map/all_gather | solution.py:177
  7.9 6.2 copy-start.25
  7.9 88.2 %all-gather.12.cloned.1.call-start = ((), (), s32[]{:S(2)}) async-start(), calls=%async_computation.11 | async-start | bytes 1327104 | tf_op jit(solution)/shard_map/all_gather | solution.py:176
  8.7 129.5 %all-gather.16.cloned.1.call-start = ((), (), s32[]{:S(2)}) async-start(), calls=%async_computation.13 | async-start | bytes 1327104 | tf_op jit(solution)/shard_map/all_gather | solution.py:178
  9.4 215.2 %all-gather.18.cloned.1.call-start = ((), (), s32[]{:S(2)}) async-start(), calls=%async_computation.14 | async-start | bytes 1327104 | tf_op jit(solution)/shard_map/all_gather | solution.py:179
  10.0 233.8 %all-gather.20.cloned.1.call-start = ((), (), s32[]{:S(2)}) async-start(), calls=%async_computation.15 | async-start | bytes 3538944 | tf_op jit(solution)/shard_map/all_gather | solution.py:194
  10.6 296.4 %all-gather.22.cloned.1.call-start = ((), (), s32[]{:S(2)}) async-start(), calls=%async_computation.16 | async-start | bytes 3538944 | tf_op jit(solution)/shard_map/all_gather | solution.py:195
  11.1 356.7 %all-gather.24.cloned.1.call-start = ((), (), s32[]{:S(2)}) async-start(), calls=%async_computation.17 | async-start | bytes 3538944 | tf_op jit(solution)/shard_map/all_gather | solution.py:196
  11.9 533.3 %all-gather.26.cloned.1.call-start = ((), (), s32[]{:S(2)}) async-start(), calls=%async_computation.18 | async-start | bytes 14155776 | tf_op jit(solution)/shard_map/all_gather | solution.py:191
  12.6 709.4 %all-gather.28.cloned.1.call-start = ((), (), s32[]{:S(2)}) async-start(), calls=%async_computation.19 | async-start | bytes 14155776 | tf_op jit(solution)/shard_map/all_gather | solution.py:192
  13.4 885.3 %all-gather.30.cloned.1.call-start = ((), (), s32[]{:S(2)}) async-start(), calls=%async_computation.20 | async-start | bytes 14155776 | tf_op jit(solution)/shard_map/all_gather | solution.py:193
  14.0 1349.2 %reduce-scatter.28.cloned.1.call-start = ((), (), s32[]{:S(2)}) async-start(), calls=%async_computation.28 | async-start | bytes 7077888 | tf_op jit(solution)/shard_map/reduce_scatter | solution.py:360
  14.9 123.3 %copy-start.13 = (bf16[1,1024,768]{1,2,0:T(8,128)(2,1)}, bf16[1,1024,768]{1,2,0:T(8,128)(2,1)S(1)}, u32[]{:S(2)}) copy-start(bf16[1,1024,768]{1,2,0:T(8,128)(2,1)S(1)} %copy.94) | copy-start | bytes 4718596
  15.3 122.9 %copy-start.67 = (f32[1024]{0:T(1024)}, f32[1024]{0:T(1024)S(1)}, u32[]{:S(2)}) copy-start(f32[1024]{0:T(1024)S(1)} %add_rsqrt_fusion.1) | copy-start | bytes 12292
  40.2 98.0 %copy-start.69 = (f32[768]{0:T(1024)}, f32[768]{0:T(1024)S(1)}, u32[]{:S(2)}) copy-start(f32[768]{0:T(1024)S(1)} %convert_element_type.232) | copy-start | bytes 9220
  40.7 60.8 %copy-start.34 = (f32[1024,32]{0,1:T(8,128)}, f32[1024,32]{0,1:T(8,128)S(1)}, u32[]{:S(2)}) copy-start(f32[1024,32]{0,1:T(8,128)S(1)} %get-tuple-element.452) | copy-start | bytes 393220
  40.7 60.8 %copy-start.36 = (f32[1024,32]{0,1:T(8,128)}, f32[1024,32]{0,1:T(8,128)S(1)}, u32[]{:S(2)}) copy-start(f32[1024,32]{0,1:T(8,128)S(1)} %get-tuple-element.453) | copy-start | bytes 393220
  104.1 38.0 %copy-start.46 = (s32[1,2]{1,0:T(1,128)S(1)}, s32[1,2]{1,0:T(1,128)}, u32[]{:S(2)}) copy-start(s32[1,2]{1,0:T(1,128)} %param.22) | copy-start | bytes 28
  144.7 24.6 copy-start.6
  156.8 15.6 copy-start
  183.2 24.5 copy-start.6
  195.4 15.5 copy-start
  219.4 5.3 copy-start.1
  219.4 5.3 copy-start.41
  219.4 5.3 copy-start.14
  230.1 159.6 %copy-start.11 = (bf16[1024,768]{0,1:T(8,128)(2,1)}, bf16[1024,768]{0,1:T(8,128)(2,1)S(1)}, u32[]{:S(2)}) copy-start(bf16[1024,768]{0,1:T(8,128)(2,1)S(1)} %multiply_convert_fusion.8) | copy-start | bytes 4718596
  251.8 116.0 %copy-start.26 = (bf16[1,1024,768]{2,1,0:T(8,128)(2,1)S(1)}, bf16[1,1024,768]{2,1,0:T(8,128)(2,1)}, u32[]{:S(2)}) copy-start(bf16[1,1024,768]{2,1,0:T(8,128)(2,1)} %param.37) | copy-start | bytes 4718596
  389.7 975.5 %reduce-scatter.30.cloned.1.call-start = ((), (), s32[]{:S(2)}) async-start(), calls=%async_computation.29 | async-start | bytes 7077888 | tf_op jit(solution)/shard_map/reduce_scatter | solution.py:361
  397.3 19.0 copy-start.74
  397.3 20.8 copy-start.81
  397.3 20.8 copy-start.80
  397.3 969.8 %reduce-scatter.32.cloned.1.call-start = ((), (), s32[]{:S(2)}) async-start(), calls=%async_computation.30 | async-start | bytes 7077888 | tf_op jit(solution)/shard_map/reduce_scatter | solution.py:362
  398.1 36.7 %copy-start.17 = (bf16[1,1024,768]{1,2,0:T(8,128)(2,1)}, bf16[1,1024,768]{1,2,0:T(8,128)(2,1)S(1)}, u32[]{:S(2)}) copy-start(bf16[1,1024,768]{1,2,0:T(8,128)(2,1)S(1)} %copy.105) | copy-start | bytes 4718596
  416.2 33.9 %copy-start.65 = (bf16[768,4]{0,1:T(4,128)(2,1)}, bf16[768,4]{0,1:T(4,128)(2,1)S(1)}, u32[]{:S(2)}) copy-start(bf16[768,4]{0,1:T(4,128)(2,1)S(1)} %reshape.728) | copy-start | bytes 18436
  416.3 62.5 %copy-start.75 = (s32[4]{0:T(128)}, s32[4]{0:T(128)S(1)}, u32[]{:S(2)}) copy-start(s32[4]{0:T(128)S(1)} %get-tuple-element.367) | copy-start | bytes 52
  434.9 5.6 copy-start.48
  451.9 18.9 copy-start.55
  451.9 18.9 copy-start.63
  470.9 8.6 copy-start.27
  487.8 881.2 %reduce-scatter.16.cloned.1.call-start = ((), (), s32[]{:S(2)}) async-start(), calls=%async_computation.22 | async-start | bytes 2654208 | tf_op jit(solution)/shard_map/reduce_scatter | solution.py:431
  489.7 7.5 copy-start.84
  489.7 7.5 copy-start.88
  497.1 48.0 %copy-start.23 = (bf16[2304,768]{1,0:T(8,128)(2,1)S(1)}, bf16[2304,768]{1,0:T(8,128)(2,1)}, u32[]{:S(2)}) copy-start(bf16[2304,768]{1,0:T(8,128)(2,1)} %gather_fusion) | copy-start | bytes 10616836
  898.7 30.5 %copy-start.72 = (f32[4,576]{1,0:T(4,128)S(1)}, f32[4,576]{1,0:T(4,128)}, u32[]{:S(2)}) copy-start(f32[4,576]{1,0:T(4,128)} %fusion.83) | copy-start | bytes 27652
  929.2 17.0 copy-start.76
  929.2 33.9 %copy-start.56 = (f32[1024]{0:T(1024)S(1)}, f32[1024]{0:T(1024)}, u32[]{:S(2)}) copy-start(f32[1024]{0:T(1024)} %copy-done.55) | copy-start | bytes 12292
  929.2 33.9 %copy-start.64 = (f32[1024]{0:T(1024)S(1)}, f32[1024]{0:T(1024)}, u32[]{:S(2)}) copy-start(f32[1024]{0:T(1024)} %copy-done.63) | copy-start | bytes 12292
  929.3 34.0 %copy-start.66 = (bf16[768,4]{0,1:T(4,128)(2,1)S(1)}, bf16[768,4]{0,1:T(4,128)(2,1)}, u32[]{:S(2)}) copy-start(bf16[768,4]{0,1:T(4,128)(2,1)} %copy-done.65) | copy-start | bytes 18436
  982.6 16.6 copy-start.49
  1044.6 20.2 copy-start.4
  1128.7 9.0 copy-start.5
  1128.7 9.1 copy-start.20
  1164.9 20.2 copy-start.4
  1248.9 9.9 copy-start.5
  1248.9 9.9 copy-start.20
  1273.3 5.8 copy-start.3
  1286.9 139.6 %reduce-scatter.14.cloned.1.call-start = ((), (), s32[]{:S(2)}) async-start(), calls=%async_computation.21 | async-start | bytes 2654208 | tf_op jit(solution)/shard_map/reduce_scatter | solution.py:430
  1291.1 207.0 %reduce-scatter.18.cloned.1.call-start = ((), (), s32[]{:S(2)}) async-start(), calls=%async_computation.23 | async-start | bytes 2654208 | tf_op jit(solution)/shard_map/reduce_scatter | solution.py:432
  1297.5 272.0 %reduce-scatter.20.cloned.1.call-start = ((), (), s32[]{:S(2)}) async-start(), calls=%async_computation.24 | async-start | bytes 2654208 | tf_op jit(solution)/shard_map/reduce_scatter | solution.py:433
  1302.4 673.6 %reduce-scatter.26.cloned.1.call-start = ((), (), s32[]{:S(2)}) async-start(), calls=%async_computation.27 | async-start | bytes 28311552 | tf_op jit(solution)/shard_map/reduce_scatter | solution.py:359
  1322.5 1060.8 %reduce-scatter.22.cloned.1.call-start = ((), (), s32[]{:S(2)}) async-start(), calls=%async_computation.25 | async-start | bytes 28311552 | tf_op jit(solution)/shard_map/reduce_scatter | solution.py:357
  1342.0 1448.6 %reduce-scatter.24.cloned.1.call-start = ((), (), s32[]{:S(2)}) async-start(), calls=%async_computation.26 | async-start | bytes 28311552 | tf_op jit(solution)/shard_map/reduce_scatter | solution.py:358
  1359.5 1505.7 %reduce-scatter.34.cloned.1.call-start = ((), (), s32[]{:S(2)}) async-start(), calls=%async_computation.31 | async-start | bytes 442368
  1362.2 1620.6 %all-reduce.10.cloned.1.call-start = ((), (), s32[]{:S(2)}) async-start(), calls=%async_computation.32 | async-start | bytes 12976128 | tf_op jit(solution)/shard_map/psum | solution.py:439
  (53 other events, 139.6 us)
Sparse Core Ops, SparseCore 0:
  10.2 43.8 all-gather.13
  56.2 39.8 all-gather.11
  98.3 39.8 all-gather.15
  140.2 39.8 all-gather.17
  181.9 61.8 all-gather.19
  245.7 61.2 all-gather.21
  309.1 58.6 all-gather.23
  369.9 175.2 all-gather.25
  547.2 174.7 all-gather.27
  724.1 174.6 all-gather.29
  902.3 116.5 reduce-scatter.27
  1022.4 117.5 reduce-scatter.29
  1143.5 117.0 reduce-scatter.31
  1287.0 67.5 reduce-scatter.15
  1358.5 67.9 reduce-scatter.13
  1429.9 68.2 reduce-scatter.17
  1501.4 68.0 reduce-scatter.19
  1573.2 402.7 reduce-scatter.25
  1979.9 403.3 reduce-scatter.21
  2387.0 403.5 reduce-scatter.23
  2794.5 60.4 reduce-scatter.33
  2859.2 123.5 all-reduce.9
where the time goes:
time: 3020 us; the launch traced here: 3000 us
  waiting for transfers between devices  2100 us (70%)
  matrix products  446 us (15%)
  other arithmetic  192 us (6%)
  local copies, waits for them, and re-layouts  173 us (6%)
  blocking collectives  66.9 us (2%)
    reduce_scatter x1, waiting for transfers between devices, body(): lax.psum_scatter(grad_edown, 'shard', scatter_dimension=1, tiled=True)  405 us
    reduce_scatter x1, waiting for transfers between devices, body(): lax.psum_scatter(expert_up_gradient, 'shard', scatter_dimension=2, tiled=...  404 us
    reduce_scatter x1, waiting for transfers between devices, body(): lax.psum_scatter(grad_egate, 'shard', scatter_dimension=2, tiled=True)  404 us
    all_gather x1, waiting for transfers between devices, body(): lax.all_gather(expert_down, 'shard', axis=1, tiled=True)  161 us
    all_gather x1, waiting for transfers between devices, body(): lax.all_gather(expert_up, 'shard', axis=2, tiled=True)  161 us
    psum x1, waiting for transfers between devices, body(): lax.psum(shard_wq.astype(jnp.bfloat16), 'rep').astype(jnp.float32)  109 us
    reduce_scatter x1, waiting for transfers between devices, body(): lax.psum_scatter(grad_wv, 'shard', scatter_dimension=0, tiled=True)  70 us
    reduce_scatter x1, waiting for transfers between devices, body(): lax.psum_scatter(grad_wout, 'shard', scatter_dimension=0, tiled=True)  69.8 us
  transfers between devices with their start and end apart: 22, of which 16 were waited for; matrix products, arithmetic and copies ran while one was open for 26% of the time, Pallas kernels for 0%

commit v1 on v0

v1 whole, which is shorter than its diff:
```python
import functools

import jax
import jax.numpy as jnp
from jax import lax
from jax.experimental import pallas as pl
from jax.experimental.pallas import tpu as pltpu
from jax.sharding import PartitionSpec as P

HEADS = 12
PIECE = 256
CAP = 576
EPSILON = 1e-06
MASKED = -1e30
F32, BF = jnp.float32, jnp.bfloat16
AXES = ("rep", "shard")
TILE = 256
SLOTS = 8
VMEM_LIMIT = 62 * 2**20
ANY = pl.BlockSpec(memory_space=pl.ANY)
SMEM = pl.BlockSpec(memory_space=pltpu.SMEM)
VMEM = pl.BlockSpec(memory_space=pltpu.VMEM)


def dot(a, b, i, j):
    return lax.dot_general(a, b, (((i,), (j,)), ((), ())), preferred_element_type=F32)


def nn(a, b):
    return dot(a, b, 1, 0)


def nt(a, b):
    return dot(a, b, 1, 1)


def tn(a, b):
    return dot(a, b, 0, 0)


def iota(shape, dim):
    return lax.broadcasted_iota(jnp.int32, shape, dim)


def ones_where(cond):
    return jnp.where(cond, 1.0, 0.0).astype(BF)


def call(kernel, out_shape, in_specs, out_specs, scratch=(), flops=0, moved=0, grid=None):
    extra = {} if grid is None else {"grid": grid}
    return pl.pallas_call(
        kernel,
        out_shape=out_shape,
        in_specs=in_specs,
        out_specs=out_specs,
        scratch_shapes=list(scratch),
        compiler_params=pltpu.CompilerParams(vmem_limit_bytes=VMEM_LIMIT),
        cost_estimate=pl.CostEstimate(flops=flops, bytes_accessed=moved, transcendentals=0),
        **extra,
    )


def shape(dims, dtype=BF):
    return jax.ShapeDtypeStruct(dims, dtype)


def permute(x, move):
    reps, shards = lax.axis_size("rep"), lax.axis_size("shard")
    pairs = []
    for r in range(reps):
        for s in range(shards):
            to_r, to_s = move(r, s)
            pairs.append((r * shards + s, to_r * shards + to_s))
    return lax.ppermute(x, AXES, pairs)


def to_rep(x, offset):
    return permute(x, lambda r, s: (r ^ offset, s))


def to_x(x):
    return permute(x, lambda r, s: (r, s ^ 1))


def to_z(x, d):
    shards = lax.axis_size("shard")
    return permute(x, lambda r, s: (r, (s + 2 * d) % shards))


def after(x, dep):
    return lax.optimization_barrier((x, dep))[0]


def gather_slots(piece):
    near = [piece] + [to_z(piece, -d) for d in (1, 2, 3)]
    return near + [to_x(part) for part in near]


def scatter_slots(parts):
    far = [to_x(parts[4 + d]) for d in range(4)]
    near = [(parts[d].astype(F32) + far[d].astype(F32)) for d in range(4)]
    got = [to_z(near[d].astype(BF), d).astype(F32) for d in (1, 2, 3)]
    return near[0] + got[0] + got[1] + got[2]


def prep_kernel(info, routes, routes_t, cot, rank_out, slot_out, *packed):
    tokens = cot.shape[0]
    rep = info[0]
    first, second = routes_t[0:1, :], routes_t[1:2, :]
    expert = iota((8, tokens), 0)
    chosen = (expert == first) | (expert == second)
    upper = ones_where(iota((tokens, tokens), 0) <= iota((tokens, tokens), 1))
    rank = nn(ones_where(chosen), upper) - 1.0
    rank_out[...] = jnp.where(chosen, rank, -1.0)
    lane = iota((tokens, 128), 1)
    one, two = routes[:, 0:1], routes[:, 1:2]
    lower = ones_where(iota((tokens, tokens), 0) >= iota((tokens, tokens), 1))
    place = nn(lower, ones_where((lane == one) | (lane == two))) - 1.0
    place = place + ((lane ^ rep) * CAP).astype(F32)
    slot_one = jnp.sum(jnp.where(lane == one, place, 0.0), axis=1, keepdims=True)
    slot_two = jnp.sum(jnp.where(lane == two, place, 0.0), axis=1, keepdims=True)
    slot_out[...] = jnp.where(lane < 64, slot_one, slot_two)
    for o, out in enumerate(packed):
        row = rank_out[pl.ds(rep ^ o, 1), :]
        pick = ones_where(iota((CAP, tokens), 0).astype(F32) == row)
        out[...] = nn(pick, cot[...]).astype(BF)


def spin(block, cosine, sine):
    lane = iota(block.shape, 1)
    partner = jnp.where(lane % 64 < 32, pltpu.roll(block, 96, 1), pltpu.roll(block, 32, 1))
    return block * cosine + partner * sine


def qkv_kernel(
    info, x, own, other, cosine, sine, q, k, v, wq, wk, wv, wo, ext, ext_all, sems
):
    tokens, width = x.shape
    rows = own.shape[1] - 16
    half = rows // 2

    def copies(low, high):
        made = []
        for j in range(SLOTS):
            at = pl.ds(pl.multiple_of(info[2 + j] * half, 32), half)
            made.append((low.at[j, pl.ds(0, half)], wq.at[at]))
            made.append((low.at[j, pl.ds(half, half)], wk.at[at]))
            made.append((low.at[j, pl.ds(rows, 16)], ext_all.at[j]))
            made.append((high.at[j, pl.ds(0, half)], wv.at[at]))
            made.append((high.at[j, pl.ds(half, half)], wo.at[at]))
        return [pltpu.make_async_copy(a, b, sems.at[i]) for i, (a, b) in enumerate(made)]

    @pl.when(info[1] == 0)
    def _():
        for copy in copies(own, other):
            copy.start()

    @pl.when(info[1] != 0)
    def _():
        for copy in copies(other, own):
            copy.start()

    for copy in copies(own, other):
        copy.wait()
    gathered = ext_all[0].astype(F32)
    for j in range(1, SLOTS):
        gathered = gathered + ext_all[j].astype(F32)
    ext[...] = gathered
    gain = gathered[4:5, :]

    def tile(t, carry):
        at = pl.ds(pl.multiple_of(t * TILE, TILE), TILE)
        rows_in = x[at, :].astype(F32)
        scale = lax.rsqrt(jnp.mean(rows_in * rows_in, axis=1, keepdims=True) + EPSILON)
        normed = (rows_in * scale * gain).astype(BF)
        cos_t, sin_t = cosine[at, :], sine[at, :]
        for weight, out, factor in ((wq, q, 0.125), (wk, k, 1.0)):
            full = nn(normed, weight[...])
            for b in range(width // 128):
                turned = spin(full[:, b * 128 : (b + 1) * 128], cos_t, sin_t)
                out[at, b * 128 : (b + 1) * 128] = turned.astype(BF) * jnp.asarray(factor, BF)
        v[at, :] = nn(normed, wv[...]).astype(BF)
        return carry

    lax.fori_loop(0, tokens // TILE, tile, 0)


def fill_bias(starts, bias):
    tokens = bias.shape[0]

    def tile(t, carry):
        at = pl.ds(pl.multiple_of(t * TILE, TILE), TILE)
        query = iota((TILE, tokens), 0) + t * TILE
        key = iota((TILE, tokens), 1)
        allowed = key <= query
        for n in range(2):
            begin = starts[0, n]
            inside = (query >= begin) & (query < begin + PIECE)
            allowed = allowed | (inside & (key >= begin) & (key < begin + PIECE))
        bias[at, :] = jnp.where(allowed, 0.0, MASKED)
        return carry

    lax.fori_loop(0, tokens // TILE, tile, 0)


def keep_half(block, h):
    low = iota(block.shape, 1) < 64
    return jnp.where(low if h == 0 else ~low, block.astype(F32), 0.0).astype(BF)


def biased(scores, bias, begin, free, end):
    tail = scores[:, free:] + bias[begin : begin + TILE, free:end]
    return tail if free == 0 else jnp.concatenate([scores[:, :free], tail], axis=1)


def attend_kernel(starts, q, k, v, out, lse, bias):
    tokens = q.shape[0]

    @pl.when(pl.program_id(0) == 0)
    def _():
        fill_bias(starts, bias)

    keys = k[...]
    low = iota((tokens, 128), 1) < 64
    values = v[...].astype(F32)
    value_one = [
        jnp.where(low, values, 1.0).astype(BF),
        jnp.where(low, 1.0, values).astype(BF),
    ]
    low = iota((TILE, 128), 1) < 64
    for t in range(tokens // TILE):
        begin = t * TILE
        end = min(tokens, begin + TILE + PIECE)
        block = q[begin : begin + TILE, :]
        results, totals = [], []
        for h in range(2):
            scores = nt(keep_half(block, h), keys[:end])
            scores = biased(scores, bias, begin, begin, end)
            row_max = jnp.max(scores, axis=1, keepdims=True)
            probs = jnp.exp(scores - row_max).astype(BF)
            mixed = nn(probs, value_one[h][:end])
            total = pltpu.roll(mixed, 64, 1)
            results.append(mixed / total)
            totals.append(row_max + jnp.log(total))
        out[begin : begin + TILE, :] = jnp.where(low, results[0], results[1]).astype(BF)
        lse[begin : begin + TILE, :] = jnp.where(low, totals[0], totals[1])


def router_rows(ext):
    rows = jnp.where(iota(ext.shape, 0) < 4, ext[...], 0.0)
    return jnp.concatenate([rows, jnp.zeros((112, ext.shape[1]), F32)], axis=0).astype(BF)


def route_probs(normed, router):
    logits = nt(normed, router)
    logits = jnp.where(iota(logits.shape, 1) < 4, logits, MASKED)
    raised = jnp.exp(logits - jnp.max(logits, axis=1, keepdims=True))
    return raised / jnp.sum(raised, axis=1, keepdims=True)


def middle_kernel(info, x, attended, wo, ext, rank, middle, normed, probs, *packed):
    tokens = x.shape[0]
    rep = info[0]
    gain = ext[5:6, :]
    router = router_rows(ext)

    def tile(t, carry):
        at = pl.ds(pl.multiple_of(t * TILE, TILE), TILE)
        rows = x[at, :].astype(F32) + nn(attended[at, :], wo[...])
        scale = lax.rsqrt(jnp.mean(rows * rows, axis=1, keepdims=True) + EPSILON)
        middle[at, :] = rows
        unit = (rows * scale * gain).astype(BF)
        normed[at, :] = unit
        probs[at, :] = route_probs(unit, router)
        return carry

    lax.fori_loop(0, tokens // TILE, tile, 0)
    for o, out in enumerate(packed):
        row = rank[pl.ds(rep ^ o, 1), :]
        pick = ones_where(iota((CAP, tokens), 0).astype(F32) == row)
        out[...] = nn(pick, normed[...]).astype(BF)


CHUNK = 512


def ffn_kernel(blocks, weights, unit, routed, chained, *refs):
    refs = list(refs)

    def take(n):
        taken = refs[:n]
        del refs[:n]
        return taken

    info, ext = take(2)
    xs, cs = take(blocks), take(blocks)
    slots = take(weights)
    before = take(weights) if chained else None
    outs, dxs = take(blocks), take(blocks)
    grads = take(weights)
    out_acc, dx_acc, gate, wbuf, dw_acc, dw_out = take(6)
    prior = take(1)[0] if chained else None
    in_sems, out_sems = take(2)
    prior_sems = take(1)[0] if chained else None
    rows = xs[0].shape[0]
    per = CHUNK // unit
    chunks = 4

    def pieces(k, banks):
        return [(banks[i // SLOTS], i % SLOTS) for i in range(k * per, (k + 1) * per)]

    def view(bank, j):
        return bank

    def ref_of(banks, k, i):
        n = k * per + i
        if weights == SLOTS:
            return banks[n]
        return banks[n % 2].at[n // 2]

    def loads(banks, buffer, sems, k, b):
        return [
            pltpu.make_async_copy(
                ref_of(banks, k, i), buffer.at[b, :, :, pl.ds(i * unit, unit)], sems.at[b, i]
            )
            for i in range(per)
        ]

    def stores(k, b):
        return [
            pltpu.make_async_copy(
                dw_out.at[b, :, :, pl.ds(i * unit, unit)], ref_of(grads, k, i), out_sems.at[b, i]
            )
            for i in range(per)
        ]

    def start_loads(k, b):
        for copy in loads(slots, wbuf, in_sems, k, b):
            copy.start()
        if chained:
            for copy in loads(before, prior, prior_sems, k, b):
                copy.start()

    start_loads(0, 0)
    if routed:
        router = router_rows(ext)
        for n in range(blocks):
            probs = route_probs(xs[n][...], router)
            lane = iota(probs.shape, 1)
            gate[n] = jnp.sum(jnp.where(lane == info[0], probs, 0.0), axis=1, keepdims=True)

    def chunk(k, carry):
        b = lax.rem(k, 2)
        for nxt in range(1, chunks):

            @pl.when(k + 1 == nxt)
            def _():
                start_loads(nxt, nxt % 2)

        for copy in loads(slots, wbuf, in_sems, 0, b):
            copy.wait()
        for n in range(blocks):
            x, c = xs[n][...], cs[n][...]
            wg, wu, wd = wbuf[b, 0], wbuf[b, 1], wbuf[b, 2]
            gate_h, up_h, back_h = nn(x, wg), nn(x, wu), nn(c, wd)
            sigma = 1.0 / (1.0 + jnp.exp(-gate_h))
            silu = gate_h * sigma
            hidden = silu * up_h
            if routed:
                share = gate[n]
                scaled = back_h * share
                weighted = (hidden * share).astype(BF)
            else:
                scaled, weighted = back_h, hidden.astype(BF)
            d_up = (scaled * silu).astype(BF)
            d_gate = (scaled * up_h * (sigma + silu * (1.0 - sigma))).astype(BF)
            product = nt(hidden.astype(BF), wd)
            d_rows = nt(d_gate, wg) + nt(d_up, wu)
            parts = (tn(x, d_gate), tn(x, d_up), tn(c, weighted))
            if routed:
                pairs = (hidden * back_h).astype(BF)
                d_share = nt(jnp.ones((16, CHUNK), BF), pairs)

            @pl.when(k == 0)
            def _():
                out_acc[n] = product
                dx_acc[n, 0:rows, :] = d_rows
                if routed:
                    dx_acc[n, rows : rows + 16, :] = jnp.zeros((16, d_rows.shape[1]), F32)
                    dx_acc[n, rows : rows + 16, 0:rows] = d_share

            @pl.when(k != 0)
            def _():
                out_acc[n] += product
                dx_acc[n, 0:rows, :] += d_rows
                if routed:
                    dx_acc[n, rows : rows + 16, 0:rows] += d_share

            for i in range(3):
                if n == 0:
                    dw_acc[i] = parts[i]
                else:
                    dw_acc[i] += parts[i]

        @pl.when(k >= 2)
        def _():
            for copy in stores(0, b):
                copy.wait()

        if chained:
            for copy in loads(before, prior, prior_sems, 0, b):
                copy.wait()
            for i in range(3):
                dw_out[b, i] = (dw_acc[i] + prior[b, i].astype(F32)).astype(BF)
        else:
            for i in range(3):
                dw_out[b, i] = dw_acc[i].astype(BF)
        for now in range(chunks):

            @pl.when(k == now)
            def _():
                for copy in stores(now, now % 2):
                    copy.start()

        return carry

    lax.fori_loop(0, chunks, chunk, 0)
    for n in range(blocks):
        outs[n][...] = out_acc[n].astype(BF)
        dxs[n][...] = dx_acc[n].astype(BF)
    for b in range(2):
        for copy in stores(0, b):
            copy.wait()


def ffn(info, ext, xs, cs, slots, before, unit, routed):
    blocks, rows, width = len(xs), xs[0].shape[0], xs[0].shape[1]
    chained = before is not None
    extra = 16 if routed else 0
    weights = len(slots)
    per = CHUNK // unit
    operands = [info, ext, *xs, *cs, *slots] + (list(before) if chained else [])
    in_specs = [SMEM, VMEM] + [VMEM] * (2 * blocks) + [ANY] * (weights * (2 if chained else 1))
    outs = [shape((rows, width))] * blocks + [shape((rows + extra, width))] * blocks
    outs += [shape(w.shape) for w in slots]
    out_specs = [VMEM] * (2 * blocks) + [ANY] * weights
    scratch = [
        pltpu.VMEM((blocks, rows, width), F32),
        pltpu.VMEM((blocks, rows + extra, width), F32),
        pltpu.VMEM((blocks, rows, 1), F32),
        pltpu.VMEM((2, 3, width, CHUNK), BF),
        pltpu.VMEM((3, width, CHUNK), F32),
        pltpu.VMEM((2, 3, width, CHUNK), BF),
    ]
    if chained:
        scratch.append(pltpu.VMEM((2, 3, width, CHUNK), BF))
    scratch += [pltpu.SemaphoreType.DMA((2, per)), pltpu.SemaphoreType.DMA((2, per))]
    if chained:
        scratch.append(pltpu.SemaphoreType.DMA((2, per)))
    results = call(
        functools.partial(ffn_kernel, blocks, weights, unit, routed, chained),
        outs,
        in_specs,
        out_specs,
        scratch,
        flops=18 * blocks * rows * width * 4 * CHUNK,
        moved=30 * 2**20,
    )(*operands)
    return results[:blocks], results[blocks : 2 * blocks], results[2 * blocks :]


def combine_kernel(
    info, slot, d0, d1, d2, d3, d_shared, probs, middle, normed, cot, ext, attended, wo,
    d_middle, d_attended, grad_wo, grad_ext, branch, router_acc, gain_acc,
):
    tokens, width = middle.shape
    rep = info[0]
    gain = ext[5:6, :]
    router = router_rows(ext)
    router_acc[...] = jnp.zeros_like(router_acc)
    gain_acc[...] = jnp.zeros_like(gain_acc)

    def tile(t, carry):
        at = pl.ds(pl.multiple_of(t * TILE, TILE), TILE)
        slot_one, slot_two = slot[at, 0:1], slot[at, 64:65]
        d_normed = d_shared[at, :].astype(F32)
        lane = iota((TILE, 128), 1)
        d_gates = jnp.zeros((TILE, 128), F32)
        for o, d in enumerate((d0, d1, d2, d3)):
            place = (iota((TILE, CAP), 1) + o * CAP).astype(F32)
            hit = (place == slot_one) | (place == slot_two)
            d_normed = d_normed + nn(ones_where(hit), d[0:CAP, :])
            share = d[CAP : CAP + 16, 0:CAP].astype(F32)[0:1, :]
            d_share = jnp.sum(jnp.where(hit, share, 0.0), axis=1, keepdims=True)
            d_gates = d_gates + jnp.where(lane == (rep ^ o), d_share, 0.0)
        p = probs[at, :]
        inner = jnp.sum(d_gates * p, axis=1, keepdims=True)
        d_logits = (p * (d_gates - inner)).astype(BF)
        d_normed = d_normed + nn(d_logits, router)
        router_acc[...] += tn(d_logits, normed[at, :])
        rows = middle[at, :]
        scale = lax.rsqrt(jnp.mean(rows * rows, axis=1, keepdims=True) + EPSILON)
        unit = rows * scale
        gain_acc[...] += jnp.sum((d_normed * unit).reshape(TILE // 8, 8, width), axis=0)
        w = d_normed * gain
        inner = jnp.mean(w * unit, axis=1, keepdims=True)
        total = cot[at, :].astype(F32) + scale * (w - unit * inner)
        d_middle[at, :] = total
        rounded = total.astype(BF)
        branch[at, :] = rounded
        d_attended[at, :] = nt(rounded, wo[...]).astype(BF)
        return carry

    lax.fori_loop(0, tokens // TILE, tile, 0)
    grad_wo[...] = tn(attended[...], branch[...]).astype(BF)
    row = iota((16, width), 0)
    total = jnp.sum(gain_acc[...], axis=0, keepdims=True)
    grad_ext[...] = jnp.where(row < 4, router_acc[0:16, :], jnp.where(row == 5, total, 0.0))


def output_kernel(info, slot, o0, o1, o2, o3, shared, probs, middle, out):
    tokens = middle.shape[0]
    rep = info[0]

    def tile(t, carry):
        at = pl.ds(pl.multiple_of(t * TILE, TILE), TILE)
        slot_one, slot_two = slot[at, 0:1], slot[at, 64:65]
        total = middle[at, :] + shared[at, :].astype(F32)
        p = probs[at, :]
        lane = iota((TILE, 128), 1)
        for o, rows in enumerate((o0, o1, o2, o3)):
            place = (iota((TILE, CAP), 1) + o * CAP).astype(F32)
            hit = (place == slot_one) | (place == slot_two)
            share = jnp.sum(jnp.where(lane == (rep ^ o), p, 0.0), axis=1, keepdims=True)
            total = total + nn(jnp.where(hit, share, 0.0).astype(BF), rows[...])
        out[at, :] = total.astype(BF)
        return carry

    lax.fori_loop(0, tokens // TILE, tile, 0)


def attend_back_kernel(
    starts, q, k, v, d_out, out, lse, cosine, sine, dq, dk, dv, bias, dk_acc, dv_acc
):
    tokens = q.shape[0]

    @pl.when(pl.program_id(0) == 0)
    def _():
        fill_bias(starts, bias)

    keys, values = k[...], v[...]
    half_keys = [keep_half(keys, 0), keep_half(keys, 1)]
    dk_acc[...] = jnp.zeros_like(dk_acc)
    dv_acc[...] = jnp.zeros_like(dv_acc)
    low = iota((TILE, 128), 1) < 64
    for t in range(tokens // TILE):
        begin = t * TILE
        end = min(tokens, begin + TILE + PIECE)
        at = slice(begin, begin + TILE)
        block, grad = q[at, :], d_out[at, :]
        product = grad.astype(F32) * out[at, :].astype(F32)
        block_lse = lse[at, :]
        d_block = None
        for h in range(2):
            block_h, grad_h = keep_half(block, h), keep_half(grad, h)
            scores = nt(block_h, keys[:end])
            scores = biased(scores, bias, begin, begin, end)
            probs = jnp.exp(scores - block_lse[:, 64 * h : 64 * h + 1])
            d_probs = nt(grad_h, values[:end])
            inner = jnp.sum(
                jnp.where(low if h == 0 else ~low, product, 0.0), axis=1, keepdims=True
            )
            d_scores = (probs * (d_probs - inner)).astype(BF)
            part = nn(d_scores, half_keys[h][:end])
            d_block = part if d_block is None else d_block + part
            dk_acc[0:end, :] += tn(d_scores, block_h)
            dv_acc[0:end, :] += tn(probs.astype(BF), grad_h)
        dq[at, :] = spin(d_block * 0.125, cosine[at, :], -sine[at, :]).astype(BF)
    dk[...] = spin(dk_acc[...], cosine[...], -sine[...]).astype(BF)
    dv[...] = dv_acc[...].astype(BF)


def tail_kernel(
    info, x, ext, dq, dk, dv, wq, wk, wv, d_middle, grad_wo, grad_ext,
    grad_in, mine, theirs, normed_all, gw, gain_acc,
):
    tokens, width = x.shape
    gain = ext[4:5, :]
    gain_acc[...] = jnp.zeros_like(gain_acc)

    def tile(t, carry):
        at = pl.ds(pl.multiple_of(t * TILE, TILE), TILE)
        rows = x[at, :].astype(F32)
        scale = lax.rsqrt(jnp.mean(rows * rows, axis=1, keepdims=True) + EPSILON)
        unit = rows * scale
        normed_all[at, :] = (unit * gain).astype(BF)
        d_normed = nt(dq[at, :], wq[...]) + nt(dk[at, :], wk[...]) + nt(dv[at, :], wv[...])
        gain_acc[...] += jnp.sum((d_normed * unit).reshape(TILE // 8, 8, width), axis=0)
        w = d_normed * gain
        inner = jnp.mean(w * unit, axis=1, keepdims=True)
        grad_in[at, :] = d_middle[at, :] + scale * (w - unit * inner)
        return carry

    lax.fori_loop(0, tokens // TILE, tile, 0)
    for i, d in enumerate((dq, dk, dv)):
        gw[i] = tn(normed_all[...], d[...]).astype(BF)
    row = iota((16, width), 0)
    total = jnp.sum(gain_acc[...], axis=0, keepdims=True)
    small = (grad_ext[...] + jnp.where(row == 4, total, 0.0)).astype(BF)
    half = width // SLOTS

    def fill(low, high):
        for j in range(SLOTS):
            at = pl.ds(pl.multiple_of(info[2 + j] * half, 32), half)
            low[j, 0:half, :] = gw[0, at, :]
            low[j, half : 2 * half, :] = gw[1, at, :]
            low[j, 2 * half : 2 * half + 16, :] = small
            high[j, 0:half, :] = gw[2, at, :]
            high[j, half : 2 * half, :] = grad_wo[at, :]
            high[j, 2 * half : 2 * half + 16, :] = jnp.zeros((16, width), BF)

    @pl.when(info[1] == 0)
    def _():
        fill(mine, theirs)

    @pl.when(info[1] != 0)
    def _():
        fill(theirs, mine)


def rope_tables(length, head_dim):
    positions = jnp.arange(length, dtype=F32)
    inverse_freq = 10000.0 ** (-2.0 * jnp.arange(head_dim // 2, dtype=F32) / head_dim)
    angle = positions[:, None] * inverse_freq[None, :]
    cosine, sine = jnp.cos(angle), jnp.sin(angle)
    return (
        jnp.concatenate([cosine] * 4, axis=1),
        jnp.concatenate([-sine, sine, -sine, sine], axis=1),
    )


def body(
    inputs,
    piece_starts,
    routes,
    attn_gain,
    query_weight,
    key_weight,
    value_weight,
    out_weight,
    ffn_gain,
    router_weight,
    expert_gate,
    expert_up,
    expert_down,
    shared_gate,
    shared_up,
    shared_down,
    cotangent,
):
    _, tokens, width = inputs.shape
    shards = lax.axis_size("shard")
    rep, shard = lax.axis_index("rep"), lax.axis_index("shard")
    core = rep % 2
    ringed = shards == SLOTS
    rows = width // shards
    units = shared_gate.shape[1]
    x, cot, chosen = inputs[0], cotangent[0], routes[0]
    if ringed:
        z, x_side = shard // 2, shard % 2
        order = [((z + d) % 4) * 2 + (x_side ^ b) for b in range(2) for d in range(4)]
    else:
        order = list(range(SLOTS))
    info = jnp.stack([jnp.asarray(n, jnp.int32) for n in [rep, core] + order])

    small = jnp.concatenate([router_weight.T, attn_gain[None], ffn_gain[None]], axis=0)
    small = jnp.pad(small, ((0, 10), (0, 0)))
    small = lax.dynamic_update_slice(jnp.zeros((16, width), BF), small, (0, shard * rows))
    blank = jnp.zeros((16, width), BF)
    if ringed:
        half_one = jnp.concatenate([query_weight, key_weight, small], axis=0)
        half_two = jnp.concatenate([value_weight, out_weight, blank], axis=0)
        piece = jnp.where(core == 0, half_one, half_two)
        attn_parts = gather_slots(piece)
        attn_own = jnp.stack(attn_parts)
        attn_other = to_rep(attn_own, 1)
    else:
        full = [
            lax.all_gather(w, "shard", axis=0, tiled=True).reshape(SLOTS, -1, width)
            for w in (query_weight, key_weight, value_weight, out_weight)
        ]
        small = lax.psum(small.astype(F32), "shard").astype(BF)
        small = jnp.concatenate([small[None], jnp.zeros((7, 16, width), BF)], axis=0)
        half_one = jnp.concatenate([full[0], full[1], small], axis=1)
        half_two = jnp.concatenate([full[2], full[3], jnp.zeros_like(small)], axis=1)
        attn_own = jnp.where(core == 0, half_one, half_two)
        attn_other = jnp.where(core == 0, half_two, half_one)

    shared_pack = jnp.stack([shared_gate, shared_up, shared_down.T])
    my_half = lax.dynamic_slice_in_dim(shared_pack, core * (units // 2), units // 2, 2)
    expert_pack = jnp.stack([expert_gate[rep], expert_up[rep], expert_down[rep].T])
    if ringed:
        my_half = after(my_half, attn_own)
        shared_own = jnp.stack(gather_slots(my_half))
        shared_other = to_rep(shared_own, 1)
        expert_pack = after(expert_pack, shared_own)
        expert_slots = gather_slots(expert_pack)
    else:

        def slotted(part):
            every = lax.all_gather(part, "shard")
            every = every.reshape(SLOTS, shards // SLOTS, 3, width, part.shape[2])
            return every.transpose(0, 2, 3, 1, 4).reshape(SLOTS, 3, width, -1)

        shared_own = slotted(my_half)
        shared_other = to_rep(shared_own, 1)
        expert_every = slotted(expert_pack)
        expert_slots = [expert_every[j] for j in range(SLOTS)]

    packed = [shape((CAP, width))] * 4
    rank, slot, *cot_out = call(
        prep_kernel,
        [shape((8, tokens), F32), shape((tokens, 128), F32)] + packed,
        [SMEM, VMEM, VMEM, VMEM],
        [VMEM] * 6,
        flops=2 * tokens * width * CAP * 4,
        moved=8 * 2**20,
    )(info, chosen, chosen.T, cot)
    cot_in = [cot_out[0]] + [to_rep(cot_out[o], o) for o in (1, 2, 3)]

    cosine, sine = rope_tables(tokens, width // HEADS)
    token_f = shape((tokens, width))
    square = shape((width, width))
    q, k, v, wq, wk, wv, wo, ext = call(
        qkv_kernel,
        [token_f] * 3 + [square] * 4 + [shape((16, width), F32)],
        [SMEM, VMEM, ANY, ANY, VMEM, VMEM],
        [VMEM] * 8,
        [pltpu.VMEM((SLOTS, 16, width), BF), pltpu.SemaphoreType.DMA((5 * SLOTS,))],
        flops=6 * tokens * width * width,
        moved=16 * 2**20,
    )(info, x, attn_own, attn_other, cosine, sine)

    pair = pl.BlockSpec((tokens, 128), lambda i: (0, i))
    table = pl.BlockSpec((tokens, 128), lambda i: (0, 0))
    attended, lse = call(
        attend_kernel,
        [token_f, shape((tokens, width), F32)],
        [SMEM, pair, pair, pair],
        [pair, pair],
        [pltpu.VMEM((tokens, tokens), F32)],
        flops=16 * tokens * tokens * width,
        moved=10 * 2**20,
        grid=(width // 128,),
    )(piece_starts, q, k, v)

    middle, normed, probs, *x_out = call(
        middle_kernel,
        [shape((tokens, width), F32), token_f, shape((tokens, 128), F32)] + packed,
        [SMEM] + [VMEM] * 5,
        [VMEM] * 7,
        flops=2 * tokens * width * (width + CAP * 4),
        moved=14 * 2**20,
    )(info, x, attended, wo, ext, rank)

    x_in = [x_out[0]] + [to_rep(x_out[o], o) for o in (1, 2, 3)]
    shared_out, shared_dx, shared_grads = ffn(
        info,
        ext,
        [normed],
        [cot],
        [shared_own, shared_other],
        None,
        units // 2 if ringed else 128,
        False,
    )
    unit = units if ringed else 256
    far_out, far_dx, far_grads = ffn(
        info, ext, x_in[2:], cot_in[2:], expert_slots, None, unit, True
    )
    far_dx = [to_rep(far_dx[0], 2), to_rep(far_dx[1], 3)]
    near_out, near_dx, grads = ffn(
        info, ext, x_in[:2], cot_in[:2], expert_slots, far_grads, unit, True
    )
    d_rows = [near_dx[0], to_rep(near_dx[1], 1)] + far_dx
    out_rows = [near_out[0], to_rep(near_out[1], 1), to_rep(far_out[0], 2), to_rep(far_out[1], 3)]

    d_middle, d_attended, grad_wo, grad_ext = call(
        combine_kernel,
        [shape((tokens, width), F32), token_f, square, shape((16, width), F32)],
        [SMEM] + [VMEM] * 13,
        [VMEM] * 4,
        [
            pltpu.VMEM((tokens, width), BF),
            pltpu.VMEM((128, width), F32),
            pltpu.VMEM((8, width), F32),
        ],
        flops=2 * tokens * width * (2 * width + 4 * CAP),
        moved=24 * 2**20,
    )(info, slot, *d_rows, shared_dx[0], probs, middle, normed, cot, ext, attended, wo)
    outputs = call(
        output_kernel,
        token_f,
        [SMEM] + [VMEM] * 8,
        VMEM,
        flops=2 * tokens * width * 4 * CAP,
        moved=12 * 2**20,
    )(info, slot, *out_rows, shared_out[0], probs, middle)

    dq, dk, dv = call(
        attend_back_kernel,
        [token_f] * 3,
        [SMEM] + [pair] * 6 + [table] * 2,
        [pair] * 3,
        [
            pltpu.VMEM((tokens, tokens), F32),
            pltpu.VMEM((tokens, 128), F32),
            pltpu.VMEM((tokens, 128), F32),
        ],
        flops=40 * tokens * tokens * width,
        moved=14 * 2**20,
        grid=(width // 128,),
    )(piece_starts, q, k, v, d_attended, attended, lse, cosine, sine)

    grad_rows = shape((SLOTS, 2 * (width // SLOTS) + 16, width))
    grad_in, mine, theirs = call(
        tail_kernel,
        [shape((tokens, width), F32), grad_rows, grad_rows],
        [SMEM] + [VMEM] * 11,
        [VMEM] * 3,
        [
            pltpu.VMEM((tokens, width), BF),
            pltpu.VMEM((3, width, width), BF),
            pltpu.VMEM((8, width), F32),
        ],
        flops=12 * tokens * width * width,
        moved=24 * 2**20,
    )(info, x, ext, dq, dk, dv, wq, wk, wv, d_middle, grad_wo, grad_ext)

    def over_rep(total):
        total = total.astype(BF)
        return [total] + [to_rep(total, o) for o in (1, 2, 3)]

    def absolute(parts, dtype):
        stacked = jnp.stack(parts)
        return jnp.take(stacked, jnp.arange(4) ^ rep, axis=0).astype(dtype)

    def unslot(every, part_units):
        every = every.reshape(SLOTS, 3, width, shards // SLOTS, part_units)
        every = every.transpose(0, 3, 1, 2, 4).reshape(shards, 3, width, part_units)
        return lax.psum_scatter(every, "shard", scatter_dimension=0)

    shared_sum = shared_grads[0].astype(F32) + to_rep(shared_grads[1], 1).astype(F32)
    if ringed:
        shared_sum = shared_sum.astype(BF)
        shared_total = scatter_slots([shared_sum[j] for j in range(SLOTS)])
        expert_total = scatter_slots(grads)
    else:
        shared_total = unslot(shared_sum.astype(BF), units // 2).astype(F32)
        expert_total = unslot(jnp.stack(grads), units).astype(F32)
    shared_total = shared_total + to_rep(shared_total.astype(BF), 2).astype(F32)
    shared_pair = to_rep(shared_total.astype(BF), 1).astype(F32)
    shared_low = jnp.where(core == 0, shared_total, shared_pair)
    shared_high = jnp.where(core == 0, shared_pair, shared_total)
    shared_full = jnp.concatenate([shared_low, shared_high], axis=2)
    expert_full = absolute(over_rep(expert_total), F32)

    summed = mine.astype(F32) + to_rep(theirs, 1).astype(F32)
    if ringed:
        summed = summed.astype(BF)
        far = to_x(summed[4:])
        near = summed[:4].astype(F32) + far.astype(F32)
        near_low = near.astype(BF)
        attn_total = near[0]
        for d in (1, 2, 3):
            attn_total = attn_total + to_z(near_low[d], d).astype(F32)
    else:
        half = width // SLOTS
        summed = summed.astype(BF)
        one = lax.psum_scatter(summed[:, :half].reshape(width, width), "shard", tiled=True)
        two = lax.psum_scatter(
            summed[:, half : 2 * half].reshape(width, width), "shard", tiled=True
        )
        three = lax.psum(summed[0, 2 * half :].astype(F32), "shard")
        attn_total = jnp.concatenate([one.astype(F32), two.astype(F32), three], axis=0)
    attn_total = attn_total + to_rep(attn_total.astype(BF), 2).astype(F32)
    attn_pair = to_rep(attn_total.astype(BF), 1).astype(F32)
    first = jnp.where(core == 0, attn_total, attn_pair)
    second = jnp.where(core == 0, attn_pair, attn_total)
    tiny = lax.dynamic_slice(first[2 * rows :], (0, shard * rows), (16, rows))
    return (
        outputs[None],
        grad_in[None],
        tiny[4],
        first[:rows],
        first[rows : 2 * rows],
        second[:rows],
        second[rows : 2 * rows],
        tiny[5],
        tiny[:4].T,
        expert_full[:, 0],
        expert_full[:, 1],
        expert_full[:, 2].transpose(0, 2, 1),
        shared_full[0],
        shared_full[1],
        shared_full[2].T,
    )


def solution(mesh):
    in_specs = (
        P(("rep", "shard"), None, None),
        P(("rep", "shard"), None),
        P(("rep", "shard"), None, None),
        P("shard"),
        P("shard", None),
        P("shard", None),
        P("shard", None),
        P("shard", None),
        P("shard"),
        P("shard", None),
        P(None, None, "shard"),
        P(None, None, "shard"),
        P(None, "shard", None),
        P(None, "shard"),
        P(None, "shard"),
        P("shard", None),
        P(("rep", "shard"), None, None),
    )
    out_specs = (
        P(("rep", "shard"), None, None),
        P(("rep", "shard"), None, None),
        P("shard"),
        P("shard", None),
        P("shard", None),
        P("shard", None),
        P("shard", None),
        P("shard"),
        P("shard", None),
        P(None, None, "shard"),
        P(None, None, "shard"),
        P(None, "shard", None),
        P(None, "shard"),
        P(None, "shard"),
        P("shard", None),
    )
    return jax.shard_map(body, mesh=mesh, in_specs=in_specs, out_specs=out_specs, check_vma=False)
```

time: 3020 us -> 911 us (0.30)
  waiting for transfers between devices: 2100 us -> 453 us
  matrix products: 446 us -> 0 us
  Pallas kernels: 0 us -> 302 us
  other arithmetic: 192 us -> 38.5 us
  local copies, waits for them, and re-layouts: 173 us -> 49.8 us
  blocking collectives: 66.9 us -> 0 us
  starting transfers between devices: 1.13 us -> 52.4 us
    reduce_scatter x10 -> x0, waiting for transfers between devices: 1410 us -> none  [the longest x1 405 us: body(): lax.psum_scatter(grad_edown, 'shard', scatter_dimension=1, tiled=True)]
    all_gather x10 -> x0, waiting for transfers between devices: 575 us -> none  [the longest x1 161 us: body(): lax.all_gather(expert_down, 'shard', axis=1, tiled=True)]
    ppermute x0 -> x62, waiting for transfers between devices: none -> 453 us  [permute(): return lax.ppermute(x, AXES, pairs)]
    dot_general x46 -> x0, matrix products: 445 us -> none  [the longest x4 47.3 us: one_block(): jnp.einsum('qhd,khd->hqk', query_tile, key_rot, preferred_element_type=jn...]
    pallas_call x0 -> x11, Pallas kernels: none -> 302 us  [the longest x3 150 us: ffn(): call(functools.partial(ffn_kernel, blocks, weights, unit, routed, chained...]
    psum x1 -> x0, waiting for transfers between devices: 109 us -> none  [body(): lax.psum(shard_wq.astype(jnp.bfloat16), 'rep').astype(jnp.float32)]
    convert_element_type x34 -> x12, other arithmetic: 88.1 us -> 16.8 us  [the longest x1 5.22 us: body(): shared_sum = shared_sum.astype(BF)]
    dynamic_update_slice x4 -> x1, local copies, waits for them, and re-layouts: 63.5 us -> 0.18 us  [body(): lax.dynamic_update_slice(jnp.zeros((16, width), BF), small, (0, shard * r...]
  transfers between devices with their start and end apart: 22 -> 62, of which waited for: 16 -> 25; matrix products, arithmetic and copies ran while one was open for 26% -> 8% of each run, Pallas kernels for 0% -> 25%
where the time goes in v1:
time: 911 us; the launch traced here: 897 us
  waiting for transfers between devices  453 us (50%)
  Pallas kernels  302 us (33%)
  starting transfers between devices  52.4 us (6%)
  local copies, waits for them, and re-layouts  49.8 us (5%)
  other arithmetic  38.5 us (4%)
    ppermute x62, waiting for transfers between devices, permute(): return lax.ppermute(x, AXES, pairs)  453 us
    pallas_call x3, Pallas kernels, ffn(): call(functools.partial(ffn_kernel, blocks, weights, unit, routed, chained...  150 us
    ppermute x62, starting transfers between devices, permute(): return lax.ppermute(x, AXES, pairs)  52.4 us
    pallas_call x1, Pallas kernels, body(): call(attend_back_kernel, [token_f] * 3, [SMEM] + [pair] * 6 + [table] * 2...  42.3 us
    pallas_call x1, Pallas kernels, body(): call(attend_kernel, [token_f, shape((tokens, width), F32)], [SMEM, pair,...  27.5 us
    unnamed x70, local copies, waits for them, and re-layouts  26.2 us
    pallas_call x1, Pallas kernels, body(): call(combine_kernel, [shape((tokens, width), F32), token_f, square, shape...  20.9 us
    pallas_call x1, Pallas kernels, body(): call(tail_kernel, [shape((tokens, width), F32), grad_rows, grad_rows], [S...  18.5 us
  transfers between devices with their start and end apart: 62, of which 25 were waited for; matrix products, arithmetic and copies ran while one was open for 8% of the time, Pallas kernels for 25%

profile of v1, /device:TPU:0, one launch (start us, length us, event | category | flops | bytes accessed | tf_op | source)
XLA Modules:
  0.0 897.0 jit_solution(15430985164450303313)
XLA Ops:
  2.9 5.2 collective-permute-start
  9.1 1.6 collective-permute-start.3
  10.6 1.7 copy.32.routes
  13.0 7.2 shard_map.280
  20.1 1.6 collective-permute-start.26
  22.3 3.3 fusion.21
  25.6 1.9 copy.34
  29.7 2.0 constant_dynamic-slice_fusion.1
  32.2 1.7 bitcast_dynamic-update-slice_fusion.14
  36.9 1.7 bitcast_dynamic-update-slice_fusion.13
  39.3 1.7 bitcast_dynamic-update-slice_fusion.12
  41.0 1.7 bitcast_dynamic-update-slice_fusion.11
  43.5 5.6 collective-permute-done.5
  49.9 3.6 collective-permute-done.6
  54.4 3.1 collective-permute-start.10
  59.5 2.3 pad_maximum_fusion.1.refs_6_
  62.6 1.8 pad_maximum_fusion.3
  64.8 6.5 collective-permute-done.10
  72.9 37.0 %collective-permute-done.11 = bf16[3,768,128]{2,1,0:T(8,128)(2,1)S(1)} collective-permute-done((bf16[3,768,128]{2,1,0:T(8,128)(2,1)S(1)}, bf16[3,768,128]{2,1,0:T(8,128)(2,1)S(1)}, u32[]{:S(2)}, u32[]{:S(2)}) %collective-permute-start.11) | collective-permute-done | bytes 589856 | tf_op jit(solution)/shard_map/ppermute | solution.py:74
  112.9 13.5 %collective-permute-done.14 = bf16[3,768,128]{2,1,0:T(8,128)(2,1)S(1)} collective-permute-done((bf16[3,768,128]{2,1,0:T(8,128)(2,1)}, bf16[3,768,128]{2,1,0:T(8,128)(2,1)S(1)}, u32[]{:S(2)}, u32[]{:S(2)}) %collective-permute-start.14) | collective-permute-done | bytes 589856 | tf_op jit(solution)/shard_map/ppermute | solution.py:74
  126.5 12.6 %collective-permute-done.15 = bf16[3,768,128]{2,1,0:T(8,128)(2,1)S(1)} collective-permute-done((bf16[3,768,128]{2,1,0:T(8,128)(2,1)S(1)}, bf16[3,768,128]{2,1,0:T(8,128)(2,1)S(1)}, u32[]{:S(2)}, u32[]{:S(2)}) %collective-permute-start.15) | collective-permute-done | bytes 589856 | tf_op jit(solution)/shard_map/ppermute | solution.py:74
  139.1 11.3 %collective-permute-done.16 = bf16[3,768,128]{2,1,0:T(8,128)(2,1)S(1)} collective-permute-done((bf16[3,768,128]{2,1,0:T(8,128)(2,1)S(1)}, bf16[3,768,128]{2,1,0:T(8,128)(2,1)S(1)}, u32[]{:S(2)}, u32[]{:S(2)}) %collective-permute-start.16) | collective-permute-done | bytes 589856 | tf_op jit(solution)/shard_map/ppermute | solution.py:74
  150.5 2.2 copy-done.21
  152.7 2.0 collective-permute-start.19
  154.7 12.0 %shard_map.281 = (bf16[1024,768]{1,0:T(8,128)(2,1)}, bf16[1024,768]{1,0:T(8,128)(2,1)}, bf16[1024,768]{1,0:T(8,128)(2,1)}, bf16[768,768]{1,0:T(8,128)(2,1)}, bf1...) custom-call(s32[10]{0:T(128)} %stack.128.info.refs_0_, ...), custom_call_target="tpu_custom_call" | custom-call | flops 3623878656 | bytes 16777216 | tf_op jit(solution)/shard_map/pallas_call | solution.py:734
  167.3 27.5 %shard_map.282 = (bf16[1024,768]{1,0:T(8,128)(2,1)}, f32[1024,768]{1,0:T(8,128)}) custom-call(s32[1,2]{1,0:T(1,128)} %starts.3, bf16[1024,768]{1,0:T(8,128)(2,1)} %get-tuple-element.80.q, bf16[1024,768]{1,0:T(8,128)(2,1)} %get-tuple-element.81.k, bf16[1024,768]{1,0:T(8,128)(2,1)} %get-tuple-element.82.v), custom_call_target="tpu_custom_call" | custom-call | flops 12884901888 | bytes 10485760 | tf_op jit(solution)/shard_map/pallas_call | solution.py:746
  194.8 1.5 collective-permute-start.21
  196.4 56.9 %collective-permute-done.18.refs_8_ = bf16[3,768,256]{2,1,0:T(8,128)(2,1)} collective-permute-done((bf16[3,768,256]{2,1,0:T(8,128)(2,1)}, bf16[3,768,256]{2,1,0:T(8,128)(2,1)}, u32[]{:S(2)}, u32[]{:S(2)}) %collective-permute-start.18) | collective-permute-done | bytes 1179680 | tf_op jit(solution)/shard_map/ppermute | solution.py:74
  255.4 11.3 %shard_map.283 = (f32[1024,768]{1,0:T(8,128)}, bf16[1024,768]{1,0:T(8,128)(2,1)}, f32[1024,128]{1,0:T(8,128)}, bf16[576,768]{1,0:T(8,128)(2,1)}, bf16[576,768]{1...) custom-call(s32[10]{0:T(128)} %stack.128.info.refs_0_, bf16[1024,768]{1,0:T(8,128)(2,1)} %bitcast.156, ...), custom_call_target="tpu_custom_call" | custom-call | flops 4831838208 | bytes 14680064 | tf_op jit(solution)/shard_map/pallas_call | solution.py:757
  267.3 22.3 %collective-permute-done.24.refs_2_ = bf16[576,768]{1,0:T(8,128)(2,1)S(1)} collective-permute-done((bf16[576,768]{1,0:T(8,128)(2,1)}, bf16[576,768]{1,0:T(8,128)(2,1)S(1)}, u32[]{:S(2)}, u32[]{:S(2)}) %collective-permute-start.24) | collective-permute-done | bytes 884768 | tf_op jit(solution)/shard_map/ppermute | solution.py:74
  289.6 13.7 %collective-permute-done.25.refs_3_ = bf16[576,768]{1,0:T(8,128)(2,1)S(1)} collective-permute-done((bf16[576,768]{1,0:T(8,128)(2,1)}, bf16[576,768]{1,0:T(8,128)(2,1)S(1)}, u32[]{:S(2)}, u32[]{:S(2)}) %collective-permute-start.25) | collective-permute-done | bytes 884768 | tf_op jit(solution)/shard_map/ppermute | solution.py:74
  303.2 1.9 collective-permute-start.31
  306.0 54.0 %shard_map.284 = (bf16[576,768]{1,0:T(8,128)(2,1)}, bf16[576,768]{1,0:T(8,128)(2,1)}, bf16[592,768]{1,0:T(8,128)(2,1)}, bf16[592,768]{1,0:T(8,128)(2,1)}, bf16[3...) custom-call(s32[10]{0:T(128)} %stack.128.info.refs_0_, ...), custom_call_target="tpu_custom_call" | custom-call | flops 32614907904 | bytes 31457280 | tf_op jit(solution)/shard_map/pallas_call | solution.py:460
  361.0 55.2 %shard_map.285 = (bf16[576,768]{1,0:T(8,128)(2,1)}, bf16[576,768]{1,0:T(8,128)(2,1)}, bf16[592,768]{1,0:T(8,128)(2,1)}, bf16[592,768]{1,0:T(8,128)(2,1)}, bf16[3...) custom-call(s32[10]{0:T(128)} %stack.128.info.refs_0_, ...), custom_call_target="tpu_custom_call" | custom-call | flops 32614907904 | bytes 31457280 | tf_op jit(solution)/shard_map/pallas_call | solution.py:460
  418.1 41.3 %shard_map.286 = (bf16[1024,768]{1,0:T(8,128)(2,1)}, bf16[1024,768]{1,0:T(8,128)(2,1)}, bf16[8,3,768,128]{3,2,1,0:T(8,128)(2,1)}, bf16[8,3,768,128]{3,2,1,0:T(8,128)(2,1)}) custom-call(s32[10]{0:T(128)} %stack.128.info.refs_0_, f32[16,768]{1,0:T(8,128)} %get-tuple-element.79.ext.refs_1_, bf16[1024,768]{1,0:T(8,128)(2,1)} %get-tuple-element.108.refs_2_.normed, ...), custom_call_target="tpu_custom_call" | custom-call | flops 28991029248 | bytes 31457280 | tf_op jit(solution)/shard_map/pallas_call | solution.py:460
  459.5 20.9 %shard_map.288 = (f32[1024,768]{1,0:T(8,128)}, bf16[1024,768]{1,0:T(8,128)(2,1)}, bf16[768,768]{1,0:T(8,128)(2,1)}, f32[16,768]{1,0:T(8,128)}) custom-call(s32[10]{0:T(128)} %stack.128.info.refs_0_, f32[1024,128]{1,0:T(8,128)} %get-tuple-element.78.slot, bf16[592,768]{1,0:T(8,128)(2,1)} %get-tuple-element.112.d0, ...), custom_call_target="tpu_custom_call" | custom-call | flops 6039797760 | bytes 25165824 | tf_op jit(solution)/shard_map/pallas_call | solution.py:788
  480.4 42.3 %shard_map.289 = (bf16[1024,768]{1,0:T(8,128)(2,1)}, bf16[1024,768]{1,0:T(8,128)(2,1)}, bf16[1024,768]{1,0:T(8,128)(2,1)}) custom-call(s32[1,2]{1,0:T(1,128)} %starts.3, bf16[1024,768]{1,0:T(8,128)(2,1)} %get-tuple-element.80.q, bf16[1024,768]{1,0:T(8,128)(2,1)} %get-tuple-element.81.k, bf16[1024,768]{1,0:T(8,128)(2,1)} %get-tuple-element.82.v, ...), custom_call_target="tpu_custom_call" | custom-call | flops 32212254720 | bytes 14680064 | tf_op jit(solution)/shard_map/pallas_call | solution.py:810
  522.7 18.5 %shard_map.290 = (f32[1024,768]{1,0:T(8,128)}, bf16[8,208,768]{2,1,0:T(8,128)(2,1)}, bf16[8,208,768]{2,1,0:T(8,128)(2,1)}) custom-call(s32[10]{0:T(128)} %stack.128.info.refs_0_, bf16[1024,768]{1,0:T(8,128)(2,1)} %bitcast.157, f32[16,768]{1,0:T(8,128)} %get-tuple-element.79.ext.refs_1_, bf16[1024,768]{1,0:T(8,128)(2,1)} %get-tuple-element.119.dq, ...), custom_call_target="tpu_custom_call" | custom-call | flops 7247757312 | bytes 25165824 | tf_op jit(solution)/shard_map/pallas_call | solution.py:826
  544.1 26.4 %collective-permute-done.47 = bf16[3,768,256]{2,1,0:T(8,128)(2,1)S(1)} collective-permute-done((bf16[3,768,256]{2,1,0:T(8,128)(2,1)}, bf16[3,768,256]{2,1,0:T(8,128)(2,1)S(1)}, u32[]{:S(2)}, u32[]{:S(2)}) %collective-permute-start.47) | collective-permute-done | bytes 1179680 | tf_op jit(solution)/shard_map/ppermute | solution.py:74
  571.4 24.4 %collective-permute-done.45 = bf16[3,768,256]{2,1,0:T(8,128)(2,1)S(1)} collective-permute-done((bf16[3,768,256]{2,1,0:T(8,128)(2,1)}, bf16[3,768,256]{2,1,0:T(8,128)(2,1)S(1)}, u32[]{:S(2)}, u32[]{:S(2)}) %collective-permute-start.45) | collective-permute-done | bytes 1179680 | tf_op jit(solution)/shard_map/ppermute | solution.py:74
  596.2 25.0 %collective-permute-done.43 = bf16[3,768,256]{2,1,0:T(8,128)(2,1)S(1)} collective-permute-done((bf16[3,768,256]{2,1,0:T(8,128)(2,1)}, bf16[3,768,256]{2,1,0:T(8,128)(2,1)S(1)}, u32[]{:S(2)}, u32[]{:S(2)}) %collective-permute-start.43) | collective-permute-done | bytes 1179680 | tf_op jit(solution)/shard_map/ppermute | solution.py:74
  621.1 3.9 collective-permute-start.46
  630.1 15.6 %collective-permute-done.42 = bf16[3,768,256]{2,1,0:T(8,128)(2,1)} collective-permute-done((bf16[3,768,256]{2,1,0:T(8,128)(2,1)}, bf16[3,768,256]{2,1,0:T(8,128)(2,1)}, u32[]{:S(2)}, u32[]{:S(2)}) %collective-permute-start.42) | collective-permute-done | bytes 1179680 | tf_op jit(solution)/shard_map/ppermute | solution.py:74
  646.3 54.2 %collective-permute-done.46 = bf16[3,768,256]{2,1,0:T(8,128)(2,1)} collective-permute-done((bf16[3,768,256]{2,1,0:T(8,128)(2,1)S(1)}, bf16[3,768,256]{2,1,0:T(8,128)(2,1)}, u32[]{:S(2)}, u32[]{:S(2)}) %collective-permute-start.46) | collective-permute-done | bytes 1179680 | tf_op jit(solution)/shard_map/ppermute | solution.py:74
  702.0 3.1 add_convert_fusion.2
  705.9 17.4 %collective-permute-done.29.o2 = bf16[576,768]{1,0:T(8,128)(2,1)} collective-permute-done((bf16[576,768]{1,0:T(8,128)(2,1)}, bf16[576,768]{1,0:T(8,128)(2,1)}, u32[]{:S(2)}, u32[]{:S(2)}) %collective-permute-start.29) | collective-permute-done | bytes 884768 | tf_op jit(solution)/shard_map/ppermute | solution.py:74
  723.9 16.5 %collective-permute-done.30.o3 = bf16[576,768]{1,0:T(8,128)(2,1)} collective-permute-done((bf16[576,768]{1,0:T(8,128)(2,1)}, bf16[576,768]{1,0:T(8,128)(2,1)}, u32[]{:S(2)}, u32[]{:S(2)}) %collective-permute-start.30) | collective-permute-done | bytes 884768 | tf_op jit(solution)/shard_map/ppermute | solution.py:74
  740.4 2.1 collective-permute-start.49
  742.4 11.5 %shard_map.287 = bf16[1024,768]{1,0:T(8,128)(2,1)} custom-call(s32[10]{0:T(128)} %stack.128.info.refs_0_, f32[1024,128]{1,0:T(8,128)} %get-tuple-element.78.slot, bf16[576,768]{1,0:T(8,128)(2,1)} %get-tuple-element.104.o0, bf16[576,768]{1,0:T(8,128)(2,1)} %collective-permute-done.28.o1, bf16[576,768]{1,0:T(8,128)(2,1)} %collective-permute-done.29.o2, ...), custom_call_target="tpu_custom_call" | custom-call | flops 3623878656 | bytes 12582912 | tf_op jit(solution)/shard_map/pallas_call | solution.py:801
  754.0 3.5 convert_add_fusion
  758.3 5.2 add_convert_fusion
  766.1 2.0 collective-permute-start.37
  768.1 22.6 %collective-permute-done.50 = bf16[3,768,256]{2,1,0:T(8,128)(2,1)} collective-permute-done((bf16[3,768,256]{2,1,0:T(8,128)(2,1)S(1)}, bf16[3,768,256]{2,1,0:T(8,128)(2,1)}, u32[]{:S(2)}, u32[]{:S(2)}) %collective-permute-start.50) | collective-permute-done | bytes 1179680 | tf_op jit(solution)/shard_map/ppermute | solution.py:74
  794.3 4.0 pad_maximum_fusion
  798.2 5.4 gather_fusion
  807.6 12.4 %collective-permute-done.58 = bf16[3,768,128]{2,1,0:T(8,128)(2,1)} collective-permute-done((bf16[3,768,128]{2,1,0:T(8,128)(2,1)}, bf16[3,768,128]{2,1,0:T(8,128)(2,1)}, u32[]{:S(2)}, u32[]{:S(2)}) %collective-permute-start.58) | collective-permute-done | bytes 589856 | tf_op jit(solution)/shard_map/ppermute | solution.py:74
  820.0 12.6 %collective-permute-done.56 = bf16[3,768,128]{2,1,0:T(8,128)(2,1)} collective-permute-done((bf16[3,768,128]{2,1,0:T(8,128)(2,1)S(1)}, bf16[3,768,128]{2,1,0:T(8,128)(2,1)}, u32[]{:S(2)}, u32[]{:S(2)}) %collective-permute-start.56) | collective-permute-done | bytes 589856 | tf_op jit(solution)/shard_map/ppermute | solution.py:74
  832.6 2.4 fusion.2
  835.2 2.2 collective-permute-start.55
  838.8 3.2 collective-permute-done.53
  842.1 6.8 collective-permute-done.59
  848.9 31.0 %collective-permute-done.57 = bf16[3,768,128]{2,1,0:T(8,128)(2,1)S(1)} collective-permute-done((bf16[3,768,128]{2,1,0:T(8,128)(2,1)S(1)}, bf16[3,768,128]{2,1,0:T(8,128)(2,1)S(1)}, u32[]{:S(2)}, u32[]{:S(2)}) %collective-permute-start.57) | collective-permute-done | bytes 589856 | tf_op jit(solution)/shard_map/ppermute | solution.py:74
  881.9 3.9 slice_bitcast_fusion
  885.9 3.5 copy.35
  (191 shorter events, 62.2 us)
Async XLA Ops:
  2.9 28.8 %collective-permute-start = (bf16[208,768]{1,0:T(8,128)(2,1)S(1)}, bf16[208,768]{1,0:T(8,128)(2,1)}, u32[]{:S(2)}, u32[]{:S(2)}) collective-permute-start(bf16[208,768]{1,0:T(8,128)(2,1)S(1)} %maximum_select_fusion.1), channel_id=1, source_target_pairs={{0,6},{1,7},{2,0},{3,1},{4,2},{5,3},{6,4},{7,5},{8,14},{9,15},{10,... | collective-permute-start | bytes 958472 | tf_op jit(solution)/shard_map/ppermute | solution.py:74
  8.1 27.3 %collective-permute-start.1 = (bf16[208,768]{1,0:T(8,128)(2,1)S(1)}, bf16[208,768]{1,0:T(8,128)(2,1)}, u32[]{:S(2)}, u32[]{:S(2)}) collective-permute-start(bf16[208,768]{1,0:T(8,128)(2,1)S(1)} %maximum_select_fusion.1), channel_id=1, source_target_pairs={{0,4},{1,5},{2,6},{3,7},{4,0},{5,1},{6,2},{7,3},{8,12},{9,13},{10,... | collective-permute-start | bytes 958472 | tf_op jit(solution)/shard_map/ppermute | solution.py:74
  8.1 30.6 %collective-permute-start.2 = (bf16[208,768]{1,0:T(8,128)(2,1)S(1)}, bf16[208,768]{1,0:T(8,128)(2,1)}, u32[]{:S(2)}, u32[]{:S(2)}) collective-permute-start(bf16[208,768]{1,0:T(8,128)(2,1)S(1)} %maximum_select_fusion.1), channel_id=1, source_target_pairs={{0,2},{1,3},{2,4},{3,5},{4,6},{5,7},{6,0},{7,1},{8,10},{9,11},{10,... | collective-permute-start | bytes 958472 | tf_op jit(solution)/shard_map/ppermute | solution.py:74
  9.1 32.0 %collective-permute-start.3 = (bf16[208,768]{1,0:T(8,128)(2,1)S(1)}, bf16[208,768]{1,0:T(8,128)(2,1)}, u32[]{:S(2)}, u32[]{:S(2)}) collective-permute-start(bf16[208,768]{1,0:T(8,128)(2,1)S(1)} %maximum_select_fusion.1), channel_id=1, source_target_pairs={{0,1},{1,0},{2,3},{3,2},{4,5},{5,4},{6,7},{7,6},{8,9},{9,8},{10,11... | collective-permute-start | bytes 958472 | tf_op jit(solution)/shard_map/ppermute | solution.py:74
  20.1 146.6 %collective-permute-start.26 = (bf16[576,768]{1,0:T(8,128)(2,1)}, bf16[576,768]{1,0:T(8,128)(2,1)}, u32[]{:S(2)}, u32[]{:S(2)}) collective-permute-start(bf16[576,768]{1,0:T(8,128)(2,1)} %get-tuple-element.94), channel_id=1, source_target_pairs={{0,16},{1,17},{2,18},{3,19},{4,20},{5,21},{6,22},{7,23},{8,24},{9,... | collective-permute-start | bytes 2654216 | tf_op jit(solution)/shard_map/ppermute | solution.py:74
  31.7 11.1 %collective-permute-start.4 = (bf16[208,768]{1,0:T(8,128)(2,1)}, bf16[208,768]{1,0:T(8,128)(2,1)S(1)}, u32[]{:S(2)}, u32[]{:S(2)}) collective-permute-start(bf16[208,768]{1,0:T(8,128)(2,1)} %collective-permute-done), channel_id=1, source_target_pairs={{0,1},{1,0},{2,3},{3,2},{4,5},{5,4},{6,7},{7,6},{8,9},{9,8},{10,11... | collective-permute-start | bytes 958472 | tf_op jit(solution)/shard_map/ppermute | solution.py:74
  35.5 13.7 %collective-permute-start.5 = (bf16[208,768]{1,0:T(8,128)(2,1)}, bf16[208,768]{1,0:T(8,128)(2,1)S(1)}, u32[]{:S(2)}, u32[]{:S(2)}) collective-permute-start(bf16[208,768]{1,0:T(8,128)(2,1)} %collective-permute-done.1), channel_id=1, source_target_pairs={{0,1},{1,0},{2,3},{3,2},{4,5},{5,4},{6,7},{7,6},{8,9},{9,8},{10,11... | collective-permute-start | bytes 958472 | tf_op jit(solution)/shard_map/ppermute | solution.py:74
  38.7 14.8 %collective-permute-start.6 = (bf16[208,768]{1,0:T(8,128)(2,1)}, bf16[208,768]{1,0:T(8,128)(2,1)S(1)}, u32[]{:S(2)}, u32[]{:S(2)}) collective-permute-start(bf16[208,768]{1,0:T(8,128)(2,1)} %collective-permute-done.2), channel_id=1, source_target_pairs={{0,1},{1,0},{2,3},{3,2},{4,5},{5,4},{6,7},{7,6},{8,9},{9,8},{10,11... | collective-permute-start | bytes 958472 | tf_op jit(solution)/shard_map/ppermute | solution.py:74
  54.2 98.5 %collective-permute-start.7 = (bf16[8,208,768]{2,1,0:T(8,128)(2,1)}, bf16[8,208,768]{2,1,0:T(8,128)(2,1)}, u32[]{:S(2)}, u32[]{:S(2)}) collective-permute-start(bf16[8,208,768]{2,1,0:T(8,128)(2,1)} %bitcast_dynamic-update-slice_fusion.8.own), channel_id=1, source_target_pairs={{0,8},{1,9},{2,10},{3,11},{4,12},{5,13},{6,14},{7,15},{8,0},{9,1},... | collective-permute-start | bytes 7667720 | tf_op jit(solution)/shard_map/ppermute | solution.py:74
  54.4 16.9 %collective-permute-start.10 = (bf16[3,768,128]{2,1,0:T(8,128)(2,1)S(1)}, bf16[3,768,128]{2,1,0:T(8,128)(2,1)}, u32[]{:S(2)}, u32[]{:S(2)}) collective-permute-start(bf16[3,768,128]{2,1,0:T(8,128)(2,1)S(1)} %fusion.15), channel_id=1, source_target_pairs={{0,6},{1,7},{2,0},{3,1},{4,2},{5,3},{6,4},{7,5},{8,14},{9,15},{10,... | collective-permute-start | bytes 1769480 | tf_op jit(solution)/shard_map/ppermute | solution.py:74
  61.8 48.2 %collective-permute-start.11 = (bf16[3,768,128]{2,1,0:T(8,128)(2,1)S(1)}, bf16[3,768,128]{2,1,0:T(8,128)(2,1)S(1)}, u32[]{:S(2)}, u32[]{:S(2)}) collective-permute-start(bf16[3,768,128]{2,1,0:T(8,128)(2,1)S(1)} %fusion.15), channel_id=1, source_target_pairs={{0,4},{1,5},{2,6},{3,7},{4,0},{5,1},{6,2},{7,3},{8,12},{9,13},{10,... | collective-permute-start | bytes 1769480 | tf_op jit(solution)/shard_map/ppermute | solution.py:74
  64.5 46.1 %collective-permute-start.12 = (bf16[3,768,128]{2,1,0:T(8,128)(2,1)S(1)}, bf16[3,768,128]{2,1,0:T(8,128)(2,1)S(1)}, u32[]{:S(2)}, u32[]{:S(2)}) collective-permute-start(bf16[3,768,128]{2,1,0:T(8,128)(2,1)S(1)} %fusion.15), channel_id=1, source_target_pairs={{0,2},{1,3},{2,4},{3,5},{4,6},{5,7},{6,0},{7,1},{8,10},{9,11},{10,... | collective-permute-start | bytes 1769480 | tf_op jit(solution)/shard_map/ppermute | solution.py:74
  71.2 41.0 %collective-permute-start.13 = (bf16[3,768,128]{2,1,0:T(8,128)(2,1)S(1)}, bf16[3,768,128]{2,1,0:T(8,128)(2,1)S(1)}, u32[]{:S(2)}, u32[]{:S(2)}) collective-permute-start(bf16[3,768,128]{2,1,0:T(8,128)(2,1)S(1)} %fusion.15), channel_id=1, source_target_pairs={{0,1},{1,0},{2,3},{3,2},{4,5},{5,4},{6,7},{7,6},{8,9},{9,8},{10,11... | collective-permute-start | bytes 1769480 | tf_op jit(solution)/shard_map/ppermute | solution.py:74
  110.0 16.4 %collective-permute-start.14 = (bf16[3,768,128]{2,1,0:T(8,128)(2,1)}, bf16[3,768,128]{2,1,0:T(8,128)(2,1)S(1)}, u32[]{:S(2)}, u32[]{:S(2)}) collective-permute-start(bf16[3,768,128]{2,1,0:T(8,128)(2,1)} %collective-permute-done.10), channel_id=1, source_target_pairs={{0,1},{1,0},{2,3},{3,2},{4,5},{5,4},{6,7},{7,6},{8,9},{9,8},{10,11... | collective-permute-start | bytes 1769480 | tf_op jit(solution)/shard_map/ppermute | solution.py:74
  110.6 28.4 %collective-permute-start.15 = (bf16[3,768,128]{2,1,0:T(8,128)(2,1)S(1)}, bf16[3,768,128]{2,1,0:T(8,128)(2,1)S(1)}, u32[]{:S(2)}, u32[]{:S(2)}) collective-permute-start(bf16[3,768,128]{2,1,0:T(8,128)(2,1)S(1)} %collective-permute-done.11), channel_id=1, source_target_pairs={{0,1},{1,0},{2,3},{3,2},{4,5},{5,4},{6,7},{7,6},{8,9},{9,8},{10,11... | collective-permute-start | bytes 1769480 | tf_op jit(solution)/shard_map/ppermute | solution.py:74
  112.2 38.2 %collective-permute-start.16 = (bf16[3,768,128]{2,1,0:T(8,128)(2,1)S(1)}, bf16[3,768,128]{2,1,0:T(8,128)(2,1)S(1)}, u32[]{:S(2)}, u32[]{:S(2)}) collective-permute-start(bf16[3,768,128]{2,1,0:T(8,128)(2,1)S(1)} %collective-permute-done.12), channel_id=1, source_target_pairs={{0,1},{1,0},{2,3},{3,2},{4,5},{5,4},{6,7},{7,6},{8,9},{9,8},{10,11... | collective-permute-start | bytes 1769480 | tf_op jit(solution)/shard_map/ppermute | solution.py:74
  126.4 140.3 %collective-permute-start.27 = (bf16[576,768]{1,0:T(8,128)(2,1)}, bf16[576,768]{1,0:T(8,128)(2,1)}, u32[]{:S(2)}, u32[]{:S(2)}) collective-permute-start(bf16[576,768]{1,0:T(8,128)(2,1)} %get-tuple-element.95), channel_id=1, source_target_pairs={{0,24},{1,25},{2,26},{3,27},{4,28},{5,29},{6,30},{7,31},{8,16},{9,... | collective-permute-start | bytes 2654216 | tf_op jit(solution)/shard_map/ppermute | solution.py:74
  152.7 42.2 %collective-permute-start.17 = (bf16[3,768,256]{2,1,0:T(8,128)(2,1)}, bf16[3,768,256]{2,1,0:T(8,128)(2,1)S(1)}, u32[]{:S(2)}, u32[]{:S(2)}) collective-permute-start(bf16[3,768,256]{2,1,0:T(8,128)(2,1)} %pad_maximum_fusion.1.refs_6_), channel_id=1, source_target_pairs={{0,6},{1,7},{2,0},{3,1},{4,2},{5,3},{6,4},{7,5},{8,14},{9,15},{10,... | collective-permute-start | bytes 3538952 | tf_op jit(solution)/shard_map/ppermute | solution.py:74
  152.7 100.6 %collective-permute-start.18 = (bf16[3,768,256]{2,1,0:T(8,128)(2,1)}, bf16[3,768,256]{2,1,0:T(8,128)(2,1)}, u32[]{:S(2)}, u32[]{:S(2)}) collective-permute-start(bf16[3,768,256]{2,1,0:T(8,128)(2,1)} %pad_maximum_fusion.1.refs_6_), channel_id=1, source_target_pairs={{0,4},{1,5},{2,6},{3,7},{4,0},{5,1},{6,2},{7,3},{8,12},{9,13},{10,... | collective-permute-start | bytes 3538952 | tf_op jit(solution)/shard_map/ppermute | solution.py:74
  152.7 101.2 %collective-permute-start.19 = (bf16[3,768,256]{2,1,0:T(8,128)(2,1)}, bf16[3,768,256]{2,1,0:T(8,128)(2,1)}, u32[]{:S(2)}, u32[]{:S(2)}) collective-permute-start(bf16[3,768,256]{2,1,0:T(8,128)(2,1)} %pad_maximum_fusion.1.refs_6_), channel_id=1, source_target_pairs={{0,2},{1,3},{2,4},{3,5},{4,6},{5,7},{6,0},{7,1},{8,10},{9,11},{10,... | collective-permute-start | bytes 3538952 | tf_op jit(solution)/shard_map/ppermute | solution.py:74
  166.7 100.6 %collective-permute-start.20 = (bf16[3,768,256]{2,1,0:T(8,128)(2,1)}, bf16[3,768,256]{2,1,0:T(8,128)(2,1)}, u32[]{:S(2)}, u32[]{:S(2)}) collective-permute-start(bf16[3,768,256]{2,1,0:T(8,128)(2,1)} %pad_maximum_fusion.1.refs_6_), channel_id=1, source_target_pairs={{0,1},{1,0},{2,3},{3,2},{4,5},{5,4},{6,7},{7,6},{8,9},{9,8},{10,11... | collective-permute-start | bytes 3538952 | tf_op jit(solution)/shard_map/ppermute | solution.py:74
  194.8 71.9 %copy-start.22 = (bf16[3,768,256]{2,1,0:T(8,128)(2,1)}, bf16[3,768,256]{2,1,0:T(8,128)(2,1)S(1)}, u32[]{:S(2)}) copy-start(bf16[3,768,256]{2,1,0:T(8,128)(2,1)S(1)} %collective-permute-done.17.refs_7_) | copy-start | bytes 3538948
  194.8 110.3 %collective-permute-start.21 = (bf16[3,768,256]{2,1,0:T(8,128)(2,1)S(1)}, bf16[3,768,256]{2,1,0:T(8,128)(2,1)}, u32[]{:S(2)}, u32[]{:S(2)}) collective-permute-start(bf16[3,768,256]{2,1,0:T(8,128)(2,1)S(1)} %collective-permute-done.17.refs_7_), channel_id=1, source_target_pairs={{0,1},{1,0},{2,3},{3,2},{4,5},{5,4},{6,7},{7,6},{8,9},{9,8},{10,11... | collective-permute-start | bytes 3538952 | tf_op jit(solution)/shard_map/ppermute | solution.py:74
  253.3 52.7 %collective-permute-start.22 = (bf16[3,768,256]{2,1,0:T(8,128)(2,1)}, bf16[3,768,256]{2,1,0:T(8,128)(2,1)}, u32[]{:S(2)}, u32[]{:S(2)}) collective-permute-start(bf16[3,768,256]{2,1,0:T(8,128)(2,1)} %collective-permute-done.18.refs_8_), channel_id=1, source_target_pairs={{0,1},{1,0},{2,3},{3,2},{4,5},{5,4},{6,7},{7,6},{8,9},{9,8},{10,11... | collective-permute-start | bytes 3538952 | tf_op jit(solution)/shard_map/ppermute | solution.py:74
  253.9 52.1 %collective-permute-start.23 = (bf16[3,768,256]{2,1,0:T(8,128)(2,1)}, bf16[3,768,256]{2,1,0:T(8,128)(2,1)}, u32[]{:S(2)}, u32[]{:S(2)}) collective-permute-start(bf16[3,768,256]{2,1,0:T(8,128)(2,1)} %collective-permute-done.19.refs_9_), channel_id=1, source_target_pairs={{0,1},{1,0},{2,3},{3,2},{4,5},{5,4},{6,7},{7,6},{8,9},{9,8},{10,11... | collective-permute-start | bytes 3538952 | tf_op jit(solution)/shard_map/ppermute | solution.py:74
  266.7 22.9 %collective-permute-start.24 = (bf16[576,768]{1,0:T(8,128)(2,1)}, bf16[576,768]{1,0:T(8,128)(2,1)S(1)}, u32[]{:S(2)}, u32[]{:S(2)}) collective-permute-start(bf16[576,768]{1,0:T(8,128)(2,1)} %get-tuple-element.92), channel_id=1, source_target_pairs={{0,16},{1,17},{2,18},{3,19},{4,20},{5,21},{6,22},{7,23},{8,24},{9,... | collective-permute-start | bytes 2654216 | tf_op jit(solution)/shard_map/ppermute | solution.py:74
  267.3 36.0 %collective-permute-start.25 = (bf16[576,768]{1,0:T(8,128)(2,1)}, bf16[576,768]{1,0:T(8,128)(2,1)S(1)}, u32[]{:S(2)}, u32[]{:S(2)}) collective-permute-start(bf16[576,768]{1,0:T(8,128)(2,1)} %get-tuple-element.93), channel_id=1, source_target_pairs={{0,24},{1,25},{2,26},{3,27},{4,28},{5,29},{6,30},{7,31},{8,16},{9,... | collective-permute-start | bytes 2654216 | tf_op jit(solution)/shard_map/ppermute | solution.py:74
  289.6 70.4 %collective-permute-start.9 = (bf16[576,768]{1,0:T(8,128)(2,1)}, bf16[576,768]{1,0:T(8,128)(2,1)}, u32[]{:S(2)}, u32[]{:S(2)}) collective-permute-start(bf16[576,768]{1,0:T(8,128)(2,1)} %get-tuple-element.89), channel_id=1, source_target_pairs={{0,8},{1,9},{2,10},{3,11},{4,12},{5,13},{6,14},{7,15},{8,0},{9,1},... | collective-permute-start | bytes 2654216 | tf_op jit(solution)/shard_map/ppermute | solution.py:74
  303.2 114.9 %collective-permute-start.31 = (bf16[8,3,768,128]{3,2,1,0:T(8,128)(2,1)}, bf16[8,3,768,128]{3,2,1,0:T(8,128)(2,1)}, u32[]{:S(2)}, u32[]{:S(2)}) collective-permute-start(bf16[8,3,768,128]{3,2,1,0:T(8,128)(2,1)} %copy-done.21), channel_id=1, source_target_pairs={{0,8},{1,9},{2,10},{3,11},{4,12},{5,13},{6,14},{7,15},{8,0},{9,1},... | collective-permute-start | bytes 14155784 | tf_op jit(solution)/shard_map/ppermute | solution.py:74
  305.1 54.9 %collective-permute-start.8 = (bf16[576,768]{1,0:T(8,128)(2,1)}, bf16[576,768]{1,0:T(8,128)(2,1)S(1)}, u32[]{:S(2)}, u32[]{:S(2)}) collective-permute-start(bf16[576,768]{1,0:T(8,128)(2,1)} %get-tuple-element.87), channel_id=1, source_target_pairs={{0,8},{1,9},{2,10},{3,11},{4,12},{5,13},{6,14},{7,15},{8,0},{9,1},... | collective-permute-start | bytes 2654216 | tf_op jit(solution)/shard_map/ppermute | solution.py:74
  416.2 43.3 %collective-permute-start.32 = (bf16[592,768]{1,0:T(8,128)(2,1)}, bf16[592,768]{1,0:T(8,128)(2,1)}, u32[]{:S(2)}, u32[]{:S(2)}) collective-permute-start(bf16[592,768]{1,0:T(8,128)(2,1)} %get-tuple-element.113), channel_id=1, source_target_pairs={{0,8},{1,9},{2,10},{3,11},{4,12},{5,13},{6,14},{7,15},{8,0},{9,1},... | collective-permute-start | bytes 2727944 | tf_op jit(solution)/shard_map/ppermute | solution.py:74
  416.3 43.2 %collective-permute-start.33 = (bf16[592,768]{1,0:T(8,128)(2,1)}, bf16[592,768]{1,0:T(8,128)(2,1)}, u32[]{:S(2)}, u32[]{:S(2)}) collective-permute-start(bf16[592,768]{1,0:T(8,128)(2,1)} %get-tuple-element.114), channel_id=1, source_target_pairs={{0,16},{1,17},{2,18},{3,19},{4,20},{5,21},{6,22},{7,23},{8,24},{9,... | collective-permute-start | bytes 2727944 | tf_op jit(solution)/shard_map/ppermute | solution.py:74
  416.8 42.6 %collective-permute-start.34 = (bf16[592,768]{1,0:T(8,128)(2,1)S(1)}, bf16[592,768]{1,0:T(8,128)(2,1)}, u32[]{:S(2)}, u32[]{:S(2)}) collective-permute-start(bf16[592,768]{1,0:T(8,128)(2,1)S(1)} %copy-done.23), channel_id=1, source_target_pairs={{0,24},{1,25},{2,26},{3,27},{4,28},{5,29},{6,30},{7,31},{8,16},{9,... | collective-permute-start | bytes 2727944 | tf_op jit(solution)/shard_map/ppermute | solution.py:74
  541.2 84.2 %collective-permute-start.35 = (bf16[8,208,768]{2,1,0:T(8,128)(2,1)}, bf16[8,208,768]{2,1,0:T(8,128)(2,1)S(1)}, u32[]{:S(2)}, u32[]{:S(2)}) collective-permute-start(bf16[8,208,768]{2,1,0:T(8,128)(2,1)} %get-tuple-element.130), channel_id=1, source_target_pairs={{0,8},{1,9},{2,10},{3,11},{4,12},{5,13},{6,14},{7,15},{8,0},{9,1},... | collective-permute-start | bytes 7667720 | tf_op jit(solution)/shard_map/ppermute | solution.py:74
  541.5 29.0 %collective-permute-start.47 = (bf16[3,768,256]{2,1,0:T(8,128)(2,1)}, bf16[3,768,256]{2,1,0:T(8,128)(2,1)S(1)}, u32[]{:S(2)}, u32[]{:S(2)}) collective-permute-start(bf16[3,768,256]{2,1,0:T(8,128)(2,1)} %get-tuple-element.138), channel_id=1, source_target_pairs={{0,1},{1,0},{2,3},{3,2},{4,5},{5,4},{6,7},{7,6},{8,9},{9,8},{10,11... | collective-permute-start | bytes 3538952 | tf_op jit(solution)/shard_map/ppermute | solution.py:74
  542.1 53.8 %collective-permute-start.45 = (bf16[3,768,256]{2,1,0:T(8,128)(2,1)}, bf16[3,768,256]{2,1,0:T(8,128)(2,1)S(1)}, u32[]{:S(2)}, u32[]{:S(2)}) collective-permute-start(bf16[3,768,256]{2,1,0:T(8,128)(2,1)} %get-tuple-element.136), channel_id=1, source_target_pairs={{0,1},{1,0},{2,3},{3,2},{4,5},{5,4},{6,7},{7,6},{8,9},{9,8},{10,11... | collective-permute-start | bytes 3538952 | tf_op jit(solution)/shard_map/ppermute | solution.py:74
  543.6 214.8 %collective-permute-start.52 = (bf16[8,3,768,128]{3,2,1,0:T(8,128)(2,1)}, bf16[8,3,768,128]{3,2,1,0:T(8,128)(2,1)}, u32[]{:S(2)}, u32[]{:S(2)}) collective-permute-start(bf16[8,3,768,128]{3,2,1,0:T(8,128)(2,1)} %get-tuple-element.140), channel_id=1, source_target_pairs={{0,8},{1,9},{2,10},{3,11},{4,12},{5,13},{6,14},{7,15},{8,0},{9,1},... | collective-permute-start | bytes 14155784 | tf_op jit(solution)/shard_map/ppermute | solution.py:74
  543.6 77.5 %collective-permute-start.43 = (bf16[3,768,256]{2,1,0:T(8,128)(2,1)}, bf16[3,768,256]{2,1,0:T(8,128)(2,1)S(1)}, u32[]{:S(2)}, u32[]{:S(2)}) collective-permute-start(bf16[3,768,256]{2,1,0:T(8,128)(2,1)} %get-tuple-element.134), channel_id=1, source_target_pairs={{0,1},{1,0},{2,3},{3,2},{4,5},{5,4},{6,7},{7,6},{8,9},{9,8},{10,11... | collective-permute-start | bytes 3538952 | tf_op jit(solution)/shard_map/ppermute | solution.py:74
  570.6 75.2 %collective-permute-start.42 = (bf16[3,768,256]{2,1,0:T(8,128)(2,1)}, bf16[3,768,256]{2,1,0:T(8,128)(2,1)}, u32[]{:S(2)}, u32[]{:S(2)}) collective-permute-start(bf16[3,768,256]{2,1,0:T(8,128)(2,1)} %get-tuple-element.132), channel_id=1, source_target_pairs={{0,1},{1,0},{2,3},{3,2},{4,5},{5,4},{6,7},{7,6},{8,9},{9,8},{10,11... | collective-permute-start | bytes 3538952 | tf_op jit(solution)/shard_map/ppermute | solution.py:74
  595.8 50.4 %collective-permute-start.48 = (bf16[3,768,256]{2,1,0:T(8,128)(2,1)S(1)}, bf16[3,768,256]{2,1,0:T(8,128)(2,1)}, u32[]{:S(2)}, u32[]{:S(2)}) collective-permute-start(bf16[3,768,256]{2,1,0:T(8,128)(2,1)S(1)} %add_convert_fusion.3), channel_id=1, source_target_pairs={{0,6},{1,7},{2,0},{3,1},{4,2},{5,3},{6,4},{7,5},{8,14},{9,15},{10,... | collective-permute-start | bytes 3538952 | tf_op jit(solution)/shard_map/ppermute | solution.py:74
  621.1 79.3 %collective-permute-start.46 = (bf16[3,768,256]{2,1,0:T(8,128)(2,1)S(1)}, bf16[3,768,256]{2,1,0:T(8,128)(2,1)}, u32[]{:S(2)}, u32[]{:S(2)}) collective-permute-start(bf16[3,768,256]{2,1,0:T(8,128)(2,1)S(1)} %add_convert_fusion.4), channel_id=1, source_target_pairs={{0,4},{1,5},{2,6},{3,7},{4,0},{5,1},{6,2},{7,3},{8,12},{9,13},{10,... | collective-permute-start | bytes 3538952 | tf_op jit(solution)/shard_map/ppermute | solution.py:74
  625.4 75.6 %collective-permute-start.44 = (bf16[3,768,256]{2,1,0:T(8,128)(2,1)S(1)}, bf16[3,768,256]{2,1,0:T(8,128)(2,1)S(1)}, u32[]{:S(2)}, u32[]{:S(2)}) collective-permute-start(bf16[3,768,256]{2,1,0:T(8,128)(2,1)S(1)} %add_convert_fusion.5), channel_id=1, source_target_pairs={{0,2},{1,3},{2,4},{3,5},{4,6},{5,7},{6,0},{7,1},{8,10},{9,11},{10,... | collective-permute-start | bytes 3538952 | tf_op jit(solution)/shard_map/ppermute | solution.py:74
  629.0 73.0 %copy-start.8 = (bf16[3,768,256]{2,1,0:T(8,128)(2,1)S(1)}, bf16[3,768,256]{2,1,0:T(8,128)(2,1)}, u32[]{:S(2)}) copy-start(bf16[3,768,256]{2,1,0:T(8,128)(2,1)} %get-tuple-element.131) | copy-start | bytes 3538948
  645.7 108.2 %collective-permute-start.36 = (bf16[4,208,768]{2,1,0:T(8,128)(2,1)}, bf16[4,208,768]{2,1,0:T(8,128)(2,1)}, u32[]{:S(2)}, u32[]{:S(2)}) collective-permute-start(bf16[4,208,768]{2,1,0:T(8,128)(2,1)} %slice.115), channel_id=1, source_target_pairs={{0,1},{1,0},{2,3},{3,2},{4,5},{5,4},{6,7},{7,6},{8,9},{9,8},{10,11... | collective-permute-start | bytes 3833864 | tf_op jit(solution)/shard_map/ppermute | solution.py:74
  646.3 58.8 %collective-permute-start.28 = (bf16[576,768]{1,0:T(8,128)(2,1)}, bf16[576,768]{1,0:T(8,128)(2,1)}, u32[]{:S(2)}, u32[]{:S(2)}) collective-permute-start(bf16[576,768]{1,0:T(8,128)(2,1)} %get-tuple-element.105), channel_id=1, source_target_pairs={{0,8},{1,9},{2,10},{3,11},{4,12},{5,13},{6,14},{7,15},{8,0},{9,1},... | collective-permute-start | bytes 2654216 | tf_op jit(solution)/shard_map/ppermute | solution.py:74
  700.5 22.9 %collective-permute-start.29 = (bf16[576,768]{1,0:T(8,128)(2,1)}, bf16[576,768]{1,0:T(8,128)(2,1)}, u32[]{:S(2)}, u32[]{:S(2)}) collective-permute-start(bf16[576,768]{1,0:T(8,128)(2,1)} %get-tuple-element.106), channel_id=1, source_target_pairs={{0,16},{1,17},{2,18},{3,19},{4,20},{5,21},{6,22},{7,23},{8,24},{9,... | collective-permute-start | bytes 2654216 | tf_op jit(solution)/shard_map/ppermute | solution.py:74
  701.0 39.4 %collective-permute-start.30 = (bf16[576,768]{1,0:T(8,128)(2,1)}, bf16[576,768]{1,0:T(8,128)(2,1)}, u32[]{:S(2)}, u32[]{:S(2)}) collective-permute-start(bf16[576,768]{1,0:T(8,128)(2,1)} %get-tuple-element.107), channel_id=1, source_target_pairs={{0,24},{1,25},{2,26},{3,27},{4,28},{5,29},{6,30},{7,31},{8,16},{9,... | collective-permute-start | bytes 2654216 | tf_op jit(solution)/shard_map/ppermute | solution.py:74
  705.1 61.0 %collective-permute-start.51 = (bf16[3,768,256]{2,1,0:T(8,128)(2,1)S(1)}, bf16[3,768,256]{2,1,0:T(8,128)(2,1)}, u32[]{:S(2)}, u32[]{:S(2)}) collective-permute-start(bf16[3,768,256]{2,1,0:T(8,128)(2,1)S(1)} %add_convert_fusion.2), channel_id=1, source_target_pairs={{0,24},{1,25},{2,26},{3,27},{4,28},{5,29},{6,30},{7,31},{8,16},{9,... | collective-permute-start | bytes 3538952 | tf_op jit(solution)/shard_map/ppermute | solution.py:74
  723.4 67.4 %collective-permute-start.50 = (bf16[3,768,256]{2,1,0:T(8,128)(2,1)S(1)}, bf16[3,768,256]{2,1,0:T(8,128)(2,1)}, u32[]{:S(2)}, u32[]{:S(2)}) collective-permute-start(bf16[3,768,256]{2,1,0:T(8,128)(2,1)S(1)} %add_convert_fusion.2), channel_id=1, source_target_pairs={{0,16},{1,17},{2,18},{3,19},{4,20},{5,21},{6,22},{7,23},{8,24},{9,... | collective-permute-start | bytes 3538952 | tf_op jit(solution)/shard_map/ppermute | solution.py:74
  740.4 51.9 %collective-permute-start.49 = (bf16[3,768,256]{2,1,0:T(8,128)(2,1)S(1)}, bf16[3,768,256]{2,1,0:T(8,128)(2,1)}, u32[]{:S(2)}, u32[]{:S(2)}) collective-permute-start(bf16[3,768,256]{2,1,0:T(8,128)(2,1)S(1)} %add_convert_fusion.2), channel_id=1, source_target_pairs={{0,8},{1,9},{2,10},{3,11},{4,12},{5,13},{6,14},{7,15},{8,0},{9,1},... | collective-permute-start | bytes 3538952 | tf_op jit(solution)/shard_map/ppermute | solution.py:74
  758.3 34.4 %collective-permute-start.39 = (bf16[208,768]{1,0:T(8,128)(2,1)S(1)}, bf16[208,768]{1,0:T(8,128)(2,1)S(1)}, u32[]{:S(2)}, u32[]{:S(2)}) collective-permute-start(bf16[208,768]{1,0:T(8,128)(2,1)S(1)} %get-tuple-element.180), channel_id=1, source_target_pairs={{0,6},{1,7},{2,0},{3,1},{4,2},{5,3},{6,4},{7,5},{8,14},{9,15},{10,... | collective-permute-start | bytes 958472 | tf_op jit(solution)/shard_map/ppermute | solution.py:74
  758.3 45.3 %collective-permute-start.38 = (bf16[208,768]{1,0:T(8,128)(2,1)}, bf16[208,768]{1,0:T(8,128)(2,1)S(1)}, u32[]{:S(2)}, u32[]{:S(2)}) collective-permute-start(bf16[208,768]{1,0:T(8,128)(2,1)} %get-tuple-element.181), channel_id=1, source_target_pairs={{0,4},{1,5},{2,6},{3,7},{4,0},{5,1},{6,2},{7,3},{8,12},{9,13},{10,... | collective-permute-start | bytes 958472 | tf_op jit(solution)/shard_map/ppermute | solution.py:74
  766.1 37.5 %collective-permute-start.37 = (bf16[208,768]{1,0:T(8,128)(2,1)}, bf16[208,768]{1,0:T(8,128)(2,1)S(1)}, u32[]{:S(2)}, u32[]{:S(2)}) collective-permute-start(bf16[208,768]{1,0:T(8,128)(2,1)} %get-tuple-element.179), channel_id=1, source_target_pairs={{0,2},{1,3},{2,4},{3,5},{4,6},{5,7},{6,0},{7,1},{8,10},{9,11},{10,... | collective-permute-start | bytes 958472 | tf_op jit(solution)/shard_map/ppermute | solution.py:74
  790.7 16.8 %collective-permute-start.54 = (bf16[3,768,128]{2,1,0:T(8,128)(2,1)}, bf16[3,768,128]{2,1,0:T(8,128)(2,1)}, u32[]{:S(2)}, u32[]{:S(2)}) collective-permute-start(bf16[3,768,128]{2,1,0:T(8,128)(2,1)} %get-tuple-element.166), channel_id=1, source_target_pairs={{0,1},{1,0},{2,3},{3,2},{4,5},{5,4},{6,7},{7,6},{8,9},{9,8},{10,11... | collective-permute-start | bytes 1769480 | tf_op jit(solution)/shard_map/ppermute | solution.py:74
  792.2 27.7 %collective-permute-start.58 = (bf16[3,768,128]{2,1,0:T(8,128)(2,1)}, bf16[3,768,128]{2,1,0:T(8,128)(2,1)}, u32[]{:S(2)}, u32[]{:S(2)}) collective-permute-start(bf16[3,768,128]{2,1,0:T(8,128)(2,1)} %get-tuple-element.164), channel_id=1, source_target_pairs={{0,1},{1,0},{2,3},{3,2},{4,5},{5,4},{6,7},{7,6},{8,9},{9,8},{10,11... | collective-permute-start | bytes 1769480 | tf_op jit(solution)/shard_map/ppermute | solution.py:74
  792.8 39.8 %collective-permute-start.56 = (bf16[3,768,128]{2,1,0:T(8,128)(2,1)S(1)}, bf16[3,768,128]{2,1,0:T(8,128)(2,1)}, u32[]{:S(2)}, u32[]{:S(2)}) collective-permute-start(bf16[3,768,128]{2,1,0:T(8,128)(2,1)S(1)} %get-tuple-element.165), channel_id=1, source_target_pairs={{0,1},{1,0},{2,3},{3,2},{4,5},{5,4},{6,7},{7,6},{8,9},{9,8},{10,11... | collective-permute-start | bytes 1769480 | tf_op jit(solution)/shard_map/ppermute | solution.py:74
  806.5 31.6 %collective-permute-start.40 = (bf16[208,768]{1,0:T(8,128)(2,1)S(1)}, bf16[208,768]{1,0:T(8,128)(2,1)S(1)}, u32[]{:S(2)}, u32[]{:S(2)}) collective-permute-start(bf16[208,768]{1,0:T(8,128)(2,1)S(1)} %get-tuple-element.158), channel_id=1, source_target_pairs={{0,16},{1,17},{2,18},{3,19},{4,20},{5,21},{6,22},{7,23},{8,24},{9,... | collective-permute-start | bytes 958472 | tf_op jit(solution)/shard_map/ppermute | solution.py:74
  807.0 35.0 %collective-permute-start.53 = (bf16[3,768,128]{2,1,0:T(8,128)(2,1)S(1)}, bf16[3,768,128]{2,1,0:T(8,128)(2,1)S(1)}, u32[]{:S(2)}, u32[]{:S(2)}) collective-permute-start(bf16[3,768,128]{2,1,0:T(8,128)(2,1)S(1)} %get-tuple-element.163), channel_id=1, source_target_pairs={{0,1},{1,0},{2,3},{3,2},{4,5},{5,4},{6,7},{7,6},{8,9},{9,8},{10,11... | collective-permute-start | bytes 1769480 | tf_op jit(solution)/shard_map/ppermute | solution.py:74
  835.0 13.8 %collective-permute-start.59 = (bf16[3,768,128]{2,1,0:T(8,128)(2,1)S(1)}, bf16[3,768,128]{2,1,0:T(8,128)(2,1)S(1)}, u32[]{:S(2)}, u32[]{:S(2)}) collective-permute-start(bf16[3,768,128]{2,1,0:T(8,128)(2,1)S(1)} %get-tuple-element.168), channel_id=1, source_target_pairs={{0,6},{1,7},{2,0},{3,1},{4,2},{5,3},{6,4},{7,5},{8,14},{9,15},{10,... | collective-permute-start | bytes 1769480 | tf_op jit(solution)/shard_map/ppermute | solution.py:74
  835.1 44.8 %collective-permute-start.57 = (bf16[3,768,128]{2,1,0:T(8,128)(2,1)S(1)}, bf16[3,768,128]{2,1,0:T(8,128)(2,1)S(1)}, u32[]{:S(2)}, u32[]{:S(2)}) collective-permute-start(bf16[3,768,128]{2,1,0:T(8,128)(2,1)S(1)} %get-tuple-element.169), channel_id=1, source_target_pairs={{0,4},{1,5},{2,6},{3,7},{4,0},{5,1},{6,2},{7,3},{8,12},{9,13},{10,... | collective-permute-start | bytes 1769480 | tf_op jit(solution)/shard_map/ppermute | solution.py:74
  835.2 44.7 %collective-permute-start.55 = (bf16[3,768,128]{2,1,0:T(8,128)(2,1)S(1)}, bf16[3,768,128]{2,1,0:T(8,128)(2,1)S(1)}, u32[]{:S(2)}, u32[]{:S(2)}) collective-permute-start(bf16[3,768,128]{2,1,0:T(8,128)(2,1)S(1)} %get-tuple-element.167), channel_id=1, source_target_pairs={{0,2},{1,3},{2,4},{3,5},{4,6},{5,7},{6,0},{7,1},{8,10},{9,11},{10,... | collective-permute-start | bytes 1769480 | tf_op jit(solution)/shard_map/ppermute | solution.py:74
  838.8 50.6 %collective-permute-start.41 = (bf16[208,768]{1,0:T(8,128)(2,1)}, bf16[208,768]{1,0:T(8,128)(2,1)}, u32[]{:S(2)}, u32[]{:S(2)}) collective-permute-start(bf16[208,768]{1,0:T(8,128)(2,1)} %fusion.20), channel_id=1, source_target_pairs={{0,8},{1,9},{2,10},{3,11},{4,12},{5,13},{6,14},{7,15},{8,0},{9,1},... | collective-permute-start | bytes 958472 | tf_op jit(solution)/shard_map/ppermute | solution.py:74
  881.3 9.9 %collective-permute-start.60 = (bf16[3,768,128]{2,1,0:T(8,128)(2,1)S(1)}, bf16[3,768,128]{2,1,0:T(8,128)(2,1)S(1)}, u32[]{:S(2)}, u32[]{:S(2)}) collective-permute-start(bf16[3,768,128]{2,1,0:T(8,128)(2,1)S(1)} %get-tuple-element.156), channel_id=1, source_target_pairs={{0,16},{1,17},{2,18},{3,19},{4,20},{5,21},{6,22},{7,23},{8,24},{9,... | collective-permute-start | bytes 1769480 | tf_op jit(solution)/shard_map/ppermute | solution.py:74
  891.4 2.4 collective-permute-start.61
  (25 other events, 359.5 us)

commit v2 on v1

--- a/solution.py
+++ b/solution.py
@@ -46,15 +46,18 @@
     return jnp.where(cond, 1.0, 0.0).astype(BF)
 
 
-def call(kernel, out_shape, in_specs, out_specs, scratch=(), flops=0, moved=0, grid=None):
+def call(
+    kernel, out_shape, in_specs, out_specs, scratch=(), flops=0, moved=0, grid=None, group=None
+):
     extra = {} if grid is None else {"grid": grid}
+    params = {} if group is None else {"collective_id": group, "has_side_effects": True}
     return pl.pallas_call(
         kernel,
         out_shape=out_shape,
         in_specs=in_specs,
         out_specs=out_specs,
         scratch_shapes=list(scratch),
-        compiler_params=pltpu.CompilerParams(vmem_limit_bytes=VMEM_LIMIT),
+        compiler_params=pltpu.CompilerParams(vmem_limit_bytes=VMEM_LIMIT, **params),
         cost_estimate=pl.CostEstimate(flops=flops, bytes_accessed=moved, transcendentals=0),
         **extra,
     )
@@ -103,9 +106,18 @@
     return near[0] + got[0] + got[1] + got[2]
 
 
-def prep_kernel(info, routes, routes_t, cot, rank_out, slot_out, *packed):
-    tokens = cot.shape[0]
-    rep = info[0]
+def spin(block, cosine, sine):
+    lane = iota(block.shape, 1)
+    partner = jnp.where(lane % 64 < 32, pltpu.roll(block, 96, 1), pltpu.roll(block, 32, 1))
+    return block * cosine + partner * sine
+
+
+def sibling(rep, o):
+    return 2 * lax.rem(lax.div(rep, 2) + o // 2, 2) + lax.rem(lax.rem(rep, 2) + o % 2, 2)
+
+
+def route_slots(rep, routes, routes_t, rank_out, slot_out):
+    tokens = routes.shape[0]
     first, second = routes_t[0:1, :], routes_t[1:2, :]
     expert = iota((8, tokens), 0)
     chosen = (expert == first) | (expert == second)
@@ -116,57 +128,24 @@
     one, two = routes[:, 0:1], routes[:, 1:2]
     lower = ones_where(iota((tokens, tokens), 0) >= iota((tokens, tokens), 1))
     place = nn(lower, ones_where((lane == one) | (lane == two))) - 1.0
-    place = place + ((lane ^ rep) * CAP).astype(F32)
+    for o in range(1, 4):
+        place = place + jnp.where(lane == sibling(rep, o), float(o * CAP), 0.0)
     slot_one = jnp.sum(jnp.where(lane == one, place, 0.0), axis=1, keepdims=True)
     slot_two = jnp.sum(jnp.where(lane == two, place, 0.0), axis=1, keepdims=True)
     slot_out[...] = jnp.where(lane < 64, slot_one, slot_two)
+
+
+def pack_rows(rep, rank, source, packed):
+    tokens = source.shape[0]
     for o, out in enumerate(packed):
-        row = rank_out[pl.ds(rep ^ o, 1), :]
+        row = rank[pl.ds(sibling(rep, o), 1), :]
         pick = ones_where(iota((CAP, tokens), 0).astype(F32) == row)
-        out[...] = nn(pick, cot[...]).astype(BF)
-
-
-def spin(block, cosine, sine):
-    lane = iota(block.shape, 1)
-    partner = jnp.where(lane % 64 < 32, pltpu.roll(block, 96, 1), pltpu.roll(block, 32, 1))
-    return block * cosine + partner * sine
-
-
-def qkv_kernel(
-    info, x, own, other, cosine, sine, q, k, v, wq, wk, wv, wo, ext, ext_all, sems
-):
+        out[...] = nn(pick, source[...]).astype(BF)
+
+
+def qkv_rows(x, ext, cosine, sine, wq, wk, wv, q, k, v):
     tokens, width = x.shape
-    rows = own.shape[1] - 16
-    half = rows // 2
-
-    def copies(low, high):
-        made = []
-        for j in range(SLOTS):
-            at = pl.ds(pl.multiple_of(info[2 + j] * half, 32), half)
-            made.append((low.at[j, pl.ds(0, half)], wq.at[at]))
-            made.append((low.at[j, pl.ds(half, half)], wk.at[at]))
-            made.append((low.at[j, pl.ds(rows, 16)], ext_all.at[j]))
-            made.append((high.at[j, pl.ds(0, half)], wv.at[at]))
-            made.append((high.at[j, pl.ds(half, half)], wo.at[at]))
-        return [pltpu.make_async_copy(a, b, sems.at[i]) for i, (a, b) in enumerate(made)]
-
-    @pl.when(info[1] == 0)
-    def _():
-        for copy in copies(own, other):
-            copy.start()
-
-    @pl.when(info[1] != 0)
-    def _():
-        for copy in copies(other, own):
-            copy.start()
-
-    for copy in copies(own, other):
-        copy.wait()
-    gathered = ext_all[0].astype(F32)
-    for j in range(1, SLOTS):
-        gathered = gathered + ext_all[j].astype(F32)
-    ext[...] = gathered
-    gain = gathered[4:5, :]
+    gain = ext[4:5, :]
 
     def tile(t, carry):
         at = pl.ds(pl.multiple_of(t * TILE, TILE), TILE)
@@ -183,6 +162,165 @@
         return carry
 
     lax.fori_loop(0, tokens // TILE, tile, 0)
+
+
+def when(cond, body):
+    if cond is True:
+        body()
+    elif cond is not False:
+        pl.when(cond)(body)
+
+
+def both(one, two):
+    if one is True or two is False:
+        return two
+    if two is True or one is False:
+        return one
+    return one & two
+
+
+class Line:
+    def __init__(self, rep, shard, bank, send, recv):
+        self.rep, self.shard, self.bank = rep, shard, bank
+        self.core, self.z = lax.rem(rep, 2), lax.div(shard, 2)
+        self.x = lax.rem(shard, 2)
+        self.send, self.recv = send, recv
+        self.mate = rep + 1 - 2 * self.core
+        self.across = shard + 1 - 2 * self.x
+        self.started = []
+
+    def near(self, k):
+        if k == 0:
+            return self.shard, True
+        if k > 0:
+            return lax.min(self.shard + 2 * k, 6 + self.x), self.z < 4 - k
+        return lax.max(self.shard + 2 * k, self.x), self.z >= -k
+
+    def copy(self, way, k, source, half, place, rep, shard):
+        event = way * 7 + k + 3
+        return pltpu.make_async_remote_copy(
+            src_ref=source,
+            dst_ref=self.bank.at[half, place],
+            send_sem=self.send.at[event],
+            recv_sem=self.recv.at[event],
+            device_id=(rep, shard),
+            device_id_type=pl.DeviceIdType.MESH,
+        )
+
+    def start(self, cond, way, k, source, half, place, rep, shard):
+        copy = self.copy(way, k, source, half, place, rep, shard)
+        when(cond, copy.start)
+        self.started.append((cond, copy))
+
+    def spread(self, k, source):
+        place, here = self.near(k)
+        if k <= 0 and k > -3:
+            up, more = self.near(1)
+            self.start(both(here, more), 0, k - 1, source, self.core, place, self.rep, up)
+        if k >= 0 and k < 3:
+            down, more = self.near(-1)
+            self.start(both(here, more), 0, k + 1, source, self.core, place, self.rep, down)
+        self.start(here, 1, k, source, self.core, place, self.rep, self.across)
+        self.start(here, 2, k, source, self.core, place, self.mate, self.shard)
+
+    def arrive(self, cond, way, k, half, place):
+        copy = self.copy(way, k, self.bank.at[half, place], half, place, self.mate, self.shard)
+        when(cond, copy.wait_recv)
+
+    def along(self, k):
+        place, here = self.near(k)
+        self.arrive(here, 0, k, self.core, place)
+        self.spread(k, self.bank.at[self.core, place])
+
+    def over(self, k):
+        place, here = self.near(k)
+        place = place + 1 - 2 * self.x
+        self.arrive(here, 1, k, self.core, place)
+        piece = self.bank.at[self.core, place]
+        self.start(here, 3, k, piece, self.core, place, self.mate, self.shard)
+
+    def finish(self):
+        for k in (0, 1, -1, 2, -2, 3, -3):
+            place, here = self.near(k)
+            self.arrive(here, 2, k, 1 - self.core, place)
+            self.arrive(here, 3, k, 1 - self.core, place + 1 - 2 * self.x)
+        for cond, copy in self.started:
+            when(cond, copy.wait_send)
+
+
+def meet(rep, shard, z_ways, others):
+    barrier = pltpu.get_barrier_semaphore()
+    z, x = lax.div(shard, 2), lax.rem(shard, 2)
+    count = len(others)
+    for to_rep_, to_shard in others:
+        pl.semaphore_signal(
+            barrier, inc=1, device_id=(to_rep_, to_shard), device_id_type=pl.DeviceIdType.MESH
+        )
+    if z_ways:
+        for cond, to_shard in (
+            (z < 3, lax.min(shard + 2, 6 + x)),
+            (z > 0, lax.max(shard - 2, x)),
+        ):
+
+            @pl.when(cond)
+            def _():
+                pl.semaphore_signal(
+                    barrier, inc=1, device_id=(rep, to_shard), device_id_type=pl.DeviceIdType.MESH
+                )
+
+        count = count + lax.min(z, 1) + lax.min(3 - z, 1)
+    pl.semaphore_wait(barrier, count)
+
+
+def head_kernel(
+    routes, routes_t, cot, x, piece, cosine, sine,
+    rank, slot, c0, c1, c2, c3, q, k, v, wq, wk, wv, wo, ext,
+    bank, send, recv, own_sem,
+):
+    width = x.shape[1]
+    half = width // SLOTS
+    rep, shard = lax.axis_index("rep"), lax.axis_index("shard")
+    line = Line(rep, shard, bank, send, recv)
+    meet(rep, shard, True, [(line.mate, shard), (rep, line.across)])
+    line.spread(0, piece)
+    own = pltpu.make_async_copy(piece, bank.at[line.core, shard], own_sem)
+    own.start()
+    route_slots(rep, routes, routes_t, rank, slot)
+    pack_rows(rep, rank, cot, (c0, c1, c2, c3))
+    line.along(1)
+    line.along(-1)
+    line.over(0)
+    line.along(2)
+    line.along(-2)
+    line.over(1)
+    line.over(-1)
+    line.along(3)
+    line.along(-3)
+    for step in (2, -2, 3, -3):
+        line.over(step)
+    own.wait()
+    line.finish()
+    gathered = bank[0, 0, 2 * half : 2 * half + 16, :].astype(F32)
+    for j in range(1, SLOTS):
+        gathered = gathered + bank[0, j, 2 * half : 2 * half + 16, :].astype(F32)
+    ext[...] = gathered
+    for j in range(SLOTS):
+        at = slice(j * half, (j + 1) * half)
+        wq[at, :] = bank[0, j, 0:half, :]
+        wk[at, :] = bank[0, j, half : 2 * half, :]
+        wv[at, :] = bank[1, j, 0:half, :]
+        wo[at, :] = bank[1, j, half : 2 * half, :]
+    qkv_rows(x, ext, cosine, sine, wq, wk, wv, q, k, v)
+
+
+def plain_head_kernel(
+    routes, routes_t, cot, x, cosine, sine, wq, wk, wv, ext,
+    rank, slot, c0, c1, c2, c3, q, k, v,
+):
+    rep = lax.axis_index("rep")
+    route_slots(rep, routes, routes_t, rank, slot)
+    pack_rows(rep, rank, cot, (c0, c1, c2, c3))
+    qkv_rows(x, ext, cosine, sine, wq, wk, wv, q, k, v)
 
 
 def fill_bias(starts, bias):
@@ -681,26 +819,48 @@
         half_one = jnp.concatenate([query_weight, key_weight, small], axis=0)
         half_two = jnp.concatenate([value_weight, out_weight, blank], axis=0)
         piece = jnp.where(core == 0, half_one, half_two)
-        attn_parts = gather_slots(piece)
-        attn_own = jnp.stack(attn_parts)
-        attn_other = to_rep(attn_own, 1)
     else:
-        full = [
-            lax.all_gather(w, "shard", axis=0, tiled=True).reshape(SLOTS, -1, width)
+        wq, wk, wv, wo = [
+            lax.all_gather(w, "shard", axis=0, tiled=True)
             for w in (query_weight, key_weight, value_weight, out_weight)
         ]
-        small = lax.psum(small.astype(F32), "shard").astype(BF)
-        small = jnp.concatenate([small[None], jnp.zeros((7, 16, width), BF)], axis=0)
-        half_one = jnp.concatenate([full[0], full[1], small], axis=1)
-        half_two = jnp.concatenate([full[2], full[3], jnp.zeros_like(small)], axis=1)
-        attn_own = jnp.where(core == 0, half_one, half_two)
-        attn_other = jnp.where(core == 0, half_two, half_one)
+        ext = lax.psum(small.astype(F32), "shard")
+
+    cosine, sine = rope_tables(tokens, width // HEADS)
+    token_f = shape((tokens, width))
+    square = shape((width, width))
+    packed = [shape((CAP, width))] * 4
+    outs = [shape((8, tokens), F32), shape((tokens, 128), F32)] + packed + [token_f] * 3
+    work = 2 * tokens * width * (CAP * 4 + 3 * width)
+    if ringed:
+        rank, slot, *heads = call(
+            head_kernel,
+            outs + [square] * 4 + [shape((16, width), F32)],
+            [VMEM] * 7,
+            [VMEM] * 14,
+            [
+                pltpu.VMEM((2, SLOTS, 2 * rows + 16, width), BF),
+                pltpu.SemaphoreType.DMA((28,)),
+                pltpu.SemaphoreType.DMA((28,)),
+                pltpu.SemaphoreType.DMA,
+            ],
+            flops=work,
+            moved=24 * 2**20,
+            group=0,
+        )(chosen, chosen.T, cot, x, piece, cosine, sine)
+        wq, wk, wv, wo, ext = heads[7:]
+    else:
+        rank, slot, *heads = call(
+            plain_head_kernel, outs, [VMEM] * 10, [VMEM] * 9, flops=work, moved=24 * 2**20
+        )(chosen, chosen.T, cot, x, cosine, sine, wq, wk, wv, ext)
+    cot_out = heads[:4]
+    q, k, v = heads[4:7]
 
     shared_pack = jnp.stack([shared_gate, shared_up, shared_down.T])
     my_half = lax.dynamic_slice_in_dim(shared_pack, core * (units // 2), units // 2, 2)
     expert_pack = jnp.stack([expert_gate[rep], expert_up[rep], expert_down[rep].T])
     if ringed:
-        my_half = after(my_half, attn_own)
+        my_half = after(my_half, q)
         shared_own = jnp.stack(gather_slots(my_half))
         shared_other = to_rep(shared_own, 1)
         expert_pack = after(expert_pack, shared_own)
@@ -717,29 +877,7 @@
         expert_every = slotted(expert_pack)
         expert_slots = [expert_every[j] for j in range(SLOTS)]
 
-    packed = [shape((CAP, width))] * 4
-    rank, slot, *cot_out = call(
-        prep_kernel,
-        [shape((8, tokens), F32), shape((tokens, 128), F32)] + packed,
-        [SMEM, VMEM, VMEM, VMEM],
-        [VMEM] * 6,
-        flops=2 * tokens * width * CAP * 4,
-        moved=8 * 2**20,
-    )(info, chosen, chosen.T, cot)
     cot_in = [cot_out[0]] + [to_rep(cot_out[o], o) for o in (1, 2, 3)]
-
-    cosine, sine = rope_tables(tokens, width // HEADS)
-    token_f = shape((tokens, width))
-    square = shape((width, width))
-    q, k, v, wq, wk, wv, wo, ext = call(
-        qkv_kernel,
-        [token_f] * 3 + [square] * 4 + [shape((16, width), F32)],
-        [SMEM, VMEM, ANY, ANY, VMEM, VMEM],
-        [VMEM] * 8,
-        [pltpu.VMEM((SLOTS, 16, width), BF), pltpu.SemaphoreType.DMA((5 * SLOTS,))],
-        flops=6 * tokens * width * width,
-        moved=16 * 2**20,
-    )(info, x, attn_own, attn_other, cosine, sine)
 
     pair = pl.BlockSpec((tokens, 128), lambda i: (0, i))
     table = pl.BlockSpec((tokens, 128), lambda i: (0, 0))

time: 911 us -> 904 us (level)
  Pallas kernels: 302 us -> 331 us
  waiting for transfers between devices: 453 us -> 437 us
  starting transfers between devices: 52.4 us -> 43.2 us
    pallas_call x2 -> x1, Pallas kernels: 19.1 us -> 48.2 us  [body(): call(head_kernel, outs + [square] * 4 + [shape((16, width), F32)], [VMEM]...]
    ppermute x62 -> x54, waiting for transfers between devices: 453 us -> 437 us  [permute(): return lax.ppermute(x, AXES, pairs)]
    ppermute x62 -> x54, starting transfers between devices: 52.4 us -> 43.2 us  [permute(): return lax.ppermute(x, AXES, pairs)]
    unnamed x70 -> x86, local copies, waits for them, and re-layouts: 26.2 us -> 23.3 us
  transfers between devices with their start and end apart: 62 -> 54, of which waited for: 25 -> 24; matrix products, arithmetic and copies ran while one was open for 8% -> 6% of each run, Pallas kernels for 25% -> 23%
where the time goes in v2:
time: 904 us; the launch traced here: 891 us
  waiting for transfers between devices  437 us (48%)
  Pallas kernels  331 us (37%)
  local copies, waits for them, and re-layouts  45.4 us (5%)
  starting transfers between devices  43.2 us (5%)
  other arithmetic  32.5 us (4%)
    ppermute x54, waiting for transfers between devices, permute(): return lax.ppermute(x, AXES, pairs)  437 us
    pallas_call x3, Pallas kernels, ffn(): call(functools.partial(ffn_kernel, blocks, weights, unit, routed, chained...  150 us
    pallas_call x1, Pallas kernels, body(): call(head_kernel, outs + [square] * 4 + [shape((16, width), F32)], [VMEM]...  48.2 us
    ppermute x54, starting transfers between devices, permute(): return lax.ppermute(x, AXES, pairs)  43.2 us
    pallas_call x1, Pallas kernels, body(): call(attend_back_kernel, [token_f] * 3, [SMEM] + [pair] * 6 + [table] * 2...  42.3 us
    pallas_call x1, Pallas kernels, body(): call(attend_kernel, [token_f, shape((tokens, width), F32)], [SMEM, pair,...  27.5 us
    unnamed x86, local copies, waits for them, and re-layouts  23.3 us
    pallas_call x1, Pallas kernels, body(): call(combine_kernel, [shape((tokens, width), F32), token_f, square, shape...  20.9 us
  transfers between devices with their start and end apart: 54, of which 24 were waited for; matrix products, arithmetic and copies ran while one was open for 6% of the time, Pallas kernels for 23%

profile of v2, /device:TPU:0, one launch (start us, length us, event | category | flops | bytes accessed | tf_op | source)
XLA Modules:
  0.0 890.7 jit_solution(2294626591374010441)
XLA Ops:
  0.7 1.8 copy.32.routes
  2.5 2.0 fusion.20
  7.7 1.8 pad_maximum_fusion.3
  11.3 48.2 %shard_map.280 = (f32[8,1024]{1,0:T(8,128)}, f32[1024,128]{1,0:T(8,128)}, bf16[576,768]{1,0:T(8,128)(2,1)}, bf16[576,768]{1,0:T(8,128)(2,1)}, bf16[576,768]{1,0:...) custom-call(s32[1024,2]{1,0:T(8,128)} %copy.32.routes, ...), custom_call_target="tpu_custom_call" | custom-call | flops 7247757312 | bytes 25165824 | tf_op jit(solution)/shard_map/pallas_call | solution.py:836
  59.6 2.1 collective-permute-start.2
  63.4 27.5 %shard_map.281 = (bf16[1024,768]{1,0:T(8,128)(2,1)}, f32[1024,768]{1,0:T(8,128)}) custom-call(s32[1,2]{1,0:T(1,128)} %starts.3, bf16[1024,768]{1,0:T(8,128)(2,1)} %get-tuple-element.80.q, bf16[1024,768]{1,0:T(8,128)(2,1)} %get-tuple-element.81.k, bf16[1024,768]{1,0:T(8,128)(2,1)} %get-tuple-element.82.v), custom_call_target="tpu_custom_call" | custom-call | flops 12884901888 | bytes 10485760 | tf_op jit(solution)/shard_map/pallas_call | solution.py:884
  91.5 11.4 %shard_map.282 = (f32[1024,768]{1,0:T(8,128)}, bf16[1024,768]{1,0:T(8,128)(2,1)}, f32[1024,128]{1,0:T(8,128)}, bf16[576,768]{1,0:T(8,128)(2,1)}, bf16[576,768]{1...) custom-call(s32[10]{0:T(128)} %stack.103.info.refs_0_, bf16[1024,768]{1,0:T(8,128)(2,1)} %bitcast.132, ...), custom_call_target="tpu_custom_call" | custom-call | flops 4831838208 | bytes 14680064 | tf_op jit(solution)/shard_map/pallas_call | solution.py:895
  102.9 1.5 collective-permute-start.16
  108.2 1.9 bitcast_dynamic-update-slice_fusion.6
  110.1 3.0 collective-permute-done.3
  113.7 2.0 bitcast_dynamic-update-slice_fusion.5
  117.1 2.0 bitcast_dynamic-update-slice_fusion.4
  119.1 1.9 bitcast_dynamic-update-slice_fusion.3
  121.0 2.3 collective-permute-done.6
  124.2 11.8 %collective-permute-done.7 = bf16[3,768,128]{2,1,0:T(8,128)(2,1)S(1)} collective-permute-done((bf16[3,768,128]{2,1,0:T(8,128)(2,1)}, bf16[3,768,128]{2,1,0:T(8,128)(2,1)S(1)}, u32[]{:S(2)}, u32[]{:S(2)}) %collective-permute-start.7) | collective-permute-done | bytes 589856 | tf_op jit(solution)/shard_map/ppermute | solution.py:77
  136.8 9.8 %collective-permute-done.8 = bf16[3,768,128]{2,1,0:T(8,128)(2,1)S(1)} collective-permute-done((bf16[3,768,128]{2,1,0:T(8,128)(2,1)}, bf16[3,768,128]{2,1,0:T(8,128)(2,1)S(1)}, u32[]{:S(2)}, u32[]{:S(2)}) %collective-permute-start.8) | collective-permute-done | bytes 589856 | tf_op jit(solution)/shard_map/ppermute | solution.py:77
  147.5 2.7 collective-permute-start.9
  152.1 21.4 %collective-permute-done.17.refs_3_ = bf16[576,768]{1,0:T(8,128)(2,1)} collective-permute-done((bf16[576,768]{1,0:T(8,128)(2,1)S(1)}, bf16[576,768]{1,0:T(8,128)(2,1)}, u32[]{:S(2)}, u32[]{:S(2)}) %collective-permute-start.17) | collective-permute-done | bytes 884768 | tf_op jit(solution)/shard_map/ppermute | solution.py:77
  173.5 1.6 collective-permute-start.12
  175.1 1.5 collective-permute-done.9.refs_7_
  176.6 1.7 collective-permute-start.13
  178.3 72.4 %collective-permute-done.10.refs_8_ = bf16[3,768,256]{2,1,0:T(8,128)(2,1)S(1)} collective-permute-done((bf16[3,768,256]{2,1,0:T(8,128)(2,1)S(1)}, bf16[3,768,256]{2,1,0:T(8,128)(2,1)S(1)}, u32[]{:S(2)}, u32[]{:S(2)}) %collective-permute-start.10) | collective-permute-done | bytes 1179680 | tf_op jit(solution)/shard_map/ppermute | solution.py:77
  250.7 1.7 collective-permute-start.14
  252.8 21.0 %collective-permute-done.19.refs_5_ = bf16[576,768]{1,0:T(8,128)(2,1)S(1)} collective-permute-done((bf16[576,768]{1,0:T(8,128)(2,1)S(1)}, bf16[576,768]{1,0:T(8,128)(2,1)S(1)}, u32[]{:S(2)}, u32[]{:S(2)}) %collective-permute-start.19) | collective-permute-done | bytes 884768 | tf_op jit(solution)/shard_map/ppermute | solution.py:77
  274.5 5.1 collective-permute-done.14.refs_12_
  280.7 20.4 %collective-permute-done.15.refs_13_ = bf16[3,768,256]{2,1,0:T(8,128)(2,1)} collective-permute-done((bf16[3,768,256]{2,1,0:T(8,128)(2,1)S(1)}, bf16[3,768,256]{2,1,0:T(8,128)(2,1)}, u32[]{:S(2)}, u32[]{:S(2)}) %collective-permute-start.15) | collective-permute-done | bytes 1179680 | tf_op jit(solution)/shard_map/ppermute | solution.py:77
  301.1 54.0 %shard_map.283 = (bf16[576,768]{1,0:T(8,128)(2,1)}, bf16[576,768]{1,0:T(8,128)(2,1)}, bf16[592,768]{1,0:T(8,128)(2,1)}, bf16[592,768]{1,0:T(8,128)(2,1)}, bf16[3...) custom-call(s32[10]{0:T(128)} %stack.103.info.refs_0_, ...), custom_call_target="tpu_custom_call" | custom-call | flops 32614907904 | bytes 31457280 | tf_op jit(solution)/shard_map/pallas_call | solution.py:598
  355.2 55.1 %shard_map.284 = (bf16[576,768]{1,0:T(8,128)(2,1)}, bf16[576,768]{1,0:T(8,128)(2,1)}, bf16[592,768]{1,0:T(8,128)(2,1)}, bf16[592,768]{1,0:T(8,128)(2,1)}, bf16[3...) custom-call(s32[10]{0:T(128)} %stack.103.info.refs_0_, ...), custom_call_target="tpu_custom_call" | custom-call | flops 32614907904 | bytes 31457280 | tf_op jit(solution)/shard_map/pallas_call | solution.py:598
  412.3 41.2 %shard_map.285 = (bf16[1024,768]{1,0:T(8,128)(2,1)}, bf16[1024,768]{1,0:T(8,128)(2,1)}, bf16[8,3,768,128]{3,2,1,0:T(8,128)(2,1)}, bf16[8,3,768,128]{3,2,1,0:T(8,128)(2,1)}) custom-call(s32[10]{0:T(128)} %stack.103.info.refs_0_, f32[16,768]{1,0:T(8,128)} %get-tuple-element.79.ext.refs_1_, bf16[1024,768]{1,0:T(8,128)(2,1)} %get-tuple-element.108.refs_2_.normed, ...), custom_call_target="tpu_custom_call" | custom-call | flops 28991029248 | bytes 31457280 | tf_op jit(solution)/shard_map/pallas_call | solution.py:598
  453.5 20.9 %shard_map.287 = (f32[1024,768]{1,0:T(8,128)}, bf16[1024,768]{1,0:T(8,128)(2,1)}, bf16[768,768]{1,0:T(8,128)(2,1)}, f32[16,768]{1,0:T(8,128)}) custom-call(s32[10]{0:T(128)} %stack.103.info.refs_0_, f32[1024,128]{1,0:T(8,128)} %get-tuple-element.78.slot, bf16[592,768]{1,0:T(8,128)(2,1)} %get-tuple-element.112.d0, ...), custom_call_target="tpu_custom_call" | custom-call | flops 6039797760 | bytes 25165824 | tf_op jit(solution)/shard_map/pallas_call | solution.py:926
  474.4 42.3 %shard_map.288 = (bf16[1024,768]{1,0:T(8,128)(2,1)}, bf16[1024,768]{1,0:T(8,128)(2,1)}, bf16[1024,768]{1,0:T(8,128)(2,1)}) custom-call(s32[1,2]{1,0:T(1,128)} %starts.3, bf16[1024,768]{1,0:T(8,128)(2,1)} %get-tuple-element.80.q, bf16[1024,768]{1,0:T(8,128)(2,1)} %get-tuple-element.81.k, bf16[1024,768]{1,0:T(8,128)(2,1)} %get-tuple-element.82.v, ...), custom_call_target="tpu_custom_call" | custom-call | flops 32212254720 | bytes 14680064 | tf_op jit(solution)/shard_map/pallas_call | solution.py:948
  516.7 18.6 %shard_map.289 = (f32[1024,768]{1,0:T(8,128)}, bf16[8,208,768]{2,1,0:T(8,128)(2,1)}, bf16[8,208,768]{2,1,0:T(8,128)(2,1)}) custom-call(s32[10]{0:T(128)} %stack.103.info.refs_0_, bf16[1024,768]{1,0:T(8,128)(2,1)} %bitcast.133, f32[16,768]{1,0:T(8,128)} %get-tuple-element.79.ext.refs_1_, bf16[1024,768]{1,0:T(8,128)(2,1)} %get-tuple-element.119.dq, ...), custom_call_target="tpu_custom_call" | custom-call | flops 7247757312 | bytes 25165824 | tf_op jit(solution)/shard_map/pallas_call | solution.py:964
  535.7 1.7 collective-permute-start.39
  537.7 1.7 collective-permute-start.35
  539.4 25.3 %collective-permute-done.39 = bf16[3,768,256]{2,1,0:T(8,128)(2,1)S(1)} collective-permute-done((bf16[3,768,256]{2,1,0:T(8,128)(2,1)}, bf16[3,768,256]{2,1,0:T(8,128)(2,1)S(1)}, u32[]{:S(2)}, u32[]{:S(2)}) %collective-permute-start.39) | collective-permute-done | bytes 1179680 | tf_op jit(solution)/shard_map/ppermute | solution.py:77
  564.7 1.7 collective-permute-start.34
  566.7 23.2 %collective-permute-done.37 = bf16[3,768,256]{2,1,0:T(8,128)(2,1)S(1)} collective-permute-done((bf16[3,768,256]{2,1,0:T(8,128)(2,1)}, bf16[3,768,256]{2,1,0:T(8,128)(2,1)S(1)}, u32[]{:S(2)}, u32[]{:S(2)}) %collective-permute-start.37) | collective-permute-done | bytes 1179680 | tf_op jit(solution)/shard_map/ppermute | solution.py:77
  590.3 25.0 %collective-permute-done.35 = bf16[3,768,256]{2,1,0:T(8,128)(2,1)S(1)} collective-permute-done((bf16[3,768,256]{2,1,0:T(8,128)(2,1)}, bf16[3,768,256]{2,1,0:T(8,128)(2,1)S(1)}, u32[]{:S(2)}, u32[]{:S(2)}) %collective-permute-start.35) | collective-permute-done | bytes 1179680 | tf_op jit(solution)/shard_map/ppermute | solution.py:77
  620.3 19.5 %collective-permute-done.34 = bf16[3,768,256]{2,1,0:T(8,128)(2,1)} collective-permute-done((bf16[3,768,256]{2,1,0:T(8,128)(2,1)}, bf16[3,768,256]{2,1,0:T(8,128)(2,1)}, u32[]{:S(2)}, u32[]{:S(2)}) %collective-permute-start.34) | collective-permute-done | bytes 1179680 | tf_op jit(solution)/shard_map/ppermute | solution.py:77
  639.8 1.7 collective-permute-start.28
  641.6 49.5 %collective-permute-done.38 = bf16[3,768,256]{2,1,0:T(8,128)(2,1)} collective-permute-done((bf16[3,768,256]{2,1,0:T(8,128)(2,1)S(1)}, bf16[3,768,256]{2,1,0:T(8,128)(2,1)}, u32[]{:S(2)}, u32[]{:S(2)}) %collective-permute-start.38) | collective-permute-done | bytes 1179680 | tf_op jit(solution)/shard_map/ppermute | solution.py:77
  692.6 3.1 add_convert_fusion.2
  696.5 17.4 %collective-permute-done.21.o2 = bf16[576,768]{1,0:T(8,128)(2,1)} collective-permute-done((bf16[576,768]{1,0:T(8,128)(2,1)}, bf16[576,768]{1,0:T(8,128)(2,1)}, u32[]{:S(2)}, u32[]{:S(2)}) %collective-permute-start.21) | collective-permute-done | bytes 884768 | tf_op jit(solution)/shard_map/ppermute | solution.py:77
  714.4 16.5 %collective-permute-done.22.o3 = bf16[576,768]{1,0:T(8,128)(2,1)} collective-permute-done((bf16[576,768]{1,0:T(8,128)(2,1)}, bf16[576,768]{1,0:T(8,128)(2,1)}, u32[]{:S(2)}, u32[]{:S(2)}) %collective-permute-start.22) | collective-permute-done | bytes 884768 | tf_op jit(solution)/shard_map/ppermute | solution.py:77
  730.9 2.1 collective-permute-start.41
  733.0 11.5 %shard_map.286 = bf16[1024,768]{1,0:T(8,128)(2,1)} custom-call(s32[10]{0:T(128)} %stack.103.info.refs_0_, f32[1024,128]{1,0:T(8,128)} %get-tuple-element.78.slot, bf16[576,768]{1,0:T(8,128)(2,1)} %get-tuple-element.104.o0, bf16[576,768]{1,0:T(8,128)(2,1)} %collective-permute-done.20.o1, bf16[576,768]{1,0:T(8,128)(2,1)} %collective-permute-done.21.o2, ...), custom_call_target="tpu_custom_call" | custom-call | flops 3623878656 | bytes 12582912 | tf_op jit(solution)/shard_map/pallas_call | solution.py:939
  744.5 3.5 convert_add_fusion
  748.9 5.2 add_convert_fusion
  756.7 2.0 collective-permute-start.29
  758.7 23.5 %collective-permute-done.42 = bf16[3,768,256]{2,1,0:T(8,128)(2,1)} collective-permute-done((bf16[3,768,256]{2,1,0:T(8,128)(2,1)S(1)}, bf16[3,768,256]{2,1,0:T(8,128)(2,1)}, u32[]{:S(2)}, u32[]{:S(2)}) %collective-permute-start.42) | collective-permute-done | bytes 1179680 | tf_op jit(solution)/shard_map/ppermute | solution.py:77
  782.2 1.7 collective-permute-start.46
  784.3 1.7 collective-permute-start.48
  786.0 4.0 pad_maximum_fusion
  789.9 5.4 gather_fusion
  799.1 12.4 %collective-permute-done.50 = bf16[3,768,128]{2,1,0:T(8,128)(2,1)} collective-permute-done((bf16[3,768,128]{2,1,0:T(8,128)(2,1)}, bf16[3,768,128]{2,1,0:T(8,128)(2,1)}, u32[]{:S(2)}, u32[]{:S(2)}) %collective-permute-start.50) | collective-permute-done | bytes 589856 | tf_op jit(solution)/shard_map/ppermute | solution.py:77
  811.5 12.6 %collective-permute-done.48 = bf16[3,768,128]{2,1,0:T(8,128)(2,1)} collective-permute-done((bf16[3,768,128]{2,1,0:T(8,128)(2,1)S(1)}, bf16[3,768,128]{2,1,0:T(8,128)(2,1)}, u32[]{:S(2)}, u32[]{:S(2)}) %collective-permute-start.48) | collective-permute-done | bytes 589856 | tf_op jit(solution)/shard_map/ppermute | solution.py:77
  824.1 2.4 fusion.2
  826.7 2.2 collective-permute-start.47
  830.4 4.1 collective-permute-done.45
  834.5 5.9 collective-permute-done.51
  840.4 32.8 %collective-permute-done.49 = bf16[3,768,128]{2,1,0:T(8,128)(2,1)S(1)} collective-permute-done((bf16[3,768,128]{2,1,0:T(8,128)(2,1)S(1)}, bf16[3,768,128]{2,1,0:T(8,128)(2,1)S(1)}, u32[]{:S(2)}, u32[]{:S(2)}) %collective-permute-start.49) | collective-permute-done | bytes 589856 | tf_op jit(solution)/shard_map/ppermute | solution.py:77
  873.2 1.5 fusion.28
  875.2 3.9 slice_bitcast_fusion
  879.2 3.5 copy.35
  (186 shorter events, 48.1 us)
Async XLA Ops:
  0.6 103.7 %copy-start = (bf16[4,256,768]{2,1,0:T(8,128)(2,1)S(1)}, bf16[4,256,768]{2,1,0:T(8,128)(2,1)}, u32[]{:S(2)}) copy-start(bf16[4,256,768]{2,1,0:T(8,128)(2,1)} %param.29) | copy-start | bytes 4718596
  59.6 47.2 %collective-permute-start.2 = (bf16[3,768,128]{2,1,0:T(8,128)(2,1)}, bf16[3,768,128]{2,1,0:T(8,128)(2,1)}, u32[]{:S(2)}, u32[]{:S(2)}) collective-permute-start(bf16[3,768,128]{2,1,0:T(8,128)(2,1)} %fusion.15), channel_id=1, source_target_pairs={{0,6},{1,7},{2,0},{3,1},{4,2},{5,3},{6,4},{7,5},{8,14},{9,15},{10,... | collective-permute-start | bytes 1769480 | tf_op jit(solution)/shard_map/ppermute | solution.py:77
  61.6 51.5 %collective-permute-start.3 = (bf16[3,768,128]{2,1,0:T(8,128)(2,1)}, bf16[3,768,128]{2,1,0:T(8,128)(2,1)}, u32[]{:S(2)}, u32[]{:S(2)}) collective-permute-start(bf16[3,768,128]{2,1,0:T(8,128)(2,1)} %fusion.15), channel_id=1, source_target_pairs={{0,4},{1,5},{2,6},{3,7},{4,0},{5,1},{6,2},{7,3},{8,12},{9,13},{10,... | collective-permute-start | bytes 1769480 | tf_op jit(solution)/shard_map/ppermute | solution.py:77
  61.6 54.1 %collective-permute-start.4 = (bf16[3,768,128]{2,1,0:T(8,128)(2,1)}, bf16[3,768,128]{2,1,0:T(8,128)(2,1)}, u32[]{:S(2)}, u32[]{:S(2)}) collective-permute-start(bf16[3,768,128]{2,1,0:T(8,128)(2,1)} %fusion.15), channel_id=1, source_target_pairs={{0,2},{1,3},{2,4},{3,5},{4,6},{5,7},{6,0},{7,1},{8,10},{9,11},{10,... | collective-permute-start | bytes 1769480 | tf_op jit(solution)/shard_map/ppermute | solution.py:77
  62.7 56.4 %collective-permute-start.5 = (bf16[3,768,128]{2,1,0:T(8,128)(2,1)}, bf16[3,768,128]{2,1,0:T(8,128)(2,1)}, u32[]{:S(2)}, u32[]{:S(2)}) collective-permute-start(bf16[3,768,128]{2,1,0:T(8,128)(2,1)} %fusion.15), channel_id=1, source_target_pairs={{0,1},{1,0},{2,3},{3,2},{4,5},{5,4},{6,7},{7,6},{8,9},{9,8},{10,11... | collective-permute-start | bytes 1769480 | tf_op jit(solution)/shard_map/ppermute | solution.py:77
  102.9 48.6 %collective-permute-start.16 = (bf16[576,768]{1,0:T(8,128)(2,1)}, bf16[576,768]{1,0:T(8,128)(2,1)S(1)}, u32[]{:S(2)}, u32[]{:S(2)}) collective-permute-start(bf16[576,768]{1,0:T(8,128)(2,1)} %get-tuple-element.92), channel_id=1, source_target_pairs={{0,16},{1,17},{2,18},{3,19},{4,20},{5,21},{6,22},{7,23},{8,24},{9,... | collective-permute-start | bytes 2654216 | tf_op jit(solution)/shard_map/ppermute | solution.py:77
  106.7 66.8 %copy-start.12 = (bf16[3,768,256]{2,1,0:T(8,128)(2,1)}, bf16[3,768,256]{2,1,0:T(8,128)(2,1)S(1)}, u32[]{:S(2)}) copy-start(bf16[3,768,256]{2,1,0:T(8,128)(2,1)S(1)} %pad_maximum_fusion.1.refs_6_) | copy-start | bytes 3538948
  106.8 16.5 %collective-permute-start.6 = (bf16[3,768,128]{2,1,0:T(8,128)(2,1)}, bf16[3,768,128]{2,1,0:T(8,128)(2,1)S(1)}, u32[]{:S(2)}, u32[]{:S(2)}) collective-permute-start(bf16[3,768,128]{2,1,0:T(8,128)(2,1)} %collective-permute-done.2), channel_id=1, source_target_pairs={{0,1},{1,0},{2,3},{3,2},{4,5},{5,4},{6,7},{7,6},{8,9},{9,8},{10,11... | collective-permute-start | bytes 1769480 | tf_op jit(solution)/shard_map/ppermute | solution.py:77
  113.1 22.8 %collective-permute-start.7 = (bf16[3,768,128]{2,1,0:T(8,128)(2,1)}, bf16[3,768,128]{2,1,0:T(8,128)(2,1)S(1)}, u32[]{:S(2)}, u32[]{:S(2)}) collective-permute-start(bf16[3,768,128]{2,1,0:T(8,128)(2,1)} %collective-permute-done.3), channel_id=1, source_target_pairs={{0,1},{1,0},{2,3},{3,2},{4,5},{5,4},{6,7},{7,6},{8,9},{9,8},{10,11... | collective-permute-start | bytes 1769480 | tf_op jit(solution)/shard_map/ppermute | solution.py:77
  115.7 30.9 %collective-permute-start.8 = (bf16[3,768,128]{2,1,0:T(8,128)(2,1)}, bf16[3,768,128]{2,1,0:T(8,128)(2,1)S(1)}, u32[]{:S(2)}, u32[]{:S(2)}) collective-permute-start(bf16[3,768,128]{2,1,0:T(8,128)(2,1)} %collective-permute-done.4), channel_id=1, source_target_pairs={{0,1},{1,0},{2,3},{3,2},{4,5},{5,4},{6,7},{7,6},{8,9},{9,8},{10,11... | collective-permute-start | bytes 1769480 | tf_op jit(solution)/shard_map/ppermute | solution.py:77
  121.0 30.4 %copy-start.35 = (bf16[576,768]{1,0:T(8,128)(2,1)S(1)}, bf16[576,768]{1,0:T(8,128)(2,1)}, u32[]{:S(2)}) copy-start(bf16[576,768]{1,0:T(8,128)(2,1)} %get-tuple-element.93) | copy-start | bytes 2654212
  121.0 30.5 %copy-start.33 = (bf16[576,768]{1,0:T(8,128)(2,1)S(1)}, bf16[576,768]{1,0:T(8,128)(2,1)}, u32[]{:S(2)}) copy-start(bf16[576,768]{1,0:T(8,128)(2,1)} %get-tuple-element.94) | copy-start | bytes 2654212
  121.0 131.7 %copy-start.32 = (bf16[576,768]{1,0:T(8,128)(2,1)S(1)}, bf16[576,768]{1,0:T(8,128)(2,1)}, u32[]{:S(2)}) copy-start(bf16[576,768]{1,0:T(8,128)(2,1)} %get-tuple-element.95) | copy-start | bytes 2654212
  147.5 29.1 %collective-permute-start.9 = (bf16[3,768,256]{2,1,0:T(8,128)(2,1)S(1)}, bf16[3,768,256]{2,1,0:T(8,128)(2,1)S(1)}, u32[]{:S(2)}, u32[]{:S(2)}) collective-permute-start(bf16[3,768,256]{2,1,0:T(8,128)(2,1)S(1)} %pad_maximum_fusion.1.refs_6_), channel_id=1, source_target_pairs={{0,6},{1,7},{2,0},{3,1},{4,2},{5,3},{6,4},{7,5},{8,14},{9,15},{10,... | collective-permute-start | bytes 3538952 | tf_op jit(solution)/shard_map/ppermute | solution.py:77
  150.1 100.6 %collective-permute-start.10 = (bf16[3,768,256]{2,1,0:T(8,128)(2,1)S(1)}, bf16[3,768,256]{2,1,0:T(8,128)(2,1)S(1)}, u32[]{:S(2)}, u32[]{:S(2)}) collective-permute-start(bf16[3,768,256]{2,1,0:T(8,128)(2,1)S(1)} %pad_maximum_fusion.1.refs_6_), channel_id=1, source_target_pairs={{0,4},{1,5},{2,6},{3,7},{4,0},{5,1},{6,2},{7,3},{8,12},{9,13},{10,... | collective-permute-start | bytes 3538952 | tf_op jit(solution)/shard_map/ppermute | solution.py:77
  151.0 101.5 %collective-permute-start.11 = (bf16[3,768,256]{2,1,0:T(8,128)(2,1)S(1)}, bf16[3,768,256]{2,1,0:T(8,128)(2,1)S(1)}, u32[]{:S(2)}, u32[]{:S(2)}) collective-permute-start(bf16[3,768,256]{2,1,0:T(8,128)(2,1)S(1)} %pad_maximum_fusion.1.refs_6_), channel_id=1, source_target_pairs={{0,2},{1,3},{2,4},{3,5},{4,6},{5,7},{6,0},{7,1},{8,10},{9,11},{10,... | collective-permute-start | bytes 3538952 | tf_op jit(solution)/shard_map/ppermute | solution.py:77
  151.5 22.0 %collective-permute-start.17 = (bf16[576,768]{1,0:T(8,128)(2,1)S(1)}, bf16[576,768]{1,0:T(8,128)(2,1)}, u32[]{:S(2)}, u32[]{:S(2)}) collective-permute-start(bf16[576,768]{1,0:T(8,128)(2,1)S(1)} %copy-done.35), channel_id=1, source_target_pairs={{0,24},{1,25},{2,26},{3,27},{4,28},{5,29},{6,30},{7,31},{8,16},{9,... | collective-permute-start | bytes 2654216 | tf_op jit(solution)/shard_map/ppermute | solution.py:77
  151.5 128.2 %copy-start.34 = (bf16[576,768]{1,0:T(8,128)(2,1)}, bf16[576,768]{1,0:T(8,128)(2,1)S(1)}, u32[]{:S(2)}) copy-start(bf16[576,768]{1,0:T(8,128)(2,1)S(1)} %collective-permute-done.16.refs_2_) | copy-start | bytes 2654212
  151.5 101.3 %collective-permute-start.18 = (bf16[576,768]{1,0:T(8,128)(2,1)S(1)}, bf16[576,768]{1,0:T(8,128)(2,1)S(1)}, u32[]{:S(2)}, u32[]{:S(2)}) collective-permute-start(bf16[576,768]{1,0:T(8,128)(2,1)S(1)} %copy-done.33), channel_id=1, source_target_pairs={{0,16},{1,17},{2,18},{3,19},{4,20},{5,21},{6,22},{7,23},{8,24},{9,... | collective-permute-start | bytes 2654216 | tf_op jit(solution)/shard_map/ppermute | solution.py:77
  173.5 100.3 %collective-permute-start.12 = (bf16[3,768,256]{2,1,0:T(8,128)(2,1)S(1)}, bf16[3,768,256]{2,1,0:T(8,128)(2,1)S(1)}, u32[]{:S(2)}, u32[]{:S(2)}) collective-permute-start(bf16[3,768,256]{2,1,0:T(8,128)(2,1)S(1)} %pad_maximum_fusion.1.refs_6_), channel_id=1, source_target_pairs={{0,1},{1,0},{2,3},{3,2},{4,5},{5,4},{6,7},{7,6},{8,9},{9,8},{10,11... | collective-permute-start | bytes 3538952 | tf_op jit(solution)/shard_map/ppermute | solution.py:77
  176.6 124.5 %copy-start.25 = (bf16[3,768,256]{2,1,0:T(8,128)(2,1)}, bf16[3,768,256]{2,1,0:T(8,128)(2,1)S(1)}, u32[]{:S(2)}) copy-start(bf16[3,768,256]{2,1,0:T(8,128)(2,1)S(1)} %collective-permute-done.9.refs_7_) | copy-start | bytes 3538948
  176.6 97.7 %collective-permute-start.13 = (bf16[3,768,256]{2,1,0:T(8,128)(2,1)S(1)}, bf16[3,768,256]{2,1,0:T(8,128)(2,1)S(1)}, u32[]{:S(2)}, u32[]{:S(2)}) collective-permute-start(bf16[3,768,256]{2,1,0:T(8,128)(2,1)S(1)} %collective-permute-done.9.refs_7_), channel_id=1, source_target_pairs={{0,1},{1,0},{2,3},{3,2},{4,5},{5,4},{6,7},{7,6},{8,9},{9,8},{10,11... | collective-permute-start | bytes 3538952 | tf_op jit(solution)/shard_map/ppermute | solution.py:77
  250.7 28.9 %collective-permute-start.14 = (bf16[3,768,256]{2,1,0:T(8,128)(2,1)S(1)}, bf16[3,768,256]{2,1,0:T(8,128)(2,1)S(1)}, u32[]{:S(2)}, u32[]{:S(2)}) collective-permute-start(bf16[3,768,256]{2,1,0:T(8,128)(2,1)S(1)} %collective-permute-done.10.refs_8_), channel_id=1, source_target_pairs={{0,1},{1,0},{2,3},{3,2},{4,5},{5,4},{6,7},{7,6},{8,9},{9,8},{10,11... | collective-permute-start | bytes 3538952 | tf_op jit(solution)/shard_map/ppermute | solution.py:77
  252.4 48.7 %collective-permute-start.15 = (bf16[3,768,256]{2,1,0:T(8,128)(2,1)S(1)}, bf16[3,768,256]{2,1,0:T(8,128)(2,1)}, u32[]{:S(2)}, u32[]{:S(2)}) collective-permute-start(bf16[3,768,256]{2,1,0:T(8,128)(2,1)S(1)} %collective-permute-done.11.refs_9_), channel_id=1, source_target_pairs={{0,1},{1,0},{2,3},{3,2},{4,5},{5,4},{6,7},{7,6},{8,9},{9,8},{10,11... | collective-permute-start | bytes 3538952 | tf_op jit(solution)/shard_map/ppermute | solution.py:77
  252.8 21.1 %collective-permute-start.19 = (bf16[576,768]{1,0:T(8,128)(2,1)S(1)}, bf16[576,768]{1,0:T(8,128)(2,1)S(1)}, u32[]{:S(2)}, u32[]{:S(2)}) collective-permute-start(bf16[576,768]{1,0:T(8,128)(2,1)S(1)} %copy-done.32), channel_id=1, source_target_pairs={{0,24},{1,25},{2,26},{3,27},{4,28},{5,29},{6,30},{7,31},{8,16},{9,... | collective-permute-start | bytes 2654216 | tf_op jit(solution)/shard_map/ppermute | solution.py:77
  273.8 81.3 %collective-permute-start = (bf16[576,768]{1,0:T(8,128)(2,1)}, bf16[576,768]{1,0:T(8,128)(2,1)}, u32[]{:S(2)}, u32[]{:S(2)}) collective-permute-start(bf16[576,768]{1,0:T(8,128)(2,1)} %get-tuple-element.87), channel_id=1, source_target_pairs={{0,8},{1,9},{2,10},{3,11},{4,12},{5,13},{6,14},{7,15},{8,0},{9,1},... | collective-permute-start | bytes 2654216 | tf_op jit(solution)/shard_map/ppermute | solution.py:77
  273.9 81.3 %collective-permute-start.1 = (bf16[576,768]{1,0:T(8,128)(2,1)}, bf16[576,768]{1,0:T(8,128)(2,1)}, u32[]{:S(2)}, u32[]{:S(2)}) collective-permute-start(bf16[576,768]{1,0:T(8,128)(2,1)} %get-tuple-element.89), channel_id=1, source_target_pairs={{0,8},{1,9},{2,10},{3,11},{4,12},{5,13},{6,14},{7,15},{8,0},{9,1},... | collective-permute-start | bytes 2654216 | tf_op jit(solution)/shard_map/ppermute | solution.py:77
  274.4 137.9 %collective-permute-start.23 = (bf16[8,3,768,128]{3,2,1,0:T(8,128)(2,1)}, bf16[8,3,768,128]{3,2,1,0:T(8,128)(2,1)}, u32[]{:S(2)}, u32[]{:S(2)}) collective-permute-start(bf16[8,3,768,128]{3,2,1,0:T(8,128)(2,1)} %bitcast_dynamic-update-slice_fusion.refs_4_), channel_id=1, source_target_pairs={{0,8},{1,9},{2,10},{3,11},{4,12},{5,13},{6,14},{7,15},{8,0},{9,1},... | collective-permute-start | bytes 14155784 | tf_op jit(solution)/shard_map/ppermute | solution.py:77
  355.2 55.8 %copy-start.31 = (bf16[592,768]{1,0:T(8,128)(2,1)S(1)}, bf16[592,768]{1,0:T(8,128)(2,1)}, u32[]{:S(2)}) copy-start(bf16[592,768]{1,0:T(8,128)(2,1)} %get-tuple-element.115) | copy-start | bytes 2727940
  410.3 43.2 %collective-permute-start.24 = (bf16[592,768]{1,0:T(8,128)(2,1)}, bf16[592,768]{1,0:T(8,128)(2,1)}, u32[]{:S(2)}, u32[]{:S(2)}) collective-permute-start(bf16[592,768]{1,0:T(8,128)(2,1)} %get-tuple-element.113), channel_id=1, source_target_pairs={{0,8},{1,9},{2,10},{3,11},{4,12},{5,13},{6,14},{7,15},{8,0},{9,1},... | collective-permute-start | bytes 2727944 | tf_op jit(solution)/shard_map/ppermute | solution.py:77
  410.4 43.1 %collective-permute-start.25 = (bf16[592,768]{1,0:T(8,128)(2,1)}, bf16[592,768]{1,0:T(8,128)(2,1)}, u32[]{:S(2)}, u32[]{:S(2)}) collective-permute-start(bf16[592,768]{1,0:T(8,128)(2,1)} %get-tuple-element.114), channel_id=1, source_target_pairs={{0,16},{1,17},{2,18},{3,19},{4,20},{5,21},{6,22},{7,23},{8,24},{9,... | collective-permute-start | bytes 2727944 | tf_op jit(solution)/shard_map/ppermute | solution.py:77
  411.0 42.6 %collective-permute-start.26 = (bf16[592,768]{1,0:T(8,128)(2,1)S(1)}, bf16[592,768]{1,0:T(8,128)(2,1)}, u32[]{:S(2)}, u32[]{:S(2)}) collective-permute-start(bf16[592,768]{1,0:T(8,128)(2,1)S(1)} %copy-done.31), channel_id=1, source_target_pairs={{0,24},{1,25},{2,26},{3,27},{4,28},{5,29},{6,30},{7,31},{8,16},{9,... | collective-permute-start | bytes 2727944 | tf_op jit(solution)/shard_map/ppermute | solution.py:77
  516.7 49.7 %copy-start.10 = (bf16[3,768,256]{2,1,0:T(8,128)(2,1)S(1)}, bf16[3,768,256]{2,1,0:T(8,128)(2,1)}, u32[]{:S(2)}) copy-start(bf16[3,768,256]{2,1,0:T(8,128)(2,1)} %get-tuple-element.137) | copy-start | bytes 3538948
  535.3 80.3 %collective-permute-start.27 = (bf16[8,208,768]{2,1,0:T(8,128)(2,1)}, bf16[8,208,768]{2,1,0:T(8,128)(2,1)S(1)}, u32[]{:S(2)}, u32[]{:S(2)}) collective-permute-start(bf16[8,208,768]{2,1,0:T(8,128)(2,1)} %get-tuple-element.130), channel_id=1, source_target_pairs={{0,8},{1,9},{2,10},{3,11},{4,12},{5,13},{6,14},{7,15},{8,0},{9,1},... | collective-permute-start | bytes 7667720 | tf_op jit(solution)/shard_map/ppermute | solution.py:77
  535.7 29.0 %collective-permute-start.39 = (bf16[3,768,256]{2,1,0:T(8,128)(2,1)}, bf16[3,768,256]{2,1,0:T(8,128)(2,1)S(1)}, u32[]{:S(2)}, u32[]{:S(2)}) collective-permute-start(bf16[3,768,256]{2,1,0:T(8,128)(2,1)} %get-tuple-element.138), channel_id=1, source_target_pairs={{0,1},{1,0},{2,3},{3,2},{4,5},{5,4},{6,7},{7,6},{8,9},{9,8},{10,11... | collective-permute-start | bytes 3538952 | tf_op jit(solution)/shard_map/ppermute | solution.py:77
  537.4 52.6 %collective-permute-start.37 = (bf16[3,768,256]{2,1,0:T(8,128)(2,1)}, bf16[3,768,256]{2,1,0:T(8,128)(2,1)S(1)}, u32[]{:S(2)}, u32[]{:S(2)}) collective-permute-start(bf16[3,768,256]{2,1,0:T(8,128)(2,1)} %get-tuple-element.136), channel_id=1, source_target_pairs={{0,1},{1,0},{2,3},{3,2},{4,5},{5,4},{6,7},{7,6},{8,9},{9,8},{10,11... | collective-permute-start | bytes 3538952 | tf_op jit(solution)/shard_map/ppermute | solution.py:77
  537.7 211.2 %collective-permute-start.44 = (bf16[8,3,768,128]{3,2,1,0:T(8,128)(2,1)}, bf16[8,3,768,128]{3,2,1,0:T(8,128)(2,1)}, u32[]{:S(2)}, u32[]{:S(2)}) collective-permute-start(bf16[8,3,768,128]{3,2,1,0:T(8,128)(2,1)} %get-tuple-element.140), channel_id=1, source_target_pairs={{0,8},{1,9},{2,10},{3,11},{4,12},{5,13},{6,14},{7,15},{8,0},{9,1},... | collective-permute-start | bytes 14155784 | tf_op jit(solution)/shard_map/ppermute | solution.py:77
  537.7 77.6 %collective-permute-start.35 = (bf16[3,768,256]{2,1,0:T(8,128)(2,1)}, bf16[3,768,256]{2,1,0:T(8,128)(2,1)S(1)}, u32[]{:S(2)}, u32[]{:S(2)}) collective-permute-start(bf16[3,768,256]{2,1,0:T(8,128)(2,1)} %get-tuple-element.134), channel_id=1, source_target_pairs={{0,1},{1,0},{2,3},{3,2},{4,5},{5,4},{6,7},{7,6},{8,9},{9,8},{10,11... | collective-permute-start | bytes 3538952 | tf_op jit(solution)/shard_map/ppermute | solution.py:77
  564.7 75.2 %collective-permute-start.34 = (bf16[3,768,256]{2,1,0:T(8,128)(2,1)}, bf16[3,768,256]{2,1,0:T(8,128)(2,1)}, u32[]{:S(2)}, u32[]{:S(2)}) collective-permute-start(bf16[3,768,256]{2,1,0:T(8,128)(2,1)} %get-tuple-element.132), channel_id=1, source_target_pairs={{0,1},{1,0},{2,3},{3,2},{4,5},{5,4},{6,7},{7,6},{8,9},{9,8},{10,11... | collective-permute-start | bytes 3538952 | tf_op jit(solution)/shard_map/ppermute | solution.py:77
  590.0 51.6 %collective-permute-start.40 = (bf16[3,768,256]{2,1,0:T(8,128)(2,1)S(1)}, bf16[3,768,256]{2,1,0:T(8,128)(2,1)}, u32[]{:S(2)}, u32[]{:S(2)}) collective-permute-start(bf16[3,768,256]{2,1,0:T(8,128)(2,1)S(1)} %add_convert_fusion.3), channel_id=1, source_target_pairs={{0,6},{1,7},{2,0},{3,1},{4,2},{5,3},{6,4},{7,5},{8,14},{9,15},{10,... | collective-permute-start | bytes 3538952 | tf_op jit(solution)/shard_map/ppermute | solution.py:77
  615.2 75.8 %collective-permute-start.38 = (bf16[3,768,256]{2,1,0:T(8,128)(2,1)S(1)}, bf16[3,768,256]{2,1,0:T(8,128)(2,1)}, u32[]{:S(2)}, u32[]{:S(2)}) collective-permute-start(bf16[3,768,256]{2,1,0:T(8,128)(2,1)S(1)} %add_convert_fusion.4), channel_id=1, source_target_pairs={{0,4},{1,5},{2,6},{3,7},{4,0},{5,1},{6,2},{7,3},{8,12},{9,13},{10,... | collective-permute-start | bytes 3538952 | tf_op jit(solution)/shard_map/ppermute | solution.py:77
  615.6 76.0 %collective-permute-start.36 = (bf16[3,768,256]{2,1,0:T(8,128)(2,1)S(1)}, bf16[3,768,256]{2,1,0:T(8,128)(2,1)S(1)}, u32[]{:S(2)}, u32[]{:S(2)}) collective-permute-start(bf16[3,768,256]{2,1,0:T(8,128)(2,1)S(1)} %add_convert_fusion.5), channel_id=1, source_target_pairs={{0,2},{1,3},{2,4},{3,5},{4,6},{5,7},{6,0},{7,1},{8,10},{9,11},{10,... | collective-permute-start | bytes 3538952 | tf_op jit(solution)/shard_map/ppermute | solution.py:77
  619.2 73.4 %copy-start.7 = (bf16[3,768,256]{2,1,0:T(8,128)(2,1)S(1)}, bf16[3,768,256]{2,1,0:T(8,128)(2,1)}, u32[]{:S(2)}) copy-start(bf16[3,768,256]{2,1,0:T(8,128)(2,1)} %get-tuple-element.131) | copy-start | bytes 3538948
  639.8 104.7 %collective-permute-start.28 = (bf16[4,208,768]{2,1,0:T(8,128)(2,1)}, bf16[4,208,768]{2,1,0:T(8,128)(2,1)}, u32[]{:S(2)}, u32[]{:S(2)}) collective-permute-start(bf16[4,208,768]{2,1,0:T(8,128)(2,1)} %slice.115), channel_id=1, source_target_pairs={{0,1},{1,0},{2,3},{3,2},{4,5},{5,4},{6,7},{7,6},{8,9},{9,8},{10,11... | collective-permute-start | bytes 3833864 | tf_op jit(solution)/shard_map/ppermute | solution.py:77
  641.6 54.1 %collective-permute-start.20 = (bf16[576,768]{1,0:T(8,128)(2,1)}, bf16[576,768]{1,0:T(8,128)(2,1)}, u32[]{:S(2)}, u32[]{:S(2)}) collective-permute-start(bf16[576,768]{1,0:T(8,128)(2,1)} %get-tuple-element.105), channel_id=1, source_target_pairs={{0,8},{1,9},{2,10},{3,11},{4,12},{5,13},{6,14},{7,15},{8,0},{9,1},... | collective-permute-start | bytes 2654216 | tf_op jit(solution)/shard_map/ppermute | solution.py:77
  691.1 22.9 %collective-permute-start.21 = (bf16[576,768]{1,0:T(8,128)(2,1)}, bf16[576,768]{1,0:T(8,128)(2,1)}, u32[]{:S(2)}, u32[]{:S(2)}) collective-permute-start(bf16[576,768]{1,0:T(8,128)(2,1)} %get-tuple-element.106), channel_id=1, source_target_pairs={{0,16},{1,17},{2,18},{3,19},{4,20},{5,21},{6,22},{7,23},{8,24},{9,... | collective-permute-start | bytes 2654216 | tf_op jit(solution)/shard_map/ppermute | solution.py:77
  691.6 39.3 %collective-permute-start.22 = (bf16[576,768]{1,0:T(8,128)(2,1)}, bf16[576,768]{1,0:T(8,128)(2,1)}, u32[]{:S(2)}, u32[]{:S(2)}) collective-permute-start(bf16[576,768]{1,0:T(8,128)(2,1)} %get-tuple-element.107), channel_id=1, source_target_pairs={{0,24},{1,25},{2,26},{3,27},{4,28},{5,29},{6,30},{7,31},{8,16},{9,... | collective-permute-start | bytes 2654216 | tf_op jit(solution)/shard_map/ppermute | solution.py:77
  695.7 61.0 %collective-permute-start.43 = (bf16[3,768,256]{2,1,0:T(8,128)(2,1)S(1)}, bf16[3,768,256]{2,1,0:T(8,128)(2,1)}, u32[]{:S(2)}, u32[]{:S(2)}) collective-permute-start(bf16[3,768,256]{2,1,0:T(8,128)(2,1)S(1)} %add_convert_fusion.2), channel_id=1, source_target_pairs={{0,24},{1,25},{2,26},{3,27},{4,28},{5,29},{6,30},{7,31},{8,16},{9,... | collective-permute-start | bytes 3538952 | tf_op jit(solution)/shard_map/ppermute | solution.py:77
  713.9 68.3 %collective-permute-start.42 = (bf16[3,768,256]{2,1,0:T(8,128)(2,1)S(1)}, bf16[3,768,256]{2,1,0:T(8,128)(2,1)}, u32[]{:S(2)}, u32[]{:S(2)}) collective-permute-start(bf16[3,768,256]{2,1,0:T(8,128)(2,1)S(1)} %add_convert_fusion.2), channel_id=1, source_target_pairs={{0,16},{1,17},{2,18},{3,19},{4,20},{5,21},{6,22},{7,23},{8,24},{9,... | collective-permute-start | bytes 3538952 | tf_op jit(solution)/shard_map/ppermute | solution.py:77
  730.9 53.0 %collective-permute-start.41 = (bf16[3,768,256]{2,1,0:T(8,128)(2,1)S(1)}, bf16[3,768,256]{2,1,0:T(8,128)(2,1)}, u32[]{:S(2)}, u32[]{:S(2)}) collective-permute-start(bf16[3,768,256]{2,1,0:T(8,128)(2,1)S(1)} %add_convert_fusion.2), channel_id=1, source_target_pairs={{0,8},{1,9},{2,10},{3,11},{4,12},{5,13},{6,14},{7,15},{8,0},{9,1},... | collective-permute-start | bytes 3538952 | tf_op jit(solution)/shard_map/ppermute | solution.py:77
  748.9 35.4 %collective-permute-start.31 = (bf16[208,768]{1,0:T(8,128)(2,1)S(1)}, bf16[208,768]{1,0:T(8,128)(2,1)S(1)}, u32[]{:S(2)}, u32[]{:S(2)}) collective-permute-start(bf16[208,768]{1,0:T(8,128)(2,1)S(1)} %get-tuple-element.180), channel_id=1, source_target_pairs={{0,6},{1,7},{2,0},{3,1},{4,2},{5,3},{6,4},{7,5},{8,14},{9,15},{10,... | collective-permute-start | bytes 958472 | tf_op jit(solution)/shard_map/ppermute | solution.py:77
  748.9 46.4 %collective-permute-start.30 = (bf16[208,768]{1,0:T(8,128)(2,1)}, bf16[208,768]{1,0:T(8,128)(2,1)S(1)}, u32[]{:S(2)}, u32[]{:S(2)}) collective-permute-start(bf16[208,768]{1,0:T(8,128)(2,1)} %get-tuple-element.181), channel_id=1, source_target_pairs={{0,4},{1,5},{2,6},{3,7},{4,0},{5,1},{6,2},{7,3},{8,12},{9,13},{10,... | collective-permute-start | bytes 958472 | tf_op jit(solution)/shard_map/ppermute | solution.py:77
  756.7 38.6 %collective-permute-start.29 = (bf16[208,768]{1,0:T(8,128)(2,1)}, bf16[208,768]{1,0:T(8,128)(2,1)S(1)}, u32[]{:S(2)}, u32[]{:S(2)}) collective-permute-start(bf16[208,768]{1,0:T(8,128)(2,1)} %get-tuple-element.179), channel_id=1, source_target_pairs={{0,2},{1,3},{2,4},{3,5},{4,6},{5,7},{6,0},{7,1},{8,10},{9,11},{10,... | collective-permute-start | bytes 958472 | tf_op jit(solution)/shard_map/ppermute | solution.py:77
  782.2 16.9 %collective-permute-start.46 = (bf16[3,768,128]{2,1,0:T(8,128)(2,1)}, bf16[3,768,128]{2,1,0:T(8,128)(2,1)}, u32[]{:S(2)}, u32[]{:S(2)}) collective-permute-start(bf16[3,768,128]{2,1,0:T(8,128)(2,1)} %get-tuple-element.166), channel_id=1, source_target_pairs={{0,1},{1,0},{2,3},{3,2},{4,5},{5,4},{6,7},{7,6},{8,9},{9,8},{10,11... | collective-permute-start | bytes 1769480 | tf_op jit(solution)/shard_map/ppermute | solution.py:77
  783.9 27.5 %collective-permute-start.50 = (bf16[3,768,128]{2,1,0:T(8,128)(2,1)}, bf16[3,768,128]{2,1,0:T(8,128)(2,1)}, u32[]{:S(2)}, u32[]{:S(2)}) collective-permute-start(bf16[3,768,128]{2,1,0:T(8,128)(2,1)} %get-tuple-element.164), channel_id=1, source_target_pairs={{0,1},{1,0},{2,3},{3,2},{4,5},{5,4},{6,7},{7,6},{8,9},{9,8},{10,11... | collective-permute-start | bytes 1769480 | tf_op jit(solution)/shard_map/ppermute | solution.py:77
  784.3 39.8 %collective-permute-start.48 = (bf16[3,768,128]{2,1,0:T(8,128)(2,1)S(1)}, bf16[3,768,128]{2,1,0:T(8,128)(2,1)}, u32[]{:S(2)}, u32[]{:S(2)}) collective-permute-start(bf16[3,768,128]{2,1,0:T(8,128)(2,1)S(1)} %get-tuple-element.165), channel_id=1, source_target_pairs={{0,1},{1,0},{2,3},{3,2},{4,5},{5,4},{6,7},{7,6},{8,9},{9,8},{10,11... | collective-permute-start | bytes 1769480 | tf_op jit(solution)/shard_map/ppermute | solution.py:77
  798.2 31.4 %collective-permute-start.32 = (bf16[208,768]{1,0:T(8,128)(2,1)S(1)}, bf16[208,768]{1,0:T(8,128)(2,1)S(1)}, u32[]{:S(2)}, u32[]{:S(2)}) collective-permute-start(bf16[208,768]{1,0:T(8,128)(2,1)S(1)} %get-tuple-element.158), channel_id=1, source_target_pairs={{0,16},{1,17},{2,18},{3,19},{4,20},{5,21},{6,22},{7,23},{8,24},{9,... | collective-permute-start | bytes 958472 | tf_op jit(solution)/shard_map/ppermute | solution.py:77
  798.7 35.7 %collective-permute-start.45 = (bf16[3,768,128]{2,1,0:T(8,128)(2,1)S(1)}, bf16[3,768,128]{2,1,0:T(8,128)(2,1)S(1)}, u32[]{:S(2)}, u32[]{:S(2)}) collective-permute-start(bf16[3,768,128]{2,1,0:T(8,128)(2,1)S(1)} %get-tuple-element.163), channel_id=1, source_target_pairs={{0,1},{1,0},{2,3},{3,2},{4,5},{5,4},{6,7},{7,6},{8,9},{9,8},{10,11... | collective-permute-start | bytes 1769480 | tf_op jit(solution)/shard_map/ppermute | solution.py:77
  826.5 13.8 %collective-permute-start.51 = (bf16[3,768,128]{2,1,0:T(8,128)(2,1)S(1)}, bf16[3,768,128]{2,1,0:T(8,128)(2,1)S(1)}, u32[]{:S(2)}, u32[]{:S(2)}) collective-permute-start(bf16[3,768,128]{2,1,0:T(8,128)(2,1)S(1)} %get-tuple-element.168), channel_id=1, source_target_pairs={{0,6},{1,7},{2,0},{3,1},{4,2},{5,3},{6,4},{7,5},{8,14},{9,15},{10,... | collective-permute-start | bytes 1769480 | tf_op jit(solution)/shard_map/ppermute | solution.py:77
  826.6 46.6 %collective-permute-start.49 = (bf16[3,768,128]{2,1,0:T(8,128)(2,1)S(1)}, bf16[3,768,128]{2,1,0:T(8,128)(2,1)S(1)}, u32[]{:S(2)}, u32[]{:S(2)}) collective-permute-start(bf16[3,768,128]{2,1,0:T(8,128)(2,1)S(1)} %get-tuple-element.169), channel_id=1, source_target_pairs={{0,4},{1,5},{2,6},{3,7},{4,0},{5,1},{6,2},{7,3},{8,12},{9,13},{10,... | collective-permute-start | bytes 1769480 | tf_op jit(solution)/shard_map/ppermute | solution.py:77
  826.7 46.5 %collective-permute-start.47 = (bf16[3,768,128]{2,1,0:T(8,128)(2,1)S(1)}, bf16[3,768,128]{2,1,0:T(8,128)(2,1)S(1)}, u32[]{:S(2)}, u32[]{:S(2)}) collective-permute-start(bf16[3,768,128]{2,1,0:T(8,128)(2,1)S(1)} %get-tuple-element.167), channel_id=1, source_target_pairs={{0,2},{1,3},{2,4},{3,5},{4,6},{5,7},{6,0},{7,1},{8,10},{9,11},{10,... | collective-permute-start | bytes 1769480 | tf_op jit(solution)/shard_map/ppermute | solution.py:77
  830.4 52.4 %collective-permute-start.33 = (bf16[208,768]{1,0:T(8,128)(2,1)}, bf16[208,768]{1,0:T(8,128)(2,1)}, u32[]{:S(2)}, u32[]{:S(2)}) collective-permute-start(bf16[208,768]{1,0:T(8,128)(2,1)} %fusion.19), channel_id=1, source_target_pairs={{0,8},{1,9},{2,10},{3,11},{4,12},{5,13},{6,14},{7,15},{8,0},{9,1},... | collective-permute-start | bytes 958472 | tf_op jit(solution)/shard_map/ppermute | solution.py:77
  874.7 10.4 %collective-permute-start.52 = (bf16[3,768,128]{2,1,0:T(8,128)(2,1)S(1)}, bf16[3,768,128]{2,1,0:T(8,128)(2,1)S(1)}, u32[]{:S(2)}, u32[]{:S(2)}) collective-permute-start(bf16[3,768,128]{2,1,0:T(8,128)(2,1)S(1)} %get-tuple-element.156), channel_id=1, source_target_pairs={{0,16},{1,17},{2,18},{3,19},{4,20},{5,21},{6,22},{7,23},{8,24},{9,... | collective-permute-start | bytes 1769480 | tf_op jit(solution)/shard_map/ppermute | solution.py:77
  885.2 2.4 collective-permute-start.53
  (28 other events, 219.6 us)

commit v3 on v2

v3 whole, which is shorter than its diff:
```python
import functools

import jax
import jax.numpy as jnp
from jax import lax
from jax.experimental import pallas as pl
from jax.experimental.pallas import tpu as pltpu
from jax.sharding import PartitionSpec as P

HEADS = 12
PIECE = 256
CAP = 576
EPSILON = 1e-06
MASKED = -1e30
F32, BF = jnp.float32, jnp.bfloat16
AXES = ("rep", "shard")
TILE = 256
SLOTS = 8
VMEM_LIMIT = 62 * 2**20
ANY = pl.BlockSpec(memory_space=pl.ANY)
SMEM = pl.BlockSpec(memory_space=pltpu.SMEM)
VMEM = pl.BlockSpec(memory_space=pltpu.VMEM)


def dot(a, b, i, j):
    return lax.dot_general(a, b, (((i,), (j,)), ((), ())), preferred_element_type=F32)


def nn(a, b):
    return dot(a, b, 1, 0)


def nt(a, b):
    return dot(a, b, 1, 1)


def tn(a, b):
    return dot(a, b, 0, 0)


def iota(shape, dim):
    return lax.broadcasted_iota(jnp.int32, shape, dim)


def ones_where(cond):
    return jnp.where(cond, 1.0, 0.0).astype(BF)


def call(
    kernel, out_shape, in_specs, out_specs, scratch=(), flops=0, moved=0, grid=None, group=None,
    alias=None,
):
    extra = {} if grid is None else {"grid": grid}
    params = {} if group is None else {"collective_id": group, "has_side_effects": True}
    return pl.pallas_call(
        kernel,
        out_shape=out_shape,
        in_specs=in_specs,
        out_specs=out_specs,
        scratch_shapes=list(scratch),
        input_output_aliases=alias or {},
        compiler_params=pltpu.CompilerParams(vmem_limit_bytes=VMEM_LIMIT, **params),
        cost_estimate=pl.CostEstimate(flops=flops, bytes_accessed=moved, transcendentals=0),
        **extra,
    )


def shape(dims, dtype=BF):
    return jax.ShapeDtypeStruct(dims, dtype)


def permute(x, move):
    reps, shards = lax.axis_size("rep"), lax.axis_size("shard")
    pairs = []
    for r in range(reps):
        for s in range(shards):
            to_r, to_s = move(r, s)
            pairs.append((r * shards + s, to_r * shards + to_s))
    return lax.ppermute(x, AXES, pairs)


def to_rep(x, offset):
    return permute(x, lambda r, s: (r ^ offset, s))


def spin(block, cosine, sine):
    lane = iota(block.shape, 1)
    partner = jnp.where(lane % 64 < 32, pltpu.roll(block, 96, 1), pltpu.roll(block, 32, 1))
    return block * cosine + partner * sine


def sibling(rep, o):
    return 2 * lax.rem(lax.div(rep, 2) + o // 2, 2) + lax.rem(lax.rem(rep, 2) + o % 2, 2)


def route_slots(rep, routes, routes_t, rank_out, slot_out):
    tokens = routes.shape[0]
    first, second = routes_t[0:1, :], routes_t[1:2, :]
    expert = iota((8, tokens), 0)
    chosen = (expert == first) | (expert == second)
    upper = ones_where(iota((tokens, tokens), 0) <= iota((tokens, tokens), 1))
    rank = nn(ones_where(chosen), upper) - 1.0
    rank_out[...] = jnp.where(chosen, rank, -1.0)
    lane = iota((tokens, 128), 1)
    one, two = routes[:, 0:1], routes[:, 1:2]
    lower = ones_where(iota((tokens, tokens), 0) >= iota((tokens, tokens), 1))
    place = nn(lower, ones_where((lane == one) | (lane == two))) - 1.0
    for o in range(1, 4):
        place = place + jnp.where(lane == sibling(rep, o), float(o * CAP), 0.0)
    slot_one = jnp.sum(jnp.where(lane == one, place, 0.0), axis=1, keepdims=True)
    slot_two = jnp.sum(jnp.where(lane == two, place, 0.0), axis=1, keepdims=True)
    slot_out[...] = jnp.where(lane < 64, slot_one, slot_two)


def pack_rows(rep, rank, source, packed):
    tokens = source.shape[0]
    for o, out in enumerate(packed):
        row = rank[pl.ds(sibling(rep, o), 1), :]
        pick = ones_where(iota((CAP, tokens), 0).astype(F32) == row)
        out[...] = nn(pick, source[...]).astype(BF)


def qkv_rows(x, ext, cosine, sine, wq, wk, wv, q, k, v):
    tokens, width = x.shape
    gain = ext[4:5, :]

    def tile(t, carry):
        at = pl.ds(pl.multiple_of(t * TILE, TILE), TILE)
        rows_in = x[at, :].astype(F32)
        scale = lax.rsqrt(jnp.mean(rows_in * rows_in, axis=1, keepdims=True) + EPSILON)
        normed = (rows_in * scale * gain).astype(BF)
        cos_t, sin_t = cosine[at, :], sine[at, :]
        for weight, out, factor in ((wq, q, 0.125), (wk, k, 1.0)):
            full = nn(normed, weight[...])
            for b in range(width // 128):
                turned = spin(full[:, b * 128 : (b + 1) * 128], cos_t, sin_t)
                out[at, b * 128 : (b + 1) * 128] = turned.astype(BF) * jnp.asarray(factor, BF)
        v[at, :] = nn(normed, wv[...]).astype(BF)
        return carry

    lax.fori_loop(0, tokens // TILE, tile, 0)


def when(cond, body):
    if cond is True:
        body()
    elif cond is not False:
        pl.when(cond)(body)


def both(one, two):
    if one is True or two is False:
        return two
    if two is True or one is False:
        return one
    return one & two


class Net:
    def __init__(self, send, recv):
        self.rep, self.shard = lax.axis_index("rep"), lax.axis_index("shard")
        self.core, self.z = lax.rem(self.rep, 2), lax.div(self.shard, 2)
        self.x = lax.rem(self.shard, 2)
        self.mate = self.rep + 1 - 2 * self.core
        self.across = self.shard + 1 - 2 * self.x
        first = lax.max(self.z - 1, 1 - self.z)
        third = 3 * (1 - lax.div(self.z, 2))
        self.levels = [self.z, first, 6 - self.z - first - third, third]
        self.up = lax.min(self.shard + 2, 6 + self.x)
        self.down = lax.max(self.shard - 2, self.x)
        self.cousins = [self.rep] + [sibling(self.rep, o) for o in (1, 2, 3)]
        self.send, self.recv = send, recv
        self.count, self.open = 0, {}

    def event(self):
        self.count += 1
        return self.count - 1

    def place(self, n, side):
        return self.levels[n] * 2 + (self.x if side == 0 else 1 - self.x)

    def cycle(self, d):
        return lax.rem(self.z + d, 4) * 2 + self.x

    def copy(self, event, source, target, rep, shard):
        return pltpu.make_async_remote_copy(
            src_ref=source,
            dst_ref=target,
            send_sem=self.send.at[event],
            recv_sem=self.recv.at[event],
            device_id=(rep, shard),
            device_id_type=pl.DeviceIdType.MESH,
        )

    def put(self, event, source, target, rep, shard, cond=True):
        when(cond, self.copy(event, source, target, rep, shard).start)
        self.open[event] = (cond, source)

    def got(self, event, like, cond=True):
        when(cond, self.copy(event, like, like, self.mate, self.shard).wait_recv)

    def close(self):
        for event, (cond, source) in self.open.items():
            when(cond, self.copy(event, source, source, self.mate, self.shard).wait_send)

    def meet(self, z_ways, others):
        barrier = pltpu.get_barrier_semaphore()

        def greet(rep, shard):
            pl.semaphore_signal(
                barrier, inc=1, device_id=(rep, shard), device_id_type=pl.DeviceIdType.MESH
            )

        count = len(others)
        for rep, shard in others:
            greet(rep, shard)
        if z_ways == "line":
            when(self.z < 3, lambda: greet(self.rep, self.up))
            when(self.z > 0, lambda: greet(self.rep, self.down))
            count = count + lax.min(self.z, 1) + lax.min(3 - self.z, 1)
        if z_ways == "all":
            for d in (1, 2, 3):
                greet(self.rep, self.cycle(d))
            count = count + 3
        pl.semaphore_wait(barrier, count)


class Line:
    def __init__(self, net, bank):
        self.net, self.bank = net, bank
        self.events = {(way, k): net.event() for way in range(4) for k in range(-3, 4)}
        self.spots = {0: (net.shard, True)}
        for k in (1, 2, 3):
            self.spots[k] = (lax.min(net.shard + 2 * k, 6 + net.x), net.z < 4 - k)
            self.spots[-k] = (lax.max(net.shard - 2 * k, net.x), net.z >= k)
        self.flips = {k: spot + 1 - 2 * net.x for k, (spot, _) in self.spots.items()}
        self.onward = {k: both(self.spots[k][1], net.z < 3) for k in self.spots}
        self.back = {k: both(self.spots[k][1], net.z > 0) for k in self.spots}

    def spread(self, k, source):
        net, (spot, here) = self.net, self.spots[k]
        target = self.bank.at[net.core, spot]
        if -3 < k <= 0:
            event = self.events[0, k - 1]
            net.put(event, source, target, net.rep, net.up, self.onward[k])
        if 0 <= k < 3:
            event = self.events[0, k + 1]
            net.put(event, source, target, net.rep, net.down, self.back[k])
        net.put(self.events[1, k], source, target, net.rep, net.across, here)
        net.put(self.events[2, k], source, target, net.mate, net.shard, here)

    def along(self, k):
        spot, here = self.spots[k]
        piece = self.bank.at[self.net.core, spot]
        self.net.got(self.events[0, k], piece, here)
        self.spread(k, piece)

    def over(self, k):
        net, here = self.net, self.spots[k][1]
        piece = self.bank.at[net.core, self.flips[k]]
        net.got(self.events[1, k], piece, here)
        net.put(self.events[3, k], piece, piece, net.mate, net.shard, here)

    def finish(self):
        other = 1 - self.net.core
        for k in (0, 1, -1, 2, -2, 3, -3):
            spot, here = self.spots[k]
            self.net.got(self.events[2, k], self.bank.at[other, spot], here)
            self.net.got(self.events[3, k], self.bank.at[other, self.flips[k]], here)


def exchange(net, sources, targets):
    events = [net.event() for _ in range(3)]
    for o in (2, 3, 1):
        net.put(events[o - 1], sources[o - 1], targets[o - 1], net.cousins[o], net.shard)
    return [(events[o], targets[o]) for o in range(3)]


def head_kernel(
    routes, routes_t, cot, x, piece, cosine, sine,
    rank, slot, q, k, v, wq, wk, wv, wo, ext, c0, c1, c2, c3,
    bank, packed, send, recv, own_sem,
):
    width = x.shape[1]
    half = width // SLOTS
    net = Net(send, recv)
    line = Line(net, bank)
    peers = [(net.cousins[o], net.shard) for o in (1, 2, 3)]
    net.meet("line", peers + [(net.rep, net.across)])
    line.spread(0, piece)
    own = pltpu.make_async_copy(piece, bank.at[net.core, net.shard], own_sem)
    own.start()
    route_slots(net.rep, routes, routes_t, rank, slot)
    pack_rows(net.rep, rank, cot, [c0] + [packed.at[o] for o in range(3)])
    arrivals = exchange(net, [packed.at[o] for o in range(3)], (c1, c2, c3))
    line.along(1)
    line.along(-1)
    line.over(0)
    line.along(2)
    line.along(-2)
    line.over(1)
    line.over(-1)
    line.along(3)
    line.along(-3)
    for step in (2, -2, 3, -3):
        line.over(step)
    own.wait()
    line.finish()
    gathered = bank[0, 0, 2 * half : 2 * half + 16, :].astype(F32)
    for j in range(1, SLOTS):
        gathered = gathered + bank[0, j, 2 * half : 2 * half + 16, :].astype(F32)
    ext[...] = gathered
    for j in range(SLOTS):
        at = slice(j * half, (j + 1) * half)
        wq[at, :] = bank[0, j, 0:half, :]
        wk[at, :] = bank[0, j, half : 2 * half, :]
        wv[at, :] = bank[1, j, 0:half, :]
        wo[at, :] = bank[1, j, half : 2 * half, :]
    qkv_rows(x, ext, cosine, sine, wq, wk, wv, q, k, v)
    for event, like in arrivals:
        net.got(event, like)
    net.close()


def plain_head_kernel(
    routes, routes_t, cot, x, cosine, sine, wq, wk, wv, ext,
    rank, slot, q, k, v, c0, c1, c2, c3,
):
    rep = lax.axis_index("rep")
    route_slots(rep, routes, routes_t, rank, slot)
    pack_rows(rep, rank, cot, (c0, c1, c2, c3))
    qkv_rows(x, ext, cosine, sine, wq, wk, wv, q, k, v)


def fill_bias(starts, bias):
    tokens = bias.shape[0]

    def tile(t, carry):
        at = pl.ds(pl.multiple_of(t * TILE, TILE), TILE)
        query = iota((TILE, tokens), 0) + t * TILE
        key = iota((TILE, tokens), 1)
        allowed = key <= query
        for n in range(2):
            begin = starts[0, n]
            inside = (query >= begin) & (query < begin + PIECE)
            allowed = allowed | (inside & (key >= begin) & (key < begin + PIECE))
        bias[at, :] = jnp.where(allowed, 0.0, MASKED)
        return carry

    lax.fori_loop(0, tokens // TILE, tile, 0)


def keep_half(block, h):
    low = iota(block.shape, 1) < 64
    return jnp.where(low if h == 0 else ~low, block.astype(F32), 0.0).astype(BF)


def biased(scores, bias, begin, free, end):
    tail = scores[:, free:] + bias[begin : begin + TILE, free:end]
    return tail if free == 0 else jnp.concatenate([scores[:, :free], tail], axis=1)


def attend_pairs(q, k, v, out, lse, bias, step):
    tokens, width = q.shape

    def pair(i, carry):
        step(i)
        cols = pl.ds(pl.multiple_of(i * 128, 128), 128)
        keys = k[:, cols]
        low = iota((tokens, 128), 1) < 64
        values = v[:, cols].astype(F32)
        value_one = [
            jnp.where(low, values, 1.0).astype(BF),
            jnp.where(low, 1.0, values).astype(BF),
        ]
        low = iota((TILE, 128), 1) < 64
        for t in range(tokens // TILE):
            begin = t * TILE
            end = min(tokens, begin + TILE + PIECE)
            block = q[begin : begin + TILE, cols]
            results, totals = [], []
            for h in range(2):
                scores = nt(keep_half(block, h), keys[:end])
                scores = biased(scores, bias, begin, begin, end)
                row_max = jnp.max(scores, axis=1, keepdims=True)
                probs = jnp.exp(scores - row_max).astype(BF)
                mixed = nn(probs, value_one[h][:end])
                total = pltpu.roll(mixed, 64, 1)
                results.append(mixed / total)
                totals.append(row_max + jnp.log(total))
            out[begin : begin + TILE, cols] = jnp.where(low, results[0], results[1]).astype(BF)
            lse[begin : begin + TILE, cols] = jnp.where(low, totals[0], totals[1])
        return carry

    lax.fori_loop(0, width // 128, pair, 0)


def router_rows(ext):
    rows = jnp.where(iota(ext.shape, 0) < 4, ext[...], 0.0)
    return jnp.concatenate([rows, jnp.zeros((112, ext.shape[1]), F32)], axis=0).astype(BF)


def route_probs(normed, router):
    logits = nt(normed, router)
    logits = jnp.where(iota(logits.shape, 1) < 4, logits, MASKED)
    raised = jnp.exp(logits - jnp.max(logits, axis=1, keepdims=True))
    return raised / jnp.sum(raised, axis=1, keepdims=True)


def middle_rows(rep, x, attended, wo, ext, rank, middle, normed, probs, packed):
    tokens = x.shape[0]
    gain = ext[5:6, :]
    router = router_rows(ext)

    def tile(t, carry):
        at = pl.ds(pl.multiple_of(t * TILE, TILE), TILE)
        rows = x[at, :].astype(F32) + nn(attended[at, :], wo[...])
        scale = lax.rsqrt(jnp.mean(rows * rows, axis=1, keepdims=True) + EPSILON)
        middle[at, :] = rows
        unit = (rows * scale * gain).astype(BF)
        normed[at, :] = unit
        probs[at, :] = route_probs(unit, router)
        return carry

    lax.fori_loop(0, tokens // TILE, tile, 0)
    pack_rows(rep, rank, normed, packed)


def forward_kernel(
    starts, q, k, v, x, wo, ext, rank, shared_piece, expert_piece,
    attended, lse, middle, normed, probs, x0, x1, x2, x3, shared_bank, expert_bank,
    bias, send, recv,
):
    net = Net(send, recv)
    line = Line(net, shared_bank)
    z_events = [net.event(), net.event()]
    net.meet("line", [(net.mate, net.shard), (net.rep, net.across)])
    line.spread(0, shared_piece)
    fill_bias(starts, bias)

    def step(i):
        @pl.when(i == 3)
        def _():
            line.along(1)
            line.along(-1)
            line.over(0)

    attend_pairs(q, k, v, attended, lse, bias, step)
    line.along(2)
    line.along(-2)
    line.over(1)
    line.over(-1)
    mine = expert_bank.at[net.shard]
    net.put(z_events[0], expert_piece, mine, net.rep, net.up, net.z < 3)
    net.put(z_events[1], expert_piece, mine, net.rep, net.down, net.z > 0)
    middle_rows(net.rep, x, attended, wo, ext, rank, middle, normed, probs, (x0, x1, x2, x3))
    line.along(3)
    line.along(-3)
    for step_k in (2, -2, 3, -3):
        line.over(step_k)
    line.finish()
    net.got(z_events[0], mine, net.z > 0)
    net.got(z_events[1], mine, net.z < 3)
    net.close()


def plain_forward_kernel(
    starts, q, k, v, x, wo, ext, rank,
    attended, lse, middle, normed, probs, x0, x1, x2, x3, bias,
):
    fill_bias(starts, bias)
    attend_pairs(q, k, v, attended, lse, bias, lambda i: None)
    rep = lax.axis_index("rep")
    middle_rows(rep, x, attended, wo, ext, rank, middle, normed, probs, (x0, x1, x2, x3))


CHUNK, CHUNKS = 512, 4


def unit_bank(expert, ext, xs, cs, source, target, before, unit, outs, dxs, scratch, ready=None):
    out_acc, dx_acc, gate, wbuf, dw_acc, dw_out, in_sems, out_sems = scratch[:8]
    routed = expert is not None
    blocks, rows = len(xs), xs[0].shape[0]
    per = CHUNK // unit

    def loads(of, buffer, sems, k, b):
        return [
            pltpu.make_async_copy(
                of(k * per + i), buffer.at[b, :, :, pl.ds(i * unit, unit)], sems.at[b, i]
            )
            for i in range(per)
        ]

    def stores(k, b):
        return [
            pltpu.make_async_copy(
                dw_out.at[b, :, :, pl.ds(i * unit, unit)],
                target(k * per + i),
                out_sems.at[b, i],
            )
            for i in range(per)
        ]

    def start_loads(k, b):
        if ready is not None:
            ready(k)
        for copy in loads(source, wbuf, in_sems, k, b):
            copy.start()
        if before is not None:
            for copy in loads(before, scratch[8], scratch[9], k, b):
                copy.start()

    start_loads(0, 0)
    if routed:
        router = router_rows(ext)
        for n in range(blocks):
            probs = route_probs(xs[n][...], router)
            lane = iota(probs.shape, 1)
            gate[n] = jnp.sum(jnp.where(lane == expert, probs, 0.0), axis=1, keepdims=True)

    def chunk(k, carry):
        b = lax.rem(k, 2)
        for copy in loads(source, wbuf, in_sems, 0, b):
            copy.wait()
        for n in range(blocks):
            x, c = xs[n][...], cs[n][...]
            wg, wu, wd = wbuf[b, 0], wbuf[b, 1], wbuf[b, 2]
            gate_h, up_h, back_h = nn(x, wg), nn(x, wu), nn(c, wd)
            sigma = 1.0 / (1.0 + jnp.exp(-gate_h))
            silu = gate_h * sigma
            hidden = silu * up_h
            if routed:
                share = gate[n]
                scaled = back_h * share
                weighted = (hidden * share).astype(BF)
            else:
                scaled, weighted = back_h, hidden.astype(BF)
            d_up = (scaled * silu).astype(BF)
            d_gate = (scaled * up_h * (sigma + silu * (1.0 - sigma))).astype(BF)
            product = nt(hidden.astype(BF), wd)
            d_rows = nt(d_gate, wg) + nt(d_up, wu)
            parts = (tn(x, d_gate), tn(x, d_up), tn(c, weighted))
            if routed:
                pairs = (hidden * back_h).astype(BF)
                d_share = nt(jnp.ones((16, CHUNK), BF), pairs)

            @pl.when(k == 0)
            def _():
                out_acc[n] = product
                dx_acc[n, 0:rows, :] = d_rows
                if routed:
                    dx_acc[n, rows : rows + 16, :] = jnp.zeros((16, d_rows.shape[1]), F32)
                    dx_acc[n, rows : rows + 16, 0:rows] = d_share

            @pl.when(k != 0)
            def _():
                out_acc[n] += product
                dx_acc[n, 0:rows, :] += d_rows
                if routed:
                    dx_acc[n, rows : rows + 16, 0:rows] += d_share

            for i in range(3):
                if n == 0:
                    dw_acc[i] = parts[i]
                else:
                    dw_acc[i] += parts[i]

        for nxt in range(1, CHUNKS):

            @pl.when(k + 1 == nxt)
            def _():
                start_loads(nxt, nxt % 2)

        @pl.when(k >= 2)
        def _():
            for copy in stores(0, b):
                copy.wait()

        if before is not None:
            for copy in loads(before, scratch[8], scratch[9], 0, b):
                copy.wait()
            for i in range(3):
                dw_out[b, i] = (dw_acc[i] + scratch[8][b, i].astype(F32)).astype(BF)
        else:
            for i in range(3):
                dw_out[b, i] = dw_acc[i].astype(BF)
        for now in range(CHUNKS):

            @pl.when(k == now)
            def _():
                for copy in stores(now, now % 2):
                    copy.start()

        return carry

    lax.fori_loop(0, CHUNKS, chunk, 0)
    for n in range(blocks):
        outs[n][...] = out_acc[n].astype(BF)
        dxs[n][...] = dx_acc[n].astype(BF)
    for b in range(2):
        for copy in stores(0, b):
            copy.wait()


def unit_scratch(blocks, rows, extra, width, per, chained):
    scratch = [
        pltpu.VMEM((blocks, rows, width), F32),
        pltpu.VMEM((blocks, rows + extra, width), F32),
        pltpu.VMEM((blocks, rows, 1), F32),
        pltpu.VMEM((2, 3, width, CHUNK), BF),
        pltpu.VMEM((3, width, CHUNK), F32),
        pltpu.VMEM((2, 3, width, CHUNK), BF),
        pltpu.SemaphoreType.DMA((2, per)),
        pltpu.SemaphoreType.DMA((2, per)),
    ]
    if chained:
        scratch += [
            pltpu.VMEM((2, 3, width, CHUNK), BF),
            pltpu.SemaphoreType.DMA((2, per)),
        ]
    return scratch


def shared_kernel(
    x, c, piece, bank, x1, x2, x3, expert_piece, expert_in,
    out, dx, grads_own, grads_other, y1, y2, y3, experts,
    send, recv, *scratch,
):
    net = Net(send, recv)
    events = [net.event() for _ in range(6)]
    peers = [(net.cousins[o], net.shard) for o in (1, 2, 3)]
    net.meet("line", peers + [(net.rep, net.across)])
    arrivals = exchange(net, (x1, x2, x3), (y1, y2, y3))
    low, high = experts.at[net.down], experts.at[net.up]
    net.put(events[0], low, low, net.rep, net.up, (net.z > 0) & (net.z < 3))
    net.put(events[1], high, high, net.rep, net.down, (net.z > 0) & (net.z < 3))
    mine = experts.at[net.shard]
    net.put(events[2], expert_piece, mine, net.rep, net.across)
    near = experts.at[net.place(1, 0)]
    net.put(events[3], near, near, net.rep, net.across)
    below = experts.at[lax.max(net.shard - 4, net.x)]
    above = experts.at[lax.min(net.shard + 4, 6 + net.x)]

    def spot(n):
        return net.place(n % 4, n // 4 % 2)

    spots = [spot(n) for n in range(8)]
    halves = [net.core, 1 - net.core]

    def source(n):
        return piece if n == 0 else bank.at[halves[n // 8], spots[n % 8]]

    def target(n):
        return (grads_own, grads_other)[n // 8].at[spots[n % 8]]

    from_below, from_above = net.z > 1, net.z < 2
    last_up, last_down = net.z == 2, net.z == 1

    def ready(k):
        if k == 3:
            net.got(events[0], below, from_below)
            net.got(events[1], above, from_above)
            net.put(events[4], below, below, net.rep, net.up, last_up)
            net.put(events[5], above, above, net.rep, net.down, last_down)

    unit_bank(None, None, [x], [c], source, target, None, 128, [out], [dx], scratch, ready)
    for event, like in arrivals:
        net.got(event, like)
    net.got(events[2], mine)
    net.got(events[3], mine)
    net.got(events[4], mine, net.z == 3)
    net.got(events[5], mine, net.z == 0)
    net.close()


def far_kernel(
    ext, xa, xb, ca, cb, expert_piece, shared_other, expert_in,
    oa, ob, da, db, grads, shared_mate, experts,
    send, recv, *scratch,
):
    net = Net(send, recv)
    events = [net.event() for _ in range(3)]
    net.meet("none", [(net.rep, net.across), (net.mate, net.shard)])
    net.put(events[2], shared_other, shared_mate, net.mate, net.shard)
    for n in (2, 3):
        piece = experts.at[net.place(n, 0)]
        net.put(events[n - 2], piece, piece, net.rep, net.across)
    spots = [net.place(n // 2, n % 2) for n in range(8)]

    def source(n):
        return expert_piece if n == 0 else experts.at[spots[n]]

    def target(n):
        return grads.at[spots[n]]

    def ready(k):
        if k >= 2:
            net.got(events[k - 2], experts.at[spots[2 * k + 1]])

    unit_bank(
        net.rep, ext, [xa, xb], [ca, cb], source, target, None, 256, [oa, ob], [da, db],
        scratch, ready,
    )
    net.got(events[2], shared_mate)
    net.close()


def near_kernel(
    ext, xa, xb, ca, cb, expert_piece, experts, before, far_a, far_b, shared_own, shared_mate,
    oa, ob, da, grads, back_a, back_b, back_c, shared_x,
    db, part_a, part_b, part_sems, send, recv, *scratch,
):
    net = Net(send, recv)
    events = [net.event() for _ in range(7)]
    peers = [(net.cousins[o], net.shard) for o in (1, 2, 3)]
    net.meet("none", peers + [(net.rep, net.across)])
    sides = [net.cycle(d) + 1 - 2 * net.x for d in range(4)]
    rows = [lax.div(side, 2) for side in sides]
    parts = []
    for d in range(4):
        parts.append((shared_own.at[sides[d]], part_a.at[d]))
        parts.append((shared_mate.at[sides[d]], part_b.at[d]))
    parts = [pltpu.make_async_copy(a, b, part_sems.at[i]) for i, (a, b) in enumerate(parts)]
    for copy in parts:
        copy.start()
    net.put(events[0], far_a, back_a, net.cousins[2], net.shard)
    net.put(events[1], far_b, back_b, net.cousins[3], net.shard)
    for copy in parts:
        copy.wait()
    for d in (2, 1, 3, 0):
        part_a[d] = (part_a[d].astype(F32) + part_b[d].astype(F32)).astype(BF)
        net.put(events[3 + d], part_a.at[d], shared_x.at[rows[d]], net.rep, net.across)
    spots = [net.place(n // 2, n % 2) for n in range(8)]

    def source(n):
        return expert_piece if n == 0 else experts.at[spots[n]]

    unit_bank(
        net.rep, ext, [xa, xb], [ca, cb], source,
        lambda n: grads.at[spots[n]], lambda n: before.at[spots[n]],
        256, [oa, ob], [da, db], scratch,
    )
    net.put(events[2], db, back_c, net.mate, net.shard)
    net.got(events[0], back_a)
    net.got(events[1], back_b)
    net.got(events[2], back_c)
    for d in range(4):
        net.got(events[3 + d], shared_x.at[rows[d]])
    net.close()


def plain_bank_kernel(blocks, unit, routed, chained, ext, *refs):
    refs = list(refs)

    def take(n):
        taken = refs[:n]
        del refs[:n]
        return taken

    xs, cs = take(blocks), take(blocks)
    bank = take(1)[0]
    before = take(1)[0] if chained else None
    outs, dxs = take(blocks), take(blocks)
    grads = take(1)[0]
    unit_bank(
        lax.axis_index("rep") if routed else None,
        ext, xs, cs,
        lambda n: bank.at[n],
        lambda n: grads.at[n],
        (lambda n: before.at[n]) if chained else None,
        unit, outs, dxs, refs,
    )


def plain_bank(ext, xs, cs, bank, before, routed):
    blocks, (rows, width) = len(xs), xs[0].shape
    chained = before is not None
    extra, unit = (16 if routed else 0), bank.shape[3]
    operands = [ext, *xs, *cs, bank] + ([before] if chained else [])
    outs = [shape((rows, width))] * blocks + [shape((rows + extra, width))] * blocks
    results = call(
        functools.partial(plain_bank_kernel, blocks, unit, routed, chained),
        outs + [shape(bank.shape)],
        [VMEM] * (1 + 2 * blocks) + [ANY] * (2 if chained else 1),
        [VMEM] * (2 * blocks) + [ANY],
        unit_scratch(blocks, rows, extra, width, CHUNK // unit, chained),
        flops=18 * blocks * rows * width * 4 * CHUNK,
        moved=30 * 2**20,
    )(*operands)
    return results[:blocks], results[blocks : 2 * blocks], results[2 * blocks]


def combine_rows(
    slot, d0, d1, d2, d3, d_shared, probs, middle, normed, cot, ext, attended, wo,
    d_middle, d_attended, grad_wo, grad_ext, branch, router_acc, gain_acc,
):
    tokens, width = middle.shape
    rep = lax.axis_index("rep")
    gain = ext[5:6, :]
    router = router_rows(ext)
    router_acc[...] = jnp.zeros_like(router_acc)
    gain_acc[...] = jnp.zeros_like(gain_acc)

    def tile(t, carry):
        at = pl.ds(pl.multiple_of(t * TILE, TILE), TILE)
        slot_one, slot_two = slot[at, 0:1], slot[at, 64:65]
        d_normed = d_shared[at, :].astype(F32)
        lane = iota((TILE, 128), 1)
        d_gates = jnp.zeros((TILE, 128), F32)
        for o, d in enumerate((d0, d1, d2, d3)):
            place = (iota((TILE, CAP), 1) + o * CAP).astype(F32)
            hit = (place == slot_one) | (place == slot_two)
            d_normed = d_normed + nn(ones_where(hit), d[0:CAP, :])
            share = d[CAP : CAP + 16, 0:CAP].astype(F32)[0:1, :]
            d_share = jnp.sum(jnp.where(hit, share, 0.0), axis=1, keepdims=True)
            d_gates = d_gates + jnp.where(lane == sibling(rep, o), d_share, 0.0)
        p = probs[at, :]
        inner = jnp.sum(d_gates * p, axis=1, keepdims=True)
        d_logits = (p * (d_gates - inner)).astype(BF)
        d_normed = d_normed + nn(d_logits, router)
        router_acc[...] += tn(d_logits, normed[at, :])
        rows = middle[at, :]
        scale = lax.rsqrt(jnp.mean(rows * rows, axis=1, keepdims=True) + EPSILON)
        unit = rows * scale
        gain_acc[...] += jnp.sum((d_normed * unit).reshape(TILE // 8, 8, width), axis=0)
        w = d_normed * gain
        inner = jnp.mean(w * unit, axis=1, keepdims=True)
        total = cot[at, :].astype(F32) + scale * (w - unit * inner)
        d_middle[at, :] = total
        rounded = total.astype(BF)
        branch[at, :] = rounded
        d_attended[at, :] = nt(rounded, wo[...]).astype(BF)
        return carry

    lax.fori_loop(0, tokens // TILE, tile, 0)
    grad_wo[...] = tn(attended[...], branch[...]).astype(BF)
    row = iota((16, width), 0)
    total = jnp.sum(gain_acc[...], axis=0, keepdims=True)
    grad_ext[...] = jnp.where(row < 4, router_acc[0:16, :], jnp.where(row == 5, total, 0.0))


def output_rows(slot, o0, o1, o2, o3, shared, probs, middle, out, first, last):
    rep = lax.axis_index("rep")

    def tile(t, carry):
        at = pl.ds(pl.multiple_of(t * TILE, TILE), TILE)
        slot_one, slot_two = slot[at, 0:1], slot[at, 64:65]
        total = middle[at, :] + shared[at, :].astype(F32)
        p = probs[at, :]
        lane = iota((TILE, 128), 1)
        for o, rows in enumerate((o0, o1, o2, o3)):
            place = (iota((TILE, CAP), 1) + o * CAP).astype(F32)
            hit = (place == slot_one) | (place == slot_two)
            share = jnp.sum(jnp.where(lane == sibling(rep, o), p, 0.0), axis=1, keepdims=True)
            total = total + nn(jnp.where(hit, share, 0.0).astype(BF), rows[...])
        out[at, :] = total.astype(BF)
        return carry

    lax.fori_loop(first, last, tile, 0)


def back_pairs(
    q, k, v, d_out, out, lse, cosine, sine, dq, dk, dv, bias, dk_acc, dv_acc, step
):
    tokens, width = q.shape

    def pair(i, carry):
        step(i)
        cols = pl.ds(pl.multiple_of(i * 128, 128), 128)
        keys, values = k[:, cols], v[:, cols]
        half_keys = [keep_half(keys, 0), keep_half(keys, 1)]
        dk_acc[...] = jnp.zeros_like(dk_acc)
        dv_acc[...] = jnp.zeros_like(dv_acc)
        low = iota((TILE, 128), 1) < 64
        for t in range(tokens // TILE):
            begin = t * TILE
            end = min(tokens, begin + TILE + PIECE)
            at = slice(begin, begin + TILE)
            block, grad = q[at, cols], d_out[at, cols]
            product = grad.astype(F32) * out[at, cols].astype(F32)
            block_lse = lse[at, cols]
            d_block = None
            for h in range(2):
                block_h, grad_h = keep_half(block, h), keep_half(grad, h)
                scores = nt(block_h, keys[:end])
                scores = biased(scores, bias, begin, begin, end)
                probs = jnp.exp(scores - block_lse[:, 64 * h : 64 * h + 1])
                d_probs = nt(grad_h, values[:end])
                inner = jnp.sum(
                    jnp.where(low if h == 0 else ~low, product, 0.0), axis=1, keepdims=True
                )
                d_scores = (probs * (d_probs - inner)).astype(BF)
                part = nn(d_scores, half_keys[h][:end])
                d_block = part if d_block is None else d_block + part
                dk_acc[0:end, :] += tn(d_scores, block_h)
                dv_acc[0:end, :] += tn(probs.astype(BF), grad_h)
            dq[at, cols] = spin(d_block * 0.125, cosine[at, :], -sine[at, :]).astype(BF)
        dk[:, cols] = spin(dk_acc[...], cosine[...], -sine[...]).astype(BF)
        dv[:, cols] = dv_acc[...].astype(BF)
        return carry

    lax.fori_loop(0, width // 128, pair, 0)


def fetch(sources, targets, sems):
    copies = [pltpu.make_async_copy(a, b, sems.at[i]) for i, (a, b) in enumerate(zip(sources, targets))]
    for copy in copies:
        copy.start()
    for copy in copies:
        copy.wait()


class Reduce:
    def __init__(self, net, own, from_x, from_z, held, spare, sems):
        self.net, self.own, self.from_x, self.from_z = net, own, from_x, from_z
        self.held, self.spare, self.sems = held, spare, sems
        self.x_events = [net.event() for _ in range(4)]
        self.z_events = [net.event() for _ in range(3)]
        self.spots = [net.cycle(d) for d in range(4)]
        self.levels = [lax.div(spot, 2) for spot in self.spots]
        self.pieces = [held.at[d] for d in range(4)]

    def send_across(self):
        net = self.net
        for d in (2, 1, 3, 0):
            source = self.own[0].at[self.spots[d] + 1 - 2 * net.x]
            target = self.from_x.at[self.levels[d]]
            net.put(self.x_events[d], source, target, net.rep, net.across)

    def add_across(self, d, wait=True):
        net = self.net
        far = self.from_x.at[self.levels[d]]
        if wait:
            net.got(self.x_events[d], far)
        sources = [own.at[self.spots[d]] for own in self.own] + [far]
        targets = [self.held.at[d]] + [self.spare.at[i] for i in range(len(self.own))]
        fetch(sources, targets, self.sems)
        total = self.held[d].astype(F32)
        for i in range(len(self.own)):
            total = total + self.spare[i].astype(F32)
        self.held[d] = total.astype(BF)
        if d:
            target = self.from_z.at[d - 1]
            net.put(self.z_events[d - 1], self.pieces[d], target, net.rep, self.spots[d])

    def total(self, out):
        for d in (1, 2, 3):
            self.net.got(self.z_events[d - 1], self.from_z.at[d - 1])
        targets = [self.held.at[d] for d in (1, 2, 3)]
        self.settle()
        fetch([self.from_z.at[d] for d in range(3)], targets, self.sems)
        total = self.held[0].astype(F32)
        for d in (1, 2, 3):
            total = total + self.held[d].astype(F32)
        out[...] = total.astype(BF)

    def settle(self):
        for event in self.z_events:
            cond, source = self.net.open.pop(event)
            self.net.copy(event, source, source, self.net.rep, self.net.shard).wait_send()


def back_kernel(
    starts, slot, d0, d1, d2, d3, d_shared, probs, middle, normed, cot, ext, attended, wo,
    q, k, v, lse, cosine, sine,
    o1, o2, o3, grads, shared_own, shared_mate, shared_x,
    d_middle, grad_wo, grad_ext, dq, dk, dv, expert_total, shared_total,
    r1, r2, r3, expert_x, expert_z, shared_z,
    d_attended, branch, router_acc, gain_acc, bias, dk_acc, dv_acc,
    held, spare, held_s, spare_s, sems, send, recv,
):
    net = Net(send, recv)
    expert = Reduce(net, [grads], expert_x, expert_z, held, spare, sems)
    shared = Reduce(net, [shared_own, shared_mate], shared_x, shared_z, held_s, spare_s, sems)
    peers = [(net.cousins[o], net.shard) for o in (1, 2, 3)]
    net.meet("all", peers + [(net.rep, net.across)])
    expert.send_across()
    arrivals = exchange(net, (o1, o2, o3), (r1, r2, r3))
    for d in (2, 1, 3, 0):
        shared.add_across(d, False)
    combine_rows(
        slot, d0, d1, d2, d3, d_shared, probs, middle, normed, cot, ext, attended, wo,
        d_middle, d_attended, grad_wo, grad_ext, branch, router_acc, gain_acc,
    )
    fill_bias(starts, bias)
    expert.add_across(2)

    def step(i):
        @pl.when(i == 3)
        def _():
            expert.add_across(1)

    back_pairs(
        q, k, v, d_attended, attended, lse, cosine, sine, dq, dk, dv, bias, dk_acc, dv_acc, step
    )
    shared.total(shared_total)
    expert.add_across(3)
    expert.add_across(0)
    for event, like in arrivals:
        net.got(event, like)
    expert.total(expert_total)
    net.close()


def plain_back_kernel(
    starts, slot, d0, d1, d2, d3, d_shared, probs, middle, normed, cot, ext, attended, wo,
    q, k, v, lse, cosine, sine,
    d_middle, grad_wo, grad_ext, dq, dk, dv,
    d_attended, branch, router_acc, gain_acc, bias, dk_acc, dv_acc,
):
    combine_rows(
        slot, d0, d1, d2, d3, d_shared, probs, middle, normed, cot, ext, attended, wo,
        d_middle, d_attended, grad_wo, grad_ext, branch, router_acc, gain_acc,
    )
    fill_bias(starts, bias)
    back_pairs(
        q, k, v, d_attended, attended, lse, cosine, sine, dq, dk, dv, bias, dk_acc, dv_acc,
        lambda i: None,
    )


def norm_rows(x, ext, normed_all):
    gain = ext[4:5, :]

    def tile(t, carry):
        at = pl.ds(pl.multiple_of(t * TILE, TILE), TILE)
        rows = x[at, :].astype(F32)
        scale = lax.rsqrt(jnp.mean(rows * rows, axis=1, keepdims=True) + EPSILON)
        normed_all[at, :] = (rows * scale * gain).astype(BF)
        return carry

    lax.fori_loop(0, x.shape[0] // TILE, tile, 0)


def input_grad(x, ext, dq, dk, dv, wq, wk, wv, d_middle, grad_in, gain_acc):
    tokens, width = x.shape
    gain = ext[4:5, :]
    gain_acc[...] = jnp.zeros_like(gain_acc)

    def tile(t, carry):
        at = pl.ds(pl.multiple_of(t * TILE, TILE), TILE)
        rows = x[at, :].astype(F32)
        scale = lax.rsqrt(jnp.mean(rows * rows, axis=1, keepdims=True) + EPSILON)
        unit = rows * scale
        d_normed = nt(dq[at, :], wq[...]) + nt(dk[at, :], wk[...]) + nt(dv[at, :], wv[...])
        gain_acc[...] += jnp.sum((d_normed * unit).reshape(TILE // 8, 8, width), axis=0)
        w = d_normed * gain
        inner = jnp.mean(w * unit, axis=1, keepdims=True)
        grad_in[at, :] = d_middle[at, :] + scale * (w - unit * inner)
        return carry

    lax.fori_loop(0, tokens // TILE, tile, 0)


def tail_kernel(
    x, ext, dq, dk, dv, wq, wk, wv, d_middle, grad_wo, grad_ext,
    slot, o0, o1, o2, o3, shared_out, probs, middle, expert_total, shared_total,
    grad_in, outputs, weights, small, shared_pair, e1, e2, e3,
    normed_all, gain_acc, gw, from_mate, from_x, from_z, from_y, result, from_core,
    tiny, tiny_in, shared_in, shared_sum, send, recv,
):
    width = x.shape[1]
    half = width // SLOTS
    net = Net(send, recv)
    e_events = [net.event() for _ in range(3)]
    s_events = [net.event() for _ in range(2)]
    m_events = [net.event() for _ in range(2)]
    x_events = [[net.event() for _ in range(2)] for _ in range(4)]
    z_events = [[net.event() for _ in range(2)] for _ in range(3)]
    y_event, c_event = net.event(), net.event()
    t_events = [net.event() for _ in range(6)]
    net.meet(
        "all", [(net.mate, net.shard), (net.cousins[2], net.shard), (net.rep, net.across)]
    )
    far = net.cousins[2]
    net.put(s_events[0], shared_total, shared_in, far, net.shard)
    net.put(e_events[1], expert_total, e2, far, net.shard)
    net.put(e_events[0], expert_total, e1, net.mate, net.shard)
    norm_rows(x, ext, normed_all)
    spots = [lax.rem(i + 2 * net.core, 4) for i in range(4)]
    gw[spots[0]] = tn(normed_all[...], dq[...]).astype(BF)
    gw[spots[1]] = tn(normed_all[...], dk[...]).astype(BF)
    gw[spots[2]] = tn(normed_all[...], dv[...]).astype(BF)
    gw[spots[3]] = grad_wo[...]
    for i in range(2):
        net.put(m_events[i], gw.at[2 + i], from_mate.at[i], net.mate, net.shard)

    def rows_of(spot):
        return pl.ds(pl.multiple_of(spot * half, 32), half)

    mine = [rows_of(net.cycle(d)) for d in range(4)]
    theirs = [rows_of(net.cycle(d) + 1 - 2 * net.x) for d in range(4)]
    for i in range(2):
        net.got(m_events[i], from_mate.at[i])
        gw[i] = (gw[i].astype(F32) + from_mate[i].astype(F32)).astype(BF)
    for d in (2, 1, 3, 0):
        for i in range(2):
            net.put(
                x_events[d][i], gw.at[i, theirs[d]], from_x.at[d, i], net.rep, net.across
            )
    input_grad(x, ext, dq, dk, dv, wq, wk, wv, d_middle, grad_in, gain_acc)
    row = iota((16, width), 0)
    total = jnp.sum(gain_acc[...], axis=0, keepdims=True)
    tiny[0] = (grad_ext[...] + jnp.where(row == 4, total, 0.0)).astype(BF)
    net.put(t_events[0], tiny.at[0], tiny_in.at[0], net.mate, net.shard)

    def add_across(d):
        for i in range(2):
            net.got(x_events[d][i], from_x.at[d, i])
            summed = gw[i, mine[d], :].astype(F32) + from_x[d, i].astype(F32)
            gw[i, mine[d], :] = summed.astype(BF)
            if d:
                net.put(
                    z_events[d - 1][i], gw.at[i, mine[d]], from_z.at[d - 1, i],
                    net.rep, net.cycle(d),
                )

    def tiny_add(n, target_rep, target_shard):
        net.got(t_events[n], tiny_in.at[n])
        tiny[n + 1] = (tiny[n].astype(F32) + tiny_in[n].astype(F32)).astype(BF)
        if target_rep is not None:
            source, target = tiny.at[n + 1], tiny_in.at[n + 1]
            net.put(t_events[n + 1], source, target, target_rep, target_shard)

    add_across(2)
    tiny_add(0, net.rep, net.across)
    output_rows(slot, o0, o1, o2, o3, shared_out, probs, middle, outputs, 0, 2)
    add_across(1)
    tiny_add(1, far, net.shard)
    net.got(s_events[0], shared_in)
    shared_sum[...] = (shared_total[...].astype(F32) + shared_in[...].astype(F32)).astype(BF)
    shared_pair[0] = shared_sum[...]
    net.put(s_events[1], shared_sum, shared_pair.at[1], net.mate, net.shard)
    output_rows(slot, o0, o1, o2, o3, shared_out, probs, middle, outputs, 2, 4)
    tiny_add(2, None, None)
    for d in (1, 2, 3):
        net.put(t_events[2 + d], tiny.at[3], tiny_in.at[2 + d], net.rep, net.cycle(d))
    add_across(3)
    add_across(0)
    for i in range(2):
        total = gw[i, mine[0], :].astype(F32)
        for d in (1, 2, 3):
            net.got(z_events[d - 1][i], from_z.at[d - 1, i])
            total = total + from_z[d - 1, i].astype(F32)
        result[0, i] = total.astype(BF)
    net.put(y_event, result.at[0], from_y, far, net.shard)
    total = tiny[3].astype(F32)
    for d in (1, 2, 3):
        net.got(t_events[2 + d], tiny_in.at[2 + d])
        total = total + tiny_in[2 + d].astype(F32)
    small[...] = total.astype(BF).astype(F32)
    net.got(e_events[1], e2)
    net.put(e_events[2], e2, e3, net.mate, net.shard)
    net.got(y_event, from_y)
    result[1] = (result[0].astype(F32) + from_y[...].astype(F32)).astype(BF)
    net.put(c_event, result.at[1], from_core, net.mate, net.shard)
    for i in range(2):
        weights[spots[i]] = result[1, i].astype(F32)
    net.got(c_event, from_core)
    for i in range(2):
        weights[spots[2 + i]] = from_core[i].astype(F32)
    net.got(e_events[0], e1)
    net.got(s_events[1], shared_pair.at[1])
    net.got(e_events[2], e3)
    net.close()


def plain_tail_kernel(
    x, ext, dq, dk, dv, wq, wk, wv, d_middle,
    slot, o0, o1, o2, o3, shared_out, probs, middle,
    grad_in, outputs, gw, gain, normed_all, gain_acc,
):
    norm_rows(x, ext, normed_all)
    for i, d in enumerate((dq, dk, dv)):
        gw[i] = tn(normed_all[...], d[...]).astype(BF)
    input_grad(x, ext, dq, dk, dv, wq, wk, wv, d_middle, grad_in, gain_acc)
    gain[...] = gain_acc[...]
    output_rows(
        slot, o0, o1, o2, o3, shared_out, probs, middle, outputs, 0, x.shape[0] // TILE
    )


def finish_kernel(e0, e1, e2, e3, pair, gate, up, down, s_gate, s_up, s_down):
    rep = lax.axis_index("rep")
    core = lax.rem(rep, 2)
    for o, part in enumerate((e0, e1, e2, e3)):
        at = sibling(rep, o)
        gate[at] = part[0].astype(F32)
        up[at] = part[1].astype(F32)
        down[at] = part[2].astype(F32).T
    span = pair.shape[3]
    for side in range(2):

        @pl.when(core == side)
        def _():
            for n in range(2):
                at = (side + n) % 2 * span
                s_gate[:, at : at + span] = pair[n, 0].astype(F32)
                s_up[:, at : at + span] = pair[n, 1].astype(F32)
                s_down[at : at + span, :] = pair[n, 2].astype(F32).T


def rope_tables(length, head_dim):
    positions = jnp.arange(length, dtype=F32)
    inverse_freq = 10000.0 ** (-2.0 * jnp.arange(head_dim // 2, dtype=F32) / head_dim)
    angle = positions[:, None] * inverse_freq[None, :]
    cosine, sine = jnp.cos(angle), jnp.sin(angle)
    return (
        jnp.concatenate([cosine] * 4, axis=1),
        jnp.concatenate([-sine, sine, -sine, sine], axis=1),
    )


def body(
    inputs,
    piece_starts,
    routes,
    attn_gain,
    query_weight,
    key_weight,
    value_weight,
    out_weight,
    ffn_gain,
    router_weight,
    expert_gate,
    expert_up,
    expert_down,
    shared_gate,
    shared_up,
    shared_down,
    cotangent,
):
    _, tokens, width = inputs.shape
    shards = lax.axis_size("shard")
    rep, shard = lax.axis_index("rep"), lax.axis_index("shard")
    core = rep % 2
    ringed = shards == SLOTS
    rows = width // shards
    units = shared_gate.shape[1]
    x, cot, chosen = inputs[0], cotangent[0], routes[0]
    small = jnp.concatenate([router_weight.T, attn_gain[None], ffn_gain[None]], axis=0)
    small = jnp.pad(small, ((0, 10), (0, 0)))
    small = lax.dynamic_update_slice(jnp.zeros((16, width), BF), small, (0, shard * rows))
    blank = jnp.zeros((16, width), BF)
    if ringed:
        half_one = jnp.concatenate([query_weight, key_weight, small], axis=0)
        half_two = jnp.concatenate([value_weight, out_weight, blank], axis=0)
        piece = jnp.where(core == 0, half_one, half_two)
    else:
        wq, wk, wv, wo = [
            lax.all_gather(w, "shard", axis=0, tiled=True)
            for w in (query_weight, key_weight, value_weight, out_weight)
        ]
        ext = lax.psum(small.astype(F32), "shard")

    shared_pack = jnp.stack([shared_gate, shared_up, shared_down.T])
    my_half = lax.dynamic_slice_in_dim(shared_pack, core * (units // 2), units // 2, 2)
    expert_pack = jnp.stack([expert_gate[rep], expert_up[rep], expert_down[rep].T])

    cosine, sine = rope_tables(tokens, width // HEADS)
    token_f = shape((tokens, width))
    square = shape((width, width))
    packed = [shape((CAP, width))] * 4
    outs = [shape((8, tokens), F32), shape((tokens, 128), F32)] + [token_f] * 3
    work = 2 * tokens * width * (CAP * 4 + 3 * width)
    if ringed:
        rank, slot, q, k, v, *heads = call(
            head_kernel,
            outs + [square] * 4 + [shape((16, width), F32)] + packed,
            [VMEM] * 7,
            [VMEM] * 10 + [VMEM] + [ANY] * 3,
            [
                pltpu.VMEM((2, SLOTS, 2 * rows + 16, width), BF),
                pltpu.VMEM((3, CAP, width), BF),
                pltpu.SemaphoreType.DMA((31,)),
                pltpu.SemaphoreType.DMA((31,)),
                pltpu.SemaphoreType.DMA,
            ],
            flops=work,
            moved=24 * 2**20,
            group=0,
        )(chosen, chosen.T, cot, x, piece, cosine, sine)
        wq, wk, wv, wo, ext, *cot_in = heads
    else:
        rank, slot, q, k, v, *cot_out = call(
            plain_head_kernel, outs + packed, [VMEM] * 10, [VMEM] * 9, flops=work,
            moved=24 * 2**20,
        )(chosen, chosen.T, cot, x, cosine, sine, wq, wk, wv, ext)
        cot_in = [cot_out[0]] + [to_rep(cot_out[o], o) for o in (1, 2, 3)]

    outs = [token_f, shape((tokens, width), F32), shape((tokens, width), F32), token_f]
    outs += [shape((tokens, 128), F32)] + packed
    work = 2 * tokens * width * (8 * tokens + width + 4 * CAP)
    bias = pltpu.VMEM((tokens, tokens), F32)
    if ringed:
        attended, lse, middle, normed, probs, *x_out, shared_bank, expert_bank = call(
            forward_kernel,
            outs + [shape((2, SLOTS) + my_half.shape), shape((SLOTS,) + expert_pack.shape)],
            [SMEM] + [VMEM] * 7 + [ANY] * 2,
            [VMEM] * 9 + [ANY] * 2,
            [bias, pltpu.SemaphoreType.DMA((30,)), pltpu.SemaphoreType.DMA((30,))],
            flops=work,
            moved=30 * 2**20,
            group=1,
        )(piece_starts, q, k, v, x, wo, ext, rank, my_half, expert_pack)
    else:
        attended, lse, middle, normed, probs, *x_out = call(
            plain_forward_kernel, outs, [SMEM] + [VMEM] * 7, [VMEM] * 9, [bias], flops=work,
            moved=30 * 2**20,
        )(piece_starts, q, k, v, x, wo, ext, rank)

    rows_out = shape((CAP, width))
    rows_back = shape((CAP + 16, width))
    if ringed:
        half_grads = shape((SLOTS,) + my_half.shape)
        shared_out, shared_dx, grads_own, grads_other, y1, y2, y3, expert_bank = call(
            shared_kernel,
            [token_f] * 2 + [half_grads] * 2 + packed[:3] + [shape(expert_bank.shape)],
            [VMEM] * 2 + [ANY] * 7,
            [VMEM] * 2 + [ANY] * 6,
            [pltpu.SemaphoreType.DMA((9,)), pltpu.SemaphoreType.DMA((9,))]
            + unit_scratch(1, tokens, 0, width, 4, False),
            flops=18 * tokens * width * CHUNK * CHUNKS,
            moved=30 * 2**20,
            group=2,
            alias={8: 7},
        )(normed, cot, my_half, shared_bank, *x_out[1:], expert_pack, expert_bank)
        x_in = [x_out[0], y1, y2, y3]
        bank = shape(expert_bank.shape)
        far_a, far_b, da, db, before, shared_mate, expert_bank = call(
            far_kernel,
            [rows_out] * 2 + [rows_back] * 2 + [bank, half_grads, bank],
            [VMEM] * 5 + [ANY] * 3,
            [VMEM] * 4 + [ANY] * 3,
            [pltpu.SemaphoreType.DMA((3,)), pltpu.SemaphoreType.DMA((3,))]
            + unit_scratch(2, CAP, 16, width, 2, False),
            flops=36 * CAP * width * CHUNK * CHUNKS,
            moved=30 * 2**20,
            group=3,
            alias={7: 6},
        )(ext, *x_in[2:], *cot_in[2:], expert_pack, grads_other, expert_bank)
        half_x = (4,) + my_half.shape
        near_a, near_b, d0, grads, d2, d3, d1, shared_x = call(
            near_kernel,
            [rows_out] * 2 + [rows_back, bank] + [rows_back] * 3 + [shape(half_x)],
            [VMEM] * 5 + [ANY] * 7,
            [VMEM] * 3 + [ANY] * 5,
            [
                pltpu.VMEM((CAP + 16, width), BF),
                pltpu.VMEM(half_x, BF),
                pltpu.VMEM(half_x, BF),
                pltpu.SemaphoreType.DMA((8,)),
                pltpu.SemaphoreType.DMA((7,)),
                pltpu.SemaphoreType.DMA((7,)),
            ]
            + unit_scratch(2, CAP, 16, width, 2, True),
            flops=36 * CAP * width * CHUNK * CHUNKS,
            moved=30 * 2**20,
            group=4,
        )(
            ext, *x_in[:2], *cot_in[:2], expert_pack, expert_bank, before, da, db,
            grads_own, shared_mate,
        )
        d_rows = [d0, d1, d2, d3]
    else:

        def slotted(part):
            every = lax.all_gather(part, "shard")
            every = every.reshape(SLOTS, shards // SLOTS, 3, width, part.shape[2])
            return every.transpose(0, 2, 3, 1, 4).reshape(SLOTS, 3, width, -1)

        shared_bank = slotted(my_half)
        shared_bank = jnp.concatenate([shared_bank, to_rep(shared_bank, 1)], axis=0)
        expert_bank = slotted(expert_pack)
        x_in = [x_out[0]] + [to_rep(x_out[o], o) for o in (1, 2, 3)]
        (shared_out,), (shared_dx,), shared_grads = plain_bank(
            ext, [normed], [cot], shared_bank, None, False
        )
        grads_own, grads_other = shared_grads[:SLOTS], shared_grads[SLOTS:]
        (far_a, far_b), (da, db), before = plain_bank(
            ext, x_in[2:], cot_in[2:], expert_bank, None, True
        )
        (near_a, near_b), (d0, d1), grads = plain_bank(
            ext, x_in[:2], cot_in[:2], expert_bank, before, True
        )
        d_rows = [d0, to_rep(d1, 1), to_rep(da, 2), to_rep(db, 3)]
    wide = shape((tokens, width), F32)
    outs = [wide, square, shape((16, width), F32)] + [token_f] * 3
    operands = (piece_starts, slot, *d_rows, shared_dx, probs, middle, normed, cot, ext, attended)
    operands += (wo, q, k, v, lse, cosine, sine)
    specs = [SMEM] + [VMEM] * 19
    scratch = [
        pltpu.VMEM((tokens, width), BF),
        pltpu.VMEM((tokens, width), BF),
        pltpu.VMEM((128, width), F32),
        pltpu.VMEM((8, width), F32),
        bias,
        pltpu.VMEM((tokens, 128), F32),
        pltpu.VMEM((tokens, 128), F32),
    ]
    work = 2 * tokens * width * (2 * width + 4 * CAP) + 40 * tokens * tokens * width
    if ringed:
        bank_x, bank_z = (4,) + expert_pack.shape, (3,) + expert_pack.shape
        half_z = (3,) + my_half.shape
        d_middle, grad_wo, grad_ext, dq, dk, dv, expert_total, shared_total, *back = call(
            back_kernel,
            outs
            + [shape(expert_pack.shape), shape(my_half.shape)]
            + [rows_out] * 3
            + [shape(bank_x), shape(bank_z), shape(half_z)],
            specs + [ANY] * 7,
            [VMEM] * 8 + [ANY] * 6,
            scratch
            + [
                pltpu.VMEM(bank_x, BF),
                pltpu.VMEM((1,) + expert_pack.shape, BF),
                pltpu.VMEM(half_x, BF),
                pltpu.VMEM((2,) + my_half.shape, BF),
                pltpu.SemaphoreType.DMA((3,)),
                pltpu.SemaphoreType.DMA((17,)),
                pltpu.SemaphoreType.DMA((17,)),
            ],
            flops=work,
            moved=40 * 2**20,
            group=5,
        )(*operands, near_b, far_a, far_b, grads, grads_own, shared_mate, shared_x)
        operands = (x, ext, dq, dk, dv, wq, wk, wv, d_middle, grad_wo, grad_ext)
        operands += (slot, near_a, *back[:3], shared_out, probs, middle)
        strip = (2, width // SLOTS, width)
        grad_in, outputs, weights, small, shared_pair, e1, e2, e3 = call(
            tail_kernel,
            [wide, token_f, shape((4, rows, width), F32), shape((16, width), F32)]
            + [shape((2,) + my_half.shape)]
            + [shape(expert_pack.shape)] * 3,
            [VMEM] * 19 + [ANY, VMEM],
            [VMEM] * 5 + [ANY] * 3,
            [
                pltpu.VMEM((tokens, width), BF),
                pltpu.VMEM((8, width), F32),
                pltpu.VMEM((4, width, width), BF),
                pltpu.VMEM((2, width, width), BF),
                pltpu.VMEM((4,) + strip, BF),
                pltpu.VMEM((3,) + strip, BF),
                pltpu.VMEM(strip, BF),
                pltpu.VMEM((2,) + strip, BF),
                pltpu.VMEM(strip, BF),
                pltpu.VMEM((4, 16, width), BF),
                pltpu.VMEM((6, 16, width), BF),
                pltpu.VMEM(my_half.shape, BF),
                pltpu.VMEM(my_half.shape, BF),
                pltpu.SemaphoreType.DMA((29,)),
                pltpu.SemaphoreType.DMA((29,)),
            ],
            flops=2 * tokens * width * (6 * width + 4 * CAP),
            moved=40 * 2**20,
            group=6,
        )(*operands, expert_total, shared_total)
        banks = [shape((4, width, units), F32)] * 2 + [shape((4, units, width), F32)]
        banks += [shape((width, units), F32)] * 2 + [shape((units, width), F32)]
        finals = call(finish_kernel, banks, [VMEM] * 5, [VMEM] * 6, moved=18 * 2**20)(
            expert_total, e1, e2, e3, shared_pair
        )
        grad_q, grad_k, grad_v, grad_o = (weights[i] for i in range(4))
    else:
        d_middle, grad_wo, grad_ext, dq, dk, dv = call(
            plain_back_kernel, outs, specs, [VMEM] * 6, scratch, flops=work, moved=40 * 2**20
        )(*operands)
        out_rows = [near_a, to_rep(near_b, 1), to_rep(far_a, 2), to_rep(far_b, 3)]
        grad_in, outputs, gw, gain = call(
            plain_tail_kernel,
            [wide, token_f, shape((3, width, width)), shape((8, width), F32)],
            [VMEM] * 17,
            [VMEM] * 4,
            [pltpu.VMEM((tokens, width), BF), pltpu.VMEM((8, width), F32)],
            flops=2 * tokens * width * (6 * width + 4 * CAP),
            moved=40 * 2**20,
        )(
            x, ext, dq, dk, dv, wq, wk, wv, d_middle, slot, *out_rows, shared_out, probs, middle
        )

        def over_rep(total):
            return lax.psum(total.astype(BF), "rep").astype(F32)

        def unslot(every, part_units):
            every = every.reshape(SLOTS, 3, width, shards // SLOTS, part_units)
            every = every.transpose(0, 3, 1, 2, 4).reshape(shards, 3, width, part_units)
            return lax.psum_scatter(every, "shard", scatter_dimension=0)

        grad_q, grad_k, grad_v, grad_o = (
            over_rep(lax.psum_scatter(w, "shard", tiled=True))
            for w in (gw[0], gw[1], gw[2], grad_wo)
        )
        small = grad_ext.at[4].add(jnp.sum(gain, axis=0))
        small = lax.psum(small, ("rep", "shard"))
        shared_sum = grads_own.astype(F32) + to_rep(grads_other, 1).astype(F32)
        total = unslot(shared_sum.astype(BF), units // 2).astype(F32)
        total = (total + to_rep(total.astype(BF), 2).astype(F32)).astype(BF)
        mate = to_rep(total, 1)
        shared_full = jnp.concatenate(
            [jnp.where(core == 0, total, mate), jnp.where(core == 0, mate, total)], axis=2
        ).astype(F32)
        expert_total = unslot(grads, units).astype(BF)
        parts = jnp.stack([expert_total] + [to_rep(expert_total, o) for o in (1, 2, 3)])
        full = jnp.take(parts, jnp.arange(4) ^ rep, axis=0).astype(F32)
        finals = (full[:, 0], full[:, 1], full[:, 2].transpose(0, 2, 1))
        finals += (shared_full[0], shared_full[1], shared_full[2].T)
    tiny = lax.dynamic_slice(small, (0, shard * rows), (16, rows))
    return (
        outputs[None],
        grad_in[None],
        tiny[4],
        grad_q,
        grad_k,
        grad_v,
        grad_o,
        tiny[5],
        tiny[:4].T,
        *finals,
    )


def solution(mesh):
    in_specs = (
        P(("rep", "shard"), None, None),
        P(("rep", "shard"), None),
        P(("rep", "shard"), None, None),
        P("shard"),
        P("shard", None),
        P("shard", None),
        P("shard", None),
        P("shard", None),
        P("shard"),
        P("shard", None),
        P(None, None, "shard"),
        P(None, None, "shard"),
        P(None, "shard", None),
        P(None, "shard"),
        P(None, "shard"),
        P("shard", None),
        P(("rep", "shard"), None, None),
    )
    out_specs = (
        P(("rep", "shard"), None, None),
        P(("rep", "shard"), None, None),
        P("shard"),
        P("shard", None),
        P("shard", None),
        P("shard", None),
        P("shard", None),
        P("shard"),
        P("shard", None),
        P(None, None, "shard"),
        P(None, None, "shard"),
        P(None, "shard", None),
        P(None, "shard"),
        P(None, "shard"),
        P("shard", None),
    )
    return jax.shard_map(body, mesh=mesh, in_specs=in_specs, out_specs=out_specs, check_vma=False)
```

time: 904 us -> 623 us (0.69)
  waiting for transfers between devices: 437 us -> 0 us
  Pallas kernels: 331 us -> 592 us
  starting transfers between devices: 43.2 us -> 0 us
  local copies, waits for them, and re-layouts: 45.4 us -> 11.5 us
  other arithmetic: 32.5 us -> 9.62 us
    ppermute x54 -> x0, waiting for transfers between devices: 437 us -> none  [permute(): return lax.ppermute(x, AXES, pairs)]
    pallas_call x10 -> x8, Pallas kernels: 331 us -> 592 us  [the longest x1 172 us: body(): call(back_kernel, outs + [shape(expert_pack.shape), shape(my_half.shape)]...]
    ppermute x54 -> x0, starting transfers between devices: 43.2 us -> none  [permute(): return lax.ppermute(x, AXES, pairs)]
    unnamed x86 -> x17, local copies, waits for them, and re-layouts: 23.3 us -> 5.2 us
    convert_element_type x12 -> x0, other arithmetic: 16.8 us -> none  [the longest x1 5.22 us: body(): shared_sum = shared_sum.astype(BF)]
  transfers between devices with their start and end apart: 54 -> 0, of which waited for: 24 -> 0; matrix products, arithmetic and copies ran while one was open for 6% -> 0% of each run, Pallas kernels for 23% -> 0%
where the time goes in v3:
time: 623 us; the launch traced here: 614 us
  Pallas kernels  592 us (95%)
  local copies, waits for them, and re-layouts  11.5 us (2%)
  other arithmetic  9.62 us (2%)
    pallas_call x1, Pallas kernels, body(): call(back_kernel, outs + [shape(expert_pack.shape), shape(my_half.shape)]...  172 us
    pallas_call x1, Pallas kernels, body(): call(forward_kernel, outs + [shape((2, SLOTS) + my_half.shape), shape((SL...  80.3 us
    pallas_call x1, Pallas kernels, body(): call(far_kernel, [rows_out] * 2 + [rows_back] * 2 + [bank, half_grads, ba...  72.8 us
    pallas_call x1, Pallas kernels, body(): call(tail_kernel, [wide, token_f, shape((4, rows, width), F32), shape((16...  72.5 us
    pallas_call x1, Pallas kernels, body(): call(near_kernel, [rows_out] * 2 + [rows_back, bank] + [rows_back] * 3 +...  68.3 us
    pallas_call x1, Pallas kernels, body(): call(shared_kernel, [token_f] * 2 + [half_grads] * 2 + packed[:3] + [shap...  63.6 us
    pallas_call x1, Pallas kernels, body(): call(head_kernel, outs + [square] * 4 + [shape((16, width), F32)] + packe...  53.8 us

profile of v3, /device:TPU:0, one launch (start us, length us, event | category | flops | bytes accessed | tf_op | source)
XLA Modules:
  0.0 614.2 jit_solution(9679887591408030811)
XLA Ops:
  0.6 0.0 copy-start
  0.7 0.8 fusion.9
  1.5 0.2 dynamic_update_slice.3
  1.7 1.9 maximum_select_fusion.piece
  3.7 2.0 fusion.4
  5.6 0.0 copy-start.6
  5.6 1.8 pad_maximum_fusion.1
  7.5 0.0 copy-done.6
  7.5 1.0 copy.34.routes
  8.5 0.0 copy-start.5
  8.5 53.8 %shard_map.280 = (f32[8,1024]{1,0:T(8,128)}, f32[1024,128]{1,0:T(8,128)}, bf16[1024,768]{1,0:T(8,128)(2,1)}, bf16[1024,768]{1,0:T(8,128)(2,1)}, bf16[1024,768]{1...) custom-call(s32[1024,2]{1,0:T(8,128)} %copy.34.routes, ...), custom_call_target="tpu_custom_call" | custom-call | flops 7247757312 | bytes 25165824 | tf_op jit(solution)/shard_map/pallas_call | solution.py:1267
  62.3 0.0 copy-done.5
  62.3 0.2 copy.35
  62.5 1.9 fusion.1.shared_piece.piece
  64.4 1.2 constant_dynamic-slice_fusion.1
  65.6 0.0 copy-done
  65.6 0.2 copy.36
  65.8 1.1 pad_maximum_fusion.expert_piece
  66.9 80.3 %shard_map.281 = (bf16[1024,768]{1,0:T(8,128)(2,1)}, f32[1024,768]{1,0:T(8,128)}, f32[1024,768]{1,0:T(8,128)}, bf16[1024,768]{1,0:T(8,128)(2,1)}, f32[1024,128]{...) custom-call(s32[1,2]{1,0:T(1,128)} %starts.3, ...), custom_call_target="tpu_custom_call" | custom-call | flops 17716740096 | bytes 31457280 | tf_op jit(solution)/shard_map/pallas_call | solution.py:1296
  147.2 63.6 %shard_map.282 = (bf16[1024,768]{1,0:T(8,128)(2,1)}, bf16[1024,768]{1,0:T(8,128)(2,1)}, bf16[8,3,768,128]{3,2,1,0:T(8,128)(2,1)}, bf16[8,3,768,128]{3,2,1,0:T(8,...) custom-call(bf16[1024,768]{1,0:T(8,128)(2,1)} %get-tuple-element.96., ...), custom_call_target="tpu_custom_call", output_to_operand_aliasing={{7}: (8, {})} | custom-call | flops 28991029248 | bytes 31457280 | tf_op jit(solution)/shard_map/pallas_call | solution.py:1316
  210.8 72.8 %shard_map.283 = (bf16[576,768]{1,0:T(8,128)(2,1)}, bf16[576,768]{1,0:T(8,128)(2,1)}, bf16[592,768]{1,0:T(8,128)(2,1)}, bf16[592,768]{1,0:T(8,128)(2,1)}, bf16[8...) custom-call(f32[16,768]{1,0:T(8,128)} %get-tuple-element.88.ext, ...), custom_call_target="tpu_custom_call", output_to_operand_aliasing={{6}: (7, {})} | custom-call | flops 32614907904 | bytes 31457280 | tf_op jit(solution)/shard_map/pallas_call | solution.py:1330
  283.7 68.3 %shard_map.284 = (bf16[576,768]{1,0:T(8,128)(2,1)}, bf16[576,768]{1,0:T(8,128)(2,1)}, bf16[592,768]{1,0:T(8,128)(2,1)}, bf16[8,3,768,256]{3,2,1,0:T(8,128)(2,1)}...) custom-call(f32[16,768]{1,0:T(8,128)} %get-tuple-element.88.ext, ...), custom_call_target="tpu_custom_call" | custom-call | flops 32614907904 | bytes 31457280 | tf_op jit(solution)/shard_map/pallas_call | solution.py:1343
  352.0 172.4 %shard_map.285 = (f32[1024,768]{1,0:T(8,128)}, bf16[768,768]{1,0:T(8,128)(2,1)}, f32[16,768]{1,0:T(8,128)}, bf16[1024,768]{1,0:T(8,128)(2,1)}, bf16[1024,768]{1,...) custom-call(s32[1,2]{1,0:T(1,128)} %starts.3, ...), custom_call_target="tpu_custom_call" | custom-call | flops 38252052480 | bytes 41943040 | tf_op jit(solution)/shard_map/pallas_call | solution.py:1405
  524.4 72.5 %shard_map.286 = (f32[1024,768]{1,0:T(8,128)}, bf16[1024,768]{1,0:T(8,128)(2,1)}, f32[4,96,768]{2,1,0:T(8,128)}, f32[16,768]{1,0:T(8,128)}, bf16[2,3,768,128]{3,...) custom-call(bf16[1024,768]{1,0:T(8,128)(2,1)} %bitcast.50, ...), custom_call_target="tpu_custom_call" | custom-call | flops 10871635968 | bytes 41943040 | tf_op jit(solution)/shard_map/pallas_call | solution.py:1430
  596.9 0.0 copy-start.4
  596.9 8.3 %shard_map.287 = (f32[4,768,256]{2,1,0:T(8,128)}, f32[4,768,256]{2,1,0:T(8,128)}, f32[4,256,768]{2,1,0:T(8,128)}, f32[768,256]{1,0:T(8,128)}, f32[768,256]{1,0:T(8,128)}, /*index=5*/f32[256,768]{1,0:T(8,128)}) custom-call(bf16[3,768,256]{2,1,0:T(8,128)(2,1)} %get-tuple-element.145.expert_total.e0, bf16[3,768,256]{2,1,0:T(8,128)(2,1)} %get-tuple-element.151.e1, ...), custom_call_target="tpu_custom_call" | custom-call | bytes 18874368 | tf_op jit(solution)/shard_map/pallas_call | solution.py:1460
  605.2 0.0 copy-start.3
  605.2 0.0 copy-done.4
  605.2 1.0 slice_bitcast_fusion
  606.2 1.4 dynamic-slice_bitcast_fusion.1
  607.6 1.3 dynamic-slice_bitcast_fusion
  608.9 0.0 copy-done.3
  608.9 0.0 copy-start.2
  608.9 1.1 copy.42
  610.1 1.3 copy-done.2
  611.4 0.0 copy-start.1
  611.4 1.7 copy.43
  613.1 0.9 copy-done.1
  (4 shorter events, 0.1 us)
Async XLA Ops:
  0.6 64.9 %copy-start = (bf16[4,256,768]{2,1,0:T(8,128)(2,1)S(1)}, bf16[4,256,768]{2,1,0:T(8,128)(2,1)}, u32[]{:S(2)}) copy-start(bf16[4,256,768]{2,1,0:T(8,128)(2,1)} %param.29) | copy-start | bytes 4718596
  5.6 1.9 copy-start.6
  8.5 53.8 %copy-start.5 = (bf16[256,768]{1,0:T(8,128)(2,1)S(1)}, bf16[256,768]{1,0:T(8,128)(2,1)}, u32[]{:S(2)}) copy-start(bf16[256,768]{1,0:T(8,128)(2,1)} %param.32) | copy-start | bytes 1179652
  596.9 8.3 %copy-start.4 = (f32[4,96,768]{2,1,0:T(8,128)S(1)}, f32[4,96,768]{2,1,0:T(8,128)}, u32[]{:S(2)}) copy-start(f32[4,96,768]{2,1,0:T(8,128)} %get-tuple-element.150) | copy-start | bytes 3538948
  605.2 3.7 copy-start.3
  608.9 2.5 copy-start.2
  611.4 2.5 copy-start.1

commit v4 on v3

--- a/solution.py
+++ b/solution.py
@@ -199,6 +199,10 @@
     def got(self, event, like, cond=True):
         when(cond, self.copy(event, like, like, self.mate, self.shard).wait_recv)
 
+    def settle(self, event):
+        cond, source = self.open.pop(event)
+        when(cond, self.copy(event, source, source, self.mate, self.shard).wait_send)
+
     def close(self):
         for event, (cond, source) in self.open.items():
             when(cond, self.copy(event, source, source, self.mate, self.shard).wait_send)
@@ -226,9 +230,9 @@
 
 
 class Line:
-    def __init__(self, net, bank):
+    def __init__(self, net, bank, ways=4):
         self.net, self.bank = net, bank
-        self.events = {(way, k): net.event() for way in range(4) for k in range(-3, 4)}
+        self.events = {(way, k): net.event() for way in range(ways) for k in range(-3, 4)}
         self.spots = {0: (net.shard, True)}
         for k in (1, 2, 3):
             self.spots[k] = (lax.min(net.shard + 2 * k, 6 + net.x), net.z < 4 - k)
@@ -267,6 +271,70 @@
             spot, here = self.spots[k]
             self.net.got(self.events[2, k], self.bank.at[other, spot], here)
             self.net.got(self.events[3, k], self.bank.at[other, self.flips[k]], here)
+
+
+class Spread:
+    def __init__(self, net, piece, bank):
+        self.net, self.piece, self.bank = net, piece, bank
+        self.line = Line(net, bank, 8)
+        self.events, self.spots, self.flips = self.line.events, self.line.spots, self.line.flips
+        self.half = piece.shape[1] // 2
+        y = lax.div(net.rep, 2)
+        self.rows = [pl.ds(pl.multiple_of(n * self.half, 128), self.half) for n in (y, 1 - y)]
+        self.far = net.cousins[2]
+
+    def view(self, core, spot, rows):
+        return self.bank.at[core, spot, :, self.rows[rows], :]
+
+    def begin(self):
+        net = self.net
+        source = self.piece.at[:, self.rows[0], :]
+        target = self.view(net.core, net.shard, 0)
+        net.put(self.events[0, -1], source, target, net.rep, net.up, self.line.onward[0])
+        net.put(self.events[0, 1], source, target, net.rep, net.down, self.line.back[0])
+        net.put(self.events[1, 0], source, target, net.rep, net.across)
+        whole = self.bank.at[net.core, net.shard]
+        net.put(self.events[2, 0], self.piece, whole, net.mate, net.shard)
+
+    def hand(self, way, k, here, piece):
+        net = self.net
+        net.put(self.events[way + 4, k], piece, piece, self.far, net.shard, here)
+        net.put(self.events[way + 2, k], piece, piece, net.mate, net.shard, here)
+
+    def along(self, k):
+        net, (spot, here) = self.net, self.spots[k]
+        piece = self.view(net.core, spot, 0)
+        net.got(self.events[0, k], piece, here)
+        if -3 < k < 0:
+            net.put(self.events[0, k - 1], piece, piece, net.rep, net.up, self.line.onward[k])
+        if 0 < k < 3:
+            net.put(self.events[0, k + 1], piece, piece, net.rep, net.down, self.line.back[k])
+        net.put(self.events[1, k], piece, piece, net.rep, net.across, here)
+        self.hand(0, k, here, piece)
+
+    def over(self, k):
+        net, here = self.net, self.spots[k][1]
+        piece = self.view(net.core, self.flips[k], 0)
+        net.got(self.events[1, k], piece, here)
+        self.hand(1, k, here, piece)
+
+    def relay(self, way, k):
+        net, here = self.net, self.spots[k][1]
+        spot = self.spots[k][0] if way == 0 else self.flips[k]
+        piece = self.view(net.core, spot, 1)
+        net.got(self.events[way + 4, k], piece, here)
+        net.put(self.events[way + 6, k], piece, piece, net.mate, net.shard, here)
+
+    def finish(self):
+        net, other = self.net, 1 - self.net.core
+        net.got(self.events[2, 0], self.bank.at[other, net.shard])
+        for k in (0, 1, -1, 2, -2, 3, -3):
+            spot, here = self.spots[k]
+            if k:
+                net.got(self.events[2, k], self.view(other, spot, 0), here)
+                net.got(self.events[6, k], self.view(other, spot, 1), here)
+            net.got(self.events[3, k], self.view(other, self.flips[k], 0), here)
+            net.got(self.events[7, k], self.view(other, self.flips[k], 1), here)
 
 
 def exchange(net, sources, targets):
@@ -432,35 +500,49 @@
     bias, send, recv,
 ):
     net = Net(send, recv)
-    line = Line(net, shared_bank)
-    z_events = [net.event(), net.event()]
-    net.meet("line", [(net.mate, net.shard), (net.rep, net.across)])
-    line.spread(0, shared_piece)
+    spread = Spread(net, shared_piece, shared_bank)
+    events = [net.event() for _ in range(3)]
+    mine = expert_bank.at[net.shard]
+    net.meet("line", [(net.mate, net.shard), (net.rep, net.across), (spread.far, net.shard)])
+    spread.begin()
     fill_bias(starts, bias)
 
     def step(i):
-        @pl.when(i == 3)
+        @pl.when(i == 2)
         def _():
-            line.along(1)
-            line.along(-1)
-            line.over(0)
+            spread.along(1)
+            spread.along(-1)
+            spread.over(0)
+
+        @pl.when(i == 4)
+        def _():
+            spread.along(2)
+            spread.along(-2)
+            spread.over(1)
+            spread.over(-1)
+            spread.relay(1, 0)
+            spread.relay(0, 1)
+            spread.relay(0, -1)
 
     attend_pairs(q, k, v, attended, lse, bias, step)
-    line.along(2)
-    line.along(-2)
-    line.over(1)
-    line.over(-1)
-    mine = expert_bank.at[net.shard]
-    net.put(z_events[0], expert_piece, mine, net.rep, net.up, net.z < 3)
-    net.put(z_events[1], expert_piece, mine, net.rep, net.down, net.z > 0)
+    spread.along(3)
+    spread.along(-3)
+    net.put(events[0], expert_piece, mine, net.rep, net.up, net.z < 3)
+    net.put(events[1], expert_piece, mine, net.rep, net.down, net.z > 0)
+    spread.over(2)
+    spread.over(-2)
     middle_rows(net.rep, x, attended, wo, ext, rank, middle, normed, probs, (x0, x1, x2, x3))
-    line.along(3)
-    line.along(-3)
-    for step_k in (2, -2, 3, -3):
-        line.over(step_k)
-    line.finish()
-    net.got(z_events[0], mine, net.z > 0)
-    net.got(z_events[1], mine, net.z < 3)
+    spread.over(3)
+    spread.over(-3)
+    net.put(events[2], expert_piece, mine, net.rep, net.across)
+    for way, k_step in ((1, 1), (1, -1), (0, 2), (0, -2), (1, 2), (1, -2)):
+        spread.relay(way, k_step)
+    for way, k_step in ((0, 3), (0, -3), (1, 3), (1, -3)):
+        spread.relay(way, k_step)
+    spread.finish()
+    net.got(events[0], mine, net.z > 0)
+    net.got(events[1], mine, net.z < 3)
+    net.got(events[2], mine)
     net.close()
 
 
@@ -477,7 +559,10 @@
 CHUNK, CHUNKS = 512, 4
 
 
-def unit_bank(expert, ext, xs, cs, source, target, before, unit, outs, dxs, scratch, ready=None):
+def unit_bank(
+    expert, ext, xs, cs, source, target, before, unit, outs, dxs, scratch, ready=None,
+    emit=None, reclaim=None,
+):
     out_acc, dx_acc, gate, wbuf, dw_acc, dw_out, in_sems, out_sems = scratch[:8]
     routed = expert is not None
     blocks, rows = len(xs), xs[0].shape[0]
@@ -576,6 +661,9 @@
             for copy in stores(0, b):
                 copy.wait()
 
+        if reclaim is not None:
+            for now in (2, 3):
+                when(k == now, functools.partial(reclaim, now))
         if before is not None:
             for copy in loads(before, scratch[8], scratch[9], 0, b):
                 copy.wait()
@@ -590,6 +678,8 @@
             def _():
                 for copy in stores(now, now % 2):
                     copy.start()
+                if emit is not None:
+                    emit(now)
 
         return carry
 
@@ -634,10 +724,8 @@
     low, high = experts.at[net.down], experts.at[net.up]
     net.put(events[0], low, low, net.rep, net.up, (net.z > 0) & (net.z < 3))
     net.put(events[1], high, high, net.rep, net.down, (net.z > 0) & (net.z < 3))
-    mine = experts.at[net.shard]
-    net.put(events[2], expert_piece, mine, net.rep, net.across)
-    near = experts.at[net.place(1, 0)]
-    net.put(events[3], near, near, net.rep, net.across)
+    near, next_near = experts.at[net.place(1, 0)], experts.at[net.place(2, 0)]
+    net.put(events[2], near, near, net.rep, net.across)
     below = experts.at[lax.max(net.shard - 4, net.x)]
     above = experts.at[lax.min(net.shard + 4, 6 + net.x)]
 
@@ -657,35 +745,38 @@
     last_up, last_down = net.z == 2, net.z == 1
 
     def ready(k):
-        if k == 3:
+        if k == 2:
             net.got(events[0], below, from_below)
             net.got(events[1], above, from_above)
+            net.put(events[3], next_near, next_near, net.rep, net.across)
             net.put(events[4], below, below, net.rep, net.up, last_up)
             net.put(events[5], above, above, net.rep, net.down, last_down)
 
     unit_bank(None, None, [x], [c], source, target, None, 128, [out], [dx], scratch, ready)
     for event, like in arrivals:
         net.got(event, like)
-    net.got(events[2], mine)
-    net.got(events[3], mine)
-    net.got(events[4], mine, net.z == 3)
-    net.got(events[5], mine, net.z == 0)
+    net.got(events[2], near)
+    net.got(events[3], near)
+    net.got(events[4], near, net.z == 3)
+    net.got(events[5], near, net.z == 0)
     net.close()
 
 
 def far_kernel(
-    ext, xa, xb, ca, cb, expert_piece, shared_other, expert_in,
-    oa, ob, da, db, grads, shared_mate, experts,
-    send, recv, *scratch,
+    ext, xa, xb, ca, cb, expert_piece, shared_own, shared_other, expert_in,
+    oa, ob, da, db, grads, shared_mate, shared_x, experts,
+    part_a, part_b, part_sems, send, recv, *scratch,
 ):
     net = Net(send, recv)
-    events = [net.event() for _ in range(3)]
+    events = [net.event() for _ in range(6)]
     net.meet("none", [(net.rep, net.across), (net.mate, net.shard)])
-    net.put(events[2], shared_other, shared_mate, net.mate, net.shard)
-    for n in (2, 3):
-        piece = experts.at[net.place(n, 0)]
-        net.put(events[n - 2], piece, piece, net.rep, net.across)
+    last = experts.at[net.place(3, 0)]
+    net.put(events[0], last, last, net.rep, net.across)
+    net.put(events[1], shared_other, shared_mate, net.mate, net.shard)
     spots = [net.place(n // 2, n % 2) for n in range(8)]
+    sides = [net.cycle(d) + 1 - 2 * net.x for d in range(4)]
+    rows = [shared_x.at[lax.div(side, 2)] for side in sides]
+    pieces = [part_a.at[d] for d in range(4)]
 
     def source(n):
         return expert_piece if n == 0 else experts.at[spots[n]]
@@ -694,58 +785,75 @@
         return grads.at[spots[n]]
 
     def ready(k):
-        if k >= 2:
-            net.got(events[k - 2], experts.at[spots[2 * k + 1]])
+        if k == 1:
+            net.got(events[1], shared_mate)
+            fetch(
+                [shared_own.at[side] for side in sides] + [shared_mate.at[side] for side in sides],
+                [part_a.at[d] for d in range(4)] + [part_b.at[d] for d in range(4)],
+                part_sems,
+            )
+            for d in (2, 1, 3, 0):
+                part_a[d] = (part_a[d].astype(F32) + part_b[d].astype(F32)).astype(BF)
+                net.put(events[2 + d], pieces[d], rows[d], net.rep, net.across)
+        if k == 3:
+            net.got(events[0], last)
 
     unit_bank(
         net.rep, ext, [xa, xb], [ca, cb], source, target, None, 256, [oa, ob], [da, db],
         scratch, ready,
     )
-    net.got(events[2], shared_mate)
+    for d in range(4):
+        net.got(events[2 + d], rows[d])
     net.close()
 
 
 def near_kernel(
-    ext, xa, xb, ca, cb, expert_piece, experts, before, far_a, far_b, shared_own, shared_mate,
-    oa, ob, da, grads, back_a, back_b, back_c, shared_x,
-    db, part_a, part_b, part_sems, send, recv, *scratch,
+    ext, xa, xb, ca, cb, expert_piece, experts, before, far_a, far_b,
+    shared_own, shared_mate, shared_x,
+    oa, ob, da, shared_total, grads, back_a, back_b, back_c, expert_x, shared_z,
+    db, held, spare, sems, send, recv, *scratch,
 ):
     net = Net(send, recv)
-    events = [net.event() for _ in range(7)]
+    events = [net.event() for _ in range(5)]
+    shared = Reduce(net, [shared_own, shared_mate], shared_x, shared_z, held, spare, sems)
     peers = [(net.cousins[o], net.shard) for o in (1, 2, 3)]
-    net.meet("none", peers + [(net.rep, net.across)])
-    sides = [net.cycle(d) + 1 - 2 * net.x for d in range(4)]
-    rows = [lax.div(side, 2) for side in sides]
-    parts = []
-    for d in range(4):
-        parts.append((shared_own.at[sides[d]], part_a.at[d]))
-        parts.append((shared_mate.at[sides[d]], part_b.at[d]))
-    parts = [pltpu.make_async_copy(a, b, part_sems.at[i]) for i, (a, b) in enumerate(parts)]
-    for copy in parts:
-        copy.start()
+    net.meet("all", peers + [(net.rep, net.across)])
     net.put(events[0], far_a, back_a, net.cousins[2], net.shard)
     net.put(events[1], far_b, back_b, net.cousins[3], net.shard)
-    for copy in parts:
-        copy.wait()
     for d in (2, 1, 3, 0):
-        part_a[d] = (part_a[d].astype(F32) + part_b[d].astype(F32)).astype(BF)
-        net.put(events[3 + d], part_a.at[d], shared_x.at[rows[d]], net.rep, net.across)
-    spots = [net.place(n // 2, n % 2) for n in range(8)]
+        shared.add_across(d, False)
+    spots = [net.place(3 - n // 2, n % 2) for n in range(8)]
+    own_slot = 6
+    dw_out, halves = scratch[5], []
+    for b in range(2):
+        halves.append(dw_out.at[b, :, :, pl.ds(256, 256)])
+    targets = [expert_x.at[net.levels[3]], expert_x.at[net.levels[2]]]
 
     def source(n):
-        return expert_piece if n == 0 else experts.at[spots[n]]
+        return expert_piece if n == own_slot else experts.at[spots[n]]
+
+    def emit(now):
+        if now < 2:
+            net.put(events[3 + now], halves[now], targets[now], net.rep, net.across)
+
+    def reclaim(now):
+        half = halves[now - 2]
+        net.copy(events[1 + now], half, half, net.mate, net.shard).wait_send()
 
     unit_bank(
         net.rep, ext, [xa, xb], [ca, cb], source,
         lambda n: grads.at[spots[n]], lambda n: before.at[spots[n]],
-        256, [oa, ob], [da, db], scratch,
+        256, [oa, ob], [da, db], scratch, None, emit, reclaim,
     )
+    for n in range(2):
+        net.open.pop(events[3 + n])
     net.put(events[2], db, back_c, net.mate, net.shard)
+    shared.total(shared_total)
     net.got(events[0], back_a)
     net.got(events[1], back_b)
     net.got(events[2], back_c)
-    for d in range(4):
-        net.got(events[3 + d], shared_x.at[rows[d]])
+    for n in range(2):
+        net.got(events[3 + n], targets[n])
     net.close()
 
 
@@ -956,49 +1064,102 @@
 
     def settle(self):
         for event in self.z_events:
-            cond, source = self.net.open.pop(event)
-            self.net.copy(event, source, source, self.net.rep, self.net.shard).wait_send()
+            self.net.settle(event)
+
+
+class Chain:
+    def __init__(self, net, own, from_x, up_in, down_in, held, spare, sems):
+        self.net, self.own, self.from_x = net, own, from_x
+        self.up_in, self.down_in = up_in, down_in
+        self.held, self.spare, self.sems = held, spare, sems
+        self.events = {(way, d): net.event() for way in range(2) for d in (1, 2, 3)}
+        self.spots = [net.place(n, 0) for n in range(4)]
+        self.sends, self.gets = {}, {}
+        z = net.z
+        for d in (1, 2, 3):
+            self.sends[0, d] = (held.at[lax.min(z + d, 3)], z < 4 - d)
+            self.sends[1, d] = (held.at[lax.max(z - d, 0)], z > d - 1)
+            self.gets[0, d] = (lax.min(z + d - 1, 3), (z > 0) & (z < 5 - d))
+            self.gets[1, d] = (lax.max(z - d + 1, 0), (z < 3) & (z > d - 2))
+
+    def level(self, n):
+        to = self.net.levels[n]
+        far = self.from_x.at[to]
+        fetch([self.own.at[self.spots[n]], far], [self.held.at[to], self.spare.at[0]], self.sems)
+        self.held[to] = (self.held[to].astype(F32) + self.spare[0].astype(F32)).astype(BF)
+
+    def send(self, d):
+        net = self.net
+        for way, to, into in ((0, net.up, self.up_in), (1, net.down, self.down_in)):
+            source, here = self.sends[way, d]
+            net.put(self.events[way, d], source, into.at[d - 1], net.rep, to, here)
+
+    def take(self, d):
+        for way, into in ((0, self.up_in), (1, self.down_in)):
+            to, here = self.gets[way, d]
+
+            def add():
+                self.net.copy(
+                    self.events[way, d], into.at[d - 1], into.at[d - 1],
+                    self.net.mate, self.net.shard,
+                ).wait_recv()
+                fetch([into.at[d - 1]], [self.spare.at[0]], self.sems)
+                total = self.held[to].astype(F32) + self.spare[0].astype(F32)
+                self.held[to] = total.astype(BF)
+
+            when(here, add)
 
 
 def back_kernel(
     starts, slot, d0, d1, d2, d3, d_shared, probs, middle, normed, cot, ext, attended, wo,
     q, k, v, lse, cosine, sine,
-    o1, o2, o3, grads, shared_own, shared_mate, shared_x,
-    d_middle, grad_wo, grad_ext, dq, dk, dv, expert_total, shared_total,
-    r1, r2, r3, expert_x, expert_z, shared_z,
+    o1, o2, o3, grads, expert_x_in,
+    d_middle, grad_wo, grad_ext, dq, dk, dv, expert_total,
+    r1, r2, r3, up_in, down_in, expert_x,
     d_attended, branch, router_acc, gain_acc, bias, dk_acc, dv_acc,
-    held, spare, held_s, spare_s, sems, send, recv,
+    held, spare, sems, send, recv,
 ):
     net = Net(send, recv)
-    expert = Reduce(net, [grads], expert_x, expert_z, held, spare, sems)
-    shared = Reduce(net, [shared_own, shared_mate], shared_x, shared_z, held_s, spare_s, sems)
+    x_events = [net.event() for _ in range(2)]
+    chain = Chain(net, grads, expert_x, up_in, down_in, held, spare, sems)
     peers = [(net.cousins[o], net.shard) for o in (1, 2, 3)]
-    net.meet("all", peers + [(net.rep, net.across)])
-    expert.send_across()
+    net.meet("line", peers + [(net.rep, net.across)])
+    targets = [expert_x.at[net.levels[n]] for n in range(2)]
+    for n in (1, 0):
+        source = grads.at[net.place(n, 1)]
+        net.put(x_events[n], source, targets[n], net.rep, net.across)
     arrivals = exchange(net, (o1, o2, o3), (r1, r2, r3))
-    for d in (2, 1, 3, 0):
-        shared.add_across(d, False)
+    chain.level(3)
+    chain.send(3)
+    chain.level(2)
     combine_rows(
         slot, d0, d1, d2, d3, d_shared, probs, middle, normed, cot, ext, attended, wo,
         d_middle, d_attended, grad_wo, grad_ext, branch, router_acc, gain_acc,
     )
     fill_bias(starts, bias)
-    expert.add_across(2)
+    chain.take(3)
+    chain.send(2)
 
     def step(i):
-        @pl.when(i == 3)
+        @pl.when(i == 1)
         def _():
-            expert.add_across(1)
+            net.got(x_events[1], targets[1])
+            chain.level(1)
+
+        @pl.when(i == 4)
+        def _():
+            chain.take(2)
+            chain.send(1)
 
     back_pairs(
         q, k, v, d_attended, attended, lse, cosine, sine, dq, dk, dv, bias, dk_acc, dv_acc, step
     )
-    shared.total(shared_total)
-    expert.add_across(3)
-    expert.add_across(0)
+    net.got(x_events[0], targets[0])
+    chain.level(0)
     for event, like in arrivals:
         net.got(event, like)
-    expert.total(expert_total)
+    chain.take(1)
+    expert_total[...] = held[net.z]
     net.close()
 
 
@@ -1298,7 +1459,7 @@
             outs + [shape((2, SLOTS) + my_half.shape), shape((SLOTS,) + expert_pack.shape)],
             [SMEM] + [VMEM] * 7 + [ANY] * 2,
             [VMEM] * 9 + [ANY] * 2,
-            [bias, pltpu.SemaphoreType.DMA((30,)), pltpu.SemaphoreType.DMA((30,))],
+            [bias, pltpu.SemaphoreType.DMA((59,)), pltpu.SemaphoreType.DMA((59,))],
             flops=work,
             moved=30 * 2**20,
             group=1,
@@ -1327,31 +1488,40 @@
         )(normed, cot, my_half, shared_bank, *x_out[1:], expert_pack, expert_bank)
         x_in = [x_out[0], y1, y2, y3]
         bank = shape(expert_bank.shape)
-        far_a, far_b, da, db, before, shared_mate, expert_bank = call(
+        half_x = (4,) + my_half.shape
+        far_a, far_b, da, db, before, shared_mate, shared_x, expert_bank = call(
             far_kernel,
-            [rows_out] * 2 + [rows_back] * 2 + [bank, half_grads, bank],
-            [VMEM] * 5 + [ANY] * 3,
-            [VMEM] * 4 + [ANY] * 3,
-            [pltpu.SemaphoreType.DMA((3,)), pltpu.SemaphoreType.DMA((3,))]
+            [rows_out] * 2 + [rows_back] * 2 + [bank, half_grads, shape(half_x), bank],
+            [VMEM] * 5 + [ANY] * 4,
+            [VMEM] * 4 + [ANY] * 4,
+            [
+                pltpu.VMEM(half_x, BF),
+                pltpu.VMEM(half_x, BF),
+                pltpu.SemaphoreType.DMA((8,)),
+                pltpu.SemaphoreType.DMA((6,)),
+                pltpu.SemaphoreType.DMA((6,)),
+            ]
             + unit_scratch(2, CAP, 16, width, 2, False),
             flops=36 * CAP * width * CHUNK * CHUNKS,
             moved=30 * 2**20,
             group=3,
-            alias={7: 6},
-        )(ext, *x_in[2:], *cot_in[2:], expert_pack, grads_other, expert_bank)
-        half_x = (4,) + my_half.shape
-        near_a, near_b, d0, grads, d2, d3, d1, shared_x = call(
+            alias={8: 7},
+        )(ext, *x_in[2:], *cot_in[2:], expert_pack, grads_own, grads_other, expert_bank)
+        bank_x, bank_z = (4,) + expert_pack.shape, (3,) + expert_pack.shape
+        half_z = (3,) + my_half.shape
+        near_a, near_b, d0, shared_total, grads, d2, d3, d1, expert_x, _ = call(
             near_kernel,
-            [rows_out] * 2 + [rows_back, bank] + [rows_back] * 3 + [shape(half_x)],
-            [VMEM] * 5 + [ANY] * 7,
-            [VMEM] * 3 + [ANY] * 5,
+            [rows_out] * 2 + [rows_back, shape(my_half.shape), bank] + [rows_back] * 3
+            + [shape(bank_x), shape(half_z)],
+            [VMEM] * 5 + [ANY] * 8,
+            [VMEM] * 4 + [ANY] * 6,
             [
                 pltpu.VMEM((CAP + 16, width), BF),
                 pltpu.VMEM(half_x, BF),
-                pltpu.VMEM(half_x, BF),
-                pltpu.SemaphoreType.DMA((8,)),
-                pltpu.SemaphoreType.DMA((7,)),
-                pltpu.SemaphoreType.DMA((7,)),
+                pltpu.VMEM((2,) + my_half.shape, BF),
+                pltpu.SemaphoreType.DMA((3,)),
+                pltpu.SemaphoreType.DMA((12,)),
+                pltpu.SemaphoreType.DMA((12,)),
             ]
             + unit_scratch(2, CAP, 16, width, 2, True),
             flops=36 * CAP * width * CHUNK * CHUNKS,
@@ -1359,7 +1529,7 @@
             group=4,
         )(
             ext, *x_in[:2], *cot_in[:2], expert_pack, expert_bank, before, da, db,
-            grads_own, shared_mate,
+            grads_own, shared_mate, shared_x,
         )
         d_rows = [d0, d1, d2, d3]
     else:
@@ -1400,30 +1570,27 @@
     ]
     work = 2 * tokens * width * (2 * width + 4 * CAP) + 40 * tokens * tokens * width
     if ringed:
-        bank_x, bank_z = (4,) + expert_pack.shape, (3,) + expert_pack.shape
-        half_z = (3,) + my_half.shape
-        d_middle, grad_wo, grad_ext, dq, dk, dv, expert_total, shared_total, *back = call(
+        d_middle, grad_wo, grad_ext, dq, dk, dv, expert_total, *back = call(
             back_kernel,
             outs
-            + [shape(expert_pack.shape), shape(my_half.shape)]
+            + [shape(expert_pack.shape)]
             + [rows_out] * 3
-            + [shape(bank_x), shape(bank_z), shape(half_z)],
-            specs + [ANY] * 7,
-            [VMEM] * 8 + [ANY] * 6,
+            + [shape(bank_z), shape(bank_z), shape(bank_x)],
+            specs + [ANY] * 5,
+            [VMEM] * 7 + [ANY] * 6,
             scratch
             + [
                 pltpu.VMEM(bank_x, BF),
                 pltpu.VMEM((1,) + expert_pack.shape, BF),
-                pltpu.VMEM(half_x, BF),
-                pltpu.VMEM((2,) + my_half.shape, BF),
-                pltpu.SemaphoreType.DMA((3,)),
-                pltpu.SemaphoreType.DMA((17,)),
-                pltpu.SemaphoreType.DMA((17,)),
+                pltpu.SemaphoreType.DMA((2,)),
+                pltpu.SemaphoreType.DMA((11,)),
+                pltpu.SemaphoreType.DMA((11,)),
             ],
             flops=work,
             moved=40 * 2**20,
             group=5,
-        )(*operands, near_b, far_a, far_b, grads, grads_own, shared_mate, shared_x)
+            alias={24: 12},
+        )(*operands, near_b, far_a, far_b, grads, expert_x)
         operands = (x, ext, dq, dk, dv, wq, wk, wv, d_middle, grad_wo, grad_ext)
         operands += (slot, near_a, *back[:3], shared_out, probs, middle)
         strip = (2, width // SLOTS, width)

time: 623 us -> 578 us (0.928)
  Pallas kernels: 592 us -> 547 us
    pallas_call x3, Pallas kernels: 314 us -> 266 us  [the longest x1 102 us: body(): call(back_kernel, outs + [shape(expert_pack.shape)] + [rows_out] * 3 + [s...]
where the time goes in v4:
time: 578 us; the launch traced here: 570 us
  Pallas kernels  547 us (95%)
  local copies, waits for them, and re-layouts  11.5 us (2%)
  other arithmetic  9.62 us (2%)
    pallas_call x1, Pallas kernels, body(): call(back_kernel, outs + [shape(expert_pack.shape)] + [rows_out] * 3 + [s...  102 us
    pallas_call x1, Pallas kernels, body(): call(far_kernel, [rows_out] * 2 + [rows_back] * 2 + [bank, half_grads, sh...  83.1 us
    pallas_call x1, Pallas kernels, body(): call(near_kernel, [rows_out] * 2 + [rows_back, shape(my_half.shape), bank...  80.4 us
    pallas_call x1, Pallas kernels, body(): call(forward_kernel, outs + [shape((2, SLOTS) + my_half.shape), shape((SL...  80.3 us
    pallas_call x1, Pallas kernels, body(): call(tail_kernel, [wide, token_f, shape((4, rows, width), F32), shape((16...  72.6 us
    pallas_call x1, Pallas kernels, body(): call(shared_kernel, [token_f] * 2 + [half_grads] * 2 + packed[:3] + [shap...  66.6 us
    pallas_call x1, Pallas kernels, body(): call(head_kernel, outs + [square] * 4 + [shape((16, width), F32)] + packe...  53.7 us

profile of v4, /device:TPU:0, one launch (start us, length us, event | category | flops | bytes accessed | tf_op | source)
XLA Modules:
  0.0 569.6 jit_solution(5589167583311041704)
XLA Ops:
  0.6 0.0 copy-start
  0.7 0.8 fusion.9
  1.5 0.2 dynamic_update_slice.3
  1.7 1.9 maximum_select_fusion.piece
  3.7 2.0 fusion.4
  5.6 0.0 copy-start.6
  5.6 1.8 pad_maximum_fusion.1
  7.5 0.0 copy-done.6
  7.5 1.0 copy.35.routes
  8.5 0.0 copy-start.5
  8.5 53.7 %shard_map.280 = (f32[8,1024]{1,0:T(8,128)}, f32[1024,128]{1,0:T(8,128)}, bf16[1024,768]{1,0:T(8,128)(2,1)}, bf16[1024,768]{1,0:T(8,128)(2,1)}, bf16[1024,768]{1...) custom-call(s32[1024,2]{1,0:T(8,128)} %copy.35.routes, ...), custom_call_target="tpu_custom_call" | custom-call | flops 7247757312 | bytes 25165824 | tf_op jit(solution)/shard_map/pallas_call | solution.py:1428
  62.3 0.0 copy-done.5
  62.3 0.2 copy.36
  62.4 1.9 fusion.1.shared_piece.piece
  64.3 1.2 constant_dynamic-slice_fusion.1
  65.5 0.0 copy-done
  65.6 0.2 copy.37
  65.7 1.1 pad_maximum_fusion.expert_piece
  66.9 80.3 %shard_map.281 = (bf16[1024,768]{1,0:T(8,128)(2,1)}, f32[1024,768]{1,0:T(8,128)}, f32[1024,768]{1,0:T(8,128)}, bf16[1024,768]{1,0:T(8,128)(2,1)}, f32[1024,128]{...) custom-call(s32[1,2]{1,0:T(1,128)} %starts.3, ...), custom_call_target="tpu_custom_call" | custom-call | flops 17716740096 | bytes 31457280 | tf_op jit(solution)/shard_map/pallas_call | solution.py:1457
  147.2 66.6 %shard_map.282 = (bf16[1024,768]{1,0:T(8,128)(2,1)}, bf16[1024,768]{1,0:T(8,128)(2,1)}, bf16[8,3,768,128]{3,2,1,0:T(8,128)(2,1)}, bf16[8,3,768,128]{3,2,1,0:T(8,...) custom-call(bf16[1024,768]{1,0:T(8,128)(2,1)} %get-tuple-element.97., ...), custom_call_target="tpu_custom_call", output_to_operand_aliasing={{7}: (8, {})} | custom-call | flops 28991029248 | bytes 31457280 | tf_op jit(solution)/shard_map/pallas_call | solution.py:1477
  213.8 83.1 %shard_map.283 = (bf16[576,768]{1,0:T(8,128)(2,1)}, bf16[576,768]{1,0:T(8,128)(2,1)}, bf16[592,768]{1,0:T(8,128)(2,1)}, bf16[592,768]{1,0:T(8,128)(2,1)}, bf16[8...) custom-call(f32[16,768]{1,0:T(8,128)} %get-tuple-element.89.ext, ...), custom_call_target="tpu_custom_call", output_to_operand_aliasing={{7}: (8, {})} | custom-call | flops 32614907904 | bytes 31457280 | tf_op jit(solution)/shard_map/pallas_call | solution.py:1492
  296.9 80.4 %shard_map.284 = (bf16[576,768]{1,0:T(8,128)(2,1)}, bf16[576,768]{1,0:T(8,128)(2,1)}, bf16[592,768]{1,0:T(8,128)(2,1)}, bf16[3,768,128]{2,1,0:T(8,128)(2,1)}, bf...) custom-call(f32[16,768]{1,0:T(8,128)} %get-tuple-element.89.ext, ...), custom_call_target="tpu_custom_call" | custom-call | flops 32614907904 | bytes 31457280 | tf_op jit(solution)/shard_map/pallas_call | solution.py:1512
  377.3 102.4 %shard_map.285 = (f32[1024,768]{1,0:T(8,128)}, bf16[768,768]{1,0:T(8,128)(2,1)}, f32[16,768]{1,0:T(8,128)}, bf16[1024,768]{1,0:T(8,128)(2,1)}, bf16[1024,768]{1,...) custom-call(s32[1,2]{1,0:T(1,128)} %starts.3, ...), custom_call_target="tpu_custom_call", output_to_operand_aliasing={{12}: (24, {})} | custom-call | flops 38252052480 | bytes 41943040 | tf_op jit(solution)/shard_map/pallas_call | solution.py:1573
  479.7 72.6 %shard_map.286 = (f32[1024,768]{1,0:T(8,128)}, bf16[1024,768]{1,0:T(8,128)(2,1)}, f32[4,96,768]{2,1,0:T(8,128)}, f32[16,768]{1,0:T(8,128)}, bf16[2,3,768,128]{3,...) custom-call(bf16[1024,768]{1,0:T(8,128)(2,1)} %bitcast.50, ...), custom_call_target="tpu_custom_call" | custom-call | flops 10871635968 | bytes 41943040 | tf_op jit(solution)/shard_map/pallas_call | solution.py:1597
  552.4 0.0 copy-start.4
  552.4 8.3 %shard_map.287 = (f32[4,768,256]{2,1,0:T(8,128)}, f32[4,768,256]{2,1,0:T(8,128)}, f32[4,256,768]{2,1,0:T(8,128)}, f32[768,256]{1,0:T(8,128)}, f32[768,256]{1,0:T(8,128)}, /*index=5*/f32[256,768]{1,0:T(8,128)}) custom-call(bf16[3,768,256]{2,1,0:T(8,128)(2,1)} %get-tuple-element.147.expert_total.e0, bf16[3,768,256]{2,1,0:T(8,128)(2,1)} %get-tuple-element.153.e1, ...), custom_call_target="tpu_custom_call" | custom-call | bytes 18874368 | tf_op jit(solution)/shard_map/pallas_call | solution.py:1627
  560.6 0.0 copy-start.3
  560.6 0.0 copy-done.4
  560.6 1.0 slice_bitcast_fusion
  561.7 1.4 dynamic-slice_bitcast_fusion.1
  563.0 1.3 dynamic-slice_bitcast_fusion
  564.4 0.0 copy-done.3
  564.4 0.0 copy-start.2
  564.4 1.1 copy.44
  565.5 1.3 copy-done.2
  566.8 0.0 copy-start.1
  566.8 1.7 copy.45
  568.5 0.9 copy-done.1
  (4 shorter events, 0.1 us)
Async XLA Ops:
  0.6 64.9 %copy-start = (bf16[4,256,768]{2,1,0:T(8,128)(2,1)S(1)}, bf16[4,256,768]{2,1,0:T(8,128)(2,1)}, u32[]{:S(2)}) copy-start(bf16[4,256,768]{2,1,0:T(8,128)(2,1)} %param.29) | copy-start | bytes 4718596
  5.6 1.9 copy-start.6
  8.5 53.7 %copy-start.5 = (bf16[256,768]{1,0:T(8,128)(2,1)S(1)}, bf16[256,768]{1,0:T(8,128)(2,1)}, u32[]{:S(2)}) copy-start(bf16[256,768]{1,0:T(8,128)(2,1)} %param.32) | copy-start | bytes 1179652
  552.4 8.3 %copy-start.4 = (f32[4,96,768]{2,1,0:T(8,128)S(1)}, f32[4,96,768]{2,1,0:T(8,128)}, u32[]{:S(2)}) copy-start(f32[4,96,768]{2,1,0:T(8,128)} %get-tuple-element.152) | copy-start | bytes 3538948
  560.6 3.7 copy-start.3
  564.4 2.5 copy-start.2
  566.8 2.5 copy-start.1

commit v5 on v4

--- a/solution.py
+++ b/solution.py
@@ -112,12 +112,15 @@
     slot_out[...] = jnp.where(lane < 64, slot_one, slot_two)
 
 
+def pack_row(rep, rank, source, o, out):
+    row = rank[pl.ds(sibling(rep, o), 1), :]
+    pick = ones_where(iota((CAP, source.shape[0]), 0).astype(F32) == row)
+    out[...] = nn(pick, source[...]).astype(BF)
+
+
 def pack_rows(rep, rank, source, packed):
-    tokens = source.shape[0]
     for o, out in enumerate(packed):
-        row = rank[pl.ds(sibling(rep, o), 1), :]
-        pick = ones_where(iota((CAP, tokens), 0).astype(F32) == row)
-        out[...] = nn(pick, source[...]).astype(BF)
+        pack_row(rep, rank, source, o, out)
 
 
 def qkv_rows(x, ext, cosine, sine, wq, wk, wv, q, k, v):
@@ -359,8 +362,12 @@
     own = pltpu.make_async_copy(piece, bank.at[net.core, net.shard], own_sem)
     own.start()
     route_slots(net.rep, routes, routes_t, rank, slot)
-    pack_rows(net.rep, rank, cot, [c0] + [packed.at[o] for o in range(3)])
-    arrivals = exchange(net, [packed.at[o] for o in range(3)], (c1, c2, c3))
+    events = [net.event() for _ in range(3)]
+    for o, far in ((2, c2), (3, c3), (1, c1)):
+        pack_row(net.rep, rank, cot, o, packed.at[o - 1])
+        net.put(events[o - 1], packed.at[o - 1], far, net.cousins[o], net.shard)
+    arrivals = [(events[0], c1), (events[1], c2), (events[2], c3)]
+    pack_row(net.rep, rank, cot, 0, c0)
     line.along(1)
     line.along(-1)
     line.over(0)
@@ -503,18 +510,19 @@
     spread = Spread(net, shared_piece, shared_bank)
     events = [net.event() for _ in range(3)]
     mine = expert_bank.at[net.shard]
+    more_up, more_down = net.z < 3, net.z > 0
     net.meet("line", [(net.mate, net.shard), (net.rep, net.across), (spread.far, net.shard)])
     spread.begin()
     fill_bias(starts, bias)
 
     def step(i):
-        @pl.when(i == 2)
+        @pl.when(i == 1)
         def _():
             spread.along(1)
             spread.along(-1)
             spread.over(0)
 
-        @pl.when(i == 4)
+        @pl.when(i == 3)
         def _():
             spread.along(2)
             spread.along(-2)
@@ -524,17 +532,20 @@
             spread.relay(0, 1)
             spread.relay(0, -1)
 
+        @pl.when(i == 5)
+        def _():
+            spread.along(3)
+            spread.along(-3)
+            net.put(events[0], expert_piece, mine, net.rep, net.up, more_up)
+            net.put(events[1], expert_piece, mine, net.rep, net.down, more_down)
+            net.put(events[2], expert_piece, mine, net.rep, net.across)
+            spread.over(2)
+            spread.over(-2)
+
     attend_pairs(q, k, v, attended, lse, bias, step)
-    spread.along(3)
-    spread.along(-3)
-    net.put(events[0], expert_piece, mine, net.rep, net.up, net.z < 3)
-    net.put(events[1], expert_piece, mine, net.rep, net.down, net.z > 0)
-    spread.over(2)
-    spread.over(-2)
-    middle_rows(net.rep, x, attended, wo, ext, rank, middle, normed, probs, (x0, x1, x2, x3))
     spread.over(3)
     spread.over(-3)
-    net.put(events[2], expert_piece, mine, net.rep, net.across)
+    middle_rows(net.rep, x, attended, wo, ext, rank, middle, normed, probs, (x0, x1, x2, x3))
     for way, k_step in ((1, 1), (1, -1), (0, 2), (0, -2), (1, 2), (1, -2)):
         spread.relay(way, k_step)
     for way, k_step in ((0, 3), (0, -3), (1, 3), (1, -3)):
@@ -764,19 +775,24 @@
 
 def far_kernel(
     ext, xa, xb, ca, cb, expert_piece, shared_own, shared_other, expert_in,
-    oa, ob, da, db, grads, shared_mate, shared_x, experts,
+    oa, ob, da, db, grads, shared_mate, shared_keep, shared_y, experts,
     part_a, part_b, part_sems, send, recv, *scratch,
 ):
     net = Net(send, recv)
-    events = [net.event() for _ in range(6)]
-    net.meet("none", [(net.rep, net.across), (net.mate, net.shard)])
+    events = [net.event() for _ in range(10)]
+    far = net.cousins[2]
+    net.meet("none", [(net.rep, net.across), (net.mate, net.shard), (far, net.shard)])
     last = experts.at[net.place(3, 0)]
     net.put(events[0], last, last, net.rep, net.across)
     net.put(events[1], shared_other, shared_mate, net.mate, net.shard)
+    own = pltpu.make_async_copy(shared_own, part_a, part_sems.at[0])
+    mate = pltpu.make_async_copy(shared_mate, part_b, part_sems.at[1])
+    own.start()
     spots = [net.place(n // 2, n % 2) for n in range(8)]
-    sides = [net.cycle(d) + 1 - 2 * net.x for d in range(4)]
-    rows = [shared_x.at[lax.div(side, 2)] for side in sides]
-    pieces = [part_a.at[d] for d in range(4)]
+    y, quarter = lax.div(net.rep, 2), part_a.shape[2] // 2
+    rows = [pl.ds(pl.multiple_of(n * quarter, 128), quarter) for n in (y, 1 - y)]
+    keep = pltpu.make_async_copy(part_a.at[:, :, rows[0], :], shared_keep, part_sems.at[2])
+    away = [part_a.at[j, :, rows[1], :] for j in range(SLOTS)]
 
     def source(n):
         return expert_piece if n == 0 else experts.at[spots[n]]
@@ -787,14 +803,18 @@
     def ready(k):
         if k == 1:
             net.got(events[1], shared_mate)
-            fetch(
-                [shared_own.at[side] for side in sides] + [shared_mate.at[side] for side in sides],
-                [part_a.at[d] for d in range(4)] + [part_b.at[d] for d in range(4)],
-                part_sems,
-            )
-            for d in (2, 1, 3, 0):
-                part_a[d] = (part_a[d].astype(F32) + part_b[d].astype(F32)).astype(BF)
-                net.put(events[2 + d], pieces[d], rows[d], net.rep, net.across)
+            mate.start()
+            own.wait()
+            mate.wait()
+
+            def add(j, carry):
+                part_a[j] = (part_a[j].astype(F32) + part_b[j].astype(F32)).astype(BF)
+                return carry
+
+            lax.fori_loop(0, SLOTS, add, 0)
+            for j in range(SLOTS):
+                net.put(events[2 + j], away[j], shared_y.at[j], far, net.shard)
+            keep.start()
         if k == 3:
             net.got(events[0], last)
 
@@ -802,58 +822,85 @@
         net.rep, ext, [xa, xb], [ca, cb], source, target, None, 256, [oa, ob], [da, db],
         scratch, ready,
     )
-    for d in range(4):
-        net.got(events[2 + d], rows[d])
+    keep.wait()
+    for j in range(SLOTS):
+        net.got(events[2 + j], shared_y.at[j])
     net.close()
 
 
 def near_kernel(
     ext, xa, xb, ca, cb, expert_piece, experts, before, far_a, far_b,
-    shared_own, shared_mate, shared_x,
-    oa, ob, da, shared_total, grads, back_a, back_b, back_c, expert_x, shared_z,
-    db, held, spare, sems, send, recv, *scratch,
+    shared_keep, shared_y,
+    oa, ob, da, shared_total, grads, back_a, back_b, back_c, expert_x,
+    db, part_a, part_b, from_x, from_z, sems, send, recv, *scratch,
 ):
     net = Net(send, recv)
-    events = [net.event() for _ in range(5)]
-    shared = Reduce(net, [shared_own, shared_mate], shared_x, shared_z, held, spare, sems)
+    events = [net.event() for _ in range(4)]
+    x_events = [net.event() for _ in range(4)]
+    z_events = [net.event() for _ in range(3)]
     peers = [(net.cousins[o], net.shard) for o in (1, 2, 3)]
+    one = pltpu.make_async_copy(shared_keep, part_a, sems.at[0])
+    two = pltpu.make_async_copy(shared_y, part_b, sems.at[1])
+    one.start()
+    two.start()
     net.meet("all", peers + [(net.rep, net.across)])
     net.put(events[0], far_a, back_a, net.cousins[2], net.shard)
     net.put(events[1], far_b, back_b, net.cousins[3], net.shard)
+    one.wait()
+    two.wait()
+
+    def add(j, carry):
+        part_a[j] = (part_a[j].astype(F32) + part_b[j].astype(F32)).astype(BF)
+        return carry
+
+    lax.fori_loop(0, SLOTS, add, 0)
+    mine = [net.cycle(d) for d in range(4)]
+    theirs = [spot + 1 - 2 * net.x for spot in mine]
     for d in (2, 1, 3, 0):
-        shared.add_across(d, False)
+        net.put(x_events[d], part_a.at[theirs[d]], from_x.at[d], net.rep, net.across)
+    pieces, lands = [part_a.at[spot] for spot in mine], [from_x.at[d] for d in range(4)]
+    ends = [from_z.at[d] for d in range(3)]
     spots = [net.place(3 - n // 2, n % 2) for n in range(8)]
     own_slot = 6
-    dw_out, halves = scratch[5], []
-    for b in range(2):
-        halves.append(dw_out.at[b, :, :, pl.ds(256, 256)])
-    targets = [expert_x.at[net.levels[3]], expert_x.at[net.levels[2]]]
+    half = scratch[5].at[0, :, :, pl.ds(256, 256)]
+    target = expert_x.at[net.levels[3]]
 
     def source(n):
         return expert_piece if n == own_slot else experts.at[spots[n]]
 
+    def ready(k):
+        if k == 2:
+            for d in (2, 1, 3, 0):
+                net.got(x_events[d], lands[d])
+                total = part_a[mine[d]].astype(F32) + from_x[d].astype(F32)
+                part_a[mine[d]] = total.astype(BF)
+                if d:
+                    net.put(z_events[d - 1], pieces[d], ends[d - 1], net.rep, mine[d])
+
     def emit(now):
-        if now < 2:
-            net.put(events[3 + now], halves[now], targets[now], net.rep, net.across)
+        if now == 0:
+            net.put(events[3], half, target, net.rep, net.across)
 
     def reclaim(now):
-        half = halves[now - 2]
-        net.copy(events[1 + now], half, half, net.mate, net.shard).wait_send()
+        if now == 2:
+            net.copy(events[3], half, half, net.mate, net.shard).wait_send()
 
     unit_bank(
         net.rep, ext, [xa, xb], [ca, cb], source,
         lambda n: grads.at[spots[n]], lambda n: before.at[spots[n]],
-        256, [oa, ob], [da, db], scratch, None, emit, reclaim,
+        256, [oa, ob], [da, db], scratch, ready, emit, reclaim,
     )
-    for n in range(2):
-        net.open.pop(events[3 + n])
+    net.open.pop(events[3])
     net.put(events[2], db, back_c, net.mate, net.shard)
-    shared.total(shared_total)
+    total = part_a[mine[0]].astype(F32)
+    for d in (1, 2, 3):
+        net.got(z_events[d - 1], ends[d - 1])
+        total = total + from_z[d - 1].astype(F32)
+    shared_total[...] = total.astype(BF)
     net.got(events[0], back_a)
     net.got(events[1], back_b)
     net.got(events[2], back_c)
-    for n in range(2):
-        net.got(events[3 + n], targets[n])
+    net.got(events[3], target)
     net.close()
 
 
@@ -1018,55 +1065,6 @@
         copy.wait()
 
 
-class Reduce:
-    def __init__(self, net, own, from_x, from_z, held, spare, sems):
-        self.net, self.own, self.from_x, self.from_z = net, own, from_x, from_z
-        self.held, self.spare, self.sems = held, spare, sems
-        self.x_events = [net.event() for _ in range(4)]
-        self.z_events = [net.event() for _ in range(3)]
-        self.spots = [net.cycle(d) for d in range(4)]
-        self.levels = [lax.div(spot, 2) for spot in self.spots]
-        self.pieces = [held.at[d] for d in range(4)]
-
-    def send_across(self):
-        net = self.net
-        for d in (2, 1, 3, 0):
-            source = self.own[0].at[self.spots[d] + 1 - 2 * net.x]
-            target = self.from_x.at[self.levels[d]]
-            net.put(self.x_events[d], source, target, net.rep, net.across)
-
-    def add_across(self, d, wait=True):
-        net = self.net
-        far = self.from_x.at[self.levels[d]]
-        if wait:
-            net.got(self.x_events[d], far)
-        sources = [own.at[self.spots[d]] for own in self.own] + [far]
-        targets = [self.held.at[d]] + [self.spare.at[i] for i in range(len(self.own))]
-        fetch(sources, targets, self.sems)
-        total = self.held[d].astype(F32)
-        for i in range(len(self.own)):
-            total = total + self.spare[i].astype(F32)
-        self.held[d] = total.astype(BF)
-        if d:
-            target = self.from_z.at[d - 1]
-            net.put(self.z_events[d - 1], self.pieces[d], target, net.rep, self.spots[d])
-
-    def total(self, out):
-        for d in (1, 2, 3):
-            self.net.got(self.z_events[d - 1], self.from_z.at[d - 1])
-        targets = [self.held.at[d] for d in (1, 2, 3)]
-        self.settle()
-        fetch([self.from_z.at[d] for d in range(3)], targets, self.sems)
-        total = self.held[0].astype(F32)
-        for d in (1, 2, 3):
-            total = total + self.held[d].astype(F32)
-        out[...] = total.astype(BF)
-
-    def settle(self):
-        for event in self.z_events:
-            self.net.settle(event)
-
-
 class Chain:
     def __init__(self, net, own, from_x, up_in, down_in, held, spare, sems):
         self.net, self.own, self.from_x = net, own, from_x
@@ -1112,33 +1110,40 @@
 
 def back_kernel(
     starts, slot, d0, d1, d2, d3, d_shared, probs, middle, normed, cot, ext, attended, wo,
-    q, k, v, lse, cosine, sine,
-    o1, o2, o3, grads, expert_x_in,
+    cosine, sine,
+    q_in, k_in, v_in, lse_in, o1, o2, o3, grads, expert_x_in,
     d_middle, grad_wo, grad_ext, dq, dk, dv, expert_total,
     r1, r2, r3, up_in, down_in, expert_x,
     d_attended, branch, router_acc, gain_acc, bias, dk_acc, dv_acc,
-    held, spare, sems, send, recv,
+    q, k, v, lse, held, spare, sems, load_sems, send, recv,
 ):
     net = Net(send, recv)
-    x_events = [net.event() for _ in range(2)]
+    x_events = [net.event() for _ in range(3)]
     chain = Chain(net, grads, expert_x, up_in, down_in, held, spare, sems)
     peers = [(net.cousins[o], net.shard) for o in (1, 2, 3)]
     net.meet("line", peers + [(net.rep, net.across)])
-    targets = [expert_x.at[net.levels[n]] for n in range(2)]
-    for n in (1, 0):
+    targets = [expert_x.at[net.levels[n]] for n in range(3)]
+    pairs = ((q_in, q), (k_in, k), (v_in, v), (lse_in, lse))
+    loads = [pltpu.make_async_copy(a, b, load_sems.at[i]) for i, (a, b) in enumerate(pairs)]
+    for n in (2, 1, 0):
         source = grads.at[net.place(n, 1)]
         net.put(x_events[n], source, targets[n], net.rep, net.across)
     arrivals = exchange(net, (o1, o2, o3), (r1, r2, r3))
     chain.level(3)
     chain.send(3)
-    chain.level(2)
+    for copy in loads:
+        copy.start()
     combine_rows(
         slot, d0, d1, d2, d3, d_shared, probs, middle, normed, cot, ext, attended, wo,
         d_middle, d_attended, grad_wo, grad_ext, branch, router_acc, gain_acc,
     )
     fill_bias(starts, bias)
+    net.got(x_events[2], targets[2])
+    chain.level(2)
     chain.take(3)
     chain.send(2)
+    for copy in loads:
+        copy.wait()
 
     def step(i):
         @pl.when(i == 1)
@@ -1214,17 +1219,19 @@
 
 
 def tail_kernel(
-    x, ext, dq, dk, dv, wq, wk, wv, d_middle, grad_wo, grad_ext,
-    slot, o0, o1, o2, o3, shared_out, probs, middle, expert_total, shared_total,
-    grad_in, outputs, weights, small, shared_pair, e1, e2, e3,
+    x, ext, dq, dk, dv, wq, wk, wv, grad_wo, grad_ext,
+    d_middle_in, slot_in, o0_in, o1_in, o2_in, o3_in, shared_in, probs_in, middle_in,
+    expert_total, shared_total,
+    grad_in, outputs, weights, small, shared_far, shared_mate, shared_cross, e1, e2, e3,
     normed_all, gain_acc, gw, from_mate, from_x, from_z, from_y, result, from_core,
-    tiny, tiny_in, shared_in, shared_sum, send, recv,
+    tiny, tiny_in, d_middle, slot, o0, o1, o2, o3, shared_out, probs, middle, load_sems,
+    send, recv,
 ):
     width = x.shape[1]
     half = width // SLOTS
     net = Net(send, recv)
     e_events = [net.event() for _ in range(3)]
-    s_events = [net.event() for _ in range(2)]
+    s_events = [net.event() for _ in range(3)]
     m_events = [net.event() for _ in range(2)]
     x_events = [[net.event() for _ in range(2)] for _ in range(4)]
     z_events = [[net.event() for _ in range(2)] for _ in range(3)]
@@ -1234,9 +1241,17 @@
         "all", [(net.mate, net.shard), (net.cousins[2], net.shard), (net.rep, net.across)]
     )
     far = net.cousins[2]
-    net.put(s_events[0], shared_total, shared_in, far, net.shard)
+    net.put(s_events[0], shared_total, shared_far, far, net.shard)
+    net.put(s_events[1], shared_total, shared_mate, net.mate, net.shard)
     net.put(e_events[1], expert_total, e2, far, net.shard)
     net.put(e_events[0], expert_total, e1, net.mate, net.shard)
+    pairs = (
+        (d_middle_in, d_middle), (slot_in, slot), (o0_in, o0), (o1_in, o1), (o2_in, o2),
+        (o3_in, o3), (shared_in, shared_out), (probs_in, probs), (middle_in, middle),
+    )
+    loads = [pltpu.make_async_copy(a, b, load_sems.at[i]) for i, (a, b) in enumerate(pairs)]
+    for copy in loads:
+        copy.start()
     norm_rows(x, ext, normed_all)
     spots = [lax.rem(i + 2 * net.core, 4) for i in range(4)]
     gw[spots[0]] = tn(normed_all[...], dq[...]).astype(BF)
@@ -1259,6 +1274,8 @@
             net.put(
                 x_events[d][i], gw.at[i, theirs[d]], from_x.at[d, i], net.rep, net.across
             )
+    for copy in loads:
+        copy.wait()
     input_grad(x, ext, dq, dk, dv, wq, wk, wv, d_middle, grad_in, gain_acc)
     row = iota((16, width), 0)
     total = jnp.sum(gain_acc[...], axis=0, keepdims=True)
@@ -1288,10 +1305,8 @@
     output_rows(slot, o0, o1, o2, o3, shared_out, probs, middle, outputs, 0, 2)
     add_across(1)
     tiny_add(1, far, net.shard)
-    net.got(s_events[0], shared_in)
-    shared_sum[...] = (shared_total[...].astype(F32) + shared_in[...].astype(F32)).astype(BF)
-    shared_pair[0] = shared_sum[...]
-    net.put(s_events[1], shared_sum, shared_pair.at[1], net.mate, net.shard)
+    net.got(s_events[0], shared_far)
+    net.put(s_events[2], shared_far, shared_cross, net.mate, net.shard)
     output_rows(slot, o0, o1, o2, o3, shared_out, probs, middle, outputs, 2, 4)
     tiny_add(2, None, None)
     for d in (1, 2, 3):
@@ -1321,7 +1336,8 @@
     for i in range(2):
         weights[spots[2 + i]] = from_core[i].astype(F32)
     net.got(e_events[0], e1)
-    net.got(s_events[1], shared_pair.at[1])
+    net.got(s_events[1], shared_mate)
+    net.got(s_events[2], shared_cross)
     net.got(e_events[2], e3)
     net.close()
 
@@ -1341,24 +1357,24 @@
     )
 
 
-def finish_kernel(e0, e1, e2, e3, pair, gate, up, down, s_gate, s_up, s_down):
+def finish_kernel(e0, e1, e2, e3, q0, q1, q2, q3, gate, up, down, s_gate, s_up, s_down):
     rep = lax.axis_index("rep")
-    core = lax.rem(rep, 2)
     for o, part in enumerate((e0, e1, e2, e3)):
         at = sibling(rep, o)
         gate[at] = part[0].astype(F32)
         up[at] = part[1].astype(F32)
         down[at] = part[2].astype(F32).T
-    span = pair.shape[3]
-    for side in range(2):
-
-        @pl.when(core == side)
-        def _():
-            for n in range(2):
-                at = (side + n) % 2 * span
-                s_gate[:, at : at + span] = pair[n, 0].astype(F32)
-                s_up[:, at : at + span] = pair[n, 1].astype(F32)
-                s_down[at : at + span, :] = pair[n, 2].astype(F32).T
+    quarter, span = q0.shape[1:]
+    for o, part in enumerate((q0, q1, q2, q3)):
+        for other in range(4):
+
+            @pl.when(sibling(rep, o) == other)
+            def _():
+                rows = slice(other // 2 * quarter, (other // 2 + 1) * quarter)
+                cols = slice(other % 2 * span, (other % 2 + 1) * span)
+                s_gate[rows, cols] = part[0].astype(F32)
+                s_up[rows, cols] = part[1].astype(F32)
+                s_down[cols, rows] = part[2].astype(F32).T
 
 
 def rope_tables(length, head_dim):
@@ -1488,40 +1504,42 @@
         )(normed, cot, my_half, shared_bank, *x_out[1:], expert_pack, expert_bank)
         x_in = [x_out[0], y1, y2, y3]
         bank = shape(expert_bank.shape)
-        half_x = (4,) + my_half.shape
-        far_a, far_b, da, db, before, shared_mate, shared_x, expert_bank = call(
+        quarter = (3, width // 2, units // 2)
+        quarters = (SLOTS,) + quarter
+        far_a, far_b, da, db, before, _, shared_keep, shared_y, expert_bank = call(
             far_kernel,
-            [rows_out] * 2 + [rows_back] * 2 + [bank, half_grads, shape(half_x), bank],
+            [rows_out] * 2 + [rows_back] * 2 + [bank, half_grads]
+            + [shape(quarters), shape(quarters), bank],
             [VMEM] * 5 + [ANY] * 4,
-            [VMEM] * 4 + [ANY] * 4,
+            [VMEM] * 4 + [ANY] * 5,
             [
-                pltpu.VMEM(half_x, BF),
-                pltpu.VMEM(half_x, BF),
-                pltpu.SemaphoreType.DMA((8,)),
-                pltpu.SemaphoreType.DMA((6,)),
-                pltpu.SemaphoreType.DMA((6,)),
+                pltpu.VMEM(half_grads.shape, BF),
+                pltpu.VMEM(half_grads.shape, BF),
+                pltpu.SemaphoreType.DMA((3,)),
+                pltpu.SemaphoreType.DMA((10,)),
+                pltpu.SemaphoreType.DMA((10,)),
             ]
             + unit_scratch(2, CAP, 16, width, 2, False),
             flops=36 * CAP * width * CHUNK * CHUNKS,
             moved=30 * 2**20,
             group=3,
-            alias={8: 7},
+            alias={8: 8},
         )(ext, *x_in[2:], *cot_in[2:], expert_pack, grads_own, grads_other, expert_bank)
         bank_x, bank_z = (4,) + expert_pack.shape, (3,) + expert_pack.shape
-        half_z = (3,) + my_half.shape
-        near_a, near_b, d0, shared_total, grads, d2, d3, d1, expert_x, _ = call(
+        near_a, near_b, d0, shared_total, grads, d2, d3, d1, expert_x = call(
             near_kernel,
-            [rows_out] * 2 + [rows_back, shape(my_half.shape), bank] + [rows_back] * 3
-            + [shape(bank_x), shape(half_z)],
-            [VMEM] * 5 + [ANY] * 8,
-            [VMEM] * 4 + [ANY] * 6,
+            [rows_out] * 2 + [rows_back, shape(quarter), bank] + [rows_back] * 3 + [shape(bank_x)],
+            [VMEM] * 5 + [ANY] * 7,
+            [VMEM] * 4 + [ANY] * 5,
             [
                 pltpu.VMEM((CAP + 16, width), BF),
-                pltpu.VMEM(half_x, BF),
-                pltpu.VMEM((2,) + my_half.shape, BF),
-                pltpu.SemaphoreType.DMA((3,)),
-                pltpu.SemaphoreType.DMA((12,)),
-                pltpu.SemaphoreType.DMA((12,)),
+                pltpu.VMEM(quarters, BF),
+                pltpu.VMEM(quarters, BF),
+                pltpu.VMEM((4,) + quarter, BF),
+                pltpu.VMEM((3,) + quarter, BF),
+                pltpu.SemaphoreType.DMA((2,)),
+                pltpu.SemaphoreType.DMA((11,)),
+                pltpu.SemaphoreType.DMA((11,)),
             ]
             + unit_scratch(2, CAP, 16, width, 2, True),
             flops=36 * CAP * width * CHUNK * CHUNKS,
@@ -1529,7 +1547,7 @@
             group=4,
         )(
             ext, *x_in[:2], *cot_in[:2], expert_pack, expert_bank, before, da, db,
-            grads_own, shared_mate, shared_x,
+            shared_keep, shared_y,
         )
         d_rows = [d0, d1, d2, d3]
     else:
@@ -1557,8 +1575,8 @@
     wide = shape((tokens, width), F32)
     outs = [wide, square, shape((16, width), F32)] + [token_f] * 3
     operands = (piece_starts, slot, *d_rows, shared_dx, probs, middle, normed, cot, ext, attended)
-    operands += (wo, q, k, v, lse, cosine, sine)
-    specs = [SMEM] + [VMEM] * 19
+    operands += (wo,)
+    specs = [SMEM] + [VMEM] * 15
     scratch = [
         pltpu.VMEM((tokens, width), BF),
         pltpu.VMEM((tokens, width), BF),
@@ -1576,31 +1594,36 @@
             + [shape(expert_pack.shape)]
             + [rows_out] * 3
             + [shape(bank_z), shape(bank_z), shape(bank_x)],
-            specs + [ANY] * 5,
+            specs + [ANY] * 9,
             [VMEM] * 7 + [ANY] * 6,
             scratch
             + [
+                pltpu.VMEM((tokens, width), BF),
+                pltpu.VMEM((tokens, width), BF),
+                pltpu.VMEM((tokens, width), BF),
+                pltpu.VMEM((tokens, width), F32),
                 pltpu.VMEM(bank_x, BF),
                 pltpu.VMEM((1,) + expert_pack.shape, BF),
                 pltpu.SemaphoreType.DMA((2,)),
-                pltpu.SemaphoreType.DMA((11,)),
-                pltpu.SemaphoreType.DMA((11,)),
+                pltpu.SemaphoreType.DMA((4,)),
+                pltpu.SemaphoreType.DMA((12,)),
+                pltpu.SemaphoreType.DMA((12,)),
             ],
             flops=work,
             moved=40 * 2**20,
             group=5,
             alias={24: 12},
-        )(*operands, near_b, far_a, far_b, grads, expert_x)
-        operands = (x, ext, dq, dk, dv, wq, wk, wv, d_middle, grad_wo, grad_ext)
-        operands += (slot, near_a, *back[:3], shared_out, probs, middle)
+        )(*operands, cosine, sine, q, k, v, lse, near_b, far_a, far_b, grads, expert_x)
+        operands = (x, ext, dq, dk, dv, wq, wk, wv, grad_wo, grad_ext)
+        operands += (d_middle, slot, near_a, *back[:3], shared_out, probs, middle)
         strip = (2, width // SLOTS, width)
-        grad_in, outputs, weights, small, shared_pair, e1, e2, e3 = call(
+        grad_in, outputs, weights, small, *rest = call(
             tail_kernel,
             [wide, token_f, shape((4, rows, width), F32), shape((16, width), F32)]
-            + [shape((2,) + my_half.shape)]
+            + [shape(quarter)] * 3
             + [shape(expert_pack.shape)] * 3,
-            [VMEM] * 19 + [ANY, VMEM],
-            [VMEM] * 5 + [ANY] * 3,
+            [VMEM] * 10 + [ANY] * 11,
+            [VMEM] * 4 + [ANY] * 6,
             [
                 pltpu.VMEM((tokens, width), BF),
                 pltpu.VMEM((8, width), F32),
@@ -1613,10 +1636,18 @@
                 pltpu.VMEM(strip, BF),
                 pltpu.VMEM((4, 16, width), BF),
                 pltpu.VMEM((6, 16, width), BF),
-                pltpu.VMEM(my_half.shape, BF),
-                pltpu.VMEM(my_half.shape, BF),
-                pltpu.SemaphoreType.DMA((29,)),
-                pltpu.SemaphoreType.DMA((29,)),
+                pltpu.VMEM((tokens, width), F32),
+                pltpu.VMEM((tokens, 128), F32),
+                pltpu.VMEM((CAP, width), BF),
+                pltpu.VMEM((CAP, width), BF),
+                pltpu.VMEM((CAP, width), BF),
+                pltpu.VMEM((CAP, width), BF),
+                pltpu.VMEM((tokens, width), BF),
+                pltpu.VMEM((tokens, 128), F32),
+                pltpu.VMEM((tokens, width), F32),
+                pltpu.SemaphoreType.DMA((9,)),
+                pltpu.SemaphoreType.DMA((30,)),
+                pltpu.SemaphoreType.DMA((30,)),
             ],
             flops=2 * tokens * width * (6 * width + 4 * CAP),
             moved=40 * 2**20,
@@ -1624,14 +1655,16 @@
         )(*operands, expert_total, shared_total)
         banks = [shape((4, width, units), F32)] * 2 + [shape((4, units, width), F32)]
         banks += [shape((width, units), F32)] * 2 + [shape((units, width), F32)]
-        finals = call(finish_kernel, banks, [VMEM] * 5, [VMEM] * 6, moved=18 * 2**20)(
-            expert_total, e1, e2, e3, shared_pair
+        shared_far, shared_mate, shared_cross, *experts = rest
+        finals = call(finish_kernel, banks, [VMEM] * 8, [VMEM] * 6, moved=18 * 2**20)(
+            expert_total, *experts, shared_total, shared_mate, shared_far, shared_cross
         )
         grad_q, grad_k, grad_v, grad_o = (weights[i] for i in range(4))
     else:
         d_middle, grad_wo, grad_ext, dq, dk, dv = call(
-            plain_back_kernel, outs, specs, [VMEM] * 6, scratch, flops=work, moved=40 * 2**20
-        )(*operands)
+            plain_back_kernel, outs, specs + [VMEM] * 4, [VMEM] * 6, scratch, flops=work,
+            moved=40 * 2**20,
+        )(*operands, q, k, v, lse, cosine, sine)
         out_rows = [near_a, to_rep(near_b, 1), to_rep(far_a, 2), to_rep(far_b, 3)]
         grad_in, outputs, gw, gain = call(
             plain_tail_kernel,

time: 578 us -> 559 us (0.967)
  Pallas kernels: 547 us -> 528 us
    pallas_call x3, Pallas kernels: 172 us -> 157 us  [the longest x1 74.3 us: body(): call(far_kernel, [rows_out] * 2 + [rows_back] * 2 + [bank, half_grads] +...]
    pallas_call x1, Pallas kernels: 102 us -> 116 us  [body(): call(back_kernel, outs + [shape(expert_pack.shape)] + [rows_out] * 3 + [s...]
where the time goes in v5:
time: 559 us; the launch traced here: 550 us
  Pallas kernels  528 us (94%)
  local copies, waits for them, and re-layouts  11.5 us (2%)
  other arithmetic  9.62 us (2%)
    pallas_call x1, Pallas kernels, body(): call(back_kernel, outs + [shape(expert_pack.shape)] + [rows_out] * 3 + [s...  116 us
    pallas_call x1, Pallas kernels, body(): call(forward_kernel, outs + [shape((2, SLOTS) + my_half.shape), shape((SL...  75.7 us
    pallas_call x1, Pallas kernels, body(): call(far_kernel, [rows_out] * 2 + [rows_back] * 2 + [bank, half_grads] +...  74.3 us
    pallas_call x1, Pallas kernels, body(): call(near_kernel, [rows_out] * 2 + [rows_back, shape(quarter), bank] + [r...  73.8 us
    pallas_call x1, Pallas kernels, body(): call(tail_kernel, [wide, token_f, shape((4, rows, width), F32), shape((16...  67.4 us
    pallas_call x1, Pallas kernels, body(): call(shared_kernel, [token_f] * 2 + [half_grads] * 2 + packed[:3] + [shap...  61 us
    pallas_call x1, Pallas kernels, body(): call(head_kernel, outs + [square] * 4 + [shape((16, width), F32)] + packe...  51.2 us

profile of v5, /device:TPU:0, one launch (start us, length us, event | category | flops | bytes accessed | tf_op | source)
XLA Modules:
  0.0 550.3 jit_solution(674681577625468441)
XLA Ops:
  0.6 0.0 copy-start
  0.7 0.8 fusion.9
  1.5 0.2 dynamic_update_slice.3
  1.7 1.9 maximum_select_fusion.piece
  3.7 2.0 fusion.4
  5.6 0.0 copy-start.6
  5.6 1.8 pad_maximum_fusion.1
  7.5 0.0 copy-done.6
  7.5 1.0 copy.35.routes
  8.5 0.0 copy-start.5
  8.5 51.2 %shard_map.280 = (f32[8,1024]{1,0:T(8,128)}, f32[1024,128]{1,0:T(8,128)}, bf16[1024,768]{1,0:T(8,128)(2,1)}, bf16[1024,768]{1,0:T(8,128)(2,1)}, bf16[1024,768]{1...) custom-call(s32[1024,2]{1,0:T(8,128)} %copy.35.routes, ...), custom_call_target="tpu_custom_call" | custom-call | flops 7247757312 | bytes 25165824 | tf_op jit(solution)/shard_map/pallas_call | solution.py:1444
  59.7 0.0 copy-done.5
  59.7 0.2 copy.36
  59.9 1.9 fusion.1.shared_piece.piece
  61.8 1.2 constant_dynamic-slice_fusion.1
  63.0 0.0 copy-done
  63.0 0.2 copy.37
  63.2 1.1 pad_maximum_fusion.expert_piece
  64.3 75.7 %shard_map.281 = (bf16[1024,768]{1,0:T(8,128)(2,1)}, f32[1024,768]{1,0:T(8,128)}, f32[1024,768]{1,0:T(8,128)}, bf16[1024,768]{1,0:T(8,128)(2,1)}, f32[1024,128]{...) custom-call(s32[1,2]{1,0:T(1,128)} %starts.3, ...), custom_call_target="tpu_custom_call" | custom-call | flops 17716740096 | bytes 31457280 | tf_op jit(solution)/shard_map/pallas_call | solution.py:1473
  140.0 61.0 %shard_map.282 = (bf16[1024,768]{1,0:T(8,128)(2,1)}, bf16[1024,768]{1,0:T(8,128)(2,1)}, bf16[8,3,768,128]{3,2,1,0:T(8,128)(2,1)}, bf16[8,3,768,128]{3,2,1,0:T(8,...) custom-call(bf16[1024,768]{1,0:T(8,128)(2,1)} %get-tuple-element.99., ...), custom_call_target="tpu_custom_call", output_to_operand_aliasing={{7}: (8, {})} | custom-call | flops 28991029248 | bytes 31457280 | tf_op jit(solution)/shard_map/pallas_call | solution.py:1493
  201.0 74.3 %shard_map.283 = (bf16[576,768]{1,0:T(8,128)(2,1)}, bf16[576,768]{1,0:T(8,128)(2,1)}, bf16[592,768]{1,0:T(8,128)(2,1)}, bf16[592,768]{1,0:T(8,128)(2,1)}, bf16[8...) custom-call(f32[16,768]{1,0:T(8,128)} %get-tuple-element.91.ext, ...), custom_call_target="tpu_custom_call", output_to_operand_aliasing={{8}: (8, {})} | custom-call | flops 32614907904 | bytes 31457280 | tf_op jit(solution)/shard_map/pallas_call | solution.py:1509
  275.3 73.8 %shard_map.284 = (bf16[576,768]{1,0:T(8,128)(2,1)}, bf16[576,768]{1,0:T(8,128)(2,1)}, bf16[592,768]{1,0:T(8,128)(2,1)}, bf16[3,384,128]{2,1,0:T(8,128)(2,1)}, bf...) custom-call(f32[16,768]{1,0:T(8,128)} %get-tuple-element.91.ext, ...), custom_call_target="tpu_custom_call" | custom-call | flops 32614907904 | bytes 31457280 | tf_op jit(solution)/shard_map/pallas_call | solution.py:1529
  349.1 116.2 %shard_map.285 = (f32[1024,768]{1,0:T(8,128)}, bf16[768,768]{1,0:T(8,128)(2,1)}, f32[16,768]{1,0:T(8,128)}, bf16[1024,768]{1,0:T(8,128)(2,1)}, bf16[1024,768]{1,...) custom-call(s32[1,2]{1,0:T(1,128)} %starts.3, ...), custom_call_target="tpu_custom_call", output_to_operand_aliasing={{12}: (24, {})} | custom-call | flops 38252052480 | bytes 41943040 | tf_op jit(solution)/shard_map/pallas_call | solution.py:1591
  465.4 67.4 %shard_map.286 = (f32[1024,768]{1,0:T(8,128)}, bf16[1024,768]{1,0:T(8,128)(2,1)}, f32[4,96,768]{2,1,0:T(8,128)}, f32[16,768]{1,0:T(8,128)}, bf16[3,384,128]{2,1,...) custom-call(bf16[1024,768]{1,0:T(8,128)(2,1)} %bitcast.50, ...), custom_call_target="tpu_custom_call" | custom-call | flops 10871635968 | bytes 41943040 | tf_op jit(solution)/shard_map/pallas_call | solution.py:1620
  532.7 0.0 copy-start.4
  532.7 8.5 %shard_map.287 = (f32[4,768,256]{2,1,0:T(8,128)}, f32[4,768,256]{2,1,0:T(8,128)}, f32[4,256,768]{2,1,0:T(8,128)}, f32[768,256]{1,0:T(8,128)}, f32[768,256]{1,0:T(8,128)}, /*index=5*/f32[256,768]{1,0:T(8,128)}) custom-call(bf16[3,768,256]{2,1,0:T(8,128)(2,1)} %get-tuple-element.149.expert_total.e0, bf16[3,768,256]{2,1,0:T(8,128)(2,1)} %get-tuple-element.155.e1, ...), custom_call_target="tpu_custom_call" | custom-call | bytes 18874368 | tf_op jit(solution)/shard_map/pallas_call | solution.py:1659
  541.2 0.0 copy-start.3
  541.2 0.0 copy-done.4
  541.2 1.0 slice_bitcast_fusion
  542.2 1.4 dynamic-slice_bitcast_fusion.1
  543.6 1.3 dynamic-slice_bitcast_fusion
  544.9 0.0 copy-done.3
  544.9 0.0 copy-start.2
  544.9 1.1 copy.44
  546.1 1.3 copy-done.2
  547.4 0.0 copy-start.1
  547.4 1.7 copy.45
  549.1 0.9 copy-done.1
  (4 shorter events, 0.1 us)
Async XLA Ops:
  0.6 62.3 %copy-start = (bf16[4,256,768]{2,1,0:T(8,128)(2,1)S(1)}, bf16[4,256,768]{2,1,0:T(8,128)(2,1)}, u32[]{:S(2)}) copy-start(bf16[4,256,768]{2,1,0:T(8,128)(2,1)} %param.29) | copy-start | bytes 4718596
  5.6 1.9 copy-start.6
  8.5 51.2 %copy-start.5 = (bf16[256,768]{1,0:T(8,128)(2,1)S(1)}, bf16[256,768]{1,0:T(8,128)(2,1)}, u32[]{:S(2)}) copy-start(bf16[256,768]{1,0:T(8,128)(2,1)} %param.32) | copy-start | bytes 1179652
  532.7 8.5 %copy-start.4 = (f32[4,96,768]{2,1,0:T(8,128)S(1)}, f32[4,96,768]{2,1,0:T(8,128)}, u32[]{:S(2)}) copy-start(f32[4,96,768]{2,1,0:T(8,128)} %get-tuple-element.154) | copy-start | bytes 3538948
  541.2 3.7 copy-start.3
  544.9 2.5 copy-start.2
  547.4 2.5 copy-start.1

commit v6 on v5

--- a/solution.py
+++ b/solution.py
@@ -348,14 +348,16 @@
 
 
 def head_kernel(
-    routes, routes_t, cot, x, piece, cosine, sine,
-    rank, slot, q, k, v, wq, wk, wv, wo, ext, c0, c1, c2, c3,
+    routes, routes_t, cot, x, piece, cosine, sine, expert_piece,
+    rank, slot, q, k, v, wq, wk, wv, wo, ext, c0, c1, c2, c3, experts,
     bank, packed, send, recv, own_sem,
 ):
     width = x.shape[1]
     half = width // SLOTS
     net = Net(send, recv)
     line = Line(net, bank)
+    e_events = [net.event() for _ in range(3)]
+    mine, most = experts.at[net.shard], experts.at[net.shard, pl.ds(0, 2)]
     peers = [(net.cousins[o], net.shard) for o in (1, 2, 3)]
     net.meet("line", peers + [(net.rep, net.across)])
     line.spread(0, piece)
@@ -373,10 +375,13 @@
     line.over(0)
     line.along(2)
     line.along(-2)
+    net.put(e_events[0], expert_piece, mine, net.rep, net.up, net.z < 3)
+    net.put(e_events[1], expert_piece, mine, net.rep, net.down, net.z > 0)
     line.over(1)
     line.over(-1)
     line.along(3)
     line.along(-3)
+    net.put(e_events[2], expert_piece.at[pl.ds(0, 2)], most, net.rep, net.across)
     for step in (2, -2, 3, -3):
         line.over(step)
     own.wait()
@@ -394,6 +399,9 @@
     qkv_rows(x, ext, cosine, sine, wq, wk, wv, q, k, v)
     for event, like in arrivals:
         net.got(event, like)
+    net.got(e_events[0], mine, net.z > 0)
+    net.got(e_events[1], mine, net.z < 3)
+    net.got(e_events[2], most)
     net.close()
 
 
@@ -502,15 +510,17 @@
 
 
 def forward_kernel(
-    starts, q, k, v, x, wo, ext, rank, shared_piece, expert_piece,
-    attended, lse, middle, normed, probs, x0, x1, x2, x3, shared_bank, expert_bank,
+    starts, q, k, v, x, wo, ext, rank, shared_piece, expert_piece, expert_in,
+    attended, lse, middle, normed, probs, x0, x1, x2, x3, shared_bank, experts,
     bias, send, recv,
 ):
     net = Net(send, recv)
     spread = Spread(net, shared_piece, shared_bank)
-    events = [net.event() for _ in range(3)]
-    mine = expert_bank.at[net.shard]
-    more_up, more_down = net.z < 3, net.z > 0
+    events = [net.event() for _ in range(4)]
+    inner = (net.z > 0) & (net.z < 3)
+    low, high = experts.at[net.down], experts.at[net.up]
+    rest, last = experts.at[net.shard, pl.ds(2, 1)], expert_piece.at[pl.ds(2, 1)]
+    near = experts.at[net.place(1, 0), pl.ds(0, 2)]
     net.meet("line", [(net.mate, net.shard), (net.rep, net.across), (spread.far, net.shard)])
     spread.begin()
     fill_bias(starts, bias)
@@ -536,9 +546,10 @@
         def _():
             spread.along(3)
             spread.along(-3)
-            net.put(events[0], expert_piece, mine, net.rep, net.up, more_up)
-            net.put(events[1], expert_piece, mine, net.rep, net.down, more_down)
-            net.put(events[2], expert_piece, mine, net.rep, net.across)
+            net.put(events[0], low, low, net.rep, net.up, inner)
+            net.put(events[1], high, high, net.rep, net.down, inner)
+            net.put(events[2], last, rest, net.rep, net.across)
+            net.put(events[3], near, near, net.rep, net.across)
             spread.over(2)
             spread.over(-2)
 
@@ -551,9 +562,10 @@
     for way, k_step in ((0, 3), (0, -3), (1, 3), (1, -3)):
         spread.relay(way, k_step)
     spread.finish()
-    net.got(events[0], mine, net.z > 0)
-    net.got(events[1], mine, net.z < 3)
-    net.got(events[2], mine)
+    net.got(events[0], low, net.z > 1)
+    net.got(events[1], low, net.z < 2)
+    net.got(events[2], rest)
+    net.got(events[3], near)
     net.close()
 
 
@@ -723,28 +735,28 @@
 
 
 def shared_kernel(
-    x, c, piece, bank, x1, x2, x3, expert_piece, expert_in,
-    out, dx, grads_own, grads_other, y1, y2, y3, experts,
+    x, c, piece, bank, x1, x2, x3, expert_in,
+    out, dx, grads_own, grads_other, shared_mate, y1, y2, y3, experts,
     send, recv, *scratch,
 ):
     net = Net(send, recv)
-    events = [net.event() for _ in range(6)]
+    events = [net.event() for _ in range(4)]
+    core_events = [net.event() for _ in range(8)]
     peers = [(net.cousins[o], net.shard) for o in (1, 2, 3)]
     net.meet("line", peers + [(net.rep, net.across)])
     arrivals = exchange(net, (x1, x2, x3), (y1, y2, y3))
-    low, high = experts.at[net.down], experts.at[net.up]
-    net.put(events[0], low, low, net.rep, net.up, (net.z > 0) & (net.z < 3))
-    net.put(events[1], high, high, net.rep, net.down, (net.z > 0) & (net.z < 3))
-    near, next_near = experts.at[net.place(1, 0)], experts.at[net.place(2, 0)]
-    net.put(events[2], near, near, net.rep, net.across)
+    near, second = experts.at[net.place(1, 0), pl.ds(2, 1)], experts.at[net.place(2, 0)]
+    net.put(events[0], near, near, net.rep, net.across)
+    net.put(events[1], second, second, net.rep, net.across)
     below = experts.at[lax.max(net.shard - 4, net.x)]
     above = experts.at[lax.min(net.shard + 4, 6 + net.x)]
-
-    def spot(n):
-        return net.place(n % 4, n // 4 % 2)
-
-    spots = [spot(n) for n in range(8)]
+    net.put(events[2], below, below, net.rep, net.up, net.z == 2)
+    net.put(events[3], above, above, net.rep, net.down, net.z == 1)
+    spots = [net.place(n % 4, n // 4 % 2) for n in range(8)]
     halves = [net.core, 1 - net.core]
+    done = scratch[5]
+    slices = [done.at[n // 4, :, :, pl.ds(n % 4 * 128, 128)] for n in range(8)]
+    places = [shared_mate.at[spot] for spot in spots]
 
     def source(n):
         return piece if n == 0 else bank.at[halves[n // 8], spots[n % 8]]
@@ -752,42 +764,39 @@
     def target(n):
         return (grads_own, grads_other)[n // 8].at[spots[n % 8]]
 
-    from_below, from_above = net.z > 1, net.z < 2
-    last_up, last_down = net.z == 2, net.z == 1
-
-    def ready(k):
-        if k == 2:
-            net.got(events[0], below, from_below)
-            net.got(events[1], above, from_above)
-            net.put(events[3], next_near, next_near, net.rep, net.across)
-            net.put(events[4], below, below, net.rep, net.up, last_up)
-            net.put(events[5], above, above, net.rep, net.down, last_down)
-
-    unit_bank(None, None, [x], [c], source, target, None, 128, [out], [dx], scratch, ready)
+    def emit(now):
+        if now >= 2:
+            for n in range(4 * now - 8, 4 * now - 4):
+                net.put(core_events[n], slices[n], places[n], net.mate, net.shard)
+
+    unit_bank(
+        None, None, [x], [c], source, target, None, 128, [out], [dx], scratch, None, emit
+    )
     for event, like in arrivals:
         net.got(event, like)
-    net.got(events[2], near)
-    net.got(events[3], near)
-    net.got(events[4], near, net.z == 3)
-    net.got(events[5], near, net.z == 0)
+    net.got(events[0], near)
+    net.got(events[1], second)
+    net.got(events[2], second, net.z == 3)
+    net.got(events[3], second, net.z == 0)
+    for n in range(8):
+        net.got(core_events[n], places[n])
     net.close()
 
 
 def far_kernel(
-    ext, xa, xb, ca, cb, expert_piece, shared_own, shared_other, expert_in,
-    oa, ob, da, db, grads, shared_mate, shared_keep, shared_y, experts,
+    ext, xa, xb, ca, cb, expert_piece, shared_own, shared_mate, expert_in,
+    oa, ob, da, db, grads, shared_keep, shared_y, experts,
     part_a, part_b, part_sems, send, recv, *scratch,
 ):
     net = Net(send, recv)
-    events = [net.event() for _ in range(10)]
+    events = [net.event() for _ in range(9)]
     far = net.cousins[2]
-    net.meet("none", [(net.rep, net.across), (net.mate, net.shard), (far, net.shard)])
+    parts = copies_of(((shared_own, part_a), (shared_mate, part_b)), part_sems)
+    for copy in parts:
+        copy.start()
+    net.meet("none", [(net.rep, net.across), (far, net.shard)])
     last = experts.at[net.place(3, 0)]
     net.put(events[0], last, last, net.rep, net.across)
-    net.put(events[1], shared_other, shared_mate, net.mate, net.shard)
-    own = pltpu.make_async_copy(shared_own, part_a, part_sems.at[0])
-    mate = pltpu.make_async_copy(shared_mate, part_b, part_sems.at[1])
-    own.start()
     spots = [net.place(n // 2, n % 2) for n in range(8)]
     y, quarter = lax.div(net.rep, 2), part_a.shape[2] // 2
     rows = [pl.ds(pl.multiple_of(n * quarter, 128), quarter) for n in (y, 1 - y)]
@@ -801,30 +810,27 @@
         return grads.at[spots[n]]
 
     def ready(k):
-        if k == 1:
-            net.got(events[1], shared_mate)
-            mate.start()
-            own.wait()
-            mate.wait()
-
-            def add(j, carry):
-                part_a[j] = (part_a[j].astype(F32) + part_b[j].astype(F32)).astype(BF)
-                return carry
-
-            lax.fori_loop(0, SLOTS, add, 0)
-            for j in range(SLOTS):
-                net.put(events[2 + j], away[j], shared_y.at[j], far, net.shard)
-            keep.start()
         if k == 3:
             net.got(events[0], last)
 
+    for copy in parts:
+        copy.wait()
+
+    def add(j, carry):
+        part_a[j] = part_a[j] + part_b[j]
+        return carry
+
+    lax.fori_loop(0, SLOTS, add, 0)
+    for j in range(SLOTS):
+        net.put(events[1 + j], away[j], shared_y.at[j], far, net.shard)
+    keep.start()
     unit_bank(
         net.rep, ext, [xa, xb], [ca, cb], source, target, None, 256, [oa, ob], [da, db],
         scratch, ready,
     )
     keep.wait()
     for j in range(SLOTS):
-        net.got(events[2 + j], shared_y.at[j])
+        net.got(events[1 + j], shared_y.at[j])
     net.close()
 
 
@@ -850,7 +856,7 @@
     two.wait()
 
     def add(j, carry):
-        part_a[j] = (part_a[j].astype(F32) + part_b[j].astype(F32)).astype(BF)
+        part_a[j] = part_a[j] + part_b[j]
         return carry
 
     lax.fori_loop(0, SLOTS, add, 0)
@@ -872,8 +878,7 @@
         if k == 2:
             for d in (2, 1, 3, 0):
                 net.got(x_events[d], lands[d])
-                total = part_a[mine[d]].astype(F32) + from_x[d].astype(F32)
-                part_a[mine[d]] = total.astype(BF)
+                part_a[mine[d]] = part_a[mine[d]] + from_x[d]
                 if d:
                     net.put(z_events[d - 1], pieces[d], ends[d - 1], net.rep, mine[d])
 
@@ -1057,8 +1062,12 @@
     lax.fori_loop(0, width // 128, pair, 0)
 
 
+def copies_of(pairs, sems):
+    return [pltpu.make_async_copy(a, b, sems.at[i]) for i, (a, b) in enumerate(pairs)]
+
+
 def fetch(sources, targets, sems):
-    copies = [pltpu.make_async_copy(a, b, sems.at[i]) for i, (a, b) in enumerate(zip(sources, targets))]
+    copies = copies_of(zip(sources, targets), sems)
     for copy in copies:
         copy.start()
     for copy in copies:
@@ -1084,7 +1093,7 @@
         to = self.net.levels[n]
         far = self.from_x.at[to]
         fetch([self.own.at[self.spots[n]], far], [self.held.at[to], self.spare.at[0]], self.sems)
-        self.held[to] = (self.held[to].astype(F32) + self.spare[0].astype(F32)).astype(BF)
+        self.held[to] = self.held[to] + self.spare[0]
 
     def send(self, d):
         net = self.net
@@ -1102,48 +1111,50 @@
                     self.net.mate, self.net.shard,
                 ).wait_recv()
                 fetch([into.at[d - 1]], [self.spare.at[0]], self.sems)
-                total = self.held[to].astype(F32) + self.spare[0].astype(F32)
-                self.held[to] = total.astype(BF)
+                self.held[to] = self.held[to] + self.spare[0]
 
             when(here, add)
 
 
-def back_kernel(
-    starts, slot, d0, d1, d2, d3, d_shared, probs, middle, normed, cot, ext, attended, wo,
-    cosine, sine,
-    q_in, k_in, v_in, lse_in, o1, o2, o3, grads, expert_x_in,
-    d_middle, grad_wo, grad_ext, dq, dk, dv, expert_total,
-    r1, r2, r3, up_in, down_in, expert_x,
-    d_attended, branch, router_acc, gain_acc, bias, dk_acc, dv_acc,
-    q, k, v, lse, held, spare, sems, load_sems, send, recv,
-):
+BACK_ROWS = 19
+
+
+def back_kernel(starts, *refs):
+    raw, refs = refs[:BACK_ROWS], refs[BACK_ROWS:]
+    o1, o2, o3, grads, expert_x_in = refs[:5]
+    d_middle, grad_wo, grad_ext, dq, dk, dv, expert_total = refs[5:12]
+    r1, r2, r3, up_in, down_in, expert_x = refs[12:18]
+    d_attended, branch, router_acc, gain_acc, bias, dk_acc, dv_acc = refs[18:25]
+    local = refs[25 : 25 + BACK_ROWS]
+    held, spare, sems, load_sems, send, recv = refs[25 + BACK_ROWS :]
+    slot, d0, d1, d2, d3, d_shared, probs, middle, normed, cot, ext, attended, wo = local[:13]
+    cosine, sine, q, k, v, lse = local[13:]
+    loads = copies_of(zip(raw, local), load_sems)
+    for copy in loads:
+        copy.start()
     net = Net(send, recv)
     x_events = [net.event() for _ in range(3)]
     chain = Chain(net, grads, expert_x, up_in, down_in, held, spare, sems)
     peers = [(net.cousins[o], net.shard) for o in (1, 2, 3)]
     net.meet("line", peers + [(net.rep, net.across)])
     targets = [expert_x.at[net.levels[n]] for n in range(3)]
-    pairs = ((q_in, q), (k_in, k), (v_in, v), (lse_in, lse))
-    loads = [pltpu.make_async_copy(a, b, load_sems.at[i]) for i, (a, b) in enumerate(pairs)]
     for n in (2, 1, 0):
         source = grads.at[net.place(n, 1)]
         net.put(x_events[n], source, targets[n], net.rep, net.across)
     arrivals = exchange(net, (o1, o2, o3), (r1, r2, r3))
     chain.level(3)
     chain.send(3)
+    fill_bias(starts, bias)
     for copy in loads:
-        copy.start()
+        copy.wait()
     combine_rows(
         slot, d0, d1, d2, d3, d_shared, probs, middle, normed, cot, ext, attended, wo,
         d_middle, d_attended, grad_wo, grad_ext, branch, router_acc, gain_acc,
     )
-    fill_bias(starts, bias)
     net.got(x_events[2], targets[2])
     chain.level(2)
     chain.take(3)
     chain.send(2)
-    for copy in loads:
-        copy.wait()
 
     def step(i):
         @pl.when(i == 1)
@@ -1254,26 +1265,31 @@
         copy.start()
     norm_rows(x, ext, normed_all)
     spots = [lax.rem(i + 2 * net.core, 4) for i in range(4)]
-    gw[spots[0]] = tn(normed_all[...], dq[...]).astype(BF)
-    gw[spots[1]] = tn(normed_all[...], dk[...]).astype(BF)
-    gw[spots[2]] = tn(normed_all[...], dv[...]).astype(BF)
-    gw[spots[3]] = grad_wo[...]
-    for i in range(2):
-        net.put(m_events[i], gw.at[2 + i], from_mate.at[i], net.mate, net.shard)
 
     def rows_of(spot):
         return pl.ds(pl.multiple_of(spot * half, 32), half)
 
     mine = [rows_of(net.cycle(d)) for d in range(4)]
     theirs = [rows_of(net.cycle(d) + 1 - 2 * net.x) for d in range(4)]
-    for i in range(2):
+
+    def hand(i):
+        net.put(m_events[i], gw.at[2 + i], from_mate.at[i], net.mate, net.shard)
+
+    def cross(i):
         net.got(m_events[i], from_mate.at[i])
-        gw[i] = (gw[i].astype(F32) + from_mate[i].astype(F32)).astype(BF)
-    for d in (2, 1, 3, 0):
-        for i in range(2):
-            net.put(
-                x_events[d][i], gw.at[i, theirs[d]], from_x.at[d, i], net.rep, net.across
-            )
+        gw[i] = gw[i] + from_mate[i]
+        for d in (2, 1, 3, 0):
+            source = gw.at[i, theirs[d]]
+            net.put(x_events[d][i], source, from_x.at[d, i], net.rep, net.across)
+
+    gw[spots[0]] = tn(normed_all[...], dq[...]).astype(BF)
+    gw[spots[2]] = tn(normed_all[...], dv[...]).astype(BF)
+    hand(0)
+    gw[spots[1]] = tn(normed_all[...], dk[...]).astype(BF)
+    gw[spots[3]] = grad_wo[...]
+    hand(1)
+    cross(0)
+    cross(1)
     for copy in loads:
         copy.wait()
     input_grad(x, ext, dq, dk, dv, wq, wk, wv, d_middle, grad_in, gain_acc)
@@ -1285,8 +1301,7 @@
     def add_across(d):
         for i in range(2):
             net.got(x_events[d][i], from_x.at[d, i])
-            summed = gw[i, mine[d], :].astype(F32) + from_x[d, i].astype(F32)
-            gw[i, mine[d], :] = summed.astype(BF)
+            gw[i, mine[d], :] = gw[i, mine[d], :] + from_x[d, i]
             if d:
                 net.put(
                     z_events[d - 1][i], gw.at[i, mine[d]], from_z.at[d - 1, i],
@@ -1357,24 +1372,43 @@
     )
 
 
-def finish_kernel(e0, e1, e2, e3, q0, q1, q2, q3, gate, up, down, s_gate, s_up, s_down):
+def finish_kernel(
+    e0, e1, e2, e3, q0, q1, q2, q3, weights,
+    gate, up, down, s_gate, s_up, s_down, grad_q, grad_k, grad_v, grad_o,
+    part, ready_gate, ready_up, ready_down, in_sems, out_sems,
+):
     rep = lax.axis_index("rep")
-    for o, part in enumerate((e0, e1, e2, e3)):
+    loads = copies_of([(e, part.at[o]) for o, e in enumerate((e0, e1, e2, e3))], in_sems)
+    for copy in loads:
+        copy.start()
+    stores = []
+    for o in range(4):
         at = sibling(rep, o)
-        gate[at] = part[0].astype(F32)
-        up[at] = part[1].astype(F32)
-        down[at] = part[2].astype(F32).T
+        pairs = ((ready_gate, gate), (ready_up, up), (ready_down, down))
+        stores.append(copies_of([(a.at[o], b.at[at]) for a, b in pairs], out_sems.at[o]))
+        loads[o].wait()
+        ready_gate[o] = part[o, 0].astype(F32)
+        ready_up[o] = part[o, 1].astype(F32)
+        ready_down[o] = part[o, 2].astype(F32).T
+        for copy in stores[o]:
+            copy.start()
     quarter, span = q0.shape[1:]
-    for o, part in enumerate((q0, q1, q2, q3)):
+    for o, piece in enumerate((q0, q1, q2, q3)):
         for other in range(4):
 
             @pl.when(sibling(rep, o) == other)
             def _():
                 rows = slice(other // 2 * quarter, (other // 2 + 1) * quarter)
                 cols = slice(other % 2 * span, (other % 2 + 1) * span)
-                s_gate[rows, cols] = part[0].astype(F32)
-                s_up[rows, cols] = part[1].astype(F32)
-                s_down[cols, rows] = part[2].astype(F32).T
+                s_gate[rows, cols] = piece[0].astype(F32)
+                s_up[rows, cols] = piece[1].astype(F32)
+                s_down[cols, rows] = piece[2].astype(F32).T
+
+    for i, out in enumerate((grad_q, grad_k, grad_v, grad_o)):
+        out[...] = weights[i]
+    for copies in stores:
+        for copy in copies:
+            copy.wait()
 
 
 def rope_tables(length, head_dim):
@@ -1443,21 +1477,22 @@
     if ringed:
         rank, slot, q, k, v, *heads = call(
             head_kernel,
-            outs + [square] * 4 + [shape((16, width), F32)] + packed,
-            [VMEM] * 7,
-            [VMEM] * 10 + [VMEM] + [ANY] * 3,
+            outs + [square] * 4 + [shape((16, width), F32)] + packed
+            + [shape((SLOTS,) + expert_pack.shape)],
+            [VMEM] * 7 + [ANY],
+            [VMEM] * 10 + [VMEM] + [ANY] * 4,
             [
                 pltpu.VMEM((2, SLOTS, 2 * rows + 16, width), BF),
                 pltpu.VMEM((3, CAP, width), BF),
-                pltpu.SemaphoreType.DMA((31,)),
-                pltpu.SemaphoreType.DMA((31,)),
+                pltpu.SemaphoreType.DMA((34,)),
+                pltpu.SemaphoreType.DMA((34,)),
                 pltpu.SemaphoreType.DMA,
             ],
             flops=work,
             moved=24 * 2**20,
             group=0,
-        )(chosen, chosen.T, cot, x, piece, cosine, sine)
-        wq, wk, wv, wo, ext, *cot_in = heads
+        )(chosen, chosen.T, cot, x, piece, cosine, sine, expert_pack)
+        wq, wk, wv, wo, ext, *cot_in, expert_bank = heads
     else:
         rank, slot, q, k, v, *cot_out = call(
             plain_head_kernel, outs + packed, [VMEM] * 10, [VMEM] * 9, flops=work,
@@ -1473,13 +1508,14 @@
         attended, lse, middle, normed, probs, *x_out, shared_bank, expert_bank = call(
             forward_kernel,
             outs + [shape((2, SLOTS) + my_half.shape), shape((SLOTS,) + expert_pack.shape)],
-            [SMEM] + [VMEM] * 7 + [ANY] * 2,
+            [SMEM] + [VMEM] * 7 + [ANY] * 3,
             [VMEM] * 9 + [ANY] * 2,
-            [bias, pltpu.SemaphoreType.DMA((59,)), pltpu.SemaphoreType.DMA((59,))],
+            [bias, pltpu.SemaphoreType.DMA((60,)), pltpu.SemaphoreType.DMA((60,))],
             flops=work,
             moved=30 * 2**20,
             group=1,
-        )(piece_starts, q, k, v, x, wo, ext, rank, my_half, expert_pack)
+            alias={10: 10},
+        )(piece_starts, q, k, v, x, wo, ext, rank, my_half, expert_pack, expert_bank)
     else:
         attended, lse, middle, normed, probs, *x_out = call(
             plain_forward_kernel, outs, [SMEM] + [VMEM] * 7, [VMEM] * 9, [bias], flops=work,
@@ -1490,41 +1526,40 @@
     rows_back = shape((CAP + 16, width))
     if ringed:
         half_grads = shape((SLOTS,) + my_half.shape)
-        shared_out, shared_dx, grads_own, grads_other, y1, y2, y3, expert_bank = call(
+        shared_out, shared_dx, grads_own, _, shared_mate, y1, y2, y3, expert_bank = call(
             shared_kernel,
-            [token_f] * 2 + [half_grads] * 2 + packed[:3] + [shape(expert_bank.shape)],
+            [token_f] * 2 + [half_grads] * 3 + packed[:3] + [shape(expert_bank.shape)],
+            [VMEM] * 2 + [ANY] * 6,
             [VMEM] * 2 + [ANY] * 7,
-            [VMEM] * 2 + [ANY] * 6,
-            [pltpu.SemaphoreType.DMA((9,)), pltpu.SemaphoreType.DMA((9,))]
+            [pltpu.SemaphoreType.DMA((15,)), pltpu.SemaphoreType.DMA((15,))]
             + unit_scratch(1, tokens, 0, width, 4, False),
             flops=18 * tokens * width * CHUNK * CHUNKS,
             moved=30 * 2**20,
             group=2,
-            alias={8: 7},
-        )(normed, cot, my_half, shared_bank, *x_out[1:], expert_pack, expert_bank)
+            alias={7: 8},
+        )(normed, cot, my_half, shared_bank, *x_out[1:], expert_bank)
         x_in = [x_out[0], y1, y2, y3]
         bank = shape(expert_bank.shape)
         quarter = (3, width // 2, units // 2)
         quarters = (SLOTS,) + quarter
-        far_a, far_b, da, db, before, _, shared_keep, shared_y, expert_bank = call(
+        far_a, far_b, da, db, before, shared_keep, shared_y, expert_bank = call(
             far_kernel,
-            [rows_out] * 2 + [rows_back] * 2 + [bank, half_grads]
-            + [shape(quarters), shape(quarters), bank],
+            [rows_out] * 2 + [rows_back] * 2 + [bank, shape(quarters), shape(quarters), bank],
             [VMEM] * 5 + [ANY] * 4,
-            [VMEM] * 4 + [ANY] * 5,
+            [VMEM] * 4 + [ANY] * 4,
             [
                 pltpu.VMEM(half_grads.shape, BF),
                 pltpu.VMEM(half_grads.shape, BF),
                 pltpu.SemaphoreType.DMA((3,)),
-                pltpu.SemaphoreType.DMA((10,)),
-                pltpu.SemaphoreType.DMA((10,)),
+                pltpu.SemaphoreType.DMA((9,)),
+                pltpu.SemaphoreType.DMA((9,)),
             ]
             + unit_scratch(2, CAP, 16, width, 2, False),
             flops=36 * CAP * width * CHUNK * CHUNKS,
             moved=30 * 2**20,
             group=3,
-            alias={8: 8},
-        )(ext, *x_in[2:], *cot_in[2:], expert_pack, grads_own, grads_other, expert_bank)
+            alias={8: 7},
+        )(ext, *x_in[2:], *cot_in[2:], expert_pack, grads_own, shared_mate, expert_bank)
         bank_x, bank_z = (4,) + expert_pack.shape, (3,) + expert_pack.shape
         near_a, near_b, d0, shared_total, grads, d2, d3, d1, expert_x = call(
             near_kernel,
@@ -1588,24 +1623,22 @@
     ]
     work = 2 * tokens * width * (2 * width + 4 * CAP) + 40 * tokens * tokens * width
     if ringed:
+        late = (*operands[1:], cosine, sine, q, k, v, lse)
         d_middle, grad_wo, grad_ext, dq, dk, dv, expert_total, *back = call(
             back_kernel,
             outs
             + [shape(expert_pack.shape)]
             + [rows_out] * 3
             + [shape(bank_z), shape(bank_z), shape(bank_x)],
-            specs + [ANY] * 9,
+            [SMEM] + [ANY] * (len(late) + 5),
             [VMEM] * 7 + [ANY] * 6,
             scratch
+            + [pltpu.VMEM(a.shape, a.dtype) for a in late]
             + [
-                pltpu.VMEM((tokens, width), BF),
-                pltpu.VMEM((tokens, width), BF),
-                pltpu.VMEM((tokens, width), BF),
-                pltpu.VMEM((tokens, width), F32),
                 pltpu.VMEM(bank_x, BF),
                 pltpu.VMEM((1,) + expert_pack.shape, BF),
                 pltpu.SemaphoreType.DMA((2,)),
-                pltpu.SemaphoreType.DMA((4,)),
+                pltpu.SemaphoreType.DMA((len(late),)),
                 pltpu.SemaphoreType.DMA((12,)),
                 pltpu.SemaphoreType.DMA((12,)),
             ],
@@ -1613,7 +1646,7 @@
             moved=40 * 2**20,
             group=5,
             alias={24: 12},
-        )(*operands, cosine, sine, q, k, v, lse, near_b, far_a, far_b, grads, expert_x)
+        )(piece_starts, *late, near_b, far_a, far_b, grads, expert_x)
         operands = (x, ext, dq, dk, dv, wq, wk, wv, grad_wo, grad_ext)
         operands += (d_middle, slot, near_a, *back[:3], shared_out, probs, middle)
         strip = (2, width // SLOTS, width)
@@ -1656,10 +1689,18 @@
         banks = [shape((4, width, units), F32)] * 2 + [shape((4, units, width), F32)]
         banks += [shape((width, units), F32)] * 2 + [shape((units, width), F32)]
         shared_far, shared_mate, shared_cross, *experts = rest
-        finals = call(finish_kernel, banks, [VMEM] * 8, [VMEM] * 6, moved=18 * 2**20)(
-            expert_total, *experts, shared_total, shared_mate, shared_far, shared_cross
+        *finals, grad_q, grad_k, grad_v, grad_o = call(
+            finish_kernel,
+            banks + [shape((rows, width), F32)] * 4,
+            [ANY] * 4 + [VMEM] * 5,
+            [ANY] * 3 + [VMEM] * 7,
+            [pltpu.VMEM((4,) + expert_pack.shape, BF)]
+            + [pltpu.VMEM(b.shape, F32) for b in banks[:3]]
+            + [pltpu.SemaphoreType.DMA((4,)), pltpu.SemaphoreType.DMA((4, 3))],
+            moved=18 * 2**20,
+        )(
+            expert_total, *experts, shared_total, shared_mate, shared_far, shared_cross, weights
         )
-        grad_q, grad_k, grad_v, grad_o = (weights[i] for i in range(4))
     else:
         d_middle, grad_wo, grad_ext, dq, dk, dv = call(
             plain_back_kernel, outs, specs + [VMEM] * 4, [VMEM] * 6, scratch, flops=work,

time: 559 us -> 540 us (0.966)
  Pallas kernels: 528 us -> 511 us
    pallas_call x3, Pallas kernels: 144 us -> 126 us  [the longest x1 65.8 us: body(): call(far_kernel, [rows_out] * 2 + [rows_back] * 2 + [bank, shape(quarters...]
    pallas_call x1, Pallas kernels: 51.2 us -> 62.6 us  [body(): call(head_kernel, outs + [square] * 4 + [shape((16, width), F32)] + packe...]
    pallas_call x1, Pallas kernels: 116 us -> 110 us  [body(): call(back_kernel, outs + [shape(expert_pack.shape)] + [rows_out] * 3 + [s...]
where the time goes in v6:
time: 540 us; the launch traced here: 532 us
  Pallas kernels  511 us (95%)
  local copies, waits for them, and re-layouts  10.5 us (2%)
  other arithmetic  8.65 us (2%)
    pallas_call x1, Pallas kernels, body(): call(back_kernel, outs + [shape(expert_pack.shape)] + [rows_out] * 3 + [s...  110 us
    pallas_call x1, Pallas kernels, body(): call(near_kernel, [rows_out] * 2 + [rows_back, shape(quarter), bank] + [r...  74.4 us
    pallas_call x1, Pallas kernels, body(): call(forward_kernel, outs + [shape((2, SLOTS) + my_half.shape), shape((SL...  71 us
    pallas_call x1, Pallas kernels, body(): call(tail_kernel, [wide, token_f, shape((4, rows, width), F32), shape((16...  67.3 us
    pallas_call x1, Pallas kernels, body(): call(far_kernel, [rows_out] * 2 + [rows_back] * 2 + [bank, shape(quarters...  65.8 us
    pallas_call x1, Pallas kernels, body(): call(head_kernel, outs + [square] * 4 + [shape((16, width), F32)] + packe...  62.6 us
    pallas_call x1, Pallas kernels, body(): call(shared_kernel, [token_f] * 2 + [half_grads] * 3 + packed[:3] + [shap...  51.5 us

profile of v6, /device:TPU:0, one launch (start us, length us, event | category | flops | bytes accessed | tf_op | source)
XLA Modules:
  0.0 531.6 jit_solution(4965662849993484007)
XLA Ops:
  0.6 0.0 copy-start
  0.7 0.8 fusion.9
  1.5 0.2 dynamic_update_slice.3
  1.7 1.9 maximum_select_fusion.piece
  3.7 1.2 constant_dynamic-slice_fusion.1
  4.8 0.0 copy-done
  4.9 0.2 copy.36
  5.1 1.1 pad_maximum_fusion.expert_piece
  6.2 2.0 fusion.4
  8.2 0.0 copy-start.7
  8.2 1.8 pad_maximum_fusion.1
  10.0 0.0 copy-done.7
  10.0 1.0 copy.37.routes
  11.1 0.0 copy-start.4
  11.1 0.0 copy-start.5
  11.1 0.0 copy-start.6
  11.1 62.6 %shard_map.280 = (f32[8,1024]{1,0:T(8,128)}, f32[1024,128]{1,0:T(8,128)}, bf16[1024,768]{1,0:T(8,128)(2,1)}, bf16[1024,768]{1,0:T(8,128)(2,1)}, bf16[1024,768]{1...) custom-call(s32[1024,2]{1,0:T(8,128)} %copy.37.routes, ...), custom_call_target="tpu_custom_call" | custom-call | flops 7247757312 | bytes 25165824 | tf_op jit(solution)/shard_map/pallas_call | solution.py:1478
  73.7 0.0 copy-done.4
  73.7 0.2 copy.38
  73.9 0.0 copy-done.5
  73.9 0.0 copy-done.6
  73.9 0.9 fusion.1.shared_piece.piece
  74.8 71.0 %shard_map.281 = (bf16[1024,768]{1,0:T(8,128)(2,1)}, f32[1024,768]{1,0:T(8,128)}, f32[1024,768]{1,0:T(8,128)}, bf16[1024,768]{1,0:T(8,128)(2,1)}, f32[1024,128]{...) custom-call(s32[1,2]{1,0:T(1,128)} %starts.3, ...), custom_call_target="tpu_custom_call", output_to_operand_aliasing={{10}: (10, {})} | custom-call | flops 17716740096 | bytes 31457280 | tf_op jit(solution)/shard_map/pallas_call | solution.py:1508
  145.8 51.5 %shard_map.282 = (bf16[1024,768]{1,0:T(8,128)(2,1)}, bf16[1024,768]{1,0:T(8,128)(2,1)}, bf16[8,3,768,128]{3,2,1,0:T(8,128)(2,1)}, bf16[8,3,768,128]{3,2,1,0:T(8,...) custom-call(bf16[1024,768]{1,0:T(8,128)(2,1)} %get-tuple-element.105, ...), custom_call_target="tpu_custom_call", output_to_operand_aliasing={{8}: (7, {})} | custom-call | flops 28991029248 | bytes 31457280 | tf_op jit(solution)/shard_map/pallas_call | solution.py:1529
  197.4 65.8 %shard_map.283 = (bf16[576,768]{1,0:T(8,128)(2,1)}, bf16[576,768]{1,0:T(8,128)(2,1)}, bf16[592,768]{1,0:T(8,128)(2,1)}, bf16[592,768]{1,0:T(8,128)(2,1)}, bf16[8...) custom-call(f32[16,768]{1,0:T(8,128)} %get-tuple-element.96.ext.refs, ...), custom_call_target="tpu_custom_call", output_to_operand_aliasing={{7}: (8, {})} | custom-call | flops 32614907904 | bytes 31457280 | tf_op jit(solution)/shard_map/pallas_call | solution.py:1545
  263.2 74.4 %shard_map.284 = (bf16[576,768]{1,0:T(8,128)(2,1)}, bf16[576,768]{1,0:T(8,128)(2,1)}, bf16[592,768]{1,0:T(8,128)(2,1)}, bf16[3,384,128]{2,1,0:T(8,128)(2,1)}, bf...) custom-call(f32[16,768]{1,0:T(8,128)} %get-tuple-element.96.ext.refs, ...), custom_call_target="tpu_custom_call" | custom-call | flops 32614907904 | bytes 31457280 | tf_op jit(solution)/shard_map/pallas_call | solution.py:1564
  337.6 109.8 %shard_map.285 = (f32[1024,768]{1,0:T(8,128)}, bf16[768,768]{1,0:T(8,128)(2,1)}, f32[16,768]{1,0:T(8,128)}, bf16[1024,768]{1,0:T(8,128)(2,1)}, bf16[1024,768]{1,...) custom-call(s32[1,2]{1,0:T(1,128)} %starts.3, ...), custom_call_target="tpu_custom_call", output_to_operand_aliasing={{12}: (24, {})} | custom-call | flops 38252052480 | bytes 41943040 | tf_op jit(solution)/shard_map/pallas_call | solution.py:1627
  447.4 67.3 %shard_map.286 = (f32[1024,768]{1,0:T(8,128)}, bf16[1024,768]{1,0:T(8,128)(2,1)}, f32[4,96,768]{2,1,0:T(8,128)}, f32[16,768]{1,0:T(8,128)}, bf16[3,384,128]{2,1,...) custom-call(bf16[1024,768]{1,0:T(8,128)(2,1)} %bitcast.42, ...), custom_call_target="tpu_custom_call" | custom-call | flops 10871635968 | bytes 41943040 | tf_op jit(solution)/shard_map/pallas_call | solution.py:1653
  514.7 0.0 copy-start.3
  514.7 8.7 %shard_map.287 = (f32[4,768,256]{2,1,0:T(8,128)}, f32[4,768,256]{2,1,0:T(8,128)}, f32[4,256,768]{2,1,0:T(8,128)}, f32[768,256]{1,0:T(8,128)}, f32[768,256]{1,0:T...) custom-call(bf16[3,768,256]{2,1,0:T(8,128)(2,1)} %get-tuple-element., ...), custom_call_target="tpu_custom_call" | custom-call | bytes 18874368 | tf_op jit(solution)/shard_map/pallas_call | solution.py:1692
  523.4 1.4 dynamic-slice_bitcast_fusion.1
  524.8 1.3 dynamic-slice_bitcast_fusion
  526.1 0.0 copy-done.3
  526.1 0.0 copy-start.2
  526.1 1.1 copy.46
  527.3 1.3 copy-done.2
  528.6 0.0 copy-start.1
  528.6 1.7 copy.47
  530.3 0.9 copy-done.1
  (4 shorter events, 0.1 us)
Async XLA Ops:
  0.6 4.2 copy-start
  8.2 1.9 copy-start.7
  11.1 62.6 %copy-start.4 = (bf16[256,768]{1,0:T(8,128)(2,1)S(1)}, bf16[256,768]{1,0:T(8,128)(2,1)}, u32[]{:S(2)}) copy-start(bf16[256,768]{1,0:T(8,128)(2,1)} %param.32) | copy-start | bytes 1179652
  11.1 62.8 %copy-start.5 = (bf16[768,256]{1,0:T(8,128)(2,1)S(1)}, bf16[768,256]{1,0:T(8,128)(2,1)}, u32[]{:S(2)}) copy-start(bf16[768,256]{1,0:T(8,128)(2,1)} %param.30) | copy-start | bytes 1179652
  11.1 62.8 %copy-start.6 = (bf16[768,256]{1,0:T(8,128)(2,1)S(1)}, bf16[768,256]{1,0:T(8,128)(2,1)}, u32[]{:S(2)}) copy-start(bf16[768,256]{1,0:T(8,128)(2,1)} %param.31) | copy-start | bytes 1179652
  514.7 11.5 %copy-start.3 = (bf16[1024,768]{1,0:T(8,128)(2,1)S(1)}, bf16[1024,768]{1,0:T(8,128)(2,1)}, u32[]{:S(2)}) copy-start(bf16[1024,768]{1,0:T(8,128)(2,1)} %get-tuple-element.157) | copy-start | bytes 4718596
  526.1 2.5 copy-start.2
  528.6 2.5 copy-start.1

commit v7 on v6

--- a/solution.py
+++ b/solution.py
@@ -348,13 +348,24 @@
 
 
 def head_kernel(
-    routes, routes_t, cot, x, piece, cosine, sine, expert_piece,
-    rank, slot, q, k, v, wq, wk, wv, wo, ext, c0, c1, c2, c3, experts,
-    bank, packed, send, recv, own_sem,
+    routes, routes_t, cot, x, wq_in, wk_in, wv_in, wo_in, small, cosine, sine, expert_piece,
+    *refs,
 ):
     width = x.shape[1]
     half = width // SLOTS
+    outs, (c1, c2, c3, experts) = refs[:11], refs[11:15]
+    bank, packed, piece, out_sems, send, recv, own_sem = refs[15:22]
+    rank, slot, q, k, v, wq, wk, wv, wo, ext, c0 = refs[22:]
+    stores = copies_of(zip(refs[22:], outs), out_sems)
     net = Net(send, recv)
+    for core, (low, high) in enumerate(((wq_in, wk_in), (wv_in, wo_in))):
+
+        @pl.when(net.core == core)
+        def _():
+            piece[0:half, :] = low[...]
+            piece[half : 2 * half, :] = high[...]
+
+    piece[2 * half : 2 * half + 16, :] = small[...]
     line = Line(net, bank)
     e_events = [net.event() for _ in range(3)]
     mine, most = experts.at[net.shard], experts.at[net.shard, pl.ds(0, 2)]
@@ -397,11 +408,15 @@
         wv[at, :] = bank[1, j, 0:half, :]
         wo[at, :] = bank[1, j, half : 2 * half, :]
     qkv_rows(x, ext, cosine, sine, wq, wk, wv, q, k, v)
+    for copy in stores:
+        copy.start()
     for event, like in arrivals:
         net.got(event, like)
     net.got(e_events[0], mine, net.z > 0)
     net.got(e_events[1], mine, net.z < 3)
     net.got(e_events[2], most)
+    for copy in stores:
+        copy.wait()
     net.close()
 
 
@@ -511,9 +526,12 @@
 
 def forward_kernel(
     starts, q, k, v, x, wo, ext, rank, shared_piece, expert_piece, expert_in,
-    attended, lse, middle, normed, probs, x0, x1, x2, x3, shared_bank, experts,
-    bias, send, recv,
+    *refs,
 ):
+    outs, shared_bank, experts = refs[:9], refs[9], refs[10]
+    bias, out_sems, send, recv = refs[11:15]
+    attended, lse, middle, normed, probs, x0, x1, x2, x3 = refs[15:]
+    stores = copies_of(zip(refs[15:], outs), out_sems)
     net = Net(send, recv)
     spread = Spread(net, shared_piece, shared_bank)
     events = [net.event() for _ in range(4)]
@@ -538,9 +556,6 @@
             spread.along(-2)
             spread.over(1)
             spread.over(-1)
-            spread.relay(1, 0)
-            spread.relay(0, 1)
-            spread.relay(0, -1)
 
         @pl.when(i == 5)
         def _():
@@ -554,9 +569,15 @@
             spread.over(-2)
 
     attend_pairs(q, k, v, attended, lse, bias, step)
+    for copy in stores[:2]:
+        copy.start()
     spread.over(3)
     spread.over(-3)
+    for way, k_step in ((1, 0), (0, 1), (0, -1)):
+        spread.relay(way, k_step)
     middle_rows(net.rep, x, attended, wo, ext, rank, middle, normed, probs, (x0, x1, x2, x3))
+    for copy in stores[2:]:
+        copy.start()
     for way, k_step in ((1, 1), (1, -1), (0, 2), (0, -2), (1, 2), (1, -2)):
         spread.relay(way, k_step)
     for way, k_step in ((0, 3), (0, -3), (1, 3), (1, -3)):
@@ -566,6 +587,8 @@
     net.got(events[1], low, net.z < 2)
     net.got(events[2], rest)
     net.got(events[3], near)
+    for copy in stores:
+        copy.wait()
     net.close()
 
 
@@ -584,7 +607,7 @@
 
 def unit_bank(
     expert, ext, xs, cs, source, target, before, unit, outs, dxs, scratch, ready=None,
-    emit=None, reclaim=None,
+    emit=None,
 ):
     out_acc, dx_acc, gate, wbuf, dw_acc, dw_out, in_sems, out_sems = scratch[:8]
     routed = expert is not None
@@ -684,9 +707,6 @@
             for copy in stores(0, b):
                 copy.wait()
 
-        if reclaim is not None:
-            for now in (2, 3):
-                when(k == now, functools.partial(reclaim, now))
         if before is not None:
             for copy in loads(before, scratch[8], scratch[9], 0, b):
                 copy.wait()
@@ -838,7 +858,7 @@
     ext, xa, xb, ca, cb, expert_piece, experts, before, far_a, far_b,
     shared_keep, shared_y,
     oa, ob, da, shared_total, grads, back_a, back_b, back_c, expert_x,
-    db, part_a, part_b, from_x, from_z, sems, send, recv, *scratch,
+    db, part_a, part_b, from_x, from_z, third, sems, send, recv, *scratch,
 ):
     net = Net(send, recv)
     events = [net.event() for _ in range(4)]
@@ -868,8 +888,7 @@
     ends = [from_z.at[d] for d in range(3)]
     spots = [net.place(3 - n // 2, n % 2) for n in range(8)]
     own_slot = 6
-    half = scratch[5].at[0, :, :, pl.ds(256, 256)]
-    target = expert_x.at[net.levels[3]]
+    done, target = scratch[5], expert_x.at[net.levels[3]]
 
     def source(n):
         return expert_piece if n == own_slot else experts.at[spots[n]]
@@ -884,18 +903,14 @@
 
     def emit(now):
         if now == 0:
-            net.put(events[3], half, target, net.rep, net.across)
-
-    def reclaim(now):
-        if now == 2:
-            net.copy(events[3], half, half, net.mate, net.shard).wait_send()
+            third[...] = done[0, :, :, 256:512]
+            net.put(events[3], third, target, net.rep, net.across)
 
     unit_bank(
         net.rep, ext, [xa, xb], [ca, cb], source,
         lambda n: grads.at[spots[n]], lambda n: before.at[spots[n]],
-        256, [oa, ob], [da, db], scratch, ready, emit, reclaim,
+        256, [oa, ob], [da, db], scratch, ready, emit,
     )
-    net.open.pop(events[3])
     net.put(events[2], db, back_c, net.mate, net.shard)
     total = part_a[mine[0]].astype(F32)
     for d in (1, 2, 3):
@@ -1122,11 +1137,13 @@
 def back_kernel(starts, *refs):
     raw, refs = refs[:BACK_ROWS], refs[BACK_ROWS:]
     o1, o2, o3, grads, expert_x_in = refs[:5]
-    d_middle, grad_wo, grad_ext, dq, dk, dv, expert_total = refs[5:12]
+    outs, expert_total = refs[5:11], refs[11]
     r1, r2, r3, up_in, down_in, expert_x = refs[12:18]
     d_attended, branch, router_acc, gain_acc, bias, dk_acc, dv_acc = refs[18:25]
     local = refs[25 : 25 + BACK_ROWS]
-    held, spare, sems, load_sems, send, recv = refs[25 + BACK_ROWS :]
+    held, spare, sems, load_sems, out_sems, send, recv = refs[25 + BACK_ROWS : 32 + BACK_ROWS]
+    d_middle, grad_wo, grad_ext, dq, dk, dv = refs[32 + BACK_ROWS :]
+    stores = copies_of(zip((d_middle, grad_wo, grad_ext, dq, dk, dv), outs), out_sems)
     slot, d0, d1, d2, d3, d_shared, probs, middle, normed, cot, ext, attended, wo = local[:13]
     cosine, sine, q, k, v, lse = local[13:]
     loads = copies_of(zip(raw, local), load_sems)
@@ -1151,13 +1168,15 @@
         slot, d0, d1, d2, d3, d_shared, probs, middle, normed, cot, ext, attended, wo,
         d_middle, d_attended, grad_wo, grad_ext, branch, router_acc, gain_acc,
     )
+    for copy in stores[:3]:
+        copy.start()
     net.got(x_events[2], targets[2])
     chain.level(2)
     chain.take(3)
     chain.send(2)
 
     def step(i):
-        @pl.when(i == 1)
+        @pl.when(i == 3)
         def _():
             net.got(x_events[1], targets[1])
             chain.level(1)
@@ -1170,12 +1189,16 @@
     back_pairs(
         q, k, v, d_attended, attended, lse, cosine, sine, dq, dk, dv, bias, dk_acc, dv_acc, step
     )
+    for copy in stores[3:]:
+        copy.start()
     net.got(x_events[0], targets[0])
     chain.level(0)
     for event, like in arrivals:
         net.got(event, like)
     chain.take(1)
     expert_total[...] = held[net.z]
+    for copy in stores:
+        copy.wait()
     net.close()
 
 
@@ -1209,10 +1232,9 @@
     lax.fori_loop(0, x.shape[0] // TILE, tile, 0)
 
 
-def input_grad(x, ext, dq, dk, dv, wq, wk, wv, d_middle, grad_in, gain_acc):
-    tokens, width = x.shape
+def input_grad(x, ext, dq, dk, dv, wq, wk, wv, d_middle, grad_in, gain_acc, first, last):
+    width = x.shape[1]
     gain = ext[4:5, :]
-    gain_acc[...] = jnp.zeros_like(gain_acc)
 
     def tile(t, carry):
         at = pl.ds(pl.multiple_of(t * TILE, TILE), TILE)
@@ -1226,7 +1248,7 @@
         grad_in[at, :] = d_middle[at, :] + scale * (w - unit * inner)
         return carry
 
-    lax.fori_loop(0, tokens // TILE, tile, 0)
+    lax.fori_loop(first, last, tile, 0)
 
 
 def tail_kernel(
@@ -1246,7 +1268,8 @@
     m_events = [net.event() for _ in range(2)]
     x_events = [[net.event() for _ in range(2)] for _ in range(4)]
     z_events = [[net.event() for _ in range(2)] for _ in range(3)]
-    y_event, c_event = net.event(), net.event()
+    y_events = [net.event() for _ in range(2)]
+    c_events = [net.event() for _ in range(2)]
     t_events = [net.event() for _ in range(6)]
     net.meet(
         "all", [(net.mate, net.shard), (net.cousins[2], net.shard), (net.rep, net.across)]
@@ -1290,23 +1313,35 @@
     hand(1)
     cross(0)
     cross(1)
+    gain_acc[...] = jnp.zeros_like(gain_acc)
     for copy in loads:
         copy.wait()
-    input_grad(x, ext, dq, dk, dv, wq, wk, wv, d_middle, grad_in, gain_acc)
-    row = iota((16, width), 0)
-    total = jnp.sum(gain_acc[...], axis=0, keepdims=True)
-    tiny[0] = (grad_ext[...] + jnp.where(row == 4, total, 0.0)).astype(BF)
-    net.put(t_events[0], tiny.at[0], tiny_in.at[0], net.mate, net.shard)
-
-    def add_across(d):
-        for i in range(2):
-            net.got(x_events[d][i], from_x.at[d, i])
-            gw[i, mine[d], :] = gw[i, mine[d], :] + from_x[d, i]
-            if d:
-                net.put(
-                    z_events[d - 1][i], gw.at[i, mine[d]], from_z.at[d - 1, i],
-                    net.rep, net.cycle(d),
-                )
+    count = x.shape[0] // TILE
+
+    def inputs(first, last):
+        input_grad(x, ext, dq, dk, dv, wq, wk, wv, d_middle, grad_in, gain_acc, first, last)
+
+    def results(first, last):
+        output_rows(
+            slot, o0, o1, o2, o3, shared_out, probs, middle, outputs, first, last
+        )
+
+    def add_across(d, i):
+        net.got(x_events[d][i], from_x.at[d, i])
+        gw[i, mine[d], :] = gw[i, mine[d], :] + from_x[d, i]
+        if d:
+            net.put(
+                z_events[d - 1][i], gw.at[i, mine[d]], from_z.at[d - 1, i],
+                net.rep, net.cycle(d),
+            )
+
+    def add_along(i):
+        total = gw[i, mine[0], :].astype(F32)
+        for d in (1, 2, 3):
+            net.got(z_events[d - 1][i], from_z.at[d - 1, i])
+            total = total + from_z[d - 1, i].astype(F32)
+        result[0, i] = total.astype(BF)
+        net.put(y_events[i], result.at[0, i], from_y.at[i], far, net.shard)
 
     def tiny_add(n, target_rep, target_shard):
         net.got(t_events[n], tiny_in.at[n])
@@ -1315,40 +1350,48 @@
             source, target = tiny.at[n + 1], tiny_in.at[n + 1]
             net.put(t_events[n + 1], source, target, target_rep, target_shard)
 
-    add_across(2)
+    inputs(0, 2)
+    add_across(2, 0)
+    add_across(1, 0)
+    inputs(2, 3)
+    add_across(3, 0)
+    inputs(3, count)
+    add_across(0, 0)
+    row = iota((16, width), 0)
+    total = jnp.sum(gain_acc[...], axis=0, keepdims=True)
+    tiny[0] = (grad_ext[...] + jnp.where(row == 4, total, 0.0)).astype(BF)
+    net.put(t_events[0], tiny.at[0], tiny_in.at[0], net.mate, net.shard)
+    results(0, 1)
+    add_across(2, 1)
     tiny_add(0, net.rep, net.across)
-    output_rows(slot, o0, o1, o2, o3, shared_out, probs, middle, outputs, 0, 2)
-    add_across(1)
+    results(1, 2)
+    add_across(1, 1)
     tiny_add(1, far, net.shard)
-    net.got(s_events[0], shared_far)
-    net.put(s_events[2], shared_far, shared_cross, net.mate, net.shard)
-    output_rows(slot, o0, o1, o2, o3, shared_out, probs, middle, outputs, 2, 4)
+    add_along(0)
+    results(2, 3)
+    add_across(3, 1)
     tiny_add(2, None, None)
     for d in (1, 2, 3):
         net.put(t_events[2 + d], tiny.at[3], tiny_in.at[2 + d], net.rep, net.cycle(d))
-    add_across(3)
-    add_across(0)
-    for i in range(2):
-        total = gw[i, mine[0], :].astype(F32)
-        for d in (1, 2, 3):
-            net.got(z_events[d - 1][i], from_z.at[d - 1, i])
-            total = total + from_z[d - 1, i].astype(F32)
-        result[0, i] = total.astype(BF)
-    net.put(y_event, result.at[0], from_y, far, net.shard)
+    net.got(s_events[0], shared_far)
+    net.put(s_events[2], shared_far, shared_cross, net.mate, net.shard)
+    results(3, count)
+    add_across(0, 1)
+    net.got(e_events[1], e2)
+    net.put(e_events[2], e2, e3, net.mate, net.shard)
     total = tiny[3].astype(F32)
     for d in (1, 2, 3):
         net.got(t_events[2 + d], tiny_in.at[2 + d])
         total = total + tiny_in[2 + d].astype(F32)
     small[...] = total.astype(BF).astype(F32)
-    net.got(e_events[1], e2)
-    net.put(e_events[2], e2, e3, net.mate, net.shard)
-    net.got(y_event, from_y)
-    result[1] = (result[0].astype(F32) + from_y[...].astype(F32)).astype(BF)
-    net.put(c_event, result.at[1], from_core, net.mate, net.shard)
+    add_along(1)
     for i in range(2):
+        net.got(y_events[i], from_y.at[i])
+        result[1, i] = (result[0, i].astype(F32) + from_y[i].astype(F32)).astype(BF)
+        net.put(c_events[i], result.at[1, i], from_core.at[i], net.mate, net.shard)
         weights[spots[i]] = result[1, i].astype(F32)
-    net.got(c_event, from_core)
     for i in range(2):
+        net.got(c_events[i], from_core.at[i])
         weights[spots[2 + i]] = from_core[i].astype(F32)
     net.got(e_events[0], e1)
     net.got(s_events[1], shared_mate)
@@ -1365,7 +1408,9 @@
     norm_rows(x, ext, normed_all)
     for i, d in enumerate((dq, dk, dv)):
         gw[i] = tn(normed_all[...], d[...]).astype(BF)
-    input_grad(x, ext, dq, dk, dv, wq, wk, wv, d_middle, grad_in, gain_acc)
+    gain_acc[...] = jnp.zeros_like(gain_acc)
+    count = x.shape[0] // TILE
+    input_grad(x, ext, dq, dk, dv, wq, wk, wv, d_middle, grad_in, gain_acc, 0, count)
     gain[...] = gain_acc[...]
     output_rows(
         slot, o0, o1, o2, o3, shared_out, probs, middle, outputs, 0, x.shape[0] // TILE
@@ -1452,12 +1497,7 @@
     small = jnp.concatenate([router_weight.T, attn_gain[None], ffn_gain[None]], axis=0)
     small = jnp.pad(small, ((0, 10), (0, 0)))
     small = lax.dynamic_update_slice(jnp.zeros((16, width), BF), small, (0, shard * rows))
-    blank = jnp.zeros((16, width), BF)
-    if ringed:
-        half_one = jnp.concatenate([query_weight, key_weight, small], axis=0)
-        half_two = jnp.concatenate([value_weight, out_weight, blank], axis=0)
-        piece = jnp.where(core == 0, half_one, half_two)
-    else:
+    if not ringed:
         wq, wk, wv, wo = [
             lax.all_gather(w, "shard", axis=0, tiled=True)
             for w in (query_weight, key_weight, value_weight, out_weight)
@@ -1475,23 +1515,29 @@
     outs = [shape((8, tokens), F32), shape((tokens, 128), F32)] + [token_f] * 3
     work = 2 * tokens * width * (CAP * 4 + 3 * width)
     if ringed:
+        firsts = outs + [square] * 4 + [shape((16, width), F32), packed[0]]
         rank, slot, q, k, v, *heads = call(
             head_kernel,
-            outs + [square] * 4 + [shape((16, width), F32)] + packed
-            + [shape((SLOTS,) + expert_pack.shape)],
-            [VMEM] * 7 + [ANY],
-            [VMEM] * 10 + [VMEM] + [ANY] * 4,
+            firsts + packed[1:] + [shape((SLOTS,) + expert_pack.shape)],
+            [VMEM] * 11 + [ANY],
+            [ANY] * 15,
             [
                 pltpu.VMEM((2, SLOTS, 2 * rows + 16, width), BF),
                 pltpu.VMEM((3, CAP, width), BF),
+                pltpu.VMEM((2 * rows + 16, width), BF),
+                pltpu.SemaphoreType.DMA((11,)),
                 pltpu.SemaphoreType.DMA((34,)),
                 pltpu.SemaphoreType.DMA((34,)),
                 pltpu.SemaphoreType.DMA,
-            ],
+            ]
+            + [pltpu.VMEM(a.shape, a.dtype) for a in firsts],
             flops=work,
             moved=24 * 2**20,
             group=0,
-        )(chosen, chosen.T, cot, x, piece, cosine, sine, expert_pack)
+        )(
+            chosen, chosen.T, cot, x, query_weight, key_weight, value_weight, out_weight, small,
+            cosine, sine, expert_pack,
+        )
         wq, wk, wv, wo, ext, *cot_in, expert_bank = heads
     else:
         rank, slot, q, k, v, *cot_out = call(
@@ -1509,8 +1555,14 @@
             forward_kernel,
             outs + [shape((2, SLOTS) + my_half.shape), shape((SLOTS,) + expert_pack.shape)],
             [SMEM] + [VMEM] * 7 + [ANY] * 3,
-            [VMEM] * 9 + [ANY] * 2,
-            [bias, pltpu.SemaphoreType.DMA((60,)), pltpu.SemaphoreType.DMA((60,))],
+            [ANY] * 11,
+            [
+                bias,
+                pltpu.SemaphoreType.DMA((9,)),
+                pltpu.SemaphoreType.DMA((60,)),
+                pltpu.SemaphoreType.DMA((60,)),
+            ]
+            + [pltpu.VMEM(a.shape, a.dtype) for a in outs],
             flops=work,
             moved=30 * 2**20,
             group=1,
@@ -1572,6 +1624,7 @@
                 pltpu.VMEM(quarters, BF),
                 pltpu.VMEM((4,) + quarter, BF),
                 pltpu.VMEM((3,) + quarter, BF),
+                pltpu.VMEM(expert_pack.shape, BF),
                 pltpu.SemaphoreType.DMA((2,)),
                 pltpu.SemaphoreType.DMA((11,)),
                 pltpu.SemaphoreType.DMA((11,)),
@@ -1631,7 +1684,7 @@
             + [rows_out] * 3
             + [shape(bank_z), shape(bank_z), shape(bank_x)],
             [SMEM] + [ANY] * (len(late) + 5),
-            [VMEM] * 7 + [ANY] * 6,
+            [ANY] * 6 + [VMEM] + [ANY] * 6,
             scratch
             + [pltpu.VMEM(a.shape, a.dtype) for a in late]
             + [
@@ -1639,9 +1692,11 @@
                 pltpu.VMEM((1,) + expert_pack.shape, BF),
                 pltpu.SemaphoreType.DMA((2,)),
                 pltpu.SemaphoreType.DMA((len(late),)),
+                pltpu.SemaphoreType.DMA((6,)),
                 pltpu.SemaphoreType.DMA((12,)),
                 pltpu.SemaphoreType.DMA((12,)),
-            ],
+            ]
+            + [pltpu.VMEM(a.shape, a.dtype) for a in outs],
             flops=work,
             moved=40 * 2**20,
             group=5,
@@ -1679,8 +1734,8 @@
                 pltpu.VMEM((tokens, 128), F32),
                 pltpu.VMEM((tokens, width), F32),
                 pltpu.SemaphoreType.DMA((9,)),
-                pltpu.SemaphoreType.DMA((30,)),
-                pltpu.SemaphoreType.DMA((30,)),
+                pltpu.SemaphoreType.DMA((32,)),
+                pltpu.SemaphoreType.DMA((32,)),
             ],
             flops=2 * tokens * width * (6 * width + 4 * CAP),
             moved=40 * 2**20,

time: 540 us -> 499 us (0.924)
  Pallas kernels: 511 us -> 470 us
    pallas_call x1, Pallas kernels: 110 us -> 96.8 us  [body(): call(back_kernel, outs + [shape(expert_pack.shape)] + [rows_out] * 3 + [s...]
    pallas_call x1, Pallas kernels: 71 us -> 61.7 us  [body(): call(forward_kernel, outs + [shape((2, SLOTS) + my_half.shape), shape((SL...]
    pallas_call x1, Pallas kernels: 67.3 us -> 59.6 us  [body(): call(tail_kernel, [wide, token_f, shape((4, rows, width), F32), shape((16...]
    pallas_call x1, Pallas kernels: 74.4 us -> 68.7 us  [body(): call(near_kernel, [rows_out] * 2 + [rows_back, shape(quarter), bank] + [r...]
where the time goes in v7:
time: 499 us; the launch traced here: 490 us
  Pallas kernels  470 us (94%)
  local copies, waits for them, and re-layouts  11.6 us (2%)
  other arithmetic  6.87 us (1%)
    pallas_call x1, Pallas kernels, body(): call(back_kernel, outs + [shape(expert_pack.shape)] + [rows_out] * 3 + [s...  96.8 us
    pallas_call x1, Pallas kernels, body(): call(near_kernel, [rows_out] * 2 + [rows_back, shape(quarter), bank] + [r...  68.7 us
    pallas_call x1, Pallas kernels, body(): call(far_kernel, [rows_out] * 2 + [rows_back] * 2 + [bank, shape(quarters...  65.8 us
    pallas_call x1, Pallas kernels, body(): call(forward_kernel, outs + [shape((2, SLOTS) + my_half.shape), shape((SL...  61.7 us
    pallas_call x1, Pallas kernels, body(): call(tail_kernel, [wide, token_f, shape((4, rows, width), F32), shape((16...  59.6 us
    pallas_call x1, Pallas kernels, body(): call(head_kernel, firsts + packed[1:] + [shape((SLOTS,) + expert_pack.sha...  58.7 us
    pallas_call x1, Pallas kernels, body(): call(shared_kernel, [token_f] * 2 + [half_grads] * 3 + packed[:3] + [shap...  50.5 us

profile of v7, /device:TPU:0, one launch (start us, length us, event | category | flops | bytes accessed | tf_op | source)
XLA Modules:
  0.0 490.2 jit_solution(10304261273269926375)
XLA Ops:
  0.6 0.0 copy-start
  0.7 1.3 copy.38
  2.0 1.9 fusion.1.shared_piece.piece
  3.9 1.2 constant_dynamic-slice_fusion.1
  5.0 0.0 copy-done
  5.1 0.0 copy-start.6
  5.1 0.0 copy-start.7
  5.1 0.0 copy-start.8
  5.1 0.2 copy.36
  5.3 1.1 pad_maximum_fusion.expert_piece
  6.4 0.0 copy-done.6
  6.4 0.0 copy-done.7
  6.4 0.0 copy-done.8
  6.5 0.2 dynamic_update_slice.3.small
  6.7 0.0 copy-start.4
  6.7 2.0 fusion.4
  8.6 0.0 copy-start.5
  8.7 1.8 pad_maximum_fusion.1
  10.5 0.0 copy-done.4
  10.5 0.0 copy-done.5
  10.5 1.0 copy.37.routes
  11.5 58.7 %shard_map.280 = (f32[8,1024]{1,0:T(8,128)}, f32[1024,128]{1,0:T(8,128)}, bf16[1024,768]{1,0:T(8,128)(2,1)}, bf16[1024,768]{1,0:T(8,128)(2,1)}, bf16[1024,768]{1...) custom-call(s32[1024,2]{1,0:T(8,128)} %copy.37.routes, ...), custom_call_target="tpu_custom_call" | custom-call | flops 7247757312 | bytes 25165824 | tf_op jit(solution)/shard_map/pallas_call | solution.py:1519
  70.3 61.7 %shard_map.281 = (bf16[1024,768]{1,0:T(8,128)(2,1)}, f32[1024,768]{1,0:T(8,128)}, f32[1024,768]{1,0:T(8,128)}, bf16[1024,768]{1,0:T(8,128)(2,1)}, f32[1024,128]{...) custom-call(s32[1,2]{1,0:T(1,128)} %starts.3, ...), custom_call_target="tpu_custom_call", output_to_operand_aliasing={{10}: (10, {})} | custom-call | flops 17716740096 | bytes 31457280 | tf_op jit(solution)/shard_map/pallas_call | solution.py:1554
  131.9 50.5 %shard_map.282 = (bf16[1024,768]{1,0:T(8,128)(2,1)}, bf16[1024,768]{1,0:T(8,128)(2,1)}, bf16[8,3,768,128]{3,2,1,0:T(8,128)(2,1)}, bf16[8,3,768,128]{3,2,1,0:T(8,...) custom-call(bf16[1024,768]{1,0:T(8,128)(2,1)} %get-tuple-element.105, ...), custom_call_target="tpu_custom_call", output_to_operand_aliasing={{8}: (7, {})} | custom-call | flops 28991029248 | bytes 31457280 | tf_op jit(solution)/shard_map/pallas_call | solution.py:1581
  182.4 65.8 %shard_map.283 = (bf16[576,768]{1,0:T(8,128)(2,1)}, bf16[576,768]{1,0:T(8,128)(2,1)}, bf16[592,768]{1,0:T(8,128)(2,1)}, bf16[592,768]{1,0:T(8,128)(2,1)}, bf16[8...) custom-call(f32[16,768]{1,0:T(8,128)} %get-tuple-element.96.ext.refs, ...), custom_call_target="tpu_custom_call", output_to_operand_aliasing={{7}: (8, {})} | custom-call | flops 32614907904 | bytes 31457280 | tf_op jit(solution)/shard_map/pallas_call | solution.py:1597
  248.2 68.7 %shard_map.284 = (bf16[576,768]{1,0:T(8,128)(2,1)}, bf16[576,768]{1,0:T(8,128)(2,1)}, bf16[592,768]{1,0:T(8,128)(2,1)}, bf16[3,384,128]{2,1,0:T(8,128)(2,1)}, bf...) custom-call(f32[16,768]{1,0:T(8,128)} %get-tuple-element.96.ext.refs, ...), custom_call_target="tpu_custom_call" | custom-call | flops 32614907904 | bytes 31457280 | tf_op jit(solution)/shard_map/pallas_call | solution.py:1616
  316.9 96.8 %shard_map.285 = (f32[1024,768]{1,0:T(8,128)}, bf16[768,768]{1,0:T(8,128)(2,1)}, f32[16,768]{1,0:T(8,128)}, bf16[1024,768]{1,0:T(8,128)(2,1)}, bf16[1024,768]{1,...) custom-call(s32[1,2]{1,0:T(1,128)} %starts.3, ...), custom_call_target="tpu_custom_call", output_to_operand_aliasing={{12}: (24, {})} | custom-call | flops 38252052480 | bytes 41943040 | tf_op jit(solution)/shard_map/pallas_call | solution.py:1680
  413.7 59.6 %shard_map.286 = (f32[1024,768]{1,0:T(8,128)}, bf16[1024,768]{1,0:T(8,128)(2,1)}, f32[4,96,768]{2,1,0:T(8,128)}, f32[16,768]{1,0:T(8,128)}, bf16[3,384,128]{2,1,...) custom-call(bf16[1024,768]{1,0:T(8,128)(2,1)} %bitcast.42, ...), custom_call_target="tpu_custom_call" | custom-call | flops 10871635968 | bytes 41943040 | tf_op jit(solution)/shard_map/pallas_call | solution.py:1708
  473.3 0.0 copy-start.3
  473.3 8.7 %shard_map.287 = (f32[4,768,256]{2,1,0:T(8,128)}, f32[4,768,256]{2,1,0:T(8,128)}, f32[4,256,768]{2,1,0:T(8,128)}, f32[768,256]{1,0:T(8,128)}, f32[768,256]{1,0:T...) custom-call(bf16[3,768,256]{2,1,0:T(8,128)(2,1)} %get-tuple-element., ...), custom_call_target="tpu_custom_call" | custom-call | bytes 18874368 | tf_op jit(solution)/shard_map/pallas_call | solution.py:1747
  482.1 1.4 dynamic-slice_bitcast_fusion.1
  483.4 1.3 dynamic-slice_bitcast_fusion
  484.8 0.0 copy-done.3
  484.8 0.0 copy-start.2
  484.8 1.1 copy.46
  485.9 1.3 copy-done.2
  487.2 0.0 copy-start.1
  487.2 1.7 copy.47
  488.9 0.9 copy-done.1
  (4 shorter events, 0.1 us)
Async XLA Ops:
  0.6 4.4 copy-start
  5.1 1.4 copy-start.6
  5.1 1.3 copy-start.7
  5.1 1.3 copy-start.8
  6.7 3.9 copy-start.4
  8.6 1.9 copy-start.5
  473.3 11.5 %copy-start.3 = (bf16[1024,768]{1,0:T(8,128)(2,1)S(1)}, bf16[1024,768]{1,0:T(8,128)(2,1)}, u32[]{:S(2)}) copy-start(bf16[1024,768]{1,0:T(8,128)(2,1)} %get-tuple-element.157) | copy-start | bytes 4718596
  484.8 2.5 copy-start.2
  487.2 2.5 copy-start.1

commit v8 on v7

--- a/solution.py
+++ b/solution.py
@@ -2,6 +2,7 @@
 
 import jax
 import jax.numpy as jnp
+import numpy as np
 from jax import lax
 from jax.experimental import pallas as pl
 from jax.experimental.pallas import tpu as pltpu
@@ -348,16 +349,32 @@
 
 
 def head_kernel(
-    routes, routes_t, cot, x, wq_in, wk_in, wv_in, wo_in, small, cosine, sine, expert_piece,
+    routes, routes_t, cot, x, wq_in, wk_in, wv_in, wo_in, small, cosine, sine,
+    e_gate, e_up, e_down, s_gate, s_up, s_down,
     *refs,
 ):
     width = x.shape[1]
     half = width // SLOTS
-    outs, (c1, c2, c3, experts) = refs[:11], refs[11:15]
-    bank, packed, piece, out_sems, send, recv, own_sem = refs[15:22]
-    rank, slot, q, k, v, wq, wk, wv, wo, ext, c0 = refs[22:]
-    stores = copies_of(zip(refs[22:], outs), out_sems)
+    outs, (c1, c2, c3, experts) = refs[:13], refs[13:17]
+    bank, packed, piece, e_raw, s_raw, pack_sems, out_sems, send, recv, own_sem = refs[17:27]
+    rank, slot, q, k, v, wq, wk, wv, wo, ext, c0, expert_piece, shared_piece = refs[27:]
+    stores = copies_of(zip(refs[27:], outs), out_sems)
     net = Net(send, recv)
+    units = s_raw.shape[0]
+    cut = pl.ds(pl.multiple_of(net.core * units, 128), units)
+    packs = copies_of(
+        (
+            (e_gate.at[net.rep], expert_piece.at[0]),
+            (e_up.at[net.rep], expert_piece.at[1]),
+            (e_down.at[net.rep], e_raw),
+            (s_gate.at[:, cut], shared_piece.at[0]),
+            (s_up.at[:, cut], shared_piece.at[1]),
+            (s_down.at[cut, :], s_raw),
+        ),
+        pack_sems,
+    )
+    for copy in packs:
+        copy.start()
     for core, (low, high) in enumerate(((wq_in, wk_in), (wv_in, wo_in))):
 
         @pl.when(net.core == core)
@@ -381,6 +398,10 @@
         net.put(events[o - 1], packed.at[o - 1], far, net.cousins[o], net.shard)
     arrivals = [(events[0], c1), (events[1], c2), (events[2], c3)]
     pack_row(net.rep, rank, cot, 0, c0)
+    for copy in packs:
+        copy.wait()
+    expert_piece[2] = e_raw[...].astype(F32).T.astype(BF)
+    shared_piece[2] = s_raw[...].astype(F32).T.astype(BF)
     line.along(1)
     line.along(-1)
     line.over(0)
@@ -609,7 +630,7 @@
     expert, ext, xs, cs, source, target, before, unit, outs, dxs, scratch, ready=None,
     emit=None,
 ):
-    out_acc, dx_acc, gate, wbuf, dw_acc, dw_out, in_sems, out_sems = scratch[:8]
+    out_acc, dx_acc, gate, wbuf, stage, dw_out, in_sems, out_sems, xc = scratch[:9]
     routed = expert is not None
     blocks, rows = len(xs), xs[0].shape[0]
     per = CHUNK // unit
@@ -638,10 +659,13 @@
         for copy in loads(source, wbuf, in_sems, k, b):
             copy.start()
         if before is not None:
-            for copy in loads(before, scratch[8], scratch[9], k, b):
+            for copy in loads(before, scratch[9], scratch[10], k, b):
                 copy.start()
 
     start_loads(0, 0)
+    for n in range(blocks):
+        xc[0, n * rows : (n + 1) * rows, :] = xs[n][...]
+        xc[1, n * rows : (n + 1) * rows, :] = cs[n][...]
     if routed:
         router = router_rows(ext)
         for n in range(blocks):
@@ -657,7 +681,7 @@
             x, c = xs[n][...], cs[n][...]
             wg, wu, wd = wbuf[b, 0], wbuf[b, 1], wbuf[b, 2]
             gate_h, up_h, back_h = nn(x, wg), nn(x, wu), nn(c, wd)
-            sigma = 1.0 / (1.0 + jnp.exp(-gate_h))
+            sigma = 0.5 * jnp.tanh(0.5 * gate_h) + 0.5
             silu = gate_h * sigma
             hidden = silu * up_h
             if routed:
@@ -670,7 +694,10 @@
             d_gate = (scaled * up_h * (sigma + silu * (1.0 - sigma))).astype(BF)
             product = nt(hidden.astype(BF), wd)
             d_rows = nt(d_gate, wg) + nt(d_up, wu)
-            parts = (tn(x, d_gate), tn(x, d_up), tn(c, weighted))
+            at = slice(n * rows, (n + 1) * rows)
+            stage[0, at, :] = d_gate
+            stage[1, at, :] = d_up
+            stage[2, at, :] = weighted
             if routed:
                 pairs = (hidden * back_h).astype(BF)
                 d_share = nt(jnp.ones((16, CHUNK), BF), pairs)
@@ -690,12 +717,6 @@
                 if routed:
                     dx_acc[n, rows : rows + 16, 0:rows] += d_share
 
-            for i in range(3):
-                if n == 0:
-                    dw_acc[i] = parts[i]
-                else:
-                    dw_acc[i] += parts[i]
-
         for nxt in range(1, CHUNKS):
 
             @pl.when(k + 1 == nxt)
@@ -708,13 +729,13 @@
                 copy.wait()
 
         if before is not None:
-            for copy in loads(before, scratch[8], scratch[9], 0, b):
+            for copy in loads(before, scratch[9], scratch[10], 0, b):
                 copy.wait()
-            for i in range(3):
-                dw_out[b, i] = (dw_acc[i] + scratch[8][b, i].astype(F32)).astype(BF)
-        else:
-            for i in range(3):
-                dw_out[b, i] = dw_acc[i].astype(BF)
+        for i in range(3):
+            part = tn(xc[i // 2], stage[i])
+            if before is not None:
+                part = part + scratch[9][b, i].astype(F32)
+            dw_out[b, i] = part.astype(BF)
         for now in range(CHUNKS):
 
             @pl.when(k == now)
@@ -741,10 +762,11 @@
         pltpu.VMEM((blocks, rows + extra, width), F32),
         pltpu.VMEM((blocks, rows, 1), F32),
         pltpu.VMEM((2, 3, width, CHUNK), BF),
-        pltpu.VMEM((3, width, CHUNK), F32),
+        pltpu.VMEM((3, blocks * rows, CHUNK), BF),
         pltpu.VMEM((2, 3, width, CHUNK), BF),
         pltpu.SemaphoreType.DMA((2, per)),
         pltpu.SemaphoreType.DMA((2, per)),
+        pltpu.VMEM((2, blocks * rows, width), BF),
     ]
     if chained:
         scratch += [
@@ -1418,52 +1440,66 @@
 
 
 def finish_kernel(
-    e0, e1, e2, e3, q0, q1, q2, q3, weights,
-    gate, up, down, s_gate, s_up, s_down, grad_q, grad_k, grad_v, grad_o,
-    part, ready_gate, ready_up, ready_down, in_sems, out_sems,
+    e0, e1, e2, e3, wide, plain, q0, q1, q2, q3, weights, small,
+    gate, up, down, wide_out, plain_out, s_gate, s_up, s_down,
+    grad_q, grad_k, grad_v, grad_o, gain_one, gain_two, grad_router,
+    part, wide_in, plain_in, ready_gate, ready_up, ready_down, in_sems, out_sems,
 ):
-    rep = lax.axis_index("rep")
-    loads = copies_of([(e, part.at[o]) for o, e in enumerate((e0, e1, e2, e3))], in_sems)
+    rep, shard = lax.axis_index("rep"), lax.axis_index("shard")
+    pairs = [(e, part.at[o]) for o, e in enumerate((e0, e1, e2, e3))]
+    loads = copies_of(pairs + [(wide, wide_in), (plain, plain_in)], in_sems)
     for copy in loads:
         copy.start()
     stores = []
     for o in range(4):
         at = sibling(rep, o)
-        pairs = ((ready_gate, gate), (ready_up, up), (ready_down, down))
-        stores.append(copies_of([(a.at[o], b.at[at]) for a, b in pairs], out_sems.at[o]))
+        pairs = [(ready_gate.at[o], gate.at[at]), (ready_up.at[o], up.at[at])]
+        pairs.append((ready_down.at[o], down.at[at]))
         loads[o].wait()
         ready_gate[o] = part[o, 0].astype(F32)
         ready_up[o] = part[o, 1].astype(F32)
         ready_down[o] = part[o, 2].astype(F32).T
-        for copy in stores[o]:
+        made = [pltpu.make_async_copy(a, b, out_sems.at[3 * o + i]) for i, (a, b) in enumerate(pairs)]
+        for copy in made:
             copy.start()
+        stores += made
+    passed = ((wide_in, wide_out), (plain_in, plain_out))
+    for i, (a, b) in enumerate(passed):
+        loads[4 + i].wait()
+        copy = pltpu.make_async_copy(a, b, out_sems.at[12 + i])
+        copy.start()
+        stores.append(copy)
     quarter, span = q0.shape[1:]
     for o, piece in enumerate((q0, q1, q2, q3)):
-        for other in range(4):
-
-            @pl.when(sibling(rep, o) == other)
-            def _():
-                rows = slice(other // 2 * quarter, (other // 2 + 1) * quarter)
-                cols = slice(other % 2 * span, (other % 2 + 1) * span)
-                s_gate[rows, cols] = piece[0].astype(F32)
-                s_up[rows, cols] = piece[1].astype(F32)
-                s_down[cols, rows] = piece[2].astype(F32).T
-
+        owner = sibling(rep, o)
+        rows = pl.ds(pl.multiple_of(lax.div(owner, 2) * quarter, 128), quarter)
+        cols = pl.ds(pl.multiple_of(lax.rem(owner, 2) * span, 128), span)
+        s_gate[rows, cols] = piece[0].astype(F32)
+        s_up[rows, cols] = piece[1].astype(F32)
+        s_down[cols, rows] = piece[2].astype(F32).T
     for i, out in enumerate((grad_q, grad_k, grad_v, grad_o)):
         out[...] = weights[i]
-    for copies in stores:
-        for copy in copies:
-            copy.wait()
+    rows, width = weights.shape[1:]
+    tiny = small[...].astype(BF)
+    pick = ones_where(iota((width, rows), 0) == iota((width, rows), 1) + shard * rows)
+    gains = nn(tiny, pick)
+    gain_one[...] = gains[4:5, :]
+    gain_two[...] = gains[5:6, :]
+    grad_router[...] = dot(pick, tiny, 0, 1)[:, 0:4]
+    for copy in stores:
+        copy.wait()
 
 
 def rope_tables(length, head_dim):
-    positions = jnp.arange(length, dtype=F32)
-    inverse_freq = 10000.0 ** (-2.0 * jnp.arange(head_dim // 2, dtype=F32) / head_dim)
+    positions = np.arange(length, dtype=np.float32)
+    inverse_freq = np.float32(10000.0) ** (
+        np.float32(-2.0) * np.arange(head_dim // 2, dtype=np.float32) / np.float32(head_dim)
+    )
     angle = positions[:, None] * inverse_freq[None, :]
-    cosine, sine = jnp.cos(angle), jnp.sin(angle)
+    cosine, sine = np.cos(angle), np.sin(angle)
     return (
-        jnp.concatenate([cosine] * 4, axis=1),
-        jnp.concatenate([-sine, sine, -sine, sine], axis=1),
+        jnp.asarray(np.concatenate([cosine] * 4, axis=1)),
+        jnp.asarray(np.concatenate([-sine, sine, -sine, sine], axis=1)),
     )
 
 
@@ -1503,10 +1539,9 @@
             for w in (query_weight, key_weight, value_weight, out_weight)
         ]
         ext = lax.psum(small.astype(F32), "shard")
-
-    shared_pack = jnp.stack([shared_gate, shared_up, shared_down.T])
-    my_half = lax.dynamic_slice_in_dim(shared_pack, core * (units // 2), units // 2, 2)
-    expert_pack = jnp.stack([expert_gate[rep], expert_up[rep], expert_down[rep].T])
+        shared_pack = jnp.stack([shared_gate, shared_up, shared_down.T])
+        my_half = lax.dynamic_slice_in_dim(shared_pack, core * (units // 2), units // 2, 2)
+        expert_pack = jnp.stack([expert_gate[rep], expert_up[rep], expert_down[rep].T])
 
     cosine, sine = rope_tables(tokens, width // HEADS)
     token_f = shape((tokens, width))
@@ -1515,17 +1550,22 @@
     outs = [shape((8, tokens), F32), shape((tokens, 128), F32)] + [token_f] * 3
     work = 2 * tokens * width * (CAP * 4 + 3 * width)
     if ringed:
+        expert_shape, half_shape = shape((3, width, units)), shape((3, width, units // 2))
         firsts = outs + [square] * 4 + [shape((16, width), F32), packed[0]]
-        rank, slot, q, k, v, *heads = call(
+        firsts += [expert_shape, half_shape]
+        rank, slot, q, k, v, wq, wk, wv, wo, ext, cot_own, expert_pack, my_half, *heads = call(
             head_kernel,
-            firsts + packed[1:] + [shape((SLOTS,) + expert_pack.shape)],
-            [VMEM] * 11 + [ANY],
-            [ANY] * 15,
+            firsts + packed[1:] + [shape((SLOTS,) + expert_shape.shape)],
+            [VMEM] * 11 + [ANY] * 6,
+            [ANY] * 17,
             [
                 pltpu.VMEM((2, SLOTS, 2 * rows + 16, width), BF),
                 pltpu.VMEM((3, CAP, width), BF),
                 pltpu.VMEM((2 * rows + 16, width), BF),
-                pltpu.SemaphoreType.DMA((11,)),
+                pltpu.VMEM((units, width), BF),
+                pltpu.VMEM((units // 2, width), BF),
+                pltpu.SemaphoreType.DMA((6,)),
+                pltpu.SemaphoreType.DMA((13,)),
                 pltpu.SemaphoreType.DMA((34,)),
                 pltpu.SemaphoreType.DMA((34,)),
                 pltpu.SemaphoreType.DMA,
@@ -1536,9 +1576,10 @@
             group=0,
         )(
             chosen, chosen.T, cot, x, query_weight, key_weight, value_weight, out_weight, small,
-            cosine, sine, expert_pack,
+            cosine, sine, expert_gate, expert_up, expert_down, shared_gate, shared_up, shared_down,
         )
-        wq, wk, wv, wo, ext, *cot_in, expert_bank = heads
+        *cot_in, expert_bank = heads
+        cot_in = [cot_own, *cot_in]
     else:
         rank, slot, q, k, v, *cot_out = call(
             plain_head_kernel, outs + packed, [VMEM] * 10, [VMEM] * 9, flops=work,
@@ -1744,18 +1785,26 @@
         banks = [shape((4, width, units), F32)] * 2 + [shape((4, units, width), F32)]
         banks += [shape((width, units), F32)] * 2 + [shape((units, width), F32)]
         shared_far, shared_mate, shared_cross, *experts = rest
-        *finals, grad_q, grad_k, grad_v, grad_o = call(
+        *finals, grad_q, grad_k, grad_v, grad_o, gain_one, gain_two, grad_router = call(
             finish_kernel,
-            banks + [shape((rows, width), F32)] * 4,
-            [ANY] * 4 + [VMEM] * 5,
-            [ANY] * 3 + [VMEM] * 7,
-            [pltpu.VMEM((4,) + expert_pack.shape, BF)]
+            banks[:3] + [wide, token_f] + banks[3:] + [shape((rows, width), F32)] * 4
+            + [shape((1, rows), F32)] * 2 + [shape((rows, 4), F32)],
+            [ANY] * 6 + [VMEM] * 6,
+            [ANY] * 5 + [VMEM] * 10,
+            [
+                pltpu.VMEM((4,) + expert_pack.shape, BF),
+                pltpu.VMEM((tokens, width), F32),
+                pltpu.VMEM((tokens, width), BF),
+            ]
             + [pltpu.VMEM(b.shape, F32) for b in banks[:3]]
-            + [pltpu.SemaphoreType.DMA((4,)), pltpu.SemaphoreType.DMA((4, 3))],
-            moved=18 * 2**20,
+            + [pltpu.SemaphoreType.DMA((6,)), pltpu.SemaphoreType.DMA((14,))],
+            moved=26 * 2**20,
         )(
-            expert_total, *experts, shared_total, shared_mate, shared_far, shared_cross, weights
+            expert_total, *experts, grad_in, outputs,
+            shared_total, shared_mate, shared_far, shared_cross, weights, small,
         )
+        grad_in, outputs = finals.pop(3), finals.pop(3)
+        gain_one, gain_two = gain_one[0], gain_two[0]
     else:
         d_middle, grad_wo, grad_ext, dq, dk, dv = call(
             plain_back_kernel, outs, specs + [VMEM] * 4, [VMEM] * 6, scratch, flops=work,
@@ -1800,17 +1849,18 @@
         full = jnp.take(parts, jnp.arange(4) ^ rep, axis=0).astype(F32)
         finals = (full[:, 0], full[:, 1], full[:, 2].transpose(0, 2, 1))
         finals += (shared_full[0], shared_full[1], shared_full[2].T)
-    tiny = lax.dynamic_slice(small, (0, shard * rows), (16, rows))
+        tiny = lax.dynamic_slice(small, (0, shard * rows), (16, rows))
+        gain_one, gain_two, grad_router = tiny[4], tiny[5], tiny[:4].T
     return (
         outputs[None],
         grad_in[None],
-        tiny[4],
+        gain_one,
         grad_q,
         grad_k,
         grad_v,
         grad_o,
-        tiny[5],
-        tiny[:4].T,
+        gain_two,
+        grad_router,
         *finals,
     )
 

time: 499 us -> 471 us (0.944)
  Pallas kernels: 470 us -> 459 us
  local copies, waits for them, and re-layouts: 11.6 us -> 3.36 us
  other arithmetic: 6.87 us -> 0.72 us
    pallas_call x1, Pallas kernels: 50.5 us -> 45.1 us  [body(): call(shared_kernel, [token_f] * 2 + [half_grads] * 3 + packed[:3] + [shap...]
    pallas_call x1, Pallas kernels: 68.7 us -> 63.7 us  [body(): call(near_kernel, [rows_out] * 2 + [rows_back, shape(quarter), bank] + [r...]
where the time goes in v8:
time: 471 us; the launch traced here: 465 us
  Pallas kernels  459 us (97%)
    pallas_call x1, Pallas kernels, body(): call(back_kernel, outs + [shape(expert_pack.shape)] + [rows_out] * 3 + [s...  97.3 us
    pallas_call x1, Pallas kernels, body(): call(near_kernel, [rows_out] * 2 + [rows_back, shape(quarter), bank] + [r...  63.7 us
    pallas_call x1, Pallas kernels, body(): call(forward_kernel, outs + [shape((2, SLOTS) + my_half.shape), shape((SL...  61.7 us
    pallas_call x1, Pallas kernels, body(): call(far_kernel, [rows_out] * 2 + [rows_back] * 2 + [bank, shape(quarters...  61.4 us
    pallas_call x1, Pallas kernels, body(): call(tail_kernel, [wide, token_f, shape((4, rows, width), F32), shape((16...  59.7 us
    pallas_call x1, Pallas kernels, body(): call(head_kernel, firsts + packed[1:] + [shape((SLOTS,) + expert_shape.sh...  58.8 us
    pallas_call x1, Pallas kernels, body(): call(shared_kernel, [token_f] * 2 + [half_grads] * 3 + packed[:3] + [shap...  45.1 us
    pallas_call x1, Pallas kernels, body(): call(finish_kernel, banks[:3] + [wide, token_f] + banks[3:] + [shape((row...  11.7 us

profile of v8, /device:TPU:0, one launch (start us, length us, event | category | flops | bytes accessed | tf_op | source)
XLA Modules:
  0.0 464.5 jit_solution(10020550677482650777)
XLA Ops:
  0.6 0.7 fusion.4
  1.4 0.2 dynamic_update_slice.3.small
  1.6 0.0 copy-start
  1.6 1.7 copy.38.routes
  3.3 0.0 copy-done
  3.3 58.8 %shard_map.298 = (f32[8,1024]{1,0:T(8,128)}, f32[1024,128]{1,0:T(8,128)}, bf16[1024,768]{1,0:T(8,128)(2,1)}, bf16[1024,768]{1,0:T(8,128)(2,1)}, bf16[1024,768]{1...) custom-call(s32[1024,2]{1,0:T(8,128)} %copy.38.routes, ...), custom_call_target="tpu_custom_call" | custom-call | flops 7247757312 | bytes 25165824 | tf_op jit(solution)/shard_map/pallas_call | solution.py:1556
  62.1 61.7 %shard_map.299 = (bf16[1024,768]{1,0:T(8,128)(2,1)}, f32[1024,768]{1,0:T(8,128)}, f32[1024,768]{1,0:T(8,128)}, bf16[1024,768]{1,0:T(8,128)(2,1)}, f32[1024,128]{...) custom-call(s32[1,2]{1,0:T(1,128)} %starts.3, ...), custom_call_target="tpu_custom_call", output_to_operand_aliasing={{10}: (10, {})} | custom-call | flops 17716740096 | bytes 31457280 | tf_op jit(solution)/shard_map/pallas_call | solution.py:1595
  123.8 45.1 %shard_map.300 = (bf16[1024,768]{1,0:T(8,128)(2,1)}, bf16[1024,768]{1,0:T(8,128)(2,1)}, bf16[8,3,768,128]{3,2,1,0:T(8,128)(2,1)}, bf16[8,3,768,128]{3,2,1,0:T(8,...) custom-call(bf16[1024,768]{1,0:T(8,128)(2,1)} %get-tuple-element.114, ...), custom_call_target="tpu_custom_call", output_to_operand_aliasing={{8}: (7, {})} | custom-call | flops 28991029248 | bytes 31457280 | tf_op jit(solution)/shard_map/pallas_call | solution.py:1622
  168.9 61.4 %shard_map.301 = (bf16[576,768]{1,0:T(8,128)(2,1)}, bf16[576,768]{1,0:T(8,128)(2,1)}, bf16[592,768]{1,0:T(8,128)(2,1)}, bf16[592,768]{1,0:T(8,128)(2,1)}, bf16[8...) custom-call(f32[16,768]{1,0:T(8,128)} %get-tuple-element.104.ext.ref, ...), custom_call_target="tpu_custom_call", output_to_operand_aliasing={{7}: (8, {})} | custom-call | flops 32614907904 | bytes 31457280 | tf_op jit(solution)/shard_map/pallas_call | solution.py:1638
  230.3 63.7 %shard_map.302 = (bf16[576,768]{1,0:T(8,128)(2,1)}, bf16[576,768]{1,0:T(8,128)(2,1)}, bf16[592,768]{1,0:T(8,128)(2,1)}, bf16[3,384,128]{2,1,0:T(8,128)(2,1)}, bf...) custom-call(f32[16,768]{1,0:T(8,128)} %get-tuple-element.104.ext.ref, ...), custom_call_target="tpu_custom_call" | custom-call | flops 32614907904 | bytes 31457280 | tf_op jit(solution)/shard_map/pallas_call | solution.py:1657
  294.0 97.3 %shard_map.303 = (f32[1024,768]{1,0:T(8,128)}, bf16[768,768]{1,0:T(8,128)(2,1)}, f32[16,768]{1,0:T(8,128)}, bf16[1024,768]{1,0:T(8,128)(2,1)}, bf16[1024,768]{1,...) custom-call(s32[1,2]{1,0:T(1,128)} %starts.3, ...), custom_call_target="tpu_custom_call", output_to_operand_aliasing={{12}: (24, {})} | custom-call | flops 38252052480 | bytes 41943040 | tf_op jit(solution)/shard_map/pallas_call | solution.py:1721
  391.3 59.7 %shard_map.304 = (f32[1024,768]{1,0:T(8,128)}, bf16[1024,768]{1,0:T(8,128)(2,1)}, f32[4,96,768]{2,1,0:T(8,128)}, f32[16,768]{1,0:T(8,128)}, bf16[3,384,128]{2,1,...) custom-call(bf16[1024,768]{1,0:T(8,128)(2,1)} %bitcast.23, ...), custom_call_target="tpu_custom_call" | custom-call | flops 10871635968 | bytes 41943040 | tf_op jit(solution)/shard_map/pallas_call | solution.py:1749
  451.0 11.7 %shard_map.305 = (f32[4,768,256]{2,1,0:T(8,128)}, f32[4,768,256]{2,1,0:T(8,128)}, f32[4,256,768]{2,1,0:T(8,128)}, f32[1024,768]{1,0:T(8,128)}, bf16[1024,768]{1,...) custom-call(bf16[3,768,256]{2,1,0:T(8,128)(2,1)} %get-tuple-element., ...), custom_call_target="tpu_custom_call" | custom-call | bytes 27262976 | tf_op jit(solution)/shard_map/pallas_call | solution.py:1788
  462.7 1.5 copy.39
  (1 shorter events, 0.0 us)
Async XLA Ops:
  1.6 1.7 copy-start

commit v9 on v8

--- a/solution.py
+++ b/solution.py
@@ -663,6 +663,8 @@
                 copy.start()
 
     start_loads(0, 0)
+    out_acc[...] = jnp.zeros_like(out_acc)
+    dx_acc[...] = jnp.zeros_like(dx_acc)
     for n in range(blocks):
         xc[0, n * rows : (n + 1) * rows, :] = xs[n][...]
         xc[1, n * rows : (n + 1) * rows, :] = cs[n][...]
@@ -702,20 +704,10 @@
                 pairs = (hidden * back_h).astype(BF)
                 d_share = nt(jnp.ones((16, CHUNK), BF), pairs)
 
-            @pl.when(k == 0)
-            def _():
-                out_acc[n] = product
-                dx_acc[n, 0:rows, :] = d_rows
-                if routed:
-                    dx_acc[n, rows : rows + 16, :] = jnp.zeros((16, d_rows.shape[1]), F32)
-                    dx_acc[n, rows : rows + 16, 0:rows] = d_share
-
-            @pl.when(k != 0)
-            def _():
-                out_acc[n] += product
-                dx_acc[n, 0:rows, :] += d_rows
-                if routed:
-                    dx_acc[n, rows : rows + 16, 0:rows] += d_share
+            out_acc[n] += product
+            dx_acc[n, 0:rows, :] += d_rows
+            if routed:
+                dx_acc[n, rows : rows + 16, 0:rows] += d_share
 
         for nxt in range(1, CHUNKS):
 
@@ -989,7 +981,7 @@
 
 def combine_rows(
     slot, d0, d1, d2, d3, d_shared, probs, middle, normed, cot, ext, attended, wo,
-    d_middle, d_attended, grad_wo, grad_ext, branch, router_acc, gain_acc,
+    d_middle, d_attended, grad_ext, branch, router_acc, gain_acc,
 ):
     tokens, width = middle.shape
     rep = lax.axis_index("rep")
@@ -1030,7 +1022,6 @@
         return carry
 
     lax.fori_loop(0, tokens // TILE, tile, 0)
-    grad_wo[...] = tn(attended[...], branch[...]).astype(BF)
     row = iota((16, width), 0)
     total = jnp.sum(gain_acc[...], axis=0, keepdims=True)
     grad_ext[...] = jnp.where(row < 4, router_acc[0:16, :], jnp.where(row == 5, total, 0.0))
@@ -1114,15 +1105,17 @@
 class Chain:
     def __init__(self, net, own, from_x, up_in, down_in, held, spare, sems):
         self.net, self.own, self.from_x = net, own, from_x
-        self.up_in, self.down_in = up_in, down_in
-        self.held, self.spare, self.sems = held, spare, sems
-        self.events = {(way, d): net.event() for way in range(2) for d in (1, 2, 3)}
+        self.into, self.held, self.spare, self.sems = (up_in, down_in), held, spare, sems
+        keys = [(way, d, m) for way in range(2) for d in (1, 2, 3) for m in range(3)]
+        self.events = {key: net.event() for key in keys}
         self.spots = [net.place(n, 0) for n in range(4)]
         self.sends, self.gets = {}, {}
         z = net.z
         for d in (1, 2, 3):
-            self.sends[0, d] = (held.at[lax.min(z + d, 3)], z < 4 - d)
-            self.sends[1, d] = (held.at[lax.max(z - d, 0)], z > d - 1)
+            up, down = lax.min(z + d, 3), lax.max(z - d, 0)
+            for m in range(3):
+                self.sends[0, d, m] = (held.at[up, m], z < 4 - d)
+                self.sends[1, d, m] = (held.at[down, m], z > d - 1)
             self.gets[0, d] = (lax.min(z + d - 1, 3), (z > 0) & (z < 5 - d))
             self.gets[1, d] = (lax.max(z - d + 1, 0), (z < 3) & (z > d - 2))
 
@@ -1132,23 +1125,24 @@
         fetch([self.own.at[self.spots[n]], far], [self.held.at[to], self.spare.at[0]], self.sems)
         self.held[to] = self.held[to] + self.spare[0]
 
-    def send(self, d):
+    def send(self, d, m):
         net = self.net
-        for way, to, into in ((0, net.up, self.up_in), (1, net.down, self.down_in)):
-            source, here = self.sends[way, d]
-            net.put(self.events[way, d], source, into.at[d - 1], net.rep, to, here)
-
-    def take(self, d):
-        for way, into in ((0, self.up_in), (1, self.down_in)):
+        for way, to in ((0, net.up), (1, net.down)):
+            source, here = self.sends[way, d, m]
+            target = self.into[way].at[d - 1, m]
+            net.put(self.events[way, d, m], source, target, net.rep, to, here)
+
+    def take(self, d, m):
+        net = self.net
+        for way in range(2):
             to, here = self.gets[way, d]
 
             def add():
-                self.net.copy(
-                    self.events[way, d], into.at[d - 1], into.at[d - 1],
-                    self.net.mate, self.net.shard,
-                ).wait_recv()
-                fetch([into.at[d - 1]], [self.spare.at[0]], self.sems)
-                self.held[to] = self.held[to] + self.spare[0]
+                source = self.into[way].at[d - 1, m]
+                event = self.events[way, d, m]
+                net.copy(event, source, source, net.mate, net.shard).wait_recv()
+                fetch([source], [self.spare.at[0, m]], self.sems)
+                self.held[to, m] = self.held[to, m] + self.spare[0, m]
 
             when(here, add)
 
@@ -1182,20 +1176,24 @@
         net.put(x_events[n], source, targets[n], net.rep, net.across)
     arrivals = exchange(net, (o1, o2, o3), (r1, r2, r3))
     chain.level(3)
-    chain.send(3)
+    for m in range(3):
+        chain.send(3, m)
     fill_bias(starts, bias)
     for copy in loads:
         copy.wait()
     combine_rows(
         slot, d0, d1, d2, d3, d_shared, probs, middle, normed, cot, ext, attended, wo,
-        d_middle, d_attended, grad_wo, grad_ext, branch, router_acc, gain_acc,
+        d_middle, d_attended, grad_ext, branch, router_acc, gain_acc,
     )
-    for copy in stores[:3]:
-        copy.start()
+    stores[0].start()
+    stores[2].start()
     net.got(x_events[2], targets[2])
     chain.level(2)
-    chain.take(3)
-    chain.send(2)
+    for m in range(3):
+        chain.take(3, m)
+        chain.send(2, m)
+    grad_wo[...] = tn(attended[...], branch[...]).astype(BF)
+    stores[1].start()
 
     def step(i):
         @pl.when(i == 3)
@@ -1205,8 +1203,9 @@
 
         @pl.when(i == 4)
         def _():
-            chain.take(2)
-            chain.send(1)
+            for m in range(3):
+                chain.take(2, m)
+                chain.send(1, m)
 
     back_pairs(
         q, k, v, d_attended, attended, lse, cosine, sine, dq, dk, dv, bias, dk_acc, dv_acc, step
@@ -1217,7 +1216,8 @@
     chain.level(0)
     for event, like in arrivals:
         net.got(event, like)
-    chain.take(1)
+    for m in range(3):
+        chain.take(1, m)
     expert_total[...] = held[net.z]
     for copy in stores:
         copy.wait()
@@ -1232,8 +1232,9 @@
 ):
     combine_rows(
         slot, d0, d1, d2, d3, d_shared, probs, middle, normed, cot, ext, attended, wo,
-        d_middle, d_attended, grad_wo, grad_ext, branch, router_acc, gain_acc,
+        d_middle, d_attended, grad_ext, branch, router_acc, gain_acc,
     )
+    grad_wo[...] = tn(attended[...], branch[...]).astype(BF)
     fill_bias(starts, bias)
     back_pairs(
         q, k, v, d_attended, attended, lse, cosine, sine, dq, dk, dv, bias, dk_acc, dv_acc,
@@ -1274,12 +1275,13 @@
 
 
 def tail_kernel(
-    x, ext, dq, dk, dv, wq, wk, wv, grad_wo, grad_ext,
+    x, ext, dq, dk_in, dv, wq_in, wk_in, wv_in, grad_wo_in, grad_ext,
     d_middle_in, slot_in, o0_in, o1_in, o2_in, o3_in, shared_in, probs_in, middle_in,
     expert_total, shared_total,
     grad_in, outputs, weights, small, shared_far, shared_mate, shared_cross, e1, e2, e3,
     normed_all, gain_acc, gw, from_mate, from_x, from_z, from_y, result, from_core,
-    tiny, tiny_in, d_middle, slot, o0, o1, o2, o3, shared_out, probs, middle, load_sems,
+    tiny, tiny_in, dk, grad_wo, wq, wk, wv,
+    d_middle, slot, o0, o1, o2, o3, shared_out, probs, middle, load_sems,
     send, recv,
 ):
     width = x.shape[1]
@@ -1302,6 +1304,7 @@
     net.put(e_events[1], expert_total, e2, far, net.shard)
     net.put(e_events[0], expert_total, e1, net.mate, net.shard)
     pairs = (
+        (dk_in, dk), (grad_wo_in, grad_wo), (wq_in, wq), (wk_in, wk), (wv_in, wv),
         (d_middle_in, d_middle), (slot_in, slot), (o0_in, o0), (o1_in, o1), (o2_in, o2),
         (o3_in, o3), (shared_in, shared_out), (probs_in, probs), (middle_in, middle),
     )
@@ -1330,13 +1333,15 @@
     gw[spots[0]] = tn(normed_all[...], dq[...]).astype(BF)
     gw[spots[2]] = tn(normed_all[...], dv[...]).astype(BF)
     hand(0)
+    loads[0].wait()
+    loads[1].wait()
     gw[spots[1]] = tn(normed_all[...], dk[...]).astype(BF)
     gw[spots[3]] = grad_wo[...]
     hand(1)
     cross(0)
     cross(1)
     gain_acc[...] = jnp.zeros_like(gain_acc)
-    for copy in loads:
+    for copy in loads[2:]:
         copy.wait()
     count = x.shape[0] // TILE
 
@@ -1734,8 +1739,8 @@
                 pltpu.SemaphoreType.DMA((2,)),
                 pltpu.SemaphoreType.DMA((len(late),)),
                 pltpu.SemaphoreType.DMA((6,)),
-                pltpu.SemaphoreType.DMA((12,)),
-                pltpu.SemaphoreType.DMA((12,)),
+                pltpu.SemaphoreType.DMA((24,)),
+                pltpu.SemaphoreType.DMA((24,)),
             ]
             + [pltpu.VMEM(a.shape, a.dtype) for a in outs],
             flops=work,
@@ -1751,7 +1756,7 @@
             [wide, token_f, shape((4, rows, width), F32), shape((16, width), F32)]
             + [shape(quarter)] * 3
             + [shape(expert_pack.shape)] * 3,
-            [VMEM] * 10 + [ANY] * 11,
+            [VMEM] * 3 + [ANY, VMEM] + [ANY] * 4 + [VMEM] + [ANY] * 11,
             [VMEM] * 4 + [ANY] * 6,
             [
                 pltpu.VMEM((tokens, width), BF),
@@ -1765,6 +1770,11 @@
                 pltpu.VMEM(strip, BF),
                 pltpu.VMEM((4, 16, width), BF),
                 pltpu.VMEM((6, 16, width), BF),
+                pltpu.VMEM((tokens, width), BF),
+                pltpu.VMEM((width, width), BF),
+                pltpu.VMEM((width, width), BF),
+                pltpu.VMEM((width, width), BF),
+                pltpu.VMEM((width, width), BF),
                 pltpu.VMEM((tokens, width), F32),
                 pltpu.VMEM((tokens, 128), F32),
                 pltpu.VMEM((CAP, width), BF),
@@ -1774,7 +1784,7 @@
                 pltpu.VMEM((tokens, width), BF),
                 pltpu.VMEM((tokens, 128), F32),
                 pltpu.VMEM((tokens, width), F32),
-                pltpu.SemaphoreType.DMA((9,)),
+                pltpu.SemaphoreType.DMA((14,)),
                 pltpu.SemaphoreType.DMA((32,)),
                 pltpu.SemaphoreType.DMA((32,)),
             ],

time: 471 us -> 468 us (level)
  no operation moved by 1% of the time
where the time goes in v9:
time: 468 us; the launch traced here: 461 us
  Pallas kernels  456 us (97%)
    pallas_call x1, Pallas kernels, body(): call(back_kernel, outs + [shape(expert_pack.shape)] + [rows_out] * 3 + [s...  97.2 us
    pallas_call x1, Pallas kernels, body(): call(near_kernel, [rows_out] * 2 + [rows_back, shape(quarter), bank] + [r...  62 us
    pallas_call x1, Pallas kernels, body(): call(forward_kernel, outs + [shape((2, SLOTS) + my_half.shape), shape((SL...  61.7 us
    pallas_call x1, Pallas kernels, body(): call(far_kernel, [rows_out] * 2 + [rows_back] * 2 + [bank, shape(quarters...  61.1 us
    pallas_call x1, Pallas kernels, body(): call(head_kernel, firsts + packed[1:] + [shape((SLOTS,) + expert_shape.sh...  58.8 us
    pallas_call x1, Pallas kernels, body(): call(tail_kernel, [wide, token_f, shape((4, rows, width), F32), shape((16...  58.7 us
    pallas_call x1, Pallas kernels, body(): call(shared_kernel, [token_f] * 2 + [half_grads] * 3 + packed[:3] + [shap...  44.9 us
    pallas_call x1, Pallas kernels, body(): call(finish_kernel, banks[:3] + [wide, token_f] + banks[3:] + [shape((row...  11.7 us

profile of v9, /device:TPU:0, one launch (start us, length us, event | category | flops | bytes accessed | tf_op | source)
XLA Modules:
  0.0 461.1 jit_solution(980122972682319807)
XLA Ops:
  0.6 0.7 fusion.4
  1.4 0.2 dynamic_update_slice.3.small
  1.6 0.0 copy-start
  1.6 1.7 copy.38.routes
  3.3 0.0 copy-done
  3.3 58.8 %shard_map.298 = (f32[8,1024]{1,0:T(8,128)}, f32[1024,128]{1,0:T(8,128)}, bf16[1024,768]{1,0:T(8,128)(2,1)}, bf16[1024,768]{1,0:T(8,128)(2,1)}, bf16[1024,768]{1...) custom-call(s32[1024,2]{1,0:T(8,128)} %copy.38.routes, ...), custom_call_target="tpu_custom_call" | custom-call | flops 7247757312 | bytes 25165824 | tf_op jit(solution)/shard_map/pallas_call | solution.py:1561
  62.1 61.7 %shard_map.299 = (bf16[1024,768]{1,0:T(8,128)(2,1)}, f32[1024,768]{1,0:T(8,128)}, f32[1024,768]{1,0:T(8,128)}, bf16[1024,768]{1,0:T(8,128)(2,1)}, f32[1024,128]{...) custom-call(s32[1,2]{1,0:T(1,128)} %starts.3, ...), custom_call_target="tpu_custom_call", output_to_operand_aliasing={{10}: (10, {})} | custom-call | flops 17716740096 | bytes 31457280 | tf_op jit(solution)/shard_map/pallas_call | solution.py:1600
  123.8 44.9 %shard_map.300 = (bf16[1024,768]{1,0:T(8,128)(2,1)}, bf16[1024,768]{1,0:T(8,128)(2,1)}, bf16[8,3,768,128]{3,2,1,0:T(8,128)(2,1)}, bf16[8,3,768,128]{3,2,1,0:T(8,...) custom-call(bf16[1024,768]{1,0:T(8,128)(2,1)} %get-tuple-element.114, ...), custom_call_target="tpu_custom_call", output_to_operand_aliasing={{8}: (7, {})} | custom-call | flops 28991029248 | bytes 31457280 | tf_op jit(solution)/shard_map/pallas_call | solution.py:1627
  168.7 61.1 %shard_map.301 = (bf16[576,768]{1,0:T(8,128)(2,1)}, bf16[576,768]{1,0:T(8,128)(2,1)}, bf16[592,768]{1,0:T(8,128)(2,1)}, bf16[592,768]{1,0:T(8,128)(2,1)}, bf16[8...) custom-call(f32[16,768]{1,0:T(8,128)} %get-tuple-element.104.ext.ref, ...), custom_call_target="tpu_custom_call", output_to_operand_aliasing={{7}: (8, {})} | custom-call | flops 32614907904 | bytes 31457280 | tf_op jit(solution)/shard_map/pallas_call | solution.py:1643
  229.8 62.0 %shard_map.302 = (bf16[576,768]{1,0:T(8,128)(2,1)}, bf16[576,768]{1,0:T(8,128)(2,1)}, bf16[592,768]{1,0:T(8,128)(2,1)}, bf16[3,384,128]{2,1,0:T(8,128)(2,1)}, bf...) custom-call(f32[16,768]{1,0:T(8,128)} %get-tuple-element.104.ext.ref, ...), custom_call_target="tpu_custom_call" | custom-call | flops 32614907904 | bytes 31457280 | tf_op jit(solution)/shard_map/pallas_call | solution.py:1662
  291.8 97.2 %shard_map.303 = (f32[1024,768]{1,0:T(8,128)}, bf16[768,768]{1,0:T(8,128)(2,1)}, f32[16,768]{1,0:T(8,128)}, bf16[1024,768]{1,0:T(8,128)(2,1)}, bf16[1024,768]{1,...) custom-call(s32[1,2]{1,0:T(1,128)} %starts.3, ...), custom_call_target="tpu_custom_call", output_to_operand_aliasing={{12}: (24, {})} | custom-call | flops 38252052480 | bytes 41943040 | tf_op jit(solution)/shard_map/pallas_call | solution.py:1726
  389.0 58.7 %shard_map.304 = (f32[1024,768]{1,0:T(8,128)}, bf16[1024,768]{1,0:T(8,128)(2,1)}, f32[4,96,768]{2,1,0:T(8,128)}, f32[16,768]{1,0:T(8,128)}, bf16[3,384,128]{2,1,...) custom-call(bf16[1024,768]{1,0:T(8,128)(2,1)} %bitcast.23, ...), custom_call_target="tpu_custom_call" | custom-call | flops 10871635968 | bytes 41943040 | tf_op jit(solution)/shard_map/pallas_call | solution.py:1754
  447.8 11.7 %shard_map.305 = (f32[4,768,256]{2,1,0:T(8,128)}, f32[4,768,256]{2,1,0:T(8,128)}, f32[4,256,768]{2,1,0:T(8,128)}, f32[1024,768]{1,0:T(8,128)}, bf16[1024,768]{1,...) custom-call(bf16[3,768,256]{2,1,0:T(8,128)(2,1)} %get-tuple-element., ...), custom_call_target="tpu_custom_call" | custom-call | bytes 27262976 | tf_op jit(solution)/shard_map/pallas_call | solution.py:1798
  459.4 1.5 copy.39
  (1 shorter events, 0.0 us)
Async XLA Ops:
  1.6 1.7 copy-start

commit v10 on v9

--- a/solution.py
+++ b/solution.py
@@ -577,6 +577,7 @@
             spread.along(-2)
             spread.over(1)
             spread.over(-1)
+            net.put(events[2], last, rest, net.rep, net.across)
 
         @pl.when(i == 5)
         def _():
@@ -584,7 +585,6 @@
             spread.along(-3)
             net.put(events[0], low, low, net.rep, net.up, inner)
             net.put(events[1], high, high, net.rep, net.down, inner)
-            net.put(events[2], last, rest, net.rep, net.across)
             net.put(events[3], near, near, net.rep, net.across)
             spread.over(2)
             spread.over(-2)
@@ -1200,9 +1200,6 @@
         def _():
             net.got(x_events[1], targets[1])
             chain.level(1)
-
-        @pl.when(i == 4)
-        def _():
             for m in range(3):
                 chain.take(2, m)
                 chain.send(1, m)
@@ -1446,13 +1443,16 @@
 
 def finish_kernel(
     e0, e1, e2, e3, wide, plain, q0, q1, q2, q3, weights, small,
-    gate, up, down, wide_out, plain_out, s_gate, s_up, s_down,
+    gate, up, down, wide_out, plain_out, s_gate_out, s_up_out, s_down_out,
     grad_q, grad_k, grad_v, grad_o, gain_one, gain_two, grad_router,
-    part, wide_in, plain_in, ready_gate, ready_up, ready_down, in_sems, out_sems,
+    part, wide_in, plain_in, quarters, weights_in, s_gate, s_up, s_down,
+    ready_gate, ready_up, ready_down, in_sems, out_sems,
 ):
     rep, shard = lax.axis_index("rep"), lax.axis_index("shard")
     pairs = [(e, part.at[o]) for o, e in enumerate((e0, e1, e2, e3))]
-    loads = copies_of(pairs + [(wide, wide_in), (plain, plain_in)], in_sems)
+    pairs += [(wide, wide_in), (plain, plain_in), (weights, weights_in)]
+    pairs += [(q, quarters.at[o]) for o, q in enumerate((q0, q1, q2, q3))]
+    loads = copies_of(pairs, in_sems)
     for copy in loads:
         copy.start()
     stores = []
@@ -1468,23 +1468,31 @@
         for copy in made:
             copy.start()
         stores += made
-    passed = ((wide_in, wide_out), (plain_in, plain_out))
-    for i, (a, b) in enumerate(passed):
-        loads[4 + i].wait()
-        copy = pltpu.make_async_copy(a, b, out_sems.at[12 + i])
+    passed = [(wide_in, wide_out), (plain_in, plain_out)]
+    grads = (grad_q, grad_k, grad_v, grad_o)
+    passed += [(weights_in.at[i], out) for i, out in enumerate(grads)]
+    for copy in loads[4:7]:
+        copy.wait()
+    made = [pltpu.make_async_copy(a, b, out_sems.at[12 + i]) for i, (a, b) in enumerate(passed)]
+    quarter, span = q0.shape[1:]
+    for copy in loads[7:]:
+        copy.wait()
+    for copy in made:
         copy.start()
-        stores.append(copy)
-    quarter, span = q0.shape[1:]
-    for o, piece in enumerate((q0, q1, q2, q3)):
-        owner = sibling(rep, o)
+    stores += made
+    for o in range(4):
+        piece, owner = quarters.at[o], sibling(rep, o)
         rows = pl.ds(pl.multiple_of(lax.div(owner, 2) * quarter, 128), quarter)
         cols = pl.ds(pl.multiple_of(lax.rem(owner, 2) * span, 128), span)
         s_gate[rows, cols] = piece[0].astype(F32)
         s_up[rows, cols] = piece[1].astype(F32)
         s_down[cols, rows] = piece[2].astype(F32).T
-    for i, out in enumerate((grad_q, grad_k, grad_v, grad_o)):
-        out[...] = weights[i]
-    rows, width = weights.shape[1:]
+    pairs = ((s_gate, s_gate_out), (s_up, s_up_out), (s_down, s_down_out))
+    made = [pltpu.make_async_copy(a, b, out_sems.at[18 + i]) for i, (a, b) in enumerate(pairs)]
+    for copy in made:
+        copy.start()
+    stores += made
+    rows, width = weights_in.shape[1:]
     tiny = small[...].astype(BF)
     pick = ones_where(iota((width, rows), 0) == iota((width, rows), 1) + shard * rows)
     gains = nn(tiny, pick)
@@ -1799,15 +1807,17 @@
             finish_kernel,
             banks[:3] + [wide, token_f] + banks[3:] + [shape((rows, width), F32)] * 4
             + [shape((1, rows), F32)] * 2 + [shape((rows, 4), F32)],
-            [ANY] * 6 + [VMEM] * 6,
-            [ANY] * 5 + [VMEM] * 10,
+            [ANY] * 11 + [VMEM],
+            [ANY] * 12 + [VMEM] * 3,
             [
                 pltpu.VMEM((4,) + expert_pack.shape, BF),
                 pltpu.VMEM((tokens, width), F32),
                 pltpu.VMEM((tokens, width), BF),
+                pltpu.VMEM((4,) + quarter, BF),
+                pltpu.VMEM((4, rows, width), F32),
             ]
-            + [pltpu.VMEM(b.shape, F32) for b in banks[:3]]
-            + [pltpu.SemaphoreType.DMA((6,)), pltpu.SemaphoreType.DMA((14,))],
+            + [pltpu.VMEM(b.shape, F32) for b in banks[3:] + banks[:3]]
+            + [pltpu.SemaphoreType.DMA((11,)), pltpu.SemaphoreType.DMA((21,))],
             moved=26 * 2**20,
         )(
             expert_total, *experts, grad_in, outputs,

time: 468 us -> 465 us (level)
    pallas_call x1, Pallas kernels: 97.2 us -> 91.4 us  [body(): call(back_kernel, outs + [shape(expert_pack.shape)] + [rows_out] * 3 + [s...]
where the time goes in v10:
time: 465 us; the launch traced here: 458 us
  Pallas kernels  453 us (97%)
    pallas_call x1, Pallas kernels, body(): call(back_kernel, outs + [shape(expert_pack.shape)] + [rows_out] * 3 + [s...  91.4 us
    pallas_call x1, Pallas kernels, body(): call(near_kernel, [rows_out] * 2 + [rows_back, shape(quarter), bank] + [r...  62.4 us
    pallas_call x1, Pallas kernels, body(): call(tail_kernel, [wide, token_f, shape((4, rows, width), F32), shape((16...  61.4 us
    pallas_call x1, Pallas kernels, body(): call(far_kernel, [rows_out] * 2 + [rows_back] * 2 + [bank, shape(quarters...  60.9 us
    pallas_call x1, Pallas kernels, body(): call(forward_kernel, outs + [shape((2, SLOTS) + my_half.shape), shape((SL...  60.1 us
    pallas_call x1, Pallas kernels, body(): call(head_kernel, firsts + packed[1:] + [shape((SLOTS,) + expert_shape.sh...  58.8 us
    pallas_call x1, Pallas kernels, body(): call(shared_kernel, [token_f] * 2 + [half_grads] * 3 + packed[:3] + [shap...  45.3 us
    pallas_call x1, Pallas kernels, body(): call(finish_kernel, banks[:3] + [wide, token_f] + banks[3:] + [shape((row...  12.6 us

profile of v10, /device:TPU:0, one launch (start us, length us, event | category | flops | bytes accessed | tf_op | source)
XLA Modules:
  0.0 457.9 jit_solution(18138832182016135317)
XLA Ops:
  0.6 0.7 fusion.4
  1.4 0.2 dynamic_update_slice.3.small
  1.6 0.0 copy-start
  1.6 1.7 copy.38.routes
  3.3 0.0 copy-done
  3.3 58.8 %shard_map.298 = (f32[8,1024]{1,0:T(8,128)}, f32[1024,128]{1,0:T(8,128)}, bf16[1024,768]{1,0:T(8,128)(2,1)}, bf16[1024,768]{1,0:T(8,128)(2,1)}, bf16[1024,768]{1...) custom-call(s32[1024,2]{1,0:T(8,128)} %copy.38.routes, ...), custom_call_target="tpu_custom_call" | custom-call | flops 7247757312 | bytes 25165824 | tf_op jit(solution)/shard_map/pallas_call | solution.py:1569
  62.1 60.1 %shard_map.299 = (bf16[1024,768]{1,0:T(8,128)(2,1)}, f32[1024,768]{1,0:T(8,128)}, f32[1024,768]{1,0:T(8,128)}, bf16[1024,768]{1,0:T(8,128)(2,1)}, f32[1024,128]{...) custom-call(s32[1,2]{1,0:T(1,128)} %starts.3, ...), custom_call_target="tpu_custom_call", output_to_operand_aliasing={{10}: (10, {})} | custom-call | flops 17716740096 | bytes 31457280 | tf_op jit(solution)/shard_map/pallas_call | solution.py:1608
  122.3 45.3 %shard_map.300 = (bf16[1024,768]{1,0:T(8,128)(2,1)}, bf16[1024,768]{1,0:T(8,128)(2,1)}, bf16[8,3,768,128]{3,2,1,0:T(8,128)(2,1)}, bf16[8,3,768,128]{3,2,1,0:T(8,...) custom-call(bf16[1024,768]{1,0:T(8,128)(2,1)} %get-tuple-element.114, ...), custom_call_target="tpu_custom_call", output_to_operand_aliasing={{8}: (7, {})} | custom-call | flops 28991029248 | bytes 31457280 | tf_op jit(solution)/shard_map/pallas_call | solution.py:1635
  167.6 60.9 %shard_map.301 = (bf16[576,768]{1,0:T(8,128)(2,1)}, bf16[576,768]{1,0:T(8,128)(2,1)}, bf16[592,768]{1,0:T(8,128)(2,1)}, bf16[592,768]{1,0:T(8,128)(2,1)}, bf16[8...) custom-call(f32[16,768]{1,0:T(8,128)} %get-tuple-element.104.ext.ref, ...), custom_call_target="tpu_custom_call", output_to_operand_aliasing={{7}: (8, {})} | custom-call | flops 32614907904 | bytes 31457280 | tf_op jit(solution)/shard_map/pallas_call | solution.py:1651
  228.5 62.4 %shard_map.302 = (bf16[576,768]{1,0:T(8,128)(2,1)}, bf16[576,768]{1,0:T(8,128)(2,1)}, bf16[592,768]{1,0:T(8,128)(2,1)}, bf16[3,384,128]{2,1,0:T(8,128)(2,1)}, bf...) custom-call(f32[16,768]{1,0:T(8,128)} %get-tuple-element.104.ext.ref, ...), custom_call_target="tpu_custom_call" | custom-call | flops 32614907904 | bytes 31457280 | tf_op jit(solution)/shard_map/pallas_call | solution.py:1670
  290.9 91.4 %shard_map.303 = (f32[1024,768]{1,0:T(8,128)}, bf16[768,768]{1,0:T(8,128)(2,1)}, f32[16,768]{1,0:T(8,128)}, bf16[1024,768]{1,0:T(8,128)(2,1)}, bf16[1024,768]{1,...) custom-call(s32[1,2]{1,0:T(1,128)} %starts.3, ...), custom_call_target="tpu_custom_call", output_to_operand_aliasing={{12}: (24, {})} | custom-call | flops 38252052480 | bytes 41943040 | tf_op jit(solution)/shard_map/pallas_call | solution.py:1734
  382.3 61.4 %shard_map.304 = (f32[1024,768]{1,0:T(8,128)}, bf16[1024,768]{1,0:T(8,128)(2,1)}, f32[4,96,768]{2,1,0:T(8,128)}, f32[16,768]{1,0:T(8,128)}, bf16[3,384,128]{2,1,...) custom-call(bf16[1024,768]{1,0:T(8,128)(2,1)} %bitcast.23, ...), custom_call_target="tpu_custom_call" | custom-call | flops 10871635968 | bytes 41943040 | tf_op jit(solution)/shard_map/pallas_call | solution.py:1762
  443.7 12.6 %shard_map.305 = (f32[4,768,256]{2,1,0:T(8,128)}, f32[4,768,256]{2,1,0:T(8,128)}, f32[4,256,768]{2,1,0:T(8,128)}, f32[1024,768]{1,0:T(8,128)}, bf16[1024,768]{1,...) custom-call(bf16[3,768,256]{2,1,0:T(8,128)(2,1)} %get-tuple-element., ...), custom_call_target="tpu_custom_call" | custom-call | bytes 27262976 | tf_op jit(solution)/shard_map/pallas_call | solution.py:1806
  456.3 1.5 copy.39
  (1 shorter events, 0.0 us)
Async XLA Ops:
  1.6 1.7 copy-start

commit v11 on v9

--- a/solution.py
+++ b/solution.py
@@ -94,22 +94,25 @@
     return 2 * lax.rem(lax.div(rep, 2) + o // 2, 2) + lax.rem(lax.rem(rep, 2) + o % 2, 2)
 
 
-def route_slots(rep, routes, routes_t, rank_out, slot_out):
-    tokens = routes.shape[0]
+def route_slots(rep, routes_t, rank_out, slot_out):
+    tokens = routes_t.shape[1]
     first, second = routes_t[0:1, :], routes_t[1:2, :]
     expert = iota((8, tokens), 0)
     chosen = (expert == first) | (expert == second)
     upper = ones_where(iota((tokens, tokens), 0) <= iota((tokens, tokens), 1))
     rank = nn(ones_where(chosen), upper) - 1.0
     rank_out[...] = jnp.where(chosen, rank, -1.0)
+    filler = jnp.zeros((6, tokens), F32)
+    named = jnp.concatenate([routes_t[...].astype(F32), filler], axis=0).T
     lane = iota((tokens, 128), 1)
-    one, two = routes[:, 0:1], routes[:, 1:2]
+    one, two = named[:, 0:1], named[:, 1:2]
+    lane_f = lane.astype(F32)
     lower = ones_where(iota((tokens, tokens), 0) >= iota((tokens, tokens), 1))
-    place = nn(lower, ones_where((lane == one) | (lane == two))) - 1.0
+    place = nn(lower, ones_where((lane_f == one) | (lane_f == two))) - 1.0
     for o in range(1, 4):
         place = place + jnp.where(lane == sibling(rep, o), float(o * CAP), 0.0)
-    slot_one = jnp.sum(jnp.where(lane == one, place, 0.0), axis=1, keepdims=True)
-    slot_two = jnp.sum(jnp.where(lane == two, place, 0.0), axis=1, keepdims=True)
+    slot_one = jnp.sum(jnp.where(lane_f == one, place, 0.0), axis=1, keepdims=True)
+    slot_two = jnp.sum(jnp.where(lane_f == two, place, 0.0), axis=1, keepdims=True)
     slot_out[...] = jnp.where(lane < 64, slot_one, slot_two)
 
 
@@ -349,7 +352,7 @@
 
 
 def head_kernel(
-    routes, routes_t, cot, x, wq_in, wk_in, wv_in, wo_in, small, cosine, sine,
+    routes_t, cot, x, wq_in, wk_in, wv_in, wo_in, small, cosine, sine,
     e_gate, e_up, e_down, s_gate, s_up, s_down,
     *refs,
 ):
@@ -391,7 +394,7 @@
     line.spread(0, piece)
     own = pltpu.make_async_copy(piece, bank.at[net.core, net.shard], own_sem)
     own.start()
-    route_slots(net.rep, routes, routes_t, rank, slot)
+    route_slots(net.rep, routes_t, rank, slot)
     events = [net.event() for _ in range(3)]
     for o, far in ((2, c2), (3, c3), (1, c1)):
         pack_row(net.rep, rank, cot, o, packed.at[o - 1])
@@ -442,11 +445,11 @@
 
 
 def plain_head_kernel(
-    routes, routes_t, cot, x, cosine, sine, wq, wk, wv, ext,
+    routes_t, cot, x, cosine, sine, wq, wk, wv, ext,
     rank, slot, q, k, v, c0, c1, c2, c3,
 ):
     rep = lax.axis_index("rep")
-    route_slots(rep, routes, routes_t, rank, slot)
+    route_slots(rep, routes_t, rank, slot)
     pack_rows(rep, rank, cot, (c0, c1, c2, c3))
     qkv_rows(x, ext, cosine, sine, wq, wk, wv, q, k, v)
 
@@ -577,6 +580,7 @@
             spread.along(-2)
             spread.over(1)
             spread.over(-1)
+            net.put(events[2], last, rest, net.rep, net.across)
 
         @pl.when(i == 5)
         def _():
@@ -584,7 +588,6 @@
             spread.along(-3)
             net.put(events[0], low, low, net.rep, net.up, inner)
             net.put(events[1], high, high, net.rep, net.down, inner)
-            net.put(events[2], last, rest, net.rep, net.across)
             net.put(events[3], near, near, net.rep, net.across)
             spread.over(2)
             spread.over(-2)
@@ -1200,9 +1203,6 @@
         def _():
             net.got(x_events[1], targets[1])
             chain.level(1)
-
-        @pl.when(i == 4)
-        def _():
             for m in range(3):
                 chain.take(2, m)
                 chain.send(1, m)
@@ -1561,7 +1561,7 @@
         rank, slot, q, k, v, wq, wk, wv, wo, ext, cot_own, expert_pack, my_half, *heads = call(
             head_kernel,
             firsts + packed[1:] + [shape((SLOTS,) + expert_shape.shape)],
-            [VMEM] * 11 + [ANY] * 6,
+            [VMEM] * 10 + [ANY] * 6,
             [ANY] * 17,
             [
                 pltpu.VMEM((2, SLOTS, 2 * rows + 16, width), BF),
@@ -1580,16 +1580,16 @@
             moved=24 * 2**20,
             group=0,
         )(
-            chosen, chosen.T, cot, x, query_weight, key_weight, value_weight, out_weight, small,
+            chosen.T, cot, x, query_weight, key_weight, value_weight, out_weight, small,
             cosine, sine, expert_gate, expert_up, expert_down, shared_gate, shared_up, shared_down,
         )
         *cot_in, expert_bank = heads
         cot_in = [cot_own, *cot_in]
     else:
         rank, slot, q, k, v, *cot_out = call(
-            plain_head_kernel, outs + packed, [VMEM] * 10, [VMEM] * 9, flops=work,
+            plain_head_kernel, outs + packed, [VMEM] * 9, [VMEM] * 9, flops=work,
             moved=24 * 2**20,
-        )(chosen, chosen.T, cot, x, cosine, sine, wq, wk, wv, ext)
+        )(chosen.T, cot, x, cosine, sine, wq, wk, wv, ext)
         cot_in = [cot_out[0]] + [to_rep(cot_out[o], o) for o in (1, 2, 3)]
 
     outs = [token_f, shape((tokens, width), F32), shape((tokens, width), F32), token_f]

time: 468 us -> 462 us (0.987)
    pallas_call x1, Pallas kernels: 97.2 us -> 91.4 us  [body(): call(back_kernel, outs + [shape(expert_pack.shape)] + [rows_out] * 3 + [s...]
where the time goes in v11:
time: 462 us; the launch traced here: 456 us
  Pallas kernels  452 us (98%)
    pallas_call x1, Pallas kernels, body(): call(back_kernel, outs + [shape(expert_pack.shape)] + [rows_out] * 3 + [s...  91.4 us
    pallas_call x1, Pallas kernels, body(): call(near_kernel, [rows_out] * 2 + [rows_back, shape(quarter), bank] + [r...  62.4 us
    pallas_call x1, Pallas kernels, body(): call(tail_kernel, [wide, token_f, shape((4, rows, width), F32), shape((16...  61.4 us
    pallas_call x1, Pallas kernels, body(): call(far_kernel, [rows_out] * 2 + [rows_back] * 2 + [bank, shape(quarters...  60.9 us
    pallas_call x1, Pallas kernels, body(): call(forward_kernel, outs + [shape((2, SLOTS) + my_half.shape), shape((SL...  60.1 us
    pallas_call x1, Pallas kernels, body(): call(head_kernel, firsts + packed[1:] + [shape((SLOTS,) + expert_shape.sh...  58.7 us
    pallas_call x1, Pallas kernels, body(): call(shared_kernel, [token_f] * 2 + [half_grads] * 3 + packed[:3] + [shap...  45.3 us
    pallas_call x1, Pallas kernels, body(): call(finish_kernel, banks[:3] + [wide, token_f] + banks[3:] + [shape((row...  11.7 us

profile of v11, /device:TPU:0, one launch (start us, length us, event | category | flops | bytes accessed | tf_op | source)
XLA Modules:
  0.0 455.8 jit_solution(9543251818845659650)
XLA Ops:
  0.6 0.7 fusion.4
  1.4 0.2 dynamic_update_slice.3.small
  1.6 0.0 copy-start
  1.6 0.6 copy-done
  2.2 58.7 %shard_map.298 = (f32[8,1024]{1,0:T(8,128)}, f32[1024,128]{1,0:T(8,128)}, bf16[1024,768]{1,0:T(8,128)(2,1)}, bf16[1024,768]{1,0:T(8,128)(2,1)}, bf16[1024,768]{1...) custom-call(s32[2,1024]{1,0:T(2,128)} %bitcast.23, ...), custom_call_target="tpu_custom_call" | custom-call | flops 7247757312 | bytes 25165824 | tf_op jit(solution)/shard_map/pallas_call | solution.py:1561
  60.9 60.1 %shard_map.299 = (bf16[1024,768]{1,0:T(8,128)(2,1)}, f32[1024,768]{1,0:T(8,128)}, f32[1024,768]{1,0:T(8,128)}, bf16[1024,768]{1,0:T(8,128)(2,1)}, f32[1024,128]{...) custom-call(s32[1,2]{1,0:T(1,128)} %starts.3, ...), custom_call_target="tpu_custom_call", output_to_operand_aliasing={{10}: (10, {})} | custom-call | flops 17716740096 | bytes 31457280 | tf_op jit(solution)/shard_map/pallas_call | solution.py:1600
  121.0 45.3 %shard_map.300 = (bf16[1024,768]{1,0:T(8,128)(2,1)}, bf16[1024,768]{1,0:T(8,128)(2,1)}, bf16[8,3,768,128]{3,2,1,0:T(8,128)(2,1)}, bf16[8,3,768,128]{3,2,1,0:T(8,...) custom-call(bf16[1024,768]{1,0:T(8,128)(2,1)} %get-tuple-element.114, ...), custom_call_target="tpu_custom_call", output_to_operand_aliasing={{8}: (7, {})} | custom-call | flops 28991029248 | bytes 31457280 | tf_op jit(solution)/shard_map/pallas_call | solution.py:1627
  166.3 60.9 %shard_map.301 = (bf16[576,768]{1,0:T(8,128)(2,1)}, bf16[576,768]{1,0:T(8,128)(2,1)}, bf16[592,768]{1,0:T(8,128)(2,1)}, bf16[592,768]{1,0:T(8,128)(2,1)}, bf16[8...) custom-call(f32[16,768]{1,0:T(8,128)} %get-tuple-element.104.ext.ref, ...), custom_call_target="tpu_custom_call", output_to_operand_aliasing={{7}: (8, {})} | custom-call | flops 32614907904 | bytes 31457280 | tf_op jit(solution)/shard_map/pallas_call | solution.py:1643
  227.2 62.4 %shard_map.302 = (bf16[576,768]{1,0:T(8,128)(2,1)}, bf16[576,768]{1,0:T(8,128)(2,1)}, bf16[592,768]{1,0:T(8,128)(2,1)}, bf16[3,384,128]{2,1,0:T(8,128)(2,1)}, bf...) custom-call(f32[16,768]{1,0:T(8,128)} %get-tuple-element.104.ext.ref, ...), custom_call_target="tpu_custom_call" | custom-call | flops 32614907904 | bytes 31457280 | tf_op jit(solution)/shard_map/pallas_call | solution.py:1662
  289.6 91.4 %shard_map.303 = (f32[1024,768]{1,0:T(8,128)}, bf16[768,768]{1,0:T(8,128)(2,1)}, f32[16,768]{1,0:T(8,128)}, bf16[1024,768]{1,0:T(8,128)(2,1)}, bf16[1024,768]{1,...) custom-call(s32[1,2]{1,0:T(1,128)} %starts.3, ...), custom_call_target="tpu_custom_call", output_to_operand_aliasing={{12}: (24, {})} | custom-call | flops 38252052480 | bytes 41943040 | tf_op jit(solution)/shard_map/pallas_call | solution.py:1726
  381.0 61.4 %shard_map.304 = (f32[1024,768]{1,0:T(8,128)}, bf16[1024,768]{1,0:T(8,128)(2,1)}, f32[4,96,768]{2,1,0:T(8,128)}, f32[16,768]{1,0:T(8,128)}, bf16[3,384,128]{2,1,...) custom-call(bf16[1024,768]{1,0:T(8,128)(2,1)} %bitcast.21, ...), custom_call_target="tpu_custom_call" | custom-call | flops 10871635968 | bytes 41943040 | tf_op jit(solution)/shard_map/pallas_call | solution.py:1754
  442.4 11.7 %shard_map.305 = (f32[4,768,256]{2,1,0:T(8,128)}, f32[4,768,256]{2,1,0:T(8,128)}, f32[4,256,768]{2,1,0:T(8,128)}, f32[1024,768]{1,0:T(8,128)}, bf16[1024,768]{1,...) custom-call(bf16[3,768,256]{2,1,0:T(8,128)(2,1)} %get-tuple-element., ...), custom_call_target="tpu_custom_call" | custom-call | bytes 27262976 | tf_op jit(solution)/shard_map/pallas_call | solution.py:1798
  454.1 1.5 copy.38
  (1 shorter events, 0.0 us)
Async XLA Ops:
  1.6 0.6 copy-start
